TPU v7x, 32 devices: a whole 2x2x4 slice. The times are simulated.
32 devices in a mesh: seq: 4 (over y, x), mp: 8 (over z, core).
Axes of the slice: x: 2, y: 2, z: 4, core: 2. Of those that a mesh axis runs over, the one named last changes fastest.
Arguments:
- incoming: bfloat16 [2048, 4096], P('seq', 'mp'), may hold values from -12 to 12
- queries: bfloat16 [2048, 4096], P('seq', 'mp'), may hold values from -5 to 5
- key_vecs: bfloat16 [2048, 4096], P('seq', 'mp'), may hold values from -5 to 5
- value_vecs: bfloat16 [2048, 4096], P('seq', 'mp'), may hold values from -6 to 6
- w_out: bfloat16 [4096, 4096], P(None, 'mp'), may hold values from -0.09375 to 0.09375
- norm_gain: float32 [4096], P('mp'), may hold values from 0.25 to 1.75
- filters: bfloat16 [4096, 256], P('mp'), may hold values from -0.375 to 0.375
- filter_len: int32 [4096], P('mp'), may hold values from 128 to 256, as said below
- skip_gain: float32 [4096], P('mp'), may hold values from 0.5 to 1.5
- slot_map: int32 [8], replicated, may hold values from 0 to 7, as said below
Outputs:
- layer_out: bfloat16 [2048, 4096], P('seq', 'mp')
Inputs may be any that keep to these rules, and one draw needn't show every extreme that they name: `slot_map`: slots 2 * i and 2 * i + 1, the rows of index i of seq, hold blocks i and 7 - i, in either order. `filter_len`: some channel uses all 256 taps.
All inputs are finite; a program needn't handle non-finite values.
Results may differ from a plain program's by a relative error of at most 0.0055.
Values may be sent and summed in bfloat16 or wider, within the bound.
No kernel may reach another device: no remote copies, remote signals or barrier semaphores. Data moves between devices by JAX's collectives and lax.ppermute only.
A program may use at most 64 MiB of HBM per device.

v0:
```python
import math

import jax
import jax.numpy as jnp
from jax import lax
from jax.sharding import PartitionSpec as P

D = 4096
HD = 128


EPS = 1e-05
NEG = -1e30


def shifted(block, axis, distance):
    devices = range(lax.axis_size(axis))
    route = [(i - distance, i) for i in devices if i - distance in devices]
    return lax.ppermute(block, axis, route)


def block_update(running, query_heads, query_pos, key_part, value_part, key_pos):
    peak_now, total_now, accum_now = running
    key_count = key_part.shape[0]
    head_count = query_heads.shape[1]
    key_heads = key_part.reshape(key_count, head_count, HD)
    value_heads = value_part.reshape(key_count, head_count, HD)
    scores = jnp.einsum(
        "thd,shd->ths", query_heads, key_heads, preferred_element_type=jnp.float32
    ) * HD ** (-0.5)
    allowed = key_pos[None, None, :] <= query_pos[:, None, None]
    masked = jnp.where(allowed, scores, NEG)
    peak_next = jnp.maximum(peak_now, jnp.max(masked, axis=2))
    weights = jnp.where(allowed, jnp.exp(masked - peak_next[:, :, None]), 0.0)
    factor = jnp.exp(peak_now - peak_next)
    total_next = total_now * factor + jnp.sum(weights, axis=2)
    summed = jnp.einsum(
        "ths,shd->thd",
        weights.astype(jnp.bfloat16),
        value_heads,
        preferred_element_type=jnp.float32,
    )
    accum_next = accum_now * factor[:, :, None] + summed
    return (peak_next, total_next, accum_next)


def guarded_update(running, query_heads, query_pos, key_part, value_part, key_pos):
    return block_update(running, query_heads, query_pos, key_part, value_part, key_pos)


def attend_keys(running, query_heads, query_pos, key_part, value_part, key_pos):
    key_count = key_part.shape[0]
    block_rows = 1024
    block_count = key_count // block_rows

    def attend_advance(state, block_item):
        return (
            guarded_update(
                state, query_heads, query_pos, block_item[0], block_item[1], block_item[2]
            ),
            None,
        )

    stacked = (
        key_part.reshape(block_count, block_rows, -1),
        value_part.reshape(block_count, block_rows, -1),
        key_pos.reshape(block_count, block_rows),
    )
    running, _ = lax.scan(attend_advance, running, stacked)
    return running


def causal_window(extended, taps_lag):
    pair_count, twice, width = extended.shape
    length = twice // 2
    tap_count = taps_lag.shape[0]
    inner = math.gcd(tap_count, 16)

    def causal_advance(block, accum):
        base = block * inner
        window = lax.dynamic_slice_in_dim(
            extended, length - base - inner + 1, length + inner - 1, 1
        ).astype(jnp.float32)
        tap_block = lax.dynamic_slice_in_dim(taps_lag, base, inner, 0).astype(jnp.float32)
        for lag in range(inner):
            offset = inner - 1 - lag
            accum = accum + tap_block[lag][None, None, :] * window[:, offset : offset + length]
        return accum

    start = jnp.zeros((pair_count, length, width), jnp.float32)
    return lax.fori_loop(0, tap_count // inner, causal_advance, start)


def on_device(
    incoming,
    queries,
    key_vecs,
    value_vecs,
    w_out,
    norm_gain,
    filters,
    filter_len,
    skip_gain,
    slot_map,
):
    tok_rows, local_width = queries.shape
    span_rows = tok_rows // 2
    head_count = local_width // HD
    all_rows = slot_map.shape[0] * span_rows
    row_ids = jnp.arange(all_rows, dtype=jnp.int32)
    position = (
        jnp.repeat(slot_map, span_rows, total_repeat_length=all_rows) * span_rows
        + row_ids % span_rows
    )
    seq_rank = lax.axis_index("seq")
    seq_size = lax.axis_size("seq")
    own_pos = lax.dynamic_slice_in_dim(position, seq_rank * tok_rows, tok_rows)
    query_heads = queries.reshape(tok_rows, head_count, HD)
    piece = (
        lax.all_gather(key_vecs, "seq", axis=0, tiled=True),
        lax.all_gather(value_vecs, "seq", axis=0, tiled=True),
    )
    key_pos = lax.slice_in_dim(position, 0, piece[0].shape[0], axis=0)
    running = attend_keys(
        (
            jnp.full((tok_rows, head_count), NEG, jnp.float32),
            jnp.zeros((tok_rows, head_count), jnp.float32),
            jnp.zeros((tok_rows, head_count, HD), jnp.float32),
        ),
        query_heads,
        own_pos,
        piece[0],
        piece[1],
        key_pos,
    )
    attention = (running[2] / running[1][:, :, None]).reshape(-1, local_width).astype(jnp.bfloat16)
    projected = jnp.dot(
        lax.all_gather(attention, "mp", axis=1, tiled=True),
        w_out,
        preferred_element_type=jnp.float32,
    )
    residual = incoming.astype(jnp.float32) + projected
    square_total = lax.psum(jnp.sum(residual * residual, axis=1), "mp")
    normed = (residual * lax.rsqrt(square_total / D + EPS)[:, None] * norm_gain[None, :]).astype(
        jnp.bfloat16
    )
    tap_count = filters.shape[1]
    taps = jnp.where(
        jnp.arange(tap_count, dtype=jnp.int32)[None, :] < filter_len[:, None],
        filters,
        jnp.zeros((), filters.dtype),
    )
    taps_lag = taps.T
    pair_ids = lax.dynamic_slice_in_dim(slot_map, 2 * seq_rank, 2)
    low_first = pair_ids[0] < pair_ids[1]
    slots = normed.reshape(2, span_rows, local_width)
    low_rows = jnp.where(low_first, slots[0], slots[1])
    high_rows = jnp.where(low_first, slots[1], slots[0])
    own_pair = jnp.stack([low_rows, high_rows])
    last_rank = seq_rank == seq_size - 1
    low_before = shifted(own_pair[0], "seq", 1)
    high_before = shifted(own_pair[1], "seq", -1)
    high_before = jnp.where(last_rank, own_pair[0], high_before)
    before_pair = jnp.stack([low_before, high_before])
    conv_pair = causal_window(jnp.concatenate([before_pair, own_pair], axis=1), taps_lag)
    conv_slots = jnp.where(low_first, conv_pair, conv_pair[::-1])
    conv_rows = conv_slots.reshape(tok_rows, local_width)
    layer_out = residual + conv_rows + skip_gain[None, :] * normed.astype(jnp.float32)
    return layer_out.astype(jnp.bfloat16)


def solution(mesh):
    placed = (
        P("seq", "mp"),
        P("seq", "mp"),
        P("seq", "mp"),
        P("seq", "mp"),
        P(None, "mp"),
        P("mp"),
        P("mp", None),
        P("mp"),
        P("mp"),
        P(),
    )
    return jax.shard_map(
        on_device, mesh=mesh, in_specs=placed, out_specs=P("seq", "mp"), check_vma=False
    )
```

profile of v0, /device:TPU:0, one launch (start us, length us, event | category | flops | bytes accessed | tf_op | source)
XLA Modules:
  0.0 262.8 jit_solution(16822269055426606901)
XLA Ops:
  6.5 0.7 all-gather.6.cloned.1.call-update
  7.3 0.7 all-gather.4.cloned.1.call-update
  8.1 1.6 fusion.44
  9.7 5.8 %select_multiply_fusion.2 = s32[2048]{0:T(1024)S(1)} fusion(pred[2048]{0:T(1024)(128)(4,1)} %constant.258, pred[2048]{0:T(1024)(128)(4,1)} %constant.259, pred[2048]{0:T(1024)(128)(4,1)} %constant.260, pred[2048]{0:T(1024)(128)(4,1)} %constant.261, pred[2048]{0:T(1024)(128)(4,1)} %constant.262, pred[2048]{0:T(1024)(128)(4,1)} %constant.263, ...), kind=kLoop, calls=%fused_computation.75 | loop fusion | flops 16384 | bytes 22560 | tf_op jit(solution)/shard_map/mul | solution.py:112
  15.5 1.3 copy.21
  16.8 0.3 copy.23
  17.2 30.0 %all-gather.6.cloned.1.call-done = bf16[2048,512]{1,0:T(8,128)(2,1)} async-done(((bf16[512,512]{1,0:T(8,128)(2,1)}), bf16[2048,512]{1,0:T(8,128)(2,1)}) %all-gather.6.cloned.1.call-update) | async-done | bytes 2097168 | tf_op jit(solution)/shard_map/all_gather | solution.py:121
  47.1 37.0 %all-gather.4.cloned.1.call-done = bf16[2048,512]{1,0:T(8,128)(2,1)} async-done(((bf16[512,512]{1,0:T(8,128)(2,1)}), bf16[2048,512]{1,0:T(8,128)(2,1)}) %all-gather.4.cloned.1.call-update) | async-done | bytes 2097168 | tf_op jit(solution)/shard_map/all_gather | solution.py:120
  84.2 43.4 %while.34 = (s32[]{:T(128)}, f32[512,4]{0,1:T(4,128)S(1)}, f32[512,4]{0,1:T(4,128)S(1)}, f32[512,4,128]{0,2,1:T(8,128)}, s32[2,1024]{1,0:T(2,128)S(1)}, /*index=...) while((s32[]{:T(128)}, f32[512,4]{0,1:T(4,128)S(1)}, ...), condition=%wide.region_3.4_spmd.clone, body=%wide.region_0.3_spmd.clone.sunk | while | flops 1102325760 | bytes 40515708 | solution.py:69
  84.2 0.4 broadcast_compare_fusion.2
  84.5 2.7 %constant_dynamic-slice_fusion.6 = (bf16[1,1024,512]{2,1,0:T(8,128)(2,1)S(1)}, bf16[1,1024,512]{2,1,0:T(8,128)(2,1)}) fusion(bf16[2,1024,512]{2,1,0:T(8,128)(2,1)} %get-tuple-element.489, s32[]{:T(128)} %get-tuple-element.470, bf16[2,1024,512]{2,1,0:T(8,128)(2,1)} %get-tuple-element.487), kind=kLoop, calls=%fused_computation.15.clone.1 | loop fusion | bytes 4194308 | tf_op jit(solution)/shard_map/while/body/jit(dynamic_index_in_dim)/dynamic_slice | solution.py:69
  87.2 1.5 copy.32
  88.7 5.0 %fusion.65 = (f32[512,4]{0,1:T(4,128)S(1)}, f32[4,1024,512]{2,1,0:T(8,128)}) fusion(pred[512,1024]{0,1:T(8,128)(4,1)S(1)} %broadcast_compare_fusion.2, bf16[1024,4,128]{0,2,1:T(8,128)(2,1)S(1)} %bitcast.122, bf16[512,4,128]{2,0,1:T(8,128)(2,1)S(1)} %get-tuple-element.488), kind=kOutput, calls=%fused_computation.2.clone.1 | convolution fusion | flops 543160320 | bytes 10493952 | tf_op jit(solution)/shard_map/while/body/eval_jaxpr/thd,shd->ths/dot_general | solution.py:28
  93.7 4.5 %fusion.66 = f32[512,4]{0,1:T(4,128)S(1)} fusion(f32[4,1024,512]{2,1,0:T(8,128)} %get-tuple-element.435, f32[512,4]{0,1:T(4,128)S(1)} %select_maximum_fusion.2, pred[512,1024]{0,1:T(8,128)(4,1)S(1)} %broadcast_compare_fusion.2), kind=kLoop, calls=%fused_computation.4.clone.1 | loop fusion | flops 10483712 | bytes 8929280 | tf_op jit(solution)/shard_map/while/body/eval_jaxpr/reduce_sum | solution.py:36
  98.2 0.5 copy.33
  98.8 7.0 %fusion.68 = f32[512,4,128]{0,2,1:T(8,128)} fusion(bf16[1024,4,128]{0,2,1:T(8,128)(2,1)S(1)} %bitcast.123, f32[4,1024,512]{2,1,0:T(8,128)} %get-tuple-element.435, f32[512,4]{0,1:T(4,128)S(1)} %select_maximum_fusion.2, pred[512,1024]{0,1:T(8,128)(4,1)S(1)} %broadcast_compare_fusion.2, f32[512,4,128]{0,2,1:T(8,128)} %get-tuple-element.473, ...), kind=kOutput, calls=%fused_computation.8.clone.1 | convolution fusion | flops 548143104 | bytes 12075009 | tf_op jit(solution)/shard_map/while/body/eval_jaxpr/ths,shd->thd/dot_general | solution.py:37
  105.7 0.4 broadcast_compare_fusion.2
  106.1 2.7 %constant_dynamic-slice_fusion.6 = (bf16[1,1024,512]{2,1,0:T(8,128)(2,1)S(1)}, bf16[1,1024,512]{2,1,0:T(8,128)(2,1)}) fusion(bf16[2,1024,512]{2,1,0:T(8,128)(2,1)} %get-tuple-element.489, s32[]{:T(128)} %get-tuple-element.470, bf16[2,1024,512]{2,1,0:T(8,128)(2,1)} %get-tuple-element.487), kind=kLoop, calls=%fused_computation.15.clone.1 | loop fusion | bytes 4194308 | tf_op jit(solution)/shard_map/while/body/jit(dynamic_index_in_dim)/dynamic_slice | solution.py:69
  108.8 1.5 copy.32
  110.3 5.0 %fusion.65 = (f32[512,4]{0,1:T(4,128)S(1)}, f32[4,1024,512]{2,1,0:T(8,128)}) fusion(pred[512,1024]{0,1:T(8,128)(4,1)S(1)} %broadcast_compare_fusion.2, bf16[1024,4,128]{0,2,1:T(8,128)(2,1)S(1)} %bitcast.122, bf16[512,4,128]{2,0,1:T(8,128)(2,1)S(1)} %get-tuple-element.488), kind=kOutput, calls=%fused_computation.2.clone.1 | convolution fusion | flops 543160320 | bytes 10493952 | tf_op jit(solution)/shard_map/while/body/eval_jaxpr/thd,shd->ths/dot_general | solution.py:28
  115.3 4.5 %fusion.66 = f32[512,4]{0,1:T(4,128)S(1)} fusion(f32[4,1024,512]{2,1,0:T(8,128)} %get-tuple-element.435, f32[512,4]{0,1:T(4,128)S(1)} %select_maximum_fusion.2, pred[512,1024]{0,1:T(8,128)(4,1)S(1)} %broadcast_compare_fusion.2), kind=kLoop, calls=%fused_computation.4.clone.1 | loop fusion | flops 10483712 | bytes 8929280 | tf_op jit(solution)/shard_map/while/body/eval_jaxpr/reduce_sum | solution.py:36
  119.8 0.5 copy.33
  120.3 7.2 %fusion.68 = f32[512,4,128]{0,2,1:T(8,128)} fusion(bf16[1024,4,128]{0,2,1:T(8,128)(2,1)S(1)} %bitcast.123, f32[4,1024,512]{2,1,0:T(8,128)} %get-tuple-element.435, f32[512,4]{0,1:T(4,128)S(1)} %select_maximum_fusion.2, pred[512,1024]{0,1:T(8,128)(4,1)S(1)} %broadcast_compare_fusion.2, f32[512,4,128]{0,2,1:T(8,128)} %get-tuple-element.473, ...), kind=kOutput, calls=%fused_computation.8.clone.1 | convolution fusion | flops 548143104 | bytes 12075009 | tf_op jit(solution)/shard_map/while/body/eval_jaxpr/ths,shd->thd/dot_general | solution.py:37
  127.5 2.1 divide_convert_fusion
  129.8 0.7 fusion.43
  131.8 44.9 %all-gather.8.cloned.1.call-done = bf16[512,4096]{0,1:T(8,128)(2,1)} async-done(((bf16[512,512]{0,1:T(8,128)(2,1)}), bf16[512,4096]{0,1:T(8,128)(2,1)}) %all-gather.8.cloned.1.call-update) | async-done | bytes 4194320 | tf_op jit(solution)/shard_map/all_gather | solution.py:138
  176.7 5.9 %multiply_reduce_fusion = (f32[512]{0:T(512)S(1)}, f32[512,512]{1,0:T(8,128)S(1)}) fusion(bf16[512,4096]{0,1:T(8,128)(2,1)} %all-gather.8.cloned.1.call-done, bf16[4096,512]{1,0:T(8,128)(2,1)} %param.20, bf16[512,512]{1,0:T(8,128)(2,1)} %param.16), kind=kOutput, calls=%fused_computation.62 | convolution fusion | flops 2148531712 | bytes 9963520 | tf_op jit(solution)/shard_map/dot_general | solution.py:137
  182.6 14.8 %psum.7 = f32[512]{0:T(512)S(1)} all-reduce(f32[512]{0:T(512)S(1)} %get-tuple-element.333), channel_id=1, replica_groups=mesh['seq'=4,'mp'=8] {'mp'}, use_global_device_ids=true, to_apply=%region_5.6 | all-reduce | flops 512 | bytes 4096 | tf_op jit(solution)/shard_map/psum | solution.py:143
  197.7 1.3 collective-permute-start.1
  199.1 7.3 %collective-permute-done.1 = bf16[256,512]{1,0:T(8,128)(2,1)S(1)} collective-permute-done((bf16[256,512]{1,0:T(8,128)(2,1)S(1)}, bf16[256,512]{1,0:T(8,128)(2,1)S(1)}, u32[]{:S(2)}, u32[]{:S(2)}) %collective-permute-start.1) | collective-permute-done | bytes 262176 | tf_op jit(solution)/shard_map/ppermute | solution.py:19
  206.5 4.3 %collective-permute-start = (bf16[256,512]{1,0:T(8,128)(2,1)S(1)}, bf16[256,512]{1,0:T(8,128)(2,1)S(1)}, u32[]{:S(2)}, u32[]{:S(2)}) collective-permute-start(bf16[256,512]{1,0:T(8,128)(2,1)S(1)} %get-tuple-element.302), channel_id=1, source_target_pairs={{0,8},{8,16},{16,24},{1,9},{9,17},{17,25},{2,10},{10,18},{18,26},{... | collective-permute-start | bytes 786440 | tf_op jit(solution)/shard_map/ppermute | solution.py:19
  210.9 3.7 %collective-permute-done = bf16[256,512]{1,0:T(8,128)(2,1)S(1)} collective-permute-done((bf16[256,512]{1,0:T(8,128)(2,1)S(1)}, bf16[256,512]{1,0:T(8,128)(2,1)S(1)}, u32[]{:S(2)}, u32[]{:S(2)}) %collective-permute-start) | collective-permute-done | bytes 262176 | tf_op jit(solution)/shard_map/ppermute | solution.py:19
  214.7 39.1 %while.35 = (s32[]{:T(128)}, f32[2,256,512]{2,1,0:T(8,128)S(1)}, bf16[256,512]{1,0:T(8,128)(2,1)S(1)}, bf16[2,512,512]{2,1,0:T(8,128)(2,1)S(1)}, s32[]{:T(128)},...) while((s32[]{:T(128)}, f32[2,256,512]{2,1,0:T(8,128)S(1)}, ...), condition=%wide.region_7.8_spmd.clone, body=%wide.region_6.7_spmd.clone.sunk | while | flops 8936459 | bytes 20687056 | solution.py:91
  214.8 0.2 dynamic-slice_convert_fusion.4
  215.0 2.2 fusion.70
  217.2 0.2 dynamic-slice_convert_fusion.4
  217.4 2.2 fusion.70
  219.7 0.2 dynamic-slice_convert_fusion.4
  219.9 2.2 fusion.70
  222.1 0.2 dynamic-slice_convert_fusion.4
  222.3 2.2 fusion.70
  224.6 0.2 dynamic-slice_convert_fusion.4
  224.8 2.2 fusion.70
  227.0 0.2 dynamic-slice_convert_fusion.4
  227.2 2.2 fusion.70
  229.5 0.2 dynamic-slice_convert_fusion.4
  229.7 2.2 fusion.70
  231.9 0.2 dynamic-slice_convert_fusion.4
  232.1 2.2 fusion.70
  234.4 0.2 dynamic-slice_convert_fusion.4
  234.6 2.2 fusion.70
  236.8 0.2 dynamic-slice_convert_fusion.4
  237.0 2.2 fusion.70
  239.3 0.2 dynamic-slice_convert_fusion.4
  239.4 2.2 fusion.70
  241.7 0.2 dynamic-slice_convert_fusion.4
  241.9 2.2 fusion.70
  244.3 2.2 fusion.70
  246.6 0.2 dynamic-slice_convert_fusion.4
  246.8 2.2 fusion.70
  249.2 2.2 fusion.70
  251.5 0.2 dynamic-slice_convert_fusion.4
  251.7 2.2 fusion.70
  254.0 2.3 fusion.33
  (75 shorter events, 2.0 us)
Async XLA Ops:
  6.5 40.6 %all-gather.6.cloned.1.call-start = ((), (), s32[]{:S(2)}) async-start(), calls=%async_computation.1 | async-start | bytes 2621440 | tf_op jit(solution)/shard_map/all_gather | solution.py:121
  7.3 76.9 %all-gather.4.cloned.1.call-start = ((), (), s32[]{:S(2)}) async-start(), calls=%async_computation | async-start | bytes 2621440 | tf_op jit(solution)/shard_map/all_gather | solution.py:120
  8.0 168.7 %all-gather.8.cloned.1.call-start = ((), (), s32[]{:S(2)}) async-start(), calls=%async_computation.2 | async-start | bytes 4718592 | tf_op jit(solution)/shard_map/all_gather | solution.py:138
  84.2 45.5 %copy-start.2 = (s32[8]{0:T(128)S(1)}, s32[8]{0:T(128)}, u32[]{:S(2)}) copy-start(s32[8]{0:T(128)} %param.25) | copy-start | bytes 100
  131.8 65.7 %copy-start.3 = (f32[512]{0:T(512)S(1)}, f32[512]{0:T(512)}, u32[]{:S(2)}) copy-start(f32[512]{0:T(512)} %param.21) | copy-start | bytes 6148
  131.8 67.2 %copy-start.1 = (bf16[512,256]{1,0:T(8,128)(2,1)S(1)}, bf16[512,256]{1,0:T(8,128)(2,1)}, u32[]{:S(2)}) copy-start(bf16[512,256]{1,0:T(8,128)(2,1)} %param.22) | copy-start | bytes 786436
  182.6 28.1 %copy-start = (f32[512,512]{1,0:T(8,128)}, f32[512,512]{1,0:T(8,128)S(1)}, u32[]{:S(2)}) copy-start(f32[512,512]{1,0:T(8,128)S(1)} %get-tuple-element.334) | copy-start | bytes 3145732
  182.6 28.2 %copy-start.4 = (s32[512]{0:T(512)S(1)}, s32[512]{0:T(512)}, u32[]{:S(2)}) copy-start(s32[512]{0:T(512)} %param.23) | copy-start | bytes 6148
  197.7 8.8 %collective-permute-start.1 = (bf16[256,512]{1,0:T(8,128)(2,1)S(1)}, bf16[256,512]{1,0:T(8,128)(2,1)S(1)}, u32[]{:S(2)}, u32[]{:S(2)}) collective-permute-start(bf16[256,512]{1,0:T(8,128)(2,1)S(1)} %broadcast_select_fusion), channel_id=1, source_target_pairs={{8,0},{16,8},{24,16},{9,1},{17,9},{25,17},{10,2},{18,10},{26,18},{... | collective-permute-start | bytes 786440 | tf_op jit(solution)/shard_map/ppermute | solution.py:19
  206.5 8.2 %collective-permute-start = (bf16[256,512]{1,0:T(8,128)(2,1)S(1)}, bf16[256,512]{1,0:T(8,128)(2,1)S(1)}, u32[]{:S(2)}, u32[]{:S(2)}) collective-permute-start(bf16[256,512]{1,0:T(8,128)(2,1)S(1)} %get-tuple-element.302), channel_id=1, source_target_pairs={{0,8},{8,16},{16,24},{1,9},{9,17},{17,25},{2,10},{10,18},{18,26},{... | collective-permute-start | bytes 786440 | tf_op jit(solution)/shard_map/ppermute | solution.py:19
  214.7 39.3 %copy-start.5 = (f32[512]{0:T(512)S(1)}, f32[512]{0:T(512)}, u32[]{:S(2)}) copy-start(f32[512]{0:T(512)} %param.24) | copy-start | bytes 6148
Sparse Core Ops, SparseCore 0:
  9.2 37.8 all-gather.5
  49.0 35.1 all-gather.3
  129.8 46.8 all-gather.7
where the time goes:
time: 263 us
  waiting for transfers between devices  124 us (47%)
  other arithmetic  58.3 us (22%)
  matrix products  30.1 us (11%)
  blocking collectives  14.8 us (6%)
  between operations  14.7 us (6%)
  local copies, waits for them, and re-layouts  13.9 us (5%)
  starting transfers between devices  5.66 us (2%)
    all_gather x1, waiting for transfers between devices, on_device(): lax.all_gather(attention, 'mp', axis=1, tiled=True)  44.9 us
    all_gather x1, waiting for transfers between devices, on_device(): lax.all_gather(key_vecs, 'seq', axis=0, tiled=True)  37 us
    add x16, other arithmetic, causal_advance(): accum + tap_block[lag][None, None, :] * window[:, offset:offset + length]  34.8 us
    all_gather x1, waiting for transfers between devices, on_device(): lax.all_gather(value_vecs, 'seq', axis=0, tiled=True)  30 us
    psum x1, blocking collectives, on_device(): square_total = lax.psum(jnp.sum(residual * residual, axis=1), 'mp')  14.8 us
    dot_general x2, matrix products, block_update(): jnp.einsum('ths,shd->thd', weights.astype(jnp.bfloat16), value_heads, pre...  14.1 us
    ppermute x2, waiting for transfers between devices, shifted(): return lax.ppermute(block, axis, route)  11 us
    dot_general x2, matrix products, block_update(): jnp.einsum('thd,shd->ths', query_heads, key_heads, preferred_element_type...  9.98 us
  transfers between devices with their start and end apart: 5, of which 5 were waited for; matrix products, arithmetic and copies ran while one was open for 4% of the time, Pallas kernels for 0%

commit v1 on v0

v1 whole, which is shorter than its diff:
```python
import functools

import jax
import jax.numpy as jnp
import numpy as np
from jax import lax
from jax.experimental import pallas as pl
from jax.experimental.pallas import tpu as pltpu
from jax.sharding import PartitionSpec as P

HD = 128
EPS = 1e-05
NEG = -1e30
LOG2E = 1.4426950408889634
BF = jnp.bfloat16
F32 = jnp.float32
VMEM = pltpu.VMEM
SMEM = pltpu.SMEM


def shifted(block, axis, distance):
    devices = range(lax.axis_size(axis))
    route = [(i - distance, i) for i in devices if i - distance in devices]
    return lax.ppermute(block, axis, route)


def block_update(running, query_heads, query_pos, key_part, value_part, key_pos):
    peak_now, total_now, accum_now = running
    key_count = key_part.shape[0]
    head_count = query_heads.shape[1]
    key_heads = key_part.reshape(key_count, head_count, HD)
    value_heads = value_part.reshape(key_count, head_count, HD)
    scores = jnp.einsum(
        "thd,shd->ths", query_heads, key_heads, preferred_element_type=F32
    ) * HD ** (-0.5)
    allowed = key_pos[None, None, :] <= query_pos[:, None, None]
    masked = jnp.where(allowed, scores, NEG)
    peak_next = jnp.maximum(peak_now, jnp.max(masked, axis=2))
    weights = jnp.where(allowed, jnp.exp(masked - peak_next[:, :, None]), 0.0)
    factor = jnp.exp(peak_now - peak_next)
    total_next = total_now * factor + jnp.sum(weights, axis=2)
    summed = jnp.einsum(
        "ths,shd->thd", weights.astype(BF), value_heads, preferred_element_type=F32
    )
    return (peak_next, total_next, accum_now * factor[:, :, None] + summed)


def attend_keys(running, query_heads, query_pos, key_part, value_part, key_pos, block_rows):
    block_count = key_part.shape[0] // block_rows

    def attend_advance(state, item):
        return block_update(state, query_heads, query_pos, *item), None

    stacked = (
        key_part.reshape(block_count, block_rows, -1),
        value_part.reshape(block_count, block_rows, -1),
        key_pos.reshape(block_count, block_rows),
    )
    running, _ = lax.scan(attend_advance, running, stacked)
    return running


def causal_window(extended, taps_lag):
    pair_count, twice, width = extended.shape
    length = twice // 2
    tap_count = taps_lag.shape[0]
    inner = int(np.gcd(tap_count, 16))

    def causal_advance(block, accum):
        base = block * inner
        window = lax.dynamic_slice_in_dim(
            extended, length - base - inner + 1, length + inner - 1, 1
        ).astype(F32)
        tap_block = lax.dynamic_slice_in_dim(taps_lag, base, inner, 0).astype(F32)
        for lag in range(inner):
            offset = inner - 1 - lag
            accum = accum + tap_block[lag][None, None, :] * window[:, offset : offset + length]
        return accum

    start = jnp.zeros((pair_count, length, width), F32)
    return lax.fori_loop(0, tap_count // inner, causal_advance, start)


def general_device(
    incoming, queries, key_vecs, value_vecs, w_out, norm_gain, filters, filter_len, skip_gain, slot_map
):
    tok_rows, local_width = queries.shape
    span_rows = tok_rows // 2
    head_count = local_width // HD
    model_width = w_out.shape[0]
    all_rows = slot_map.shape[0] * span_rows
    row_ids = jnp.arange(all_rows, dtype=jnp.int32)
    position = (
        jnp.repeat(slot_map, span_rows, total_repeat_length=all_rows) * span_rows
        + row_ids % span_rows
    )
    seq_rank = lax.axis_index("seq")
    seq_size = lax.axis_size("seq")
    own_pos = lax.dynamic_slice_in_dim(position, seq_rank * tok_rows, tok_rows)
    query_heads = queries.reshape(tok_rows, head_count, HD)
    keys_all = lax.all_gather(key_vecs, "seq", axis=0, tiled=True)
    values_all = lax.all_gather(value_vecs, "seq", axis=0, tiled=True)
    running = attend_keys(
        (
            jnp.full((tok_rows, head_count), NEG, F32),
            jnp.zeros((tok_rows, head_count), F32),
            jnp.zeros((tok_rows, head_count, HD), F32),
        ),
        query_heads,
        own_pos,
        keys_all,
        values_all,
        position,
        2 * tok_rows,
    )
    attention = (running[2] / running[1][:, :, None]).reshape(-1, local_width).astype(BF)
    projected = jnp.dot(
        lax.all_gather(attention, "mp", axis=1, tiled=True), w_out, preferred_element_type=F32
    )
    residual = incoming.astype(F32) + projected
    square_total = lax.psum(jnp.sum(residual * residual, axis=1), "mp")
    scale = lax.rsqrt(square_total / model_width + EPS)
    normed = (residual * scale[:, None] * norm_gain[None, :]).astype(BF)
    tap_count = filters.shape[1]
    taps = jnp.where(
        jnp.arange(tap_count, dtype=jnp.int32)[None, :] < filter_len[:, None],
        filters,
        jnp.zeros((), filters.dtype),
    )
    pair_ids = lax.dynamic_slice_in_dim(slot_map, 2 * seq_rank, 2)
    low_first = pair_ids[0] < pair_ids[1]
    slots = normed.reshape(2, span_rows, local_width)
    low_rows = jnp.where(low_first, slots[0], slots[1])
    high_rows = jnp.where(low_first, slots[1], slots[0])
    own_pair = jnp.stack([low_rows, high_rows])
    low_before = shifted(low_rows, "seq", 1)
    high_before = shifted(high_rows, "seq", -1)
    high_before = jnp.where(seq_rank == seq_size - 1, low_rows, high_before)
    before_pair = jnp.stack([low_before, high_before])
    conv_pair = causal_window(jnp.concatenate([before_pair, own_pair], axis=1), taps.T)
    conv_slots = jnp.where(low_first, conv_pair, conv_pair[::-1])
    conv_rows = conv_slots.reshape(tok_rows, local_width)
    layer_out = residual + conv_rows + skip_gain[None, :] * normed.astype(F32)
    return layer_out.astype(BF)


def params(megabytes=20):
    return pltpu.CompilerParams(vmem_limit_bytes=megabytes << 20)


def cost(flops, moved, exps=0):
    return pl.CostEstimate(flops=int(flops), bytes_accessed=int(moved), transcendentals=int(exps))


def vm():
    return pl.BlockSpec(memory_space=VMEM)


def sm():
    return pl.BlockSpec(memory_space=SMEM)


def xor_route(count, k):
    return [(i, i ^ k) for i in range(count)]


def half_index(slots_ref, ids_ref, high):
    rank = ids_ref[0]
    first_is_high = slots_ref[2 * rank] > slots_ref[2 * rank + 1]
    return jnp.where(first_is_high, 1 - high, high).astype(jnp.int32)


def pack_kernel(n, slots_ref, ids_ref, q_ref, k_ref, v_ref, *outs):
    rank = ids_ref[0]
    rows, width = q_ref.shape
    wide = width // n
    for k in range(n):
        cols = pl.ds(pl.multiple_of((rank ^ k) * wide, wide), wide)
        for a, ref in enumerate((q_ref, k_ref, v_ref)):
            outs[k][a * rows : (a + 1) * rows, :] = ref[:, cols]


def pack(n, high, slots, ids, q, k, v):
    rows, width = q.shape[0] // 2, q.shape[1]
    spec = pl.BlockSpec((rows, width), lambda i, s, d: (half_index(s, d, high), 0))
    piece = jax.ShapeDtypeStruct((3 * rows, width // n), BF)
    return pl.pallas_call(
        functools.partial(pack_kernel, n),
        out_shape=[piece] * n,
        grid_spec=pltpu.PrefetchScalarGridSpec(
            num_scalar_prefetch=2,
            grid=(1,),
            in_specs=[spec] * 3,
            out_specs=[pl.BlockSpec((3 * rows, width // n), lambda i, s, d: (0, 0))] * n,
        ),
        compiler_params=params(),
        cost_estimate=cost(0, 12 * rows * width),
        name="pack_high" if high else "pack_low",
    )(slots, ids, q, k, v)


def attend_kernel(n, high, rows, ids_ref, *refs):
    chunks = 2 if high else 1
    ins = refs[: chunks * n]
    outs = refs[chunks * n : chunks * n + n]
    q_all, k_all, v_all, o_all = refs[chunks * n + n :]
    rank = ids_ref[0]
    wide = outs[0].shape[1]

    def place(block):
        return pl.ds(pl.multiple_of(block * rows, rows), rows)

    for c in range(chunks):
        for k in range(n):
            source = rank ^ k
            block = source if c == 0 else 2 * n - 1 - source
            piece = ins[c * n + k]
            if c == chunks - 1:
                q_all[place(block - c * n), :] = piece[0:rows, :]
            k_all[place(block), :] = piece[rows : 2 * rows, :]
            v_all[place(block), :] = piece[2 * rows : 3 * rows, :]
    base = n if high else 0
    row_id = lax.broadcasted_iota(jnp.int32, (rows, rows), 0)
    col_id = lax.broadcasted_iota(jnp.int32, (rows, rows), 1)
    causal = col_id <= row_id
    factor = HD ** (-0.5) * LOG2E
    nt = (((1,), (1,)), ((), ()))
    for b in range(n):
        past = (base + b) * rows
        for h in range(wide // HD):
            cols = slice(h * HD, (h + 1) * HD)
            q = q_all[b * rows : (b + 1) * rows, cols]
            near = lax.dot_general(
                q, k_all[past : past + rows, cols], nt, preferred_element_type=F32
            )
            near = jnp.where(causal, near, NEG)
            peak = jnp.max(near, axis=1, keepdims=True)
            if past:
                far = lax.dot_general(q, k_all[0:past, cols], nt, preferred_element_type=F32)
                peak = jnp.maximum(peak, jnp.max(far, axis=1, keepdims=True))
            w_near = jnp.exp2((near - peak) * factor)
            total = jnp.sum(w_near, axis=1, keepdims=True)
            summed = jnp.dot(
                w_near.astype(BF), v_all[past : past + rows, cols], preferred_element_type=F32
            )
            if past:
                w_far = jnp.exp2((far - peak) * factor)
                total = total + jnp.sum(w_far, axis=1, keepdims=True)
                summed = summed + jnp.dot(
                    w_far.astype(BF), v_all[0:past, cols], preferred_element_type=F32
                )
            owner = n - 1 - b if high else b
            o_all[owner * rows : (owner + 1) * rows, cols] = (summed / total).astype(BF)
    for k in range(n):
        outs[k][...] = o_all[place(rank ^ k), :]


def attend(n, high, rows, ids, pieces):
    wide = pieces[0].shape[1]
    chunks = 2 if high else 1
    pairs = n * (n + 1) // 2 + (n * n if high else 0)
    area = pairs * rows * rows * (wide // HD)
    return pl.pallas_call(
        functools.partial(attend_kernel, n, high, rows),
        out_shape=[jax.ShapeDtypeStruct((rows, wide), BF)] * n,
        in_specs=[sm()] + [vm()] * len(pieces),
        out_specs=[vm()] * n,
        scratch_shapes=[
            VMEM((n * rows, wide), BF),
            VMEM((chunks * n * rows, wide), BF),
            VMEM((chunks * n * rows, wide), BF),
            VMEM((n * rows, wide), BF),
        ],
        compiler_params=params(32),
        cost_estimate=cost(4 * area * HD, 8 * n * rows * wide * chunks, area),
        name="attend_high" if high else "attend_low",
    )(ids, *pieces)


def project_kernel(n, high, slots_ref, ids_ref, inc_ref, w_ref, *refs):
    parts = refs[:-3]
    res_ref, sq_ref, lhs = refs[-3:]
    rank = ids_ref[0]
    me = ids_ref[1]
    rows = res_ref.shape[0]
    width = lhs.shape[1]
    wide = width // n
    half = half_index(slots_ref, ids_ref, high)
    total = inc_ref[pl.ds(pl.multiple_of(half * rows, rows), rows), :].astype(F32)
    for index, part in enumerate(parts):
        for k in range(n):
            cols = pl.ds(pl.multiple_of((rank ^ k) * wide, wide), wide)
            lhs[:, cols] = part[k * rows : (k + 1) * rows, :]
        depth = pl.ds(pl.multiple_of((me ^ index) * width, width), width)
        total = total + jnp.dot(lhs[...], w_ref[depth, :], preferred_element_type=F32)
    res_ref[...] = total
    squares = total * total
    lanes = squares[:, 0:HD]
    for g in range(1, squares.shape[1] // HD):
        lanes = lanes + squares[:, g * HD : (g + 1) * HD]
    sq_ref[...] = jnp.sum(lanes.T, axis=0, keepdims=True)


def project(n, high, slots, ids, incoming, w_out, parts):
    rows, width = incoming.shape[0] // 2, incoming.shape[1]
    return pl.pallas_call(
        functools.partial(project_kernel, n, high),
        out_shape=[
            jax.ShapeDtypeStruct((rows, width), F32),
            jax.ShapeDtypeStruct((1, rows), F32),
        ],
        in_specs=[sm(), sm()] + [vm()] * (2 + len(parts)),
        out_specs=[vm(), vm()],
        scratch_shapes=[VMEM((rows, width), BF)],
        compiler_params=params(20),
        cost_estimate=cost(2 * rows * width * w_out.shape[0], 2 * w_out.size * 1.5),
        name="project_high" if high else "project_low",
    )(slots, ids, incoming, w_out, *parts)


def normed_rows(res, sq_row, gain, model_width):
    rows, width = res.shape
    scale = lax.rsqrt(sq_row / model_width + EPS)
    column = jnp.broadcast_to(scale, (HD, rows)).T
    parts = [
        (res[:, g * HD : (g + 1) * HD] * column * gain[:, g * HD : (g + 1) * HD]).astype(BF)
        for g in range(width // HD)
    ]
    return jnp.concatenate(parts, axis=1)


def norm_kernel(model_width, res_ref, sq_ref, gain_ref, out_ref):
    out_ref[...] = normed_rows(res_ref[...], sq_ref[...], gain_ref[...], model_width)


def norm(model_width, res, sq, gain, name):
    return pl.pallas_call(
        functools.partial(norm_kernel, model_width),
        out_shape=jax.ShapeDtypeStruct(res.shape, BF),
        in_specs=[vm()] * 3,
        out_specs=vm(),
        compiler_params=params(8),
        cost_estimate=cost(4 * res.size, 6 * res.size),
        name=name,
    )(res, sq, gain)


def split(array):
    high = array.astype(jnp.bfloat16)
    low = (array - high.astype(np.float64)).astype(jnp.bfloat16)
    return high, low


def transform_tables(rows):
    size = 2 * rows
    freq = np.arange(rows)[:, None].astype(np.float64)
    time = np.arange(rows)[None, :].astype(np.float64)
    angle = 2 * np.pi * ((freq * time) % size) / size
    cosine = np.cos(angle)
    sine = -np.sin(angle)
    nyquist = np.where(np.arange(rows) % 2 == 0, 1.0, -1.0)
    sine[0] = nyquist
    forward = np.concatenate([cosine, sine], axis=0)
    late = 2 * np.pi * ((freq * (time + rows)) % size) / size
    back_cos = 2 * np.cos(late)
    back_cos[0] = 1.0
    back_sin = -2 * np.sin(late)
    back_sin[0] = np.where((np.arange(rows) + rows) % 2 == 0, 1.0, -1.0)
    backward = np.concatenate([back_cos, back_sin], axis=0).T / size
    return split(forward), split(backward)


def spectrum_kernel(filters_ref, len_ref, fh_ref, fl_ref, out_ref):
    taps = filters_ref.shape[1]
    lag = lax.broadcasted_iota(jnp.int32, filters_ref.shape, 1)
    used = jnp.where(lag < len_ref[...], filters_ref[...].astype(F32), 0.0).astype(BF)
    nt = (((1,), (1,)), ((), ()))
    fh = fh_ref[:, 0:taps]
    fl = fl_ref[:, 0:taps]
    out_ref[...] = lax.dot_general(fh, used, nt, preferred_element_type=F32) + lax.dot_general(
        fl, used, nt, preferred_element_type=F32
    )


def spectrum(filters, filter_len, forward):
    return pl.pallas_call(
        spectrum_kernel,
        out_shape=jax.ShapeDtypeStruct((forward[0].shape[0], filters.shape[0]), F32),
        in_specs=[vm()] * 4,
        out_specs=vm(),
        compiler_params=params(12),
        cost_estimate=cost(4 * forward[0].size * filters.shape[0], 8 * filters.size),
        name="spectrum",
    )(filters, filter_len.reshape(-1, 1), *forward)


def conv_rows(before, own, fh, fl, gh, gl, spec):
    rows = own.shape[0]

    def two(a_high, a_low, b):
        return jnp.dot(a_high, b, preferred_element_type=F32) + jnp.dot(
            a_low, b, preferred_element_type=F32
        )

    row_id = lax.broadcasted_iota(jnp.int32, (rows, 1), 0)
    sign = jnp.where(row_id % 2 == 0, 1.0, -1.0)
    first = row_id == 0
    spec_b = two(fh, fl, before)
    spec_o = two(fh, fl, own)
    x_re = spec_b[:rows] + sign * spec_o[:rows]
    x_im = spec_b[rows:] + jnp.where(first, 1.0, sign) * spec_o[rows:]
    h_re, h_im = spec[:rows], spec[rows:]
    h_cross = jnp.where(first, 0.0, h_im)
    h_own = jnp.where(first, h_im, h_re)
    y_re = x_re * h_re - x_im * h_cross
    y_im = x_re * h_cross + x_im * h_own
    y = jnp.concatenate([y_re, y_im], axis=0)
    y_high = y.astype(BF)
    y_low = (y - y_high.astype(F32)).astype(BF)
    return two(gh, gl, y_high) + jnp.dot(gh, y_low, preferred_element_type=F32)


def finish(res, normed, conv, skip):
    return (res + conv + skip * normed.astype(F32)).astype(BF)


def conv_low_kernel(res_ref, own_ref, before_ref, spec_ref, skip_ref, fh, fl, gh, gl, out_ref):
    conv = conv_rows(
        before_ref[...], own_ref[...], fh[...], fl[...], gh[...], gl[...], spec_ref[...]
    )
    out_ref[...] = finish(res_ref[...], own_ref[...], conv, skip_ref[...])


def conv_high_kernel(
    n, slots_ref, ids_ref, res_ref, own_ref, before_ref, low_ref, done_ref, spec_ref, skip_ref,
    fh, fl, gh, gl, out_ref,
):
    rows = res_ref.shape[0]
    last = ids_ref[0] == n - 1
    before = jnp.where(last, low_ref[...].astype(F32), before_ref[...].astype(F32)).astype(BF)
    conv = conv_rows(before, own_ref[...], fh[...], fl[...], gh[...], gl[...], spec_ref[...])
    half = half_index(slots_ref, ids_ref, 1)
    out_ref[pl.ds(pl.multiple_of((1 - half) * rows, rows), rows), :] = done_ref[...]
    out_ref[pl.ds(pl.multiple_of(half * rows, rows), rows), :] = finish(
        res_ref[...], own_ref[...], conv, skip_ref[...]
    )


def gather_mp(own, size):
    chips = size // 2
    pieces = [own]
    for k in range(1, chips - 1):
        pieces.append(lax.ppermute(own, "mp", xor_route(size, 2 * k)))
    inner = [(i, i ^ (size - 2)) for i in range(2, size - 2)]
    direct = lax.ppermute(own, "mp", inner)
    ends = [(2, 0), (3, 1), (size - 4, size - 2), (size - 3, size - 1)]
    relayed = lax.ppermute(pieces[chips - 2], "mp", ends)
    pieces.append(direct + relayed)
    parts = []
    for piece in pieces:
        parts.append(piece)
        parts.append(lax.ppermute(piece, "mp", xor_route(size, 1)))
    return parts


def total_mp(part, size):
    k = 1
    while k < size:
        part = part + lax.ppermute(part, "mp", xor_route(size, k))
        k *= 2
    return part


def fast_device(
    incoming, queries, key_vecs, value_vecs, w_out, norm_gain, filters, filter_len, skip_gain, slot_map
):
    n = lax.axis_size("seq")
    mp_size = lax.axis_size("mp")
    rows, width = queries.shape[0] // 2, queries.shape[1]
    model_width = w_out.shape[0]
    ids = jnp.stack([lax.axis_index("seq"), lax.axis_index("mp")]).astype(jnp.int32)
    gain = norm_gain.reshape(1, -1)
    skip = skip_gain.reshape(1, -1)
    forward, backward = transform_tables(rows)
    forward = tuple(jnp.asarray(t) for t in forward)
    backward = tuple(jnp.asarray(t) for t in backward)

    def exchange(pieces):
        return [pieces[0]] + [
            lax.ppermute(pieces[k], "seq", xor_route(n, k)) for k in range(1, n)
        ]

    low = exchange(pack(n, 0, slot_map, ids, queries, key_vecs, value_vecs))
    high = exchange(pack(n, 1, slot_map, ids, queries, key_vecs, value_vecs))
    spec = spectrum(filters, filter_len, forward)

    att_low = exchange(attend(n, 0, rows, ids, low))
    parts_low = gather_mp(jnp.concatenate(att_low, axis=0), mp_size)
    att_high = exchange(attend(n, 1, rows, ids, low + high))
    parts_high = gather_mp(jnp.concatenate(att_high, axis=0), mp_size)

    res_low, sq_low = project(n, 0, slot_map, ids, incoming, w_out, parts_low)
    norm_low = norm(model_width, res_low, total_mp(sq_low, mp_size), gain, "norm_low")
    before_low = shifted(norm_low, "seq", 1)
    done_low = pl.pallas_call(
        conv_low_kernel,
        out_shape=jax.ShapeDtypeStruct((rows, width), BF),
        in_specs=[vm()] * 9,
        out_specs=vm(),
        compiler_params=params(20),
        cost_estimate=cost(14 * rows * rows * width, 12 * rows * width),
        name="conv_low",
    )(res_low, norm_low, before_low, spec, skip, *forward, *backward)

    res_high, sq_high = project(n, 1, slot_map, ids, incoming, w_out, parts_high)
    norm_high = norm(model_width, res_high, total_mp(sq_high, mp_size), gain, "norm_high")
    before_high = shifted(norm_high, "seq", -1)
    return pl.pallas_call(
        functools.partial(conv_high_kernel, n),
        out_shape=jax.ShapeDtypeStruct((2 * rows, width), BF),
        in_specs=[sm(), sm()] + [vm()] * 11,
        out_specs=vm(),
        compiler_params=params(20),
        cost_estimate=cost(14 * rows * rows * width, 12 * rows * width),
        name="conv_high",
    )(
        slot_map, ids, res_high, norm_high, before_high, norm_low, done_low, spec, skip,
        *forward, *backward,
    )


def power_of_two(value):
    return value & (value - 1) == 0


def on_device(*arrays):
    n = lax.axis_size("seq")
    size = lax.axis_size("mp")
    queries, filters = arrays[1], arrays[6]
    rows = queries.shape[0] // 2
    heads = queries.shape[1] // HD
    fits = (
        heads % n == 0
        and power_of_two(n)
        and power_of_two(size)
        and size >= 8
        and rows % 256 == 0
        and filters.shape[1] <= rows
    )
    return (fast_device if fits else general_device)(*arrays)


def solution(mesh):
    placed = (
        P("seq", "mp"),
        P("seq", "mp"),
        P("seq", "mp"),
        P("seq", "mp"),
        P(None, "mp"),
        P("mp"),
        P("mp", None),
        P("mp"),
        P("mp"),
        P(),
    )
    return jax.shard_map(
        on_device, mesh=mesh, in_specs=placed, out_specs=P("seq", "mp"), check_vma=False
    )
```

time: 263 us -> 123 us (0.47)
  waiting for transfers between devices: 124 us -> 55.3 us
  other arithmetic: 58.3 us -> 0.24 us
  starting transfers between devices: 5.66 us -> 45.8 us
  matrix products: 30.1 us -> 0 us
  Pallas kernels: 0 us -> 16.1 us
  blocking collectives: 14.8 us -> 0 us
  between operations: 14.7 us -> 0.39 us
  local copies, waits for them, and re-layouts: 13.9 us -> 5.01 us
    all_gather x3 -> x0, waiting for transfers between devices: 112 us -> none  [the longest x1 44.9 us: on_device(): lax.all_gather(attention, 'mp', axis=1, tiled=True)]
    ppermute x0 -> x34, waiting for transfers between devices: none -> 51.7 us  [the longest x4 18.1 us: gather_mp(): pieces.append(lax.ppermute(own, 'mp', xor_route(size, 2 * k)))]
    ppermute x0 -> x34, starting transfers between devices: none -> 41.5 us  [the longest x12 18.2 us: exchange(): lax.ppermute(pieces[k], 'seq', xor_route(n, k))]
    add x20 -> x8, other arithmetic: 34.9 us -> 0.16 us  [the longest x2 0.14 us: gather_mp(): pieces.append(direct + relayed)]
    dot_general x5 -> x0, matrix products: 30.1 us -> none  [the longest x2 14.1 us: block_update(): jnp.einsum('ths,shd->thd', weights.astype(jnp.bfloat16), value_heads, pre...]
    pallas_call x0 -> x11, Pallas kernels: none -> 16.1 us  [the longest x2 5.9 us: attend(): pl.pallas_call(functools.partial(attend_kernel, n, high, rows), out_shape...]
    psum x1 -> x0, blocking collectives: 14.8 us -> none  [on_device(): square_total = lax.psum(jnp.sum(residual * residual, axis=1), 'mp')]
    dynamic_slice x9 -> x0, local copies, waits for them, and re-layouts: 9.45 us -> none  [the longest x8 9.38 us: attend_keys(): running, _ = lax.scan(attend_advance, running, stacked)]
  transfers between devices with their start and end apart: 5 -> 36, of which waited for: 5 -> 16; matrix products, arithmetic and copies ran while one was open for 4% -> 0% of each run, Pallas kernels for 0% -> 7%
where the time goes in v1:
time: 123 us
  waiting for transfers between devices  55.3 us (45%)
  starting transfers between devices  45.8 us (37%)
  Pallas kernels  16.1 us (13%)
  local copies, waits for them, and re-layouts  5.01 us (4%)
    ppermute x12, starting transfers between devices, exchange(): lax.ppermute(pieces[k], 'seq', xor_route(n, k))  18.2 us
    ppermute x4, waiting for transfers between devices, gather_mp(): pieces.append(lax.ppermute(own, 'mp', xor_route(size, 2 * k)))  18.1 us
    ppermute x12, waiting for transfers between devices, exchange(): lax.ppermute(pieces[k], 'seq', xor_route(n, k))  16.1 us
    ppermute x6, waiting for transfers between devices, total_mp(): part = part + lax.ppermute(part, 'mp', xor_route(size, k))  13.1 us
    ppermute x4, starting transfers between devices, gather_mp(): pieces.append(lax.ppermute(own, 'mp', xor_route(size, 2 * k)))  12.4 us
    pallas_call x2, Pallas kernels, attend(): pl.pallas_call(functools.partial(attend_kernel, n, high, rows), out_shape...  5.9 us
    ppermute x6, starting transfers between devices, total_mp(): part = part + lax.ppermute(part, 'mp', xor_route(size, k))  5.39 us
    unnamed x36, local copies, waits for them, and re-layouts  4.84 us
  transfers between devices with their start and end apart: 36, of which 16 were waited for; matrix products, arithmetic and copies ran while one was open for 0% of the time, Pallas kernels for 7%

profile of v1, /device:TPU:0, one launch (start us, length us, event | category | flops | bytes accessed | tf_op | source)
XLA Modules:
  0.0 122.9 jit_solution(14402293546519290785)
XLA Ops:
  0.0 0.1 pad_add_fusion.ids_ref
  0.1 1.0 copy-done.4
  1.1 1.0 copy-done.5
  2.2 1.0 copy-done.6
  3.2 0.7 copy-done.10
  3.9 0.7 pack_low.1
  4.6 3.0 %collective-permute-start = (bf16[768,128]{1,0:T(8,128)(2,1)S(1)}, bf16[768,128]{1,0:T(8,128)(2,1)S(1)}, u32[]{:S(2)}, u32[]{:S(2)}) collective-permute-start(bf16[768,128]{1,0:T(8,128)(2,1)S(1)} %get-tuple-element.26), channel_id=1, source_target_pairs={{0,8},{8,0},{16,24},{24,16},{1,9},{9,1},{17,25},{25,17},{2,10},{10... | collective-permute-start | bytes 589832 | tf_op jit(solution)/shard_map/ppermute | solution.py:490
  7.6 1.5 %collective-permute-start.1 = (bf16[768,128]{1,0:T(8,128)(2,1)S(1)}, bf16[768,128]{1,0:T(8,128)(2,1)S(1)}, u32[]{:S(2)}, u32[]{:S(2)}) collective-permute-start(bf16[768,128]{1,0:T(8,128)(2,1)S(1)} %get-tuple-element.27), channel_id=1, source_target_pairs={{0,16},{8,24},{16,0},{24,8},{1,17},{9,25},{17,1},{25,9},{2,18},{10... | collective-permute-start | bytes 589832 | tf_op jit(solution)/shard_map/ppermute | solution.py:490
  9.2 0.7 pack_high.1
  9.9 2.0 %collective-permute-start.3 = (bf16[768,128]{1,0:T(8,128)(2,1)S(1)}, bf16[768,128]{1,0:T(8,128)(2,1)S(1)}, u32[]{:S(2)}, u32[]{:S(2)}) collective-permute-start(bf16[768,128]{1,0:T(8,128)(2,1)S(1)} %get-tuple-element.30), channel_id=1, source_target_pairs={{0,8},{8,0},{16,24},{24,16},{1,9},{9,1},{17,25},{25,17},{2,10},{10... | collective-permute-start | bytes 589832 | tf_op jit(solution)/shard_map/ppermute | solution.py:490
  11.8 1.5 %collective-permute-start.4 = (bf16[768,128]{1,0:T(8,128)(2,1)S(1)}, bf16[768,128]{1,0:T(8,128)(2,1)S(1)}, u32[]{:S(2)}, u32[]{:S(2)}) collective-permute-start(bf16[768,128]{1,0:T(8,128)(2,1)S(1)} %get-tuple-element.31), channel_id=1, source_target_pairs={{0,16},{8,24},{16,0},{24,8},{1,17},{9,25},{17,1},{25,9},{2,18},{10... | collective-permute-start | bytes 589832 | tf_op jit(solution)/shard_map/ppermute | solution.py:490
  13.4 2.9 %collective-permute-start.5 = (bf16[768,128]{1,0:T(8,128)(2,1)S(1)}, bf16[768,128]{1,0:T(8,128)(2,1)S(1)}, u32[]{:S(2)}, u32[]{:S(2)}) collective-permute-start(bf16[768,128]{1,0:T(8,128)(2,1)S(1)} %get-tuple-element.32), channel_id=1, source_target_pairs={{0,24},{8,16},{16,8},{24,0},{1,25},{9,17},{17,9},{25,1},{2,26},{10... | collective-permute-start | bytes 589832 | tf_op jit(solution)/shard_map/ppermute | solution.py:490
  16.3 2.9 %collective-permute-done.1.refs_2_ = bf16[768,128]{1,0:T(8,128)(2,1)S(1)} collective-permute-done((bf16[768,128]{1,0:T(8,128)(2,1)S(1)}, bf16[768,128]{1,0:T(8,128)(2,1)S(1)}, u32[]{:S(2)}, u32[]{:S(2)}) %collective-permute-start.1) | collective-permute-done | bytes 196640 | tf_op jit(solution)/shard_map/ppermute | solution.py:490
  19.3 2.6 %collective-permute-done.3.refs_5_ = bf16[768,128]{1,0:T(8,128)(2,1)S(1)} collective-permute-done((bf16[768,128]{1,0:T(8,128)(2,1)S(1)}, bf16[768,128]{1,0:T(8,128)(2,1)S(1)}, u32[]{:S(2)}, u32[]{:S(2)}) %collective-permute-start.3) | collective-permute-done | bytes 196640 | tf_op jit(solution)/shard_map/ppermute | solution.py:490
  21.8 4.8 %collective-permute-done.4.refs_6_ = bf16[768,128]{1,0:T(8,128)(2,1)S(1)} collective-permute-done((bf16[768,128]{1,0:T(8,128)(2,1)S(1)}, bf16[768,128]{1,0:T(8,128)(2,1)S(1)}, u32[]{:S(2)}, u32[]{:S(2)}) %collective-permute-start.4) | collective-permute-done | bytes 196640 | tf_op jit(solution)/shard_map/ppermute | solution.py:490
  26.6 3.6 %attend_high.1 = (bf16[256,128]{1,0:T(8,128)(2,1)S(1)}, bf16[256,128]{1,0:T(8,128)(2,1)S(1)}, bf16[256,128]{1,0:T(8,128)(2,1)S(1)}, bf16[256,128]{1,0:T(8,128)(2,1)S(1)}) custom-call(s32[2]{0:T(128)S(1)} %pad_add_fusion.ids_ref, bf16[768,128]{1,0:T(8,128)(2,1)S(1)} %get-tuple-element.25.refs_0_, bf16[768,128]{1,0:T(8,128)(2,1)S(1)} %collective-permute-done.refs_1_, ...), custom_call_target="tpu_custom_call" | custom-call | flops 872415232 | bytes 2097152 | tf_op jit(solution)/shard_map/attend_high/pallas_call | solution.py:263
  30.2 1.3 %collective-permute-start.6 = (bf16[256,128]{1,0:T(8,128)(2,1)S(1)}, bf16[256,128]{1,0:T(8,128)(2,1)S(1)}, u32[]{:S(2)}, u32[]{:S(2)}) collective-permute-start(bf16[256,128]{1,0:T(8,128)(2,1)S(1)} %get-tuple-element.34), channel_id=1, source_target_pairs={{0,8},{8,0},{16,24},{24,16},{1,9},{9,1},{17,25},{25,17},{2,10},{10... | collective-permute-start | bytes 196616 | tf_op jit(solution)/shard_map/ppermute | solution.py:490
  31.6 0.8 collective-permute-start.7
  32.3 1.4 %collective-permute-start.8 = (bf16[256,128]{1,0:T(8,128)(2,1)S(1)}, bf16[256,128]{1,0:T(8,128)(2,1)S(1)}, u32[]{:S(2)}, u32[]{:S(2)}) collective-permute-start(bf16[256,128]{1,0:T(8,128)(2,1)S(1)} %get-tuple-element.36), channel_id=1, source_target_pairs={{0,24},{8,16},{16,8},{24,0},{1,25},{9,17},{17,9},{25,1},{2,26},{10... | collective-permute-start | bytes 196616 | tf_op jit(solution)/shard_map/ppermute | solution.py:490
  33.8 2.3 %attend_low.1 = (bf16[256,128]{1,0:T(8,128)(2,1)S(1)}, bf16[256,128]{1,0:T(8,128)(2,1)S(1)}, bf16[256,128]{1,0:T(8,128)(2,1)S(1)}, bf16[256,128]{1,0:T(8,128)(2,1)S(1)}) custom-call(s32[2]{0:T(128)S(1)} %pad_add_fusion.ids_ref, bf16[768,128]{1,0:T(8,128)(2,1)S(1)} %get-tuple-element.25.refs_0_, bf16[768,128]{1,0:T(8,128)(2,1)S(1)} %collective-permute-done.refs_1_, ...), custom_call_target="tpu_custom_call" | custom-call | flops 335544320 | bytes 1048576 | tf_op jit(solution)/shard_map/attend_low/pallas_call | solution.py:263
  36.1 1.3 %collective-permute-start.21 = (bf16[256,128]{1,0:T(8,128)(2,1)S(1)}, bf16[256,128]{1,0:T(8,128)(2,1)S(1)}, u32[]{:S(2)}, u32[]{:S(2)}) collective-permute-start(bf16[256,128]{1,0:T(8,128)(2,1)S(1)} %get-tuple-element.40), channel_id=1, source_target_pairs={{0,8},{8,0},{16,24},{24,16},{1,9},{9,1},{17,25},{25,17},{2,10},{10... | collective-permute-start | bytes 196616 | tf_op jit(solution)/shard_map/ppermute | solution.py:490
  37.4 0.8 collective-permute-start.22
  38.2 2.2 %collective-permute-done.21 = bf16[256,128]{1,0:T(8,128)(2,1)S(1)} collective-permute-done((bf16[256,128]{1,0:T(8,128)(2,1)S(1)}, bf16[256,128]{1,0:T(8,128)(2,1)S(1)}, u32[]{:S(2)}, u32[]{:S(2)}) %collective-permute-start.21) | collective-permute-done | bytes 65568 | tf_op jit(solution)/shard_map/ppermute | solution.py:490
  40.4 1.5 %collective-permute-start.23 = (bf16[256,128]{1,0:T(8,128)(2,1)S(1)}, bf16[256,128]{1,0:T(8,128)(2,1)S(1)}, u32[]{:S(2)}, u32[]{:S(2)}) collective-permute-start(bf16[256,128]{1,0:T(8,128)(2,1)S(1)} %get-tuple-element.42), channel_id=1, source_target_pairs={{0,24},{8,16},{16,8},{24,0},{1,25},{9,17},{17,9},{25,1},{2,26},{10... | collective-permute-start | bytes 196616 | tf_op jit(solution)/shard_map/ppermute | solution.py:490
  41.9 3.6 %collective-permute-done.23 = bf16[256,128]{1,0:T(8,128)(2,1)S(1)} collective-permute-done((bf16[256,128]{1,0:T(8,128)(2,1)S(1)}, bf16[256,128]{1,0:T(8,128)(2,1)S(1)}, u32[]{:S(2)}, u32[]{:S(2)}) %collective-permute-start.23) | collective-permute-done | bytes 65568 | tf_op jit(solution)/shard_map/ppermute | solution.py:490
  45.6 2.7 %collective-permute-start.27 = (bf16[1024,128]{1,0:T(8,128)(2,1)S(1)}, bf16[1024,128]{1,0:T(8,128)(2,1)S(1)}, u32[]{:S(2)}, u32[]{:S(2)}) collective-permute-start(bf16[1024,128]{1,0:T(8,128)(2,1)S(1)} %constant_dynamic-update-slice_fusion.4.refs_0_), channel_id=1, source_target_pairs={{0,4},{1,5},{2,6},{3,7},{4,0},{5,1},{6,2},{7,3},{8,12},{9,13},{10,... | collective-permute-start | bytes 786440 | tf_op jit(solution)/shard_map/ppermute | solution.py:453
  48.3 0.4 collective-permute-start.12
  48.7 0.7 collective-permute-start.14
  49.4 4.4 %collective-permute-start.25 = (bf16[1024,128]{1,0:T(8,128)(2,1)S(1)}, bf16[1024,128]{1,0:T(8,128)(2,1)S(1)}, u32[]{:S(2)}, u32[]{:S(2)}) collective-permute-start(bf16[1024,128]{1,0:T(8,128)(2,1)S(1)} %constant_dynamic-update-slice_fusion.4.refs_0_), channel_id=1, source_target_pairs={{0,2},{1,3},{2,0},{3,1},{4,6},{5,7},{6,4},{7,5},{8,10},{9,11},{10,... | collective-permute-start | bytes 786440 | tf_op jit(solution)/shard_map/ppermute | solution.py:453
  53.9 0.7 collective-permute-start.29
  54.5 9.2 %collective-permute-done.27.refs_4_ = bf16[1024,128]{1,0:T(8,128)(2,1)S(1)} collective-permute-done((bf16[1024,128]{1,0:T(8,128)(2,1)S(1)}, bf16[1024,128]{1,0:T(8,128)(2,1)S(1)}, u32[]{:S(2)}, u32[]{:S(2)}) %collective-permute-start.27) | collective-permute-done | bytes 262176 | tf_op jit(solution)/shard_map/ppermute | solution.py:453
  63.7 1.3 %collective-permute-start.30 = (bf16[1024,128]{1,0:T(8,128)(2,1)S(1)}, bf16[1024,128]{1,0:T(8,128)(2,1)S(1)}, u32[]{:S(2)}, u32[]{:S(2)}) collective-permute-start(bf16[1024,128]{1,0:T(8,128)(2,1)S(1)} %collective-permute-done.27.refs_4_), channel_id=1, source_target_pairs={{2,0},{3,1},{4,6},{5,7},{10,8},{11,9},{12,14},{13,15},{18,16},{19,... | collective-permute-start | bytes 786440 | tf_op jit(solution)/shard_map/ppermute | solution.py:457
  65.0 4.3 %collective-permute-done.12.refs_4_ = bf16[1024,128]{1,0:T(8,128)(2,1)S(1)} collective-permute-done((bf16[1024,128]{1,0:T(8,128)(2,1)S(1)}, bf16[1024,128]{1,0:T(8,128)(2,1)S(1)}, u32[]{:S(2)}, u32[]{:S(2)}) %collective-permute-start.12) | collective-permute-done | bytes 262176 | tf_op jit(solution)/shard_map/ppermute | solution.py:453
  69.4 1.3 %collective-permute-start.15 = (bf16[1024,128]{1,0:T(8,128)(2,1)S(1)}, bf16[1024,128]{1,0:T(8,128)(2,1)S(1)}, u32[]{:S(2)}, u32[]{:S(2)}) collective-permute-start(bf16[1024,128]{1,0:T(8,128)(2,1)S(1)} %collective-permute-done.12.refs_4_), channel_id=1, source_target_pairs={{2,0},{3,1},{4,6},{5,7},{10,8},{11,9},{12,14},{13,15},{18,16},{19,... | collective-permute-start | bytes 786440 | tf_op jit(solution)/shard_map/ppermute | solution.py:457
  70.7 4.9 %collective-permute-start.10 = (bf16[1024,128]{1,0:T(8,128)(2,1)S(1)}, bf16[1024,128]{1,0:T(8,128)(2,1)S(1)}, u32[]{:S(2)}, u32[]{:S(2)}) collective-permute-start(bf16[1024,128]{1,0:T(8,128)(2,1)S(1)} %constant_dynamic-update-slice_fusion.refs_0_), channel_id=1, source_target_pairs={{0,2},{1,3},{2,0},{3,1},{4,6},{5,7},{6,4},{7,5},{8,10},{9,11},{10,... | collective-permute-start | bytes 786440 | tf_op jit(solution)/shard_map/ppermute | solution.py:453
  75.6 0.5 collective-permute-start.26
  76.1 0.1 add.28.refs_6_
  76.2 4.3 %collective-permute-done.15 = bf16[1024,128]{1,0:T(8,128)(2,1)S(1)} collective-permute-done((bf16[1024,128]{1,0:T(8,128)(2,1)S(1)}, bf16[1024,128]{1,0:T(8,128)(2,1)S(1)}, u32[]{:S(2)}, u32[]{:S(2)}) %collective-permute-start.15) | collective-permute-done | bytes 262176 | tf_op jit(solution)/shard_map/ppermute | solution.py:457
  80.5 0.1 add.24.refs_6_
  80.6 4.5 %collective-permute-done.10.refs_2_ = bf16[1024,128]{1,0:T(8,128)(2,1)S(1)} collective-permute-done((bf16[1024,128]{1,0:T(8,128)(2,1)S(1)}, bf16[1024,128]{1,0:T(8,128)(2,1)S(1)}, u32[]{:S(2)}, u32[]{:S(2)}) %collective-permute-start.10) | collective-permute-done | bytes 262176 | tf_op jit(solution)/shard_map/ppermute | solution.py:453
  85.1 0.5 collective-permute-start.13
  85.7 0.4 collective-permute-start.16
  86.2 2.0 %project_low.1 = (f32[256,512]{1,0:T(8,128)S(1)}, f32[1,256]{1,0:T(1,128)S(1)}) custom-call(s32[8]{0:T(128)S(1)} %copy-done.11, s32[2]{0:T(128)S(1)} %pad_add_fusion.ids_ref, bf16[512,512]{1,0:T(8,128)(2,1)S(1)} %copy-done.3, bf16[4096,512]{1,0:T(8,128)(2,1)S(1)} %copy-done, bf16[1024,128]{1,0:T(8,128)(2,1)S(1)} %constant_dynamic-update-slice_fusion.4.refs_0_, ...), custom_call_target="tpu_custom_call" | custom-call | flops 1073741824 | bytes 6291456 | tf_op jit(solution)/shard_map/project_low/pallas_call | solution.py:306
  88.1 0.1 collective-permute-start.32
  88.2 1.1 collective-permute-done.32
  89.4 3.6 %collective-permute-done.33 = f32[1,256]{1,0:T(1,128)S(1)} collective-permute-done((f32[1,256]{1,0:T(1,128)S(1)}, f32[1,256]{1,0:T(1,128)S(1)}, u32[]{:S(2)}, u32[]{:S(2)}) %collective-permute-start.33) | collective-permute-done | bytes 1056 | tf_op jit(solution)/shard_map/ppermute | solution.py:469
  92.9 2.0 %collective-permute-start.34 = (f32[1,256]{1,0:T(1,128)S(1)}, f32[1,256]{1,0:T(1,128)S(1)}, u32[]{:S(2)}, u32[]{:S(2)}) collective-permute-start(f32[1,256]{1,0:T(1,128)S(1)} %add.30), channel_id=1, source_target_pairs={{0,4},{1,5},{2,6},{3,7},{4,0},{5,1},{6,2},{7,3},{8,12},{9,13},{10,... | collective-permute-start | bytes 3080 | tf_op jit(solution)/shard_map/ppermute | solution.py:469
  95.0 2.4 %collective-permute-done.34 = f32[1,256]{1,0:T(1,128)S(1)} collective-permute-done((f32[1,256]{1,0:T(1,128)S(1)}, f32[1,256]{1,0:T(1,128)S(1)}, u32[]{:S(2)}, u32[]{:S(2)}) %collective-permute-start.34) | collective-permute-done | bytes 1056 | tf_op jit(solution)/shard_map/ppermute | solution.py:469
  97.4 0.1 norm_low.1.own_ref.low_ref
  97.6 2.8 %collective-permute-start.35 = (bf16[256,512]{1,0:T(8,128)(2,1)S(1)}, bf16[256,512]{1,0:T(8,128)(2,1)S(1)}, u32[]{:S(2)}, u32[]{:S(2)}) collective-permute-start(bf16[256,512]{1,0:T(8,128)(2,1)S(1)} %norm_low.1.own_ref.low_ref), channel_id=1, source_target_pairs={{0,8},{8,16},{16,24},{1,9},{9,17},{17,25},{2,10},{10,18},{18,26},{... | collective-permute-start | bytes 786440 | tf_op jit(solution)/shard_map/ppermute | solution.py:24
  100.5 1.9 %project_high.1 = (f32[256,512]{1,0:T(8,128)S(1)}, f32[1,256]{1,0:T(1,128)S(1)}) custom-call(s32[8]{0:T(128)S(1)} %copy-done.11, s32[2]{0:T(128)S(1)} %pad_add_fusion.ids_ref, bf16[512,512]{1,0:T(8,128)(2,1)S(1)} %copy-done.3, bf16[4096,512]{1,0:T(8,128)(2,1)S(1)} %copy-done, bf16[1024,128]{1,0:T(8,128)(2,1)S(1)} %constant_dynamic-update-slice_fusion.refs_0_, ...), custom_call_target="tpu_custom_call" | custom-call | flops 1073741824 | bytes 6291456 | tf_op jit(solution)/shard_map/project_high/pallas_call | solution.py:306
  102.5 1.1 collective-permute-done.17
  103.6 1.1 collective-permute-start.18
  104.8 2.4 %collective-permute-done.18 = f32[1,256]{1,0:T(1,128)S(1)} collective-permute-done((f32[1,256]{1,0:T(1,128)S(1)}, f32[1,256]{1,0:T(1,128)S(1)}, u32[]{:S(2)}, u32[]{:S(2)}) %collective-permute-start.18) | collective-permute-done | bytes 1056 | tf_op jit(solution)/shard_map/ppermute | solution.py:469
  107.2 2.0 %collective-permute-start.19 = (f32[1,256]{1,0:T(1,128)S(1)}, f32[1,256]{1,0:T(1,128)S(1)}, u32[]{:S(2)}, u32[]{:S(2)}) collective-permute-start(f32[1,256]{1,0:T(1,128)S(1)} %add.26), channel_id=1, source_target_pairs={{0,4},{1,5},{2,6},{3,7},{4,0},{5,1},{6,2},{7,3},{8,12},{9,13},{10,... | collective-permute-start | bytes 3080 | tf_op jit(solution)/shard_map/ppermute | solution.py:469
  109.3 2.4 %collective-permute-done.19 = f32[1,256]{1,0:T(1,128)S(1)} collective-permute-done((f32[1,256]{1,0:T(1,128)S(1)}, f32[1,256]{1,0:T(1,128)S(1)}, u32[]{:S(2)}, u32[]{:S(2)}) %collective-permute-start.19) | collective-permute-done | bytes 1056 | tf_op jit(solution)/shard_map/ppermute | solution.py:469
  111.7 0.1 norm_high.1.own_ref
  111.8 1.5 %collective-permute-start.20 = (bf16[256,512]{1,0:T(8,128)(2,1)S(1)}, bf16[256,512]{1,0:T(8,128)(2,1)S(1)}, u32[]{:S(2)}, u32[]{:S(2)}) collective-permute-start(bf16[256,512]{1,0:T(8,128)(2,1)S(1)} %norm_high.1.own_ref), channel_id=1, source_target_pairs={{8,0},{16,8},{24,16},{9,1},{17,9},{25,17},{10,2},{18,10},{26,18},{... | collective-permute-start | bytes 786440 | tf_op jit(solution)/shard_map/ppermute | solution.py:24
  113.3 0.1 copy.15.len_ref
  113.5 0.9 copy-done.9
  114.5 0.5 spectrum.1.spec_ref
  115.0 1.4 %conv_low.1.done_ref = bf16[256,512]{1,0:T(8,128)(2,1)S(1)} custom-call(f32[256,512]{1,0:T(8,128)S(1)} %get-tuple-element.43.res_ref, bf16[256,512]{1,0:T(8,128)(2,1)S(1)} %norm_low.1.own_ref.low_ref, bf16[256,512]{1,0:T(8,128)(2,1)S(1)} %collective-permute-done.35.before_ref, f32[512,512]{1,0:T(8,128)S(1)} %spectrum.1.spec_ref, f32[1,512]{1,0:T(1,128)S(1)} %bitcast.7, ...), custom_call_target="tpu_custom_call" | custom-call | flops 469762048 | bytes 1572864 | tf_op jit(solution)/shard_map/conv_low/pallas_call | solution.py:505
  116.5 3.6 %collective-permute-done.20.before_ref = bf16[256,512]{1,0:T(8,128)(2,1)S(1)} collective-permute-done((bf16[256,512]{1,0:T(8,128)(2,1)S(1)}, bf16[256,512]{1,0:T(8,128)(2,1)S(1)}, u32[]{:S(2)}, u32[]{:S(2)}) %collective-permute-start.20) | collective-permute-done | bytes 262176 | tf_op jit(solution)/shard_map/ppermute | solution.py:24
  120.1 2.8 %conv_high.1 = bf16[512,512]{1,0:T(8,128)(2,1)} custom-call(s32[8]{0:T(128)S(1)} %copy-done.11, s32[2]{0:T(128)S(1)} %pad_add_fusion.ids_ref, f32[256,512]{1,0:T(8,128)S(1)} %get-tuple-element.37.res_ref, bf16[256,512]{1,0:T(8,128)(2,1)S(1)} %norm_high.1.own_ref, bf16[256,512]{1,0:T(8,128)(2,1)S(1)} %collective-permute-done.20.before_ref, ...), custom_call_target="tpu_custom_call" | custom-call | flops 469762048 | bytes 1572864 | tf_op jit(solution)/shard_map/conv_high/pallas_call | solution.py:518
  (67 shorter events, 0.5 us)
Async XLA Ops:
  0.1 1.0 copy-start.4
  1.1 1.0 copy-start.5
  2.2 1.0 copy-start.6
  3.2 0.7 copy-start.10
  4.6 8.8 %collective-permute-start = (bf16[768,128]{1,0:T(8,128)(2,1)S(1)}, bf16[768,128]{1,0:T(8,128)(2,1)S(1)}, u32[]{:S(2)}, u32[]{:S(2)}) collective-permute-start(bf16[768,128]{1,0:T(8,128)(2,1)S(1)} %get-tuple-element.26), channel_id=1, source_target_pairs={{0,8},{8,0},{16,24},{24,16},{1,9},{9,1},{17,25},{25,17},{2,10},{10... | collective-permute-start | bytes 589832 | tf_op jit(solution)/shard_map/ppermute | solution.py:490
  7.6 11.7 %collective-permute-start.1 = (bf16[768,128]{1,0:T(8,128)(2,1)S(1)}, bf16[768,128]{1,0:T(8,128)(2,1)S(1)}, u32[]{:S(2)}, u32[]{:S(2)}) collective-permute-start(bf16[768,128]{1,0:T(8,128)(2,1)S(1)} %get-tuple-element.27), channel_id=1, source_target_pairs={{0,16},{8,24},{16,0},{24,8},{1,17},{9,25},{17,1},{25,9},{2,18},{10... | collective-permute-start | bytes 589832 | tf_op jit(solution)/shard_map/ppermute | solution.py:490
  9.1 77.0 %copy-start = (bf16[4096,512]{1,0:T(8,128)(2,1)S(1)}, bf16[4096,512]{1,0:T(8,128)(2,1)}, u32[]{:S(2)}) copy-start(bf16[4096,512]{1,0:T(8,128)(2,1)} %w_ref.3) | copy-start | bytes 12582916
  9.1 77.0 %copy-start.3 = (bf16[512,512]{1,0:T(8,128)(2,1)S(1)}, bf16[512,512]{1,0:T(8,128)(2,1)}, u32[]{:S(2)}) copy-start(bf16[512,512]{1,0:T(8,128)(2,1)} %inc_ref.3) | copy-start | bytes 1572868
  9.1 77.0 %copy-start.11 = (s32[8]{0:T(128)S(1)}, s32[8]{0:T(128)}, u32[]{:S(2)}) copy-start(s32[8]{0:T(128)} %slots_ref.9) | copy-start | bytes 100
  9.1 10.1 %collective-permute-start.2 = (bf16[768,128]{1,0:T(8,128)(2,1)S(1)}, bf16[768,128]{1,0:T(8,128)(2,1)S(1)}, u32[]{:S(2)}, u32[]{:S(2)}) collective-permute-start(bf16[768,128]{1,0:T(8,128)(2,1)S(1)} %get-tuple-element.28), channel_id=1, source_target_pairs={{0,24},{8,16},{16,8},{24,0},{1,25},{9,17},{17,9},{25,1},{2,26},{10... | collective-permute-start | bytes 589832 | tf_op jit(solution)/shard_map/ppermute | solution.py:490
  9.9 11.9 %collective-permute-start.3 = (bf16[768,128]{1,0:T(8,128)(2,1)S(1)}, bf16[768,128]{1,0:T(8,128)(2,1)S(1)}, u32[]{:S(2)}, u32[]{:S(2)}) collective-permute-start(bf16[768,128]{1,0:T(8,128)(2,1)S(1)} %get-tuple-element.30), channel_id=1, source_target_pairs={{0,8},{8,0},{16,24},{24,16},{1,9},{9,1},{17,25},{25,17},{2,10},{10... | collective-permute-start | bytes 589832 | tf_op jit(solution)/shard_map/ppermute | solution.py:490
  11.8 14.7 %collective-permute-start.4 = (bf16[768,128]{1,0:T(8,128)(2,1)S(1)}, bf16[768,128]{1,0:T(8,128)(2,1)S(1)}, u32[]{:S(2)}, u32[]{:S(2)}) collective-permute-start(bf16[768,128]{1,0:T(8,128)(2,1)S(1)} %get-tuple-element.31), channel_id=1, source_target_pairs={{0,16},{8,24},{16,0},{24,8},{1,17},{9,25},{17,1},{25,9},{2,18},{10... | collective-permute-start | bytes 589832 | tf_op jit(solution)/shard_map/ppermute | solution.py:490
  13.4 13.2 %collective-permute-start.5 = (bf16[768,128]{1,0:T(8,128)(2,1)S(1)}, bf16[768,128]{1,0:T(8,128)(2,1)S(1)}, u32[]{:S(2)}, u32[]{:S(2)}) collective-permute-start(bf16[768,128]{1,0:T(8,128)(2,1)S(1)} %get-tuple-element.32), channel_id=1, source_target_pairs={{0,24},{8,16},{16,8},{24,0},{1,25},{9,17},{17,9},{25,1},{2,26},{10... | collective-permute-start | bytes 589832 | tf_op jit(solution)/shard_map/ppermute | solution.py:490
  30.2 18.0 %collective-permute-start.6 = (bf16[256,128]{1,0:T(8,128)(2,1)S(1)}, bf16[256,128]{1,0:T(8,128)(2,1)S(1)}, u32[]{:S(2)}, u32[]{:S(2)}) collective-permute-start(bf16[256,128]{1,0:T(8,128)(2,1)S(1)} %get-tuple-element.34), channel_id=1, source_target_pairs={{0,8},{8,0},{16,24},{24,16},{1,9},{9,1},{17,25},{25,17},{2,10},{10... | collective-permute-start | bytes 196616 | tf_op jit(solution)/shard_map/ppermute | solution.py:490
  31.6 16.7 %collective-permute-start.7 = (bf16[256,128]{1,0:T(8,128)(2,1)S(1)}, bf16[256,128]{1,0:T(8,128)(2,1)S(1)}, u32[]{:S(2)}, u32[]{:S(2)}) collective-permute-start(bf16[256,128]{1,0:T(8,128)(2,1)S(1)} %get-tuple-element.35), channel_id=1, source_target_pairs={{0,16},{8,24},{16,0},{24,8},{1,17},{9,25},{17,1},{25,9},{2,18},{10... | collective-permute-start | bytes 196616 | tf_op jit(solution)/shard_map/ppermute | solution.py:490
  32.3 16.0 %collective-permute-start.8 = (bf16[256,128]{1,0:T(8,128)(2,1)S(1)}, bf16[256,128]{1,0:T(8,128)(2,1)S(1)}, u32[]{:S(2)}, u32[]{:S(2)}) collective-permute-start(bf16[256,128]{1,0:T(8,128)(2,1)S(1)} %get-tuple-element.36), channel_id=1, source_target_pairs={{0,24},{8,16},{16,8},{24,0},{1,25},{9,17},{17,9},{25,1},{2,26},{10... | collective-permute-start | bytes 196616 | tf_op jit(solution)/shard_map/ppermute | solution.py:490
  36.1 4.3 %collective-permute-start.21 = (bf16[256,128]{1,0:T(8,128)(2,1)S(1)}, bf16[256,128]{1,0:T(8,128)(2,1)S(1)}, u32[]{:S(2)}, u32[]{:S(2)}) collective-permute-start(bf16[256,128]{1,0:T(8,128)(2,1)S(1)} %get-tuple-element.40), channel_id=1, source_target_pairs={{0,8},{8,0},{16,24},{24,16},{1,9},{9,1},{17,25},{25,17},{2,10},{10... | collective-permute-start | bytes 196616 | tf_op jit(solution)/shard_map/ppermute | solution.py:490
  37.4 4.5 %collective-permute-start.22 = (bf16[256,128]{1,0:T(8,128)(2,1)S(1)}, bf16[256,128]{1,0:T(8,128)(2,1)S(1)}, u32[]{:S(2)}, u32[]{:S(2)}) collective-permute-start(bf16[256,128]{1,0:T(8,128)(2,1)S(1)} %get-tuple-element.41), channel_id=1, source_target_pairs={{0,16},{8,24},{16,0},{24,8},{1,17},{9,25},{17,1},{25,9},{2,18},{10... | collective-permute-start | bytes 196616 | tf_op jit(solution)/shard_map/ppermute | solution.py:490
  40.4 5.2 %collective-permute-start.23 = (bf16[256,128]{1,0:T(8,128)(2,1)S(1)}, bf16[256,128]{1,0:T(8,128)(2,1)S(1)}, u32[]{:S(2)}, u32[]{:S(2)}) collective-permute-start(bf16[256,128]{1,0:T(8,128)(2,1)S(1)} %get-tuple-element.42), channel_id=1, source_target_pairs={{0,24},{8,16},{16,8},{24,0},{1,25},{9,17},{17,9},{25,1},{2,26},{10... | collective-permute-start | bytes 196616 | tf_op jit(solution)/shard_map/ppermute | solution.py:490
  45.6 18.2 %collective-permute-start.27 = (bf16[1024,128]{1,0:T(8,128)(2,1)S(1)}, bf16[1024,128]{1,0:T(8,128)(2,1)S(1)}, u32[]{:S(2)}, u32[]{:S(2)}) collective-permute-start(bf16[1024,128]{1,0:T(8,128)(2,1)S(1)} %constant_dynamic-update-slice_fusion.4.refs_0_), channel_id=1, source_target_pairs={{0,4},{1,5},{2,6},{3,7},{4,0},{5,1},{6,2},{7,3},{8,12},{9,13},{10,... | collective-permute-start | bytes 786440 | tf_op jit(solution)/shard_map/ppermute | solution.py:453
  48.3 49.1 %copy-start.12 = (f32[512]{0:T(512)S(1)}, f32[512]{0:T(512)}, u32[]{:S(2)}) copy-start(f32[512]{0:T(512)} %param.19) | copy-start | bytes 6148
  48.3 21.0 %collective-permute-start.12 = (bf16[1024,128]{1,0:T(8,128)(2,1)S(1)}, bf16[1024,128]{1,0:T(8,128)(2,1)S(1)}, u32[]{:S(2)}, u32[]{:S(2)}) collective-permute-start(bf16[1024,128]{1,0:T(8,128)(2,1)S(1)} %constant_dynamic-update-slice_fusion.refs_0_), channel_id=1, source_target_pairs={{0,4},{1,5},{2,6},{3,7},{4,0},{5,1},{6,2},{7,3},{8,12},{9,13},{10,... | collective-permute-start | bytes 786440 | tf_op jit(solution)/shard_map/ppermute | solution.py:453
  48.7 21.9 %collective-permute-start.14 = (bf16[1024,128]{1,0:T(8,128)(2,1)S(1)}, bf16[1024,128]{1,0:T(8,128)(2,1)S(1)}, u32[]{:S(2)}, u32[]{:S(2)}) collective-permute-start(bf16[1024,128]{1,0:T(8,128)(2,1)S(1)} %constant_dynamic-update-slice_fusion.refs_0_), channel_id=1, source_target_pairs={{2,4},{3,5},{4,2},{5,3},{10,12},{11,13},{12,10},{13,11},{18,20},{1... | collective-permute-start | bytes 786440 | tf_op jit(solution)/shard_map/ppermute | solution.py:455
  49.4 26.1 %collective-permute-start.25 = (bf16[1024,128]{1,0:T(8,128)(2,1)S(1)}, bf16[1024,128]{1,0:T(8,128)(2,1)S(1)}, u32[]{:S(2)}, u32[]{:S(2)}) collective-permute-start(bf16[1024,128]{1,0:T(8,128)(2,1)S(1)} %constant_dynamic-update-slice_fusion.4.refs_0_), channel_id=1, source_target_pairs={{0,2},{1,3},{2,0},{3,1},{4,6},{5,7},{6,4},{7,5},{8,10},{9,11},{10,... | collective-permute-start | bytes 786440 | tf_op jit(solution)/shard_map/ppermute | solution.py:453
  53.9 21.7 %collective-permute-start.29 = (bf16[1024,128]{1,0:T(8,128)(2,1)S(1)}, bf16[1024,128]{1,0:T(8,128)(2,1)S(1)}, u32[]{:S(2)}, u32[]{:S(2)}) collective-permute-start(bf16[1024,128]{1,0:T(8,128)(2,1)S(1)} %constant_dynamic-update-slice_fusion.4.refs_0_), channel_id=1, source_target_pairs={{2,4},{3,5},{4,2},{5,3},{10,12},{11,13},{12,10},{13,11},{18,20},{1... | collective-permute-start | bytes 786440 | tf_op jit(solution)/shard_map/ppermute | solution.py:455
  63.7 12.3 %collective-permute-start.30 = (bf16[1024,128]{1,0:T(8,128)(2,1)S(1)}, bf16[1024,128]{1,0:T(8,128)(2,1)S(1)}, u32[]{:S(2)}, u32[]{:S(2)}) collective-permute-start(bf16[1024,128]{1,0:T(8,128)(2,1)S(1)} %collective-permute-done.27.refs_4_), channel_id=1, source_target_pairs={{2,0},{3,1},{4,6},{5,7},{10,8},{11,9},{12,14},{13,15},{18,16},{19,... | collective-permute-start | bytes 786440 | tf_op jit(solution)/shard_map/ppermute | solution.py:457
  69.4 11.1 %collective-permute-start.15 = (bf16[1024,128]{1,0:T(8,128)(2,1)S(1)}, bf16[1024,128]{1,0:T(8,128)(2,1)S(1)}, u32[]{:S(2)}, u32[]{:S(2)}) collective-permute-start(bf16[1024,128]{1,0:T(8,128)(2,1)S(1)} %collective-permute-done.12.refs_4_), channel_id=1, source_target_pairs={{2,0},{3,1},{4,6},{5,7},{10,8},{11,9},{12,14},{13,15},{18,16},{19,... | collective-permute-start | bytes 786440 | tf_op jit(solution)/shard_map/ppermute | solution.py:457
  70.7 14.4 %collective-permute-start.10 = (bf16[1024,128]{1,0:T(8,128)(2,1)S(1)}, bf16[1024,128]{1,0:T(8,128)(2,1)S(1)}, u32[]{:S(2)}, u32[]{:S(2)}) collective-permute-start(bf16[1024,128]{1,0:T(8,128)(2,1)S(1)} %constant_dynamic-update-slice_fusion.refs_0_), channel_id=1, source_target_pairs={{0,2},{1,3},{2,0},{3,1},{4,6},{5,7},{6,4},{7,5},{8,10},{9,11},{10,... | collective-permute-start | bytes 786440 | tf_op jit(solution)/shard_map/ppermute | solution.py:453
  75.5 9.6 %collective-permute-start.24 = (bf16[1024,128]{1,0:T(8,128)(2,1)S(1)}, bf16[1024,128]{1,0:T(8,128)(2,1)S(1)}, u32[]{:S(2)}, u32[]{:S(2)}) collective-permute-start(bf16[1024,128]{1,0:T(8,128)(2,1)S(1)} %constant_dynamic-update-slice_fusion.4.refs_0_), channel_id=1, source_target_pairs={{0,1},{1,0},{2,3},{3,2},{4,5},{5,4},{6,7},{7,6},{8,9},{9,8},{10,11... | collective-permute-start | bytes 786440 | tf_op jit(solution)/shard_map/ppermute | solution.py:462
  75.6 10.1 %collective-permute-start.26 = (bf16[1024,128]{1,0:T(8,128)(2,1)S(1)}, bf16[1024,128]{1,0:T(8,128)(2,1)S(1)}, u32[]{:S(2)}, u32[]{:S(2)}) collective-permute-start(bf16[1024,128]{1,0:T(8,128)(2,1)S(1)} %collective-permute-done.25.refs_2_), channel_id=1, source_target_pairs={{0,1},{1,0},{2,3},{3,2},{4,5},{5,4},{6,7},{7,6},{8,9},{9,8},{10,11... | collective-permute-start | bytes 786440 | tf_op jit(solution)/shard_map/ppermute | solution.py:462
  76.1 9.6 %collective-permute-start.28 = (bf16[1024,128]{1,0:T(8,128)(2,1)S(1)}, bf16[1024,128]{1,0:T(8,128)(2,1)S(1)}, u32[]{:S(2)}, u32[]{:S(2)}) collective-permute-start(bf16[1024,128]{1,0:T(8,128)(2,1)S(1)} %collective-permute-done.27.refs_4_), channel_id=1, source_target_pairs={{0,1},{1,0},{2,3},{3,2},{4,5},{5,4},{6,7},{7,6},{8,9},{9,8},{10,11... | collective-permute-start | bytes 786440 | tf_op jit(solution)/shard_map/ppermute | solution.py:462
  80.5 5.6 %collective-permute-start.31 = (bf16[1024,128]{1,0:T(8,128)(2,1)S(1)}, bf16[1024,128]{1,0:T(8,128)(2,1)S(1)}, u32[]{:S(2)}, u32[]{:S(2)}) collective-permute-start(bf16[1024,128]{1,0:T(8,128)(2,1)S(1)} %add.28.refs_6_), channel_id=1, source_target_pairs={{0,1},{1,0},{2,3},{3,2},{4,5},{5,4},{6,7},{7,6},{8,9},{9,8},{10,11... | collective-permute-start | bytes 786440 | tf_op jit(solution)/shard_map/ppermute | solution.py:462
  85.1 15.3 %collective-permute-start.9 = (bf16[1024,128]{1,0:T(8,128)(2,1)S(1)}, bf16[1024,128]{1,0:T(8,128)(2,1)S(1)}, u32[]{:S(2)}, u32[]{:S(2)}) collective-permute-start(bf16[1024,128]{1,0:T(8,128)(2,1)S(1)} %constant_dynamic-update-slice_fusion.refs_0_), channel_id=1, source_target_pairs={{0,1},{1,0},{2,3},{3,2},{4,5},{5,4},{6,7},{7,6},{8,9},{9,8},{10,11... | collective-permute-start | bytes 786440 | tf_op jit(solution)/shard_map/ppermute | solution.py:462
  85.1 15.3 %collective-permute-start.13 = (bf16[1024,128]{1,0:T(8,128)(2,1)S(1)}, bf16[1024,128]{1,0:T(8,128)(2,1)S(1)}, u32[]{:S(2)}, u32[]{:S(2)}) collective-permute-start(bf16[1024,128]{1,0:T(8,128)(2,1)S(1)} %collective-permute-done.12.refs_4_), channel_id=1, source_target_pairs={{0,1},{1,0},{2,3},{3,2},{4,5},{5,4},{6,7},{7,6},{8,9},{9,8},{10,11... | collective-permute-start | bytes 786440 | tf_op jit(solution)/shard_map/ppermute | solution.py:462
  85.6 14.8 %collective-permute-start.11 = (bf16[1024,128]{1,0:T(8,128)(2,1)S(1)}, bf16[1024,128]{1,0:T(8,128)(2,1)S(1)}, u32[]{:S(2)}, u32[]{:S(2)}) collective-permute-start(bf16[1024,128]{1,0:T(8,128)(2,1)S(1)} %collective-permute-done.10.refs_2_), channel_id=1, source_target_pairs={{0,1},{1,0},{2,3},{3,2},{4,5},{5,4},{6,7},{7,6},{8,9},{9,8},{10,11... | collective-permute-start | bytes 786440 | tf_op jit(solution)/shard_map/ppermute | solution.py:462
  85.7 14.8 %collective-permute-start.16 = (bf16[1024,128]{1,0:T(8,128)(2,1)S(1)}, bf16[1024,128]{1,0:T(8,128)(2,1)S(1)}, u32[]{:S(2)}, u32[]{:S(2)}) collective-permute-start(bf16[1024,128]{1,0:T(8,128)(2,1)S(1)} %add.24.refs_6_), channel_id=1, source_target_pairs={{0,1},{1,0},{2,3},{3,2},{4,5},{5,4},{6,7},{7,6},{8,9},{9,8},{10,11... | collective-permute-start | bytes 786440 | tf_op jit(solution)/shard_map/ppermute | solution.py:462
  88.1 1.2 collective-permute-start.32
  89.3 3.6 %collective-permute-start.33 = (f32[1,256]{1,0:T(1,128)S(1)}, f32[1,256]{1,0:T(1,128)S(1)}, u32[]{:S(2)}, u32[]{:S(2)}) collective-permute-start(f32[1,256]{1,0:T(1,128)S(1)} %add.29), channel_id=1, source_target_pairs={{0,2},{1,3},{2,0},{3,1},{4,6},{5,7},{6,4},{7,5},{8,10},{9,11},{10,... | collective-permute-start | bytes 3080 | tf_op jit(solution)/shard_map/ppermute | solution.py:469
  92.9 4.5 %collective-permute-start.34 = (f32[1,256]{1,0:T(1,128)S(1)}, f32[1,256]{1,0:T(1,128)S(1)}, u32[]{:S(2)}, u32[]{:S(2)}) collective-permute-start(f32[1,256]{1,0:T(1,128)S(1)} %add.30), channel_id=1, source_target_pairs={{0,4},{1,5},{2,6},{3,7},{4,0},{5,1},{6,2},{7,3},{8,12},{9,13},{10,... | collective-permute-start | bytes 3080 | tf_op jit(solution)/shard_map/ppermute | solution.py:469
  97.4 15.9 %copy-start.14 = (s32[512]{0:T(512)S(1)}, s32[512]{0:T(512)}, u32[]{:S(2)}) copy-start(s32[512]{0:T(512)} %param.21) | copy-start | bytes 6148
  97.4 16.1 %copy-start.1 = (bf16[512,256]{1,0:T(8,128)(2,1)S(1)}, bf16[512,256]{1,0:T(8,128)(2,1)}, u32[]{:S(2)}) copy-start(bf16[512,256]{1,0:T(8,128)(2,1)} %constant.16.clone.fh_ref.fh) | copy-start | bytes 786436
  97.4 16.1 %copy-start.2 = (bf16[512,256]{1,0:T(8,128)(2,1)S(1)}, bf16[512,256]{1,0:T(8,128)(2,1)}, u32[]{:S(2)}) copy-start(bf16[512,256]{1,0:T(8,128)(2,1)} %constant.17.clone.fl_ref.fl) | copy-start | bytes 786436
  97.6 17.4 %copy-start.7 = (bf16[256,512]{1,0:T(8,128)(2,1)S(1)}, bf16[256,512]{1,0:T(8,128)(2,1)}, u32[]{:S(2)}) copy-start(bf16[256,512]{1,0:T(8,128)(2,1)} %constant.18.clone.gh) | copy-start | bytes 786436
  97.6 17.4 %copy-start.8 = (bf16[256,512]{1,0:T(8,128)(2,1)S(1)}, bf16[256,512]{1,0:T(8,128)(2,1)}, u32[]{:S(2)}) copy-start(bf16[256,512]{1,0:T(8,128)(2,1)} %constant.19.clone.gl) | copy-start | bytes 786436
  97.6 17.4 %copy-start.13 = (f32[512]{0:T(512)S(1)}, f32[512]{0:T(512)}, u32[]{:S(2)}) copy-start(f32[512]{0:T(512)} %param.22) | copy-start | bytes 6148
  97.6 17.4 %collective-permute-start.35 = (bf16[256,512]{1,0:T(8,128)(2,1)S(1)}, bf16[256,512]{1,0:T(8,128)(2,1)S(1)}, u32[]{:S(2)}, u32[]{:S(2)}) collective-permute-start(bf16[256,512]{1,0:T(8,128)(2,1)S(1)} %norm_low.1.own_ref.low_ref), channel_id=1, source_target_pairs={{0,8},{8,16},{16,24},{1,9},{9,17},{17,25},{2,10},{10,18},{18,26},{... | collective-permute-start | bytes 786440 | tf_op jit(solution)/shard_map/ppermute | solution.py:24
  102.4 1.2 collective-permute-start.17
  103.6 3.6 %collective-permute-start.18 = (f32[1,256]{1,0:T(1,128)S(1)}, f32[1,256]{1,0:T(1,128)S(1)}, u32[]{:S(2)}, u32[]{:S(2)}) collective-permute-start(f32[1,256]{1,0:T(1,128)S(1)} %add.25), channel_id=1, source_target_pairs={{0,2},{1,3},{2,0},{3,1},{4,6},{5,7},{6,4},{7,5},{8,10},{9,11},{10,... | collective-permute-start | bytes 3080 | tf_op jit(solution)/shard_map/ppermute | solution.py:469
  107.2 4.5 %collective-permute-start.19 = (f32[1,256]{1,0:T(1,128)S(1)}, f32[1,256]{1,0:T(1,128)S(1)}, u32[]{:S(2)}, u32[]{:S(2)}) collective-permute-start(f32[1,256]{1,0:T(1,128)S(1)} %add.26), channel_id=1, source_target_pairs={{0,4},{1,5},{2,6},{3,7},{4,0},{5,1},{6,2},{7,3},{8,12},{9,13},{10,... | collective-permute-start | bytes 3080 | tf_op jit(solution)/shard_map/ppermute | solution.py:469
  111.8 8.3 %collective-permute-start.20 = (bf16[256,512]{1,0:T(8,128)(2,1)S(1)}, bf16[256,512]{1,0:T(8,128)(2,1)S(1)}, u32[]{:S(2)}, u32[]{:S(2)}) collective-permute-start(bf16[256,512]{1,0:T(8,128)(2,1)S(1)} %norm_high.1.own_ref), channel_id=1, source_target_pairs={{8,0},{16,8},{24,16},{9,1},{17,9},{25,17},{10,2},{18,10},{26,18},{... | collective-permute-start | bytes 786440 | tf_op jit(solution)/shard_map/ppermute | solution.py:24
  113.5 1.0 copy-start.9

commit v2 on v1

--- a/solution.py
+++ b/solution.py
@@ -7,6 +7,7 @@
 from jax.experimental import pallas as pl
 from jax.experimental.pallas import tpu as pltpu
 from jax.sharding import PartitionSpec as P
+
 
 HD = 128
 EPS = 1e-05
@@ -170,30 +171,38 @@
     return jnp.where(first_is_high, 1 - high, high).astype(jnp.int32)
 
 
-def pack_kernel(n, slots_ref, ids_ref, q_ref, k_ref, v_ref, *outs):
+def pack_kernel(n, high, slots_ref, ids_ref, q_ref, k_ref, v_ref, *rest):
+    outs, sem = rest[:n], rest[n]
     rank = ids_ref[0]
-    rows, width = q_ref.shape
-    wide = width // n
+    rows = outs[0].shape[0] // 3
+    wide = outs[0].shape[1]
+    half = half_index(slots_ref, ids_ref, high)
+    source_rows = pl.ds(pl.multiple_of(half * rows, rows), rows)
+    copies = []
     for k in range(n):
         cols = pl.ds(pl.multiple_of((rank ^ k) * wide, wide), wide)
         for a, ref in enumerate((q_ref, k_ref, v_ref)):
-            outs[k][a * rows : (a + 1) * rows, :] = ref[:, cols]
+            copy = pltpu.make_async_copy(
+                ref.at[source_rows, cols],
+                outs[k].at[a * rows : (a + 1) * rows, :],
+                sem.at[k, a],
+            )
+            copy.start()
+            copies.append(copy)
+    for copy in copies:
+        copy.wait()
 
 
 def pack(n, high, slots, ids, q, k, v):
     rows, width = q.shape[0] // 2, q.shape[1]
-    spec = pl.BlockSpec((rows, width), lambda i, s, d: (half_index(s, d, high), 0))
     piece = jax.ShapeDtypeStruct((3 * rows, width // n), BF)
     return pl.pallas_call(
-        functools.partial(pack_kernel, n),
+        functools.partial(pack_kernel, n, high),
         out_shape=[piece] * n,
-        grid_spec=pltpu.PrefetchScalarGridSpec(
-            num_scalar_prefetch=2,
-            grid=(1,),
-            in_specs=[spec] * 3,
-            out_specs=[pl.BlockSpec((3 * rows, width // n), lambda i, s, d: (0, 0))] * n,
-        ),
-        compiler_params=params(),
+        in_specs=[sm(), sm()] + [pl.BlockSpec(memory_space=pltpu.HBM)] * 3,
+        out_specs=[vm()] * n,
+        scratch_shapes=[pltpu.SemaphoreType.DMA((n, 3))],
+        compiler_params=params(8),
         cost_estimate=cost(0, 12 * rows * width),
         name="pack_high" if high else "pack_low",
     )(slots, ids, q, k, v)
@@ -278,8 +287,8 @@
 
 
 def project_kernel(n, high, slots_ref, ids_ref, inc_ref, w_ref, *refs):
-    parts = refs[:-3]
-    res_ref, sq_ref, lhs = refs[-3:]
+    parts = refs[:-4]
+    res_ref, raw_ref, sq_ref, lhs = refs[-4:]
     rank = ids_ref[0]
     me = ids_ref[1]
     rows = res_ref.shape[0]
@@ -294,6 +303,7 @@
         depth = pl.ds(pl.multiple_of((me ^ index) * width, width), width)
         total = total + jnp.dot(lhs[...], w_ref[depth, :], preferred_element_type=F32)
     res_ref[...] = total
+    raw_ref[...] = total.astype(BF)
     squares = total * total
     lanes = squares[:, 0:HD]
     for g in range(1, squares.shape[1] // HD):
@@ -307,10 +317,11 @@
         functools.partial(project_kernel, n, high),
         out_shape=[
             jax.ShapeDtypeStruct((rows, width), F32),
+            jax.ShapeDtypeStruct((rows, width), BF),
             jax.ShapeDtypeStruct((1, rows), F32),
         ],
         in_specs=[sm(), sm()] + [vm()] * (2 + len(parts)),
-        out_specs=[vm(), vm()],
+        out_specs=[vm()] * 3,
         scratch_shapes=[VMEM((rows, width), BF)],
         compiler_params=params(20),
         cost_estimate=cost(2 * rows * width * w_out.shape[0], 2 * w_out.size * 1.5),
@@ -333,7 +344,7 @@
     out_ref[...] = normed_rows(res_ref[...], sq_ref[...], gain_ref[...], model_width)
 
 
-def norm(model_width, res, sq, gain, name):
+def norm(model_width, res, sq, gain):
     return pl.pallas_call(
         functools.partial(norm_kernel, model_width),
         out_shape=jax.ShapeDtypeStruct(res.shape, BF),
@@ -341,7 +352,6 @@
         out_specs=vm(),
         compiler_params=params(8),
         cost_estimate=cost(4 * res.size, 6 * res.size),
-        name=name,
     )(res, sq, gain)
 
 
@@ -432,43 +442,54 @@
 
 
 def conv_high_kernel(
-    n, slots_ref, ids_ref, res_ref, own_ref, before_ref, low_ref, done_ref, spec_ref, skip_ref,
-    fh, fl, gh, gl, out_ref,
+    n, model_width, slots_ref, ids_ref, res_ref, sq_ref, raw_ref, raw_sq_ref, low_ref, done_ref,
+    spec_ref, gain_ref, skip_ref, fh, fl, gh, gl, out_ref,
 ):
     rows = res_ref.shape[0]
     last = ids_ref[0] == n - 1
-    before = jnp.where(last, low_ref[...].astype(F32), before_ref[...].astype(F32)).astype(BF)
-    conv = conv_rows(before, own_ref[...], fh[...], fl[...], gh[...], gl[...], spec_ref[...])
+    own = normed_rows(res_ref[...], sq_ref[...], gain_ref[...], model_width)
+    raw = normed_rows(raw_ref[...].astype(F32), raw_sq_ref[...], gain_ref[...], model_width)
+    before = jnp.where(last, low_ref[...].astype(F32), raw.astype(F32)).astype(BF)
+    conv = conv_rows(before, own, fh[...], fl[...], gh[...], gl[...], spec_ref[...])
     half = half_index(slots_ref, ids_ref, 1)
     out_ref[pl.ds(pl.multiple_of((1 - half) * rows, rows), rows), :] = done_ref[...]
     out_ref[pl.ds(pl.multiple_of(half * rows, rows), rows), :] = finish(
-        res_ref[...], own_ref[...], conv, skip_ref[...]
-    )
+        res_ref[...], own, conv, skip_ref[...]
+    )
+
+
+def moved(block, axis, route):
+    return lax.ppermute(block, axis, route)
 
 
 def gather_mp(own, size):
     chips = size // 2
     pieces = [own]
     for k in range(1, chips - 1):
-        pieces.append(lax.ppermute(own, "mp", xor_route(size, 2 * k)))
+        pieces.append(moved(own, "mp", xor_route(size, 2 * k)))
     inner = [(i, i ^ (size - 2)) for i in range(2, size - 2)]
-    direct = lax.ppermute(own, "mp", inner)
+    direct = moved(own, "mp", inner)
     ends = [(2, 0), (3, 1), (size - 4, size - 2), (size - 3, size - 1)]
-    relayed = lax.ppermute(pieces[chips - 2], "mp", ends)
+    relayed = moved(pieces[chips - 2], "mp", ends)
     pieces.append(direct + relayed)
     parts = []
     for piece in pieces:
         parts.append(piece)
-        parts.append(lax.ppermute(piece, "mp", xor_route(size, 1)))
+        parts.append(moved(piece, "mp", xor_route(size, 1)))
     return parts
 
 
 def total_mp(part, size):
     k = 1
     while k < size:
-        part = part + lax.ppermute(part, "mp", xor_route(size, k))
+        part = part + moved(part, "mp", xor_route(size, k))
         k *= 2
     return part
+
+
+def before_rows(block, distance):
+    devices = range(lax.axis_size("seq"))
+    return moved(block, "seq", [(i - distance, i) for i in devices if i - distance in devices])
 
 
 def fast_device(
@@ -486,9 +507,7 @@
     backward = tuple(jnp.asarray(t) for t in backward)
 
     def exchange(pieces):
-        return [pieces[0]] + [
-            lax.ppermute(pieces[k], "seq", xor_route(n, k)) for k in range(1, n)
-        ]
+        return [pieces[0]] + [moved(pieces[k], "seq", xor_route(n, k)) for k in range(1, n)]
 
     low = exchange(pack(n, 0, slot_map, ids, queries, key_vecs, value_vecs))
     high = exchange(pack(n, 1, slot_map, ids, queries, key_vecs, value_vecs))
@@ -499,9 +518,9 @@
     att_high = exchange(attend(n, 1, rows, ids, low + high))
     parts_high = gather_mp(jnp.concatenate(att_high, axis=0), mp_size)
 
-    res_low, sq_low = project(n, 0, slot_map, ids, incoming, w_out, parts_low)
-    norm_low = norm(model_width, res_low, total_mp(sq_low, mp_size), gain, "norm_low")
-    before_low = shifted(norm_low, "seq", 1)
+    res_low, _, sq_low = project(n, 0, slot_map, ids, incoming, w_out, parts_low)
+    norm_low = norm(model_width, res_low, total_mp(sq_low, mp_size), gain)
+    before_low = before_rows(norm_low, 1)
     done_low = pl.pallas_call(
         conv_low_kernel,
         out_shape=jax.ShapeDtypeStruct((rows, width), BF),
@@ -512,20 +531,21 @@
         name="conv_low",
     )(res_low, norm_low, before_low, spec, skip, *forward, *backward)
 
-    res_high, sq_high = project(n, 1, slot_map, ids, incoming, w_out, parts_high)
-    norm_high = norm(model_width, res_high, total_mp(sq_high, mp_size), gain, "norm_high")
-    before_high = shifted(norm_high, "seq", -1)
+    res_high, raw_high, sq_high = project(n, 1, slot_map, ids, incoming, w_out, parts_high)
+    raw_before = before_rows(raw_high, -1)
+    sq_high = total_mp(sq_high, mp_size)
+    sq_before = before_rows(sq_high, -1)
     return pl.pallas_call(
-        functools.partial(conv_high_kernel, n),
+        functools.partial(conv_high_kernel, n, model_width),
         out_shape=jax.ShapeDtypeStruct((2 * rows, width), BF),
-        in_specs=[sm(), sm()] + [vm()] * 11,
+        in_specs=[sm(), sm()] + [vm()] * 13,
         out_specs=vm(),
         compiler_params=params(20),
         cost_estimate=cost(14 * rows * rows * width, 12 * rows * width),
         name="conv_high",
     )(
-        slot_map, ids, res_high, norm_high, before_high, norm_low, done_low, spec, skip,
-        *forward, *backward,
+        slot_map, ids, res_high, sq_high, raw_before, sq_before, norm_low, done_low, spec, gain,
+        skip, *forward, *backward,
     )
 
 
@@ -547,7 +567,9 @@
         and rows % 256 == 0
         and filters.shape[1] <= rows
     )
-    return (fast_device if fits else general_device)(*arrays)
+    if not fits:
+        return general_device(*arrays)
+    return fast_device(*arrays)
 
 
 def solution(mesh):

time: 123 us -> 124 us (level)
  Pallas kernels: 16.1 us -> 17.7 us
    pallas_call x2, Pallas kernels: 3.89 us -> 5.16 us  [project(): pl.pallas_call(functools.partial(project_kernel, n, high), out_shape=[jax...]
    ppermute x36 -> x37, waiting for transfers between devices: 55.3 us -> 54.3 us  [moved(): return lax.ppermute(block, axis, route)]
    ppermute x36 -> x37, starting transfers between devices: 45.8 us -> 46.7 us  [moved(): return lax.ppermute(block, axis, route)]
  transfers between devices with their start and end apart: 36 -> 37, of which waited for: 16 -> 16; matrix products, arithmetic and copies ran while one was open for 0% -> 0% of each run, Pallas kernels for 7% -> 8%
where the time goes in v2:
time: 124 us; the launch traced here: 123 us
  waiting for transfers between devices  54.3 us (44%)
  starting transfers between devices  46.7 us (38%)
  Pallas kernels  17.7 us (14%)
  local copies, waits for them, and re-layouts  4.07 us (3%)
    ppermute x37, waiting for transfers between devices, moved(): return lax.ppermute(block, axis, route)  54.3 us
    ppermute x37, starting transfers between devices, moved(): return lax.ppermute(block, axis, route)  46.7 us
    pallas_call x2, Pallas kernels, attend(): pl.pallas_call(functools.partial(attend_kernel, n, high, rows), out_shape...  5.9 us
    pallas_call x2, Pallas kernels, project(): pl.pallas_call(functools.partial(project_kernel, n, high), out_shape=[jax...  5.16 us
    unnamed x36, local copies, waits for them, and re-layouts  3.9 us
    pallas_call x1, Pallas kernels, fast_device(): pl.pallas_call(functools.partial(conv_high_kernel, n, model_width), out_s...  2.91 us
  transfers between devices with their start and end apart: 37, of which 16 were waited for; matrix products, arithmetic and copies ran while one was open for 0% of the time, Pallas kernels for 8%

profile of v2, /device:TPU:0, one launch (start us, length us, event | category | flops | bytes accessed | tf_op | source)
XLA Modules:
  0.0 123.4 jit_solution(4851724474276689410)
XLA Ops:
  0.0 0.1 pad_add_fusion.ids_ref
  0.1 1.0 copy-done.4
  1.1 1.0 copy-done.5
  2.2 1.0 copy-done.6
  3.2 0.7 copy-done.10
  3.9 0.8 pack_low.1
  4.7 3.0 %collective-permute-start = (bf16[768,128]{1,0:T(8,128)(2,1)S(1)}, bf16[768,128]{1,0:T(8,128)(2,1)S(1)}, u32[]{:S(2)}, u32[]{:S(2)}) collective-permute-start(bf16[768,128]{1,0:T(8,128)(2,1)S(1)} %get-tuple-element.27), channel_id=1, source_target_pairs={{0,8},{8,0},{16,24},{24,16},{1,9},{9,1},{17,25},{25,17},{2,10},{10... | collective-permute-start | bytes 589832 | tf_op jit(solution)/shard_map/ppermute | solution.py:462
  7.7 1.5 %collective-permute-start.1 = (bf16[768,128]{1,0:T(8,128)(2,1)S(1)}, bf16[768,128]{1,0:T(8,128)(2,1)S(1)}, u32[]{:S(2)}, u32[]{:S(2)}) collective-permute-start(bf16[768,128]{1,0:T(8,128)(2,1)S(1)} %get-tuple-element.28), channel_id=1, source_target_pairs={{0,16},{8,24},{16,0},{24,8},{1,17},{9,25},{17,1},{25,9},{2,18},{10... | collective-permute-start | bytes 589832 | tf_op jit(solution)/shard_map/ppermute | solution.py:462
  9.3 0.8 pack_high.1
  10.2 2.0 %collective-permute-start.3 = (bf16[768,128]{1,0:T(8,128)(2,1)S(1)}, bf16[768,128]{1,0:T(8,128)(2,1)S(1)}, u32[]{:S(2)}, u32[]{:S(2)}) collective-permute-start(bf16[768,128]{1,0:T(8,128)(2,1)S(1)} %get-tuple-element.31), channel_id=1, source_target_pairs={{0,8},{8,0},{16,24},{24,16},{1,9},{9,1},{17,25},{25,17},{2,10},{10... | collective-permute-start | bytes 589832 | tf_op jit(solution)/shard_map/ppermute | solution.py:462
  12.1 1.5 %collective-permute-start.4 = (bf16[768,128]{1,0:T(8,128)(2,1)S(1)}, bf16[768,128]{1,0:T(8,128)(2,1)S(1)}, u32[]{:S(2)}, u32[]{:S(2)}) collective-permute-start(bf16[768,128]{1,0:T(8,128)(2,1)S(1)} %get-tuple-element.32), channel_id=1, source_target_pairs={{0,16},{8,24},{16,0},{24,8},{1,17},{9,25},{17,1},{25,9},{2,18},{10... | collective-permute-start | bytes 589832 | tf_op jit(solution)/shard_map/ppermute | solution.py:462
  13.7 2.8 %collective-permute-start.5 = (bf16[768,128]{1,0:T(8,128)(2,1)S(1)}, bf16[768,128]{1,0:T(8,128)(2,1)S(1)}, u32[]{:S(2)}, u32[]{:S(2)}) collective-permute-start(bf16[768,128]{1,0:T(8,128)(2,1)S(1)} %get-tuple-element.33), channel_id=1, source_target_pairs={{0,24},{8,16},{16,8},{24,0},{1,25},{9,17},{17,9},{25,1},{2,26},{10... | collective-permute-start | bytes 589832 | tf_op jit(solution)/shard_map/ppermute | solution.py:462
  16.5 2.9 %collective-permute-done.1.refs_2_ = bf16[768,128]{1,0:T(8,128)(2,1)S(1)} collective-permute-done((bf16[768,128]{1,0:T(8,128)(2,1)S(1)}, bf16[768,128]{1,0:T(8,128)(2,1)S(1)}, u32[]{:S(2)}, u32[]{:S(2)}) %collective-permute-start.1) | collective-permute-done | bytes 196640 | tf_op jit(solution)/shard_map/ppermute | solution.py:462
  19.3 2.6 %collective-permute-done.3.refs_5_ = bf16[768,128]{1,0:T(8,128)(2,1)S(1)} collective-permute-done((bf16[768,128]{1,0:T(8,128)(2,1)S(1)}, bf16[768,128]{1,0:T(8,128)(2,1)S(1)}, u32[]{:S(2)}, u32[]{:S(2)}) %collective-permute-start.3) | collective-permute-done | bytes 196640 | tf_op jit(solution)/shard_map/ppermute | solution.py:462
  22.0 4.8 %collective-permute-done.4.refs_6_ = bf16[768,128]{1,0:T(8,128)(2,1)S(1)} collective-permute-done((bf16[768,128]{1,0:T(8,128)(2,1)S(1)}, bf16[768,128]{1,0:T(8,128)(2,1)S(1)}, u32[]{:S(2)}, u32[]{:S(2)}) %collective-permute-start.4) | collective-permute-done | bytes 196640 | tf_op jit(solution)/shard_map/ppermute | solution.py:462
  26.7 3.6 %attend_high.1 = (bf16[256,128]{1,0:T(8,128)(2,1)S(1)}, bf16[256,128]{1,0:T(8,128)(2,1)S(1)}, bf16[256,128]{1,0:T(8,128)(2,1)S(1)}, bf16[256,128]{1,0:T(8,128)(2,1)S(1)}) custom-call(s32[2]{0:T(128)S(1)} %pad_add_fusion.ids_ref, bf16[768,128]{1,0:T(8,128)(2,1)S(1)} %get-tuple-element.26.refs_0_, bf16[768,128]{1,0:T(8,128)(2,1)S(1)} %collective-permute-done.refs_1_, ...), custom_call_target="tpu_custom_call" | custom-call | flops 872415232 | bytes 2097152 | tf_op jit(solution)/shard_map/attend_high/pallas_call | solution.py:272
  30.4 1.3 %collective-permute-start.6 = (bf16[256,128]{1,0:T(8,128)(2,1)S(1)}, bf16[256,128]{1,0:T(8,128)(2,1)S(1)}, u32[]{:S(2)}, u32[]{:S(2)}) collective-permute-start(bf16[256,128]{1,0:T(8,128)(2,1)S(1)} %get-tuple-element.35), channel_id=1, source_target_pairs={{0,8},{8,0},{16,24},{24,16},{1,9},{9,1},{17,25},{25,17},{2,10},{10... | collective-permute-start | bytes 196616 | tf_op jit(solution)/shard_map/ppermute | solution.py:462
  31.7 0.8 collective-permute-start.7
  32.5 1.4 %collective-permute-start.8 = (bf16[256,128]{1,0:T(8,128)(2,1)S(1)}, bf16[256,128]{1,0:T(8,128)(2,1)S(1)}, u32[]{:S(2)}, u32[]{:S(2)}) collective-permute-start(bf16[256,128]{1,0:T(8,128)(2,1)S(1)} %get-tuple-element.37), channel_id=1, source_target_pairs={{0,24},{8,16},{16,8},{24,0},{1,25},{9,17},{17,9},{25,1},{2,26},{10... | collective-permute-start | bytes 196616 | tf_op jit(solution)/shard_map/ppermute | solution.py:462
  33.9 2.3 %attend_low.1 = (bf16[256,128]{1,0:T(8,128)(2,1)S(1)}, bf16[256,128]{1,0:T(8,128)(2,1)S(1)}, bf16[256,128]{1,0:T(8,128)(2,1)S(1)}, bf16[256,128]{1,0:T(8,128)(2,1)S(1)}) custom-call(s32[2]{0:T(128)S(1)} %pad_add_fusion.ids_ref, bf16[768,128]{1,0:T(8,128)(2,1)S(1)} %get-tuple-element.26.refs_0_, bf16[768,128]{1,0:T(8,128)(2,1)S(1)} %collective-permute-done.refs_1_, ...), custom_call_target="tpu_custom_call" | custom-call | flops 335544320 | bytes 1048576 | tf_op jit(solution)/shard_map/attend_low/pallas_call | solution.py:272
  36.2 1.3 %collective-permute-start.22 = (bf16[256,128]{1,0:T(8,128)(2,1)S(1)}, bf16[256,128]{1,0:T(8,128)(2,1)S(1)}, u32[]{:S(2)}, u32[]{:S(2)}) collective-permute-start(bf16[256,128]{1,0:T(8,128)(2,1)S(1)} %get-tuple-element.42), channel_id=1, source_target_pairs={{0,8},{8,0},{16,24},{24,16},{1,9},{9,1},{17,25},{25,17},{2,10},{10... | collective-permute-start | bytes 196616 | tf_op jit(solution)/shard_map/ppermute | solution.py:462
  37.6 0.8 collective-permute-start.23
  38.4 2.2 %collective-permute-done.22 = bf16[256,128]{1,0:T(8,128)(2,1)S(1)} collective-permute-done((bf16[256,128]{1,0:T(8,128)(2,1)S(1)}, bf16[256,128]{1,0:T(8,128)(2,1)S(1)}, u32[]{:S(2)}, u32[]{:S(2)}) %collective-permute-start.22) | collective-permute-done | bytes 65568 | tf_op jit(solution)/shard_map/ppermute | solution.py:462
  40.6 1.5 %collective-permute-start.24 = (bf16[256,128]{1,0:T(8,128)(2,1)S(1)}, bf16[256,128]{1,0:T(8,128)(2,1)S(1)}, u32[]{:S(2)}, u32[]{:S(2)}) collective-permute-start(bf16[256,128]{1,0:T(8,128)(2,1)S(1)} %get-tuple-element.44), channel_id=1, source_target_pairs={{0,24},{8,16},{16,8},{24,0},{1,25},{9,17},{17,9},{25,1},{2,26},{10... | collective-permute-start | bytes 196616 | tf_op jit(solution)/shard_map/ppermute | solution.py:462
  42.1 3.6 %collective-permute-done.24 = bf16[256,128]{1,0:T(8,128)(2,1)S(1)} collective-permute-done((bf16[256,128]{1,0:T(8,128)(2,1)S(1)}, bf16[256,128]{1,0:T(8,128)(2,1)S(1)}, u32[]{:S(2)}, u32[]{:S(2)}) %collective-permute-start.24) | collective-permute-done | bytes 65568 | tf_op jit(solution)/shard_map/ppermute | solution.py:462
  45.7 2.7 %collective-permute-start.28 = (bf16[1024,128]{1,0:T(8,128)(2,1)S(1)}, bf16[1024,128]{1,0:T(8,128)(2,1)S(1)}, u32[]{:S(2)}, u32[]{:S(2)}) collective-permute-start(bf16[1024,128]{1,0:T(8,128)(2,1)S(1)} %constant_dynamic-update-slice_fusion.4.refs_0_), channel_id=1, source_target_pairs={{0,4},{1,5},{2,6},{3,7},{4,0},{5,1},{6,2},{7,3},{8,12},{9,13},{10,... | collective-permute-start | bytes 786440 | tf_op jit(solution)/shard_map/ppermute | solution.py:462
  48.5 0.4 collective-permute-start.12
  48.9 0.7 collective-permute-start.14
  49.6 4.4 %collective-permute-start.26 = (bf16[1024,128]{1,0:T(8,128)(2,1)S(1)}, bf16[1024,128]{1,0:T(8,128)(2,1)S(1)}, u32[]{:S(2)}, u32[]{:S(2)}) collective-permute-start(bf16[1024,128]{1,0:T(8,128)(2,1)S(1)} %constant_dynamic-update-slice_fusion.4.refs_0_), channel_id=1, source_target_pairs={{0,2},{1,3},{2,0},{3,1},{4,6},{5,7},{6,4},{7,5},{8,10},{9,11},{10,... | collective-permute-start | bytes 786440 | tf_op jit(solution)/shard_map/ppermute | solution.py:462
  54.0 0.7 collective-permute-start.30
  54.7 9.2 %collective-permute-done.28.refs_4_ = bf16[1024,128]{1,0:T(8,128)(2,1)S(1)} collective-permute-done((bf16[1024,128]{1,0:T(8,128)(2,1)S(1)}, bf16[1024,128]{1,0:T(8,128)(2,1)S(1)}, u32[]{:S(2)}, u32[]{:S(2)}) %collective-permute-start.28) | collective-permute-done | bytes 262176 | tf_op jit(solution)/shard_map/ppermute | solution.py:462
  63.9 1.3 %collective-permute-start.31 = (bf16[1024,128]{1,0:T(8,128)(2,1)S(1)}, bf16[1024,128]{1,0:T(8,128)(2,1)S(1)}, u32[]{:S(2)}, u32[]{:S(2)}) collective-permute-start(bf16[1024,128]{1,0:T(8,128)(2,1)S(1)} %collective-permute-done.28.refs_4_), channel_id=1, source_target_pairs={{2,0},{3,1},{4,6},{5,7},{10,8},{11,9},{12,14},{13,15},{18,16},{19,... | collective-permute-start | bytes 786440 | tf_op jit(solution)/shard_map/ppermute | solution.py:462
  65.2 4.3 %collective-permute-done.12.refs_4_ = bf16[1024,128]{1,0:T(8,128)(2,1)S(1)} collective-permute-done((bf16[1024,128]{1,0:T(8,128)(2,1)S(1)}, bf16[1024,128]{1,0:T(8,128)(2,1)S(1)}, u32[]{:S(2)}, u32[]{:S(2)}) %collective-permute-start.12) | collective-permute-done | bytes 262176 | tf_op jit(solution)/shard_map/ppermute | solution.py:462
  69.5 1.3 %collective-permute-start.15 = (bf16[1024,128]{1,0:T(8,128)(2,1)S(1)}, bf16[1024,128]{1,0:T(8,128)(2,1)S(1)}, u32[]{:S(2)}, u32[]{:S(2)}) collective-permute-start(bf16[1024,128]{1,0:T(8,128)(2,1)S(1)} %collective-permute-done.12.refs_4_), channel_id=1, source_target_pairs={{2,0},{3,1},{4,6},{5,7},{10,8},{11,9},{12,14},{13,15},{18,16},{19,... | collective-permute-start | bytes 786440 | tf_op jit(solution)/shard_map/ppermute | solution.py:462
  70.8 4.9 %collective-permute-start.10 = (bf16[1024,128]{1,0:T(8,128)(2,1)S(1)}, bf16[1024,128]{1,0:T(8,128)(2,1)S(1)}, u32[]{:S(2)}, u32[]{:S(2)}) collective-permute-start(bf16[1024,128]{1,0:T(8,128)(2,1)S(1)} %constant_dynamic-update-slice_fusion.refs_0_), channel_id=1, source_target_pairs={{0,2},{1,3},{2,0},{3,1},{4,6},{5,7},{6,4},{7,5},{8,10},{9,11},{10,... | collective-permute-start | bytes 786440 | tf_op jit(solution)/shard_map/ppermute | solution.py:462
  75.7 0.5 collective-permute-start.27
  76.3 0.1 add.28.refs_6_
  76.4 4.3 %collective-permute-done.15 = bf16[1024,128]{1,0:T(8,128)(2,1)S(1)} collective-permute-done((bf16[1024,128]{1,0:T(8,128)(2,1)S(1)}, bf16[1024,128]{1,0:T(8,128)(2,1)S(1)}, u32[]{:S(2)}, u32[]{:S(2)}) %collective-permute-start.15) | collective-permute-done | bytes 262176 | tf_op jit(solution)/shard_map/ppermute | solution.py:462
  80.7 0.1 add.24.refs_6_
  80.7 4.5 %collective-permute-done.10.refs_2_ = bf16[1024,128]{1,0:T(8,128)(2,1)S(1)} collective-permute-done((bf16[1024,128]{1,0:T(8,128)(2,1)S(1)}, bf16[1024,128]{1,0:T(8,128)(2,1)S(1)}, u32[]{:S(2)}, u32[]{:S(2)}) %collective-permute-start.10) | collective-permute-done | bytes 262176 | tf_op jit(solution)/shard_map/ppermute | solution.py:462
  85.3 0.5 collective-permute-start.13
  85.8 0.4 collective-permute-start.16
  86.3 2.6 %project_low.1 = (f32[256,512]{1,0:T(8,128)S(1)}, bf16[256,512]{1,0:T(8,128)(2,1)}, f32[1,256]{1,0:T(1,128)S(1)}) custom-call(s32[8]{0:T(128)S(1)} %copy-done.11, s32[2]{0:T(128)S(1)} %pad_add_fusion.ids_ref, bf16[512,512]{1,0:T(8,128)(2,1)S(1)} %copy-done.3, bf16[4096,512]{1,0:T(8,128)(2,1)S(1)} %copy-done, ...), custom_call_target="tpu_custom_call" | custom-call | flops 1073741824 | bytes 6291456 | tf_op jit(solution)/shard_map/project_low/pallas_call | solution.py:316
  88.9 0.1 collective-permute-start.33
  89.0 1.1 collective-permute-done.33
  90.1 3.6 %collective-permute-done.34 = f32[1,256]{1,0:T(1,128)S(1)} collective-permute-done((f32[1,256]{1,0:T(1,128)S(1)}, f32[1,256]{1,0:T(1,128)S(1)}, u32[]{:S(2)}, u32[]{:S(2)}) %collective-permute-start.34) | collective-permute-done | bytes 1056 | tf_op jit(solution)/shard_map/ppermute | solution.py:462
  93.7 2.0 %collective-permute-start.35 = (f32[1,256]{1,0:T(1,128)S(1)}, f32[1,256]{1,0:T(1,128)S(1)}, u32[]{:S(2)}, u32[]{:S(2)}) collective-permute-start(f32[1,256]{1,0:T(1,128)S(1)} %add.30), channel_id=1, source_target_pairs={{0,4},{1,5},{2,6},{3,7},{4,0},{5,1},{6,2},{7,3},{8,12},{9,13},{10,... | collective-permute-start | bytes 3080 | tf_op jit(solution)/shard_map/ppermute | solution.py:462
  95.7 2.4 %collective-permute-done.35 = f32[1,256]{1,0:T(1,128)S(1)} collective-permute-done((f32[1,256]{1,0:T(1,128)S(1)}, f32[1,256]{1,0:T(1,128)S(1)}, u32[]{:S(2)}, u32[]{:S(2)}) %collective-permute-start.35) | collective-permute-done | bytes 1056 | tf_op jit(solution)/shard_map/ppermute | solution.py:462
  98.2 0.1 shard_map.136.own_ref.low_ref
  98.4 2.8 %collective-permute-start.36 = (bf16[256,512]{1,0:T(8,128)(2,1)S(1)}, bf16[256,512]{1,0:T(8,128)(2,1)S(1)}, u32[]{:S(2)}, u32[]{:S(2)}) collective-permute-start(bf16[256,512]{1,0:T(8,128)(2,1)S(1)} %shard_map.136.own_ref.low_ref), channel_id=1, source_target_pairs={{0,8},{8,16},{16,24},{1,9},{9,17},{17,25},{2,10},{10,18},{18,26},{... | collective-permute-start | bytes 786440 | tf_op jit(solution)/shard_map/ppermute | solution.py:462
  101.2 2.6 %project_high.1 = (f32[256,512]{1,0:T(8,128)S(1)}, bf16[256,512]{1,0:T(8,128)(2,1)}, f32[1,256]{1,0:T(1,128)S(1)}) custom-call(s32[8]{0:T(128)S(1)} %copy-done.11, s32[2]{0:T(128)S(1)} %pad_add_fusion.ids_ref, bf16[512,512]{1,0:T(8,128)(2,1)S(1)} %copy-done.3, bf16[4096,512]{1,0:T(8,128)(2,1)S(1)} %copy-done, ...), custom_call_target="tpu_custom_call" | custom-call | flops 1073741824 | bytes 6291456 | tf_op jit(solution)/shard_map/project_high/pallas_call | solution.py:316
  103.8 1.3 %collective-permute-start.20 = (bf16[256,512]{1,0:T(8,128)(2,1)}, bf16[256,512]{1,0:T(8,128)(2,1)S(1)}, u32[]{:S(2)}, u32[]{:S(2)}) collective-permute-start(bf16[256,512]{1,0:T(8,128)(2,1)} %get-tuple-element.40), channel_id=1, source_target_pairs={{8,0},{16,8},{24,16},{9,1},{17,9},{25,17},{10,2},{18,10},{26,18},{... | collective-permute-start | bytes 786440 | tf_op jit(solution)/shard_map/ppermute | solution.py:462
  105.1 0.1 collective-permute-start.17
  105.2 1.1 collective-permute-done.17
  106.3 1.1 collective-permute-start.18
  107.5 0.1 copy.15.len_ref
  107.6 2.3 %collective-permute-done.18 = f32[1,256]{1,0:T(1,128)S(1)} collective-permute-done((f32[1,256]{1,0:T(1,128)S(1)}, f32[1,256]{1,0:T(1,128)S(1)}, u32[]{:S(2)}, u32[]{:S(2)}) %collective-permute-start.18) | collective-permute-done | bytes 1056 | tf_op jit(solution)/shard_map/ppermute | solution.py:462
  109.9 2.0 %collective-permute-start.19 = (f32[1,256]{1,0:T(1,128)S(1)}, f32[1,256]{1,0:T(1,128)S(1)}, u32[]{:S(2)}, u32[]{:S(2)}) collective-permute-start(f32[1,256]{1,0:T(1,128)S(1)} %add.26), channel_id=1, source_target_pairs={{0,4},{1,5},{2,6},{3,7},{4,0},{5,1},{6,2},{7,3},{8,12},{9,13},{10,... | collective-permute-start | bytes 3080 | tf_op jit(solution)/shard_map/ppermute | solution.py:462
  111.9 0.5 spectrum.1.spec_ref
  112.5 1.9 %collective-permute-done.19 = f32[1,256]{1,0:T(1,128)S(1)} collective-permute-done((f32[1,256]{1,0:T(1,128)S(1)}, f32[1,256]{1,0:T(1,128)S(1)}, u32[]{:S(2)}, u32[]{:S(2)}) %collective-permute-start.19) | collective-permute-done | bytes 1056 | tf_op jit(solution)/shard_map/ppermute | solution.py:462
  114.4 1.3 %collective-permute-start.21 = (f32[1,256]{1,0:T(1,128)S(1)}, f32[1,256]{1,0:T(1,128)S(1)}, u32[]{:S(2)}, u32[]{:S(2)}) collective-permute-start(f32[1,256]{1,0:T(1,128)S(1)} %add.27.sq_ref), channel_id=1, source_target_pairs={{8,0},{16,8},{24,16},{9,1},{17,9},{25,17},{10,2},{18,10},{26,18},{... | collective-permute-start | bytes 3080 | tf_op jit(solution)/shard_map/ppermute | solution.py:462
  115.7 1.4 %conv_low.1.done_ref = bf16[256,512]{1,0:T(8,128)(2,1)S(1)} custom-call(f32[256,512]{1,0:T(8,128)S(1)} %get-tuple-element.45.res_ref, bf16[256,512]{1,0:T(8,128)(2,1)S(1)} %shard_map.136.own_ref.low_ref, bf16[256,512]{1,0:T(8,128)(2,1)S(1)} %collective-permute-done.36.before_ref, f32[512,512]{1,0:T(8,128)S(1)} %spectrum.1.spec_ref, f32[1,512]{1,0:T(1,128)S(1)} %bitcast.7, ...), custom_call_target="tpu_custom_call" | custom-call | flops 469762048 | bytes 1572864 | tf_op jit(solution)/shard_map/conv_low/pallas_call | solution.py:524
  117.1 3.3 %collective-permute-done.21.raw_sq_ref = f32[1,256]{1,0:T(1,128)S(1)} collective-permute-done((f32[1,256]{1,0:T(1,128)S(1)}, f32[1,256]{1,0:T(1,128)S(1)}, u32[]{:S(2)}, u32[]{:S(2)}) %collective-permute-start.21) | collective-permute-done | bytes 1056 | tf_op jit(solution)/shard_map/ppermute | solution.py:462
  120.5 2.9 %conv_high.1 = bf16[512,512]{1,0:T(8,128)(2,1)} custom-call(s32[8]{0:T(128)S(1)} %copy-done.11, s32[2]{0:T(128)S(1)} %pad_add_fusion.ids_ref, f32[256,512]{1,0:T(8,128)S(1)} %get-tuple-element.38.res_ref, f32[1,256]{1,0:T(1,128)S(1)} %add.27.sq_ref, bf16[256,512]{1,0:T(8,128)(2,1)S(1)} %collective-permute-done.20.raw_ref, ...), custom_call_target="tpu_custom_call" | custom-call | flops 469762048 | bytes 1572864 | tf_op jit(solution)/shard_map/conv_high/pallas_call | solution.py:538
  (68 shorter events, 0.4 us)
Async XLA Ops:
  0.1 1.0 copy-start.4
  1.1 1.0 copy-start.5
  2.2 1.0 copy-start.6
  3.2 0.7 copy-start.10
  4.7 9.0 %collective-permute-start = (bf16[768,128]{1,0:T(8,128)(2,1)S(1)}, bf16[768,128]{1,0:T(8,128)(2,1)S(1)}, u32[]{:S(2)}, u32[]{:S(2)}) collective-permute-start(bf16[768,128]{1,0:T(8,128)(2,1)S(1)} %get-tuple-element.27), channel_id=1, source_target_pairs={{0,8},{8,0},{16,24},{24,16},{1,9},{9,1},{17,25},{25,17},{2,10},{10... | collective-permute-start | bytes 589832 | tf_op jit(solution)/shard_map/ppermute | solution.py:462
  7.7 11.6 %collective-permute-start.1 = (bf16[768,128]{1,0:T(8,128)(2,1)S(1)}, bf16[768,128]{1,0:T(8,128)(2,1)S(1)}, u32[]{:S(2)}, u32[]{:S(2)}) collective-permute-start(bf16[768,128]{1,0:T(8,128)(2,1)S(1)} %get-tuple-element.28), channel_id=1, source_target_pairs={{0,16},{8,24},{16,0},{24,8},{1,17},{9,25},{17,1},{25,9},{2,18},{10... | collective-permute-start | bytes 589832 | tf_op jit(solution)/shard_map/ppermute | solution.py:462
  9.3 77.0 %copy-start = (bf16[4096,512]{1,0:T(8,128)(2,1)S(1)}, bf16[4096,512]{1,0:T(8,128)(2,1)}, u32[]{:S(2)}) copy-start(bf16[4096,512]{1,0:T(8,128)(2,1)} %w_ref.3) | copy-start | bytes 12582916
  9.3 77.0 %copy-start.3 = (bf16[512,512]{1,0:T(8,128)(2,1)S(1)}, bf16[512,512]{1,0:T(8,128)(2,1)}, u32[]{:S(2)}) copy-start(bf16[512,512]{1,0:T(8,128)(2,1)} %inc_ref.3) | copy-start | bytes 1572868
  9.3 77.0 %copy-start.11 = (s32[8]{0:T(128)S(1)}, s32[8]{0:T(128)}, u32[]{:S(2)}) copy-start(s32[8]{0:T(128)} %slots_ref.9) | copy-start | bytes 100
  9.3 10.1 %collective-permute-start.2 = (bf16[768,128]{1,0:T(8,128)(2,1)S(1)}, bf16[768,128]{1,0:T(8,128)(2,1)S(1)}, u32[]{:S(2)}, u32[]{:S(2)}) collective-permute-start(bf16[768,128]{1,0:T(8,128)(2,1)S(1)} %get-tuple-element.29), channel_id=1, source_target_pairs={{0,24},{8,16},{16,8},{24,0},{1,25},{9,17},{17,9},{25,1},{2,26},{10... | collective-permute-start | bytes 589832 | tf_op jit(solution)/shard_map/ppermute | solution.py:462
  10.2 11.8 %collective-permute-start.3 = (bf16[768,128]{1,0:T(8,128)(2,1)S(1)}, bf16[768,128]{1,0:T(8,128)(2,1)S(1)}, u32[]{:S(2)}, u32[]{:S(2)}) collective-permute-start(bf16[768,128]{1,0:T(8,128)(2,1)S(1)} %get-tuple-element.31), channel_id=1, source_target_pairs={{0,8},{8,0},{16,24},{24,16},{1,9},{9,1},{17,25},{25,17},{2,10},{10... | collective-permute-start | bytes 589832 | tf_op jit(solution)/shard_map/ppermute | solution.py:462
  12.1 14.6 %collective-permute-start.4 = (bf16[768,128]{1,0:T(8,128)(2,1)S(1)}, bf16[768,128]{1,0:T(8,128)(2,1)S(1)}, u32[]{:S(2)}, u32[]{:S(2)}) collective-permute-start(bf16[768,128]{1,0:T(8,128)(2,1)S(1)} %get-tuple-element.32), channel_id=1, source_target_pairs={{0,16},{8,24},{16,0},{24,8},{1,17},{9,25},{17,1},{25,9},{2,18},{10... | collective-permute-start | bytes 589832 | tf_op jit(solution)/shard_map/ppermute | solution.py:462
  13.7 13.1 %collective-permute-start.5 = (bf16[768,128]{1,0:T(8,128)(2,1)S(1)}, bf16[768,128]{1,0:T(8,128)(2,1)S(1)}, u32[]{:S(2)}, u32[]{:S(2)}) collective-permute-start(bf16[768,128]{1,0:T(8,128)(2,1)S(1)} %get-tuple-element.33), channel_id=1, source_target_pairs={{0,24},{8,16},{16,8},{24,0},{1,25},{9,17},{17,9},{25,1},{2,26},{10... | collective-permute-start | bytes 589832 | tf_op jit(solution)/shard_map/ppermute | solution.py:462
  30.4 18.0 %collective-permute-start.6 = (bf16[256,128]{1,0:T(8,128)(2,1)S(1)}, bf16[256,128]{1,0:T(8,128)(2,1)S(1)}, u32[]{:S(2)}, u32[]{:S(2)}) collective-permute-start(bf16[256,128]{1,0:T(8,128)(2,1)S(1)} %get-tuple-element.35), channel_id=1, source_target_pairs={{0,8},{8,0},{16,24},{24,16},{1,9},{9,1},{17,25},{25,17},{2,10},{10... | collective-permute-start | bytes 196616 | tf_op jit(solution)/shard_map/ppermute | solution.py:462
  31.7 16.7 %collective-permute-start.7 = (bf16[256,128]{1,0:T(8,128)(2,1)S(1)}, bf16[256,128]{1,0:T(8,128)(2,1)S(1)}, u32[]{:S(2)}, u32[]{:S(2)}) collective-permute-start(bf16[256,128]{1,0:T(8,128)(2,1)S(1)} %get-tuple-element.36), channel_id=1, source_target_pairs={{0,16},{8,24},{16,0},{24,8},{1,17},{9,25},{17,1},{25,9},{2,18},{10... | collective-permute-start | bytes 196616 | tf_op jit(solution)/shard_map/ppermute | solution.py:462
  32.5 16.0 %collective-permute-start.8 = (bf16[256,128]{1,0:T(8,128)(2,1)S(1)}, bf16[256,128]{1,0:T(8,128)(2,1)S(1)}, u32[]{:S(2)}, u32[]{:S(2)}) collective-permute-start(bf16[256,128]{1,0:T(8,128)(2,1)S(1)} %get-tuple-element.37), channel_id=1, source_target_pairs={{0,24},{8,16},{16,8},{24,0},{1,25},{9,17},{17,9},{25,1},{2,26},{10... | collective-permute-start | bytes 196616 | tf_op jit(solution)/shard_map/ppermute | solution.py:462
  36.2 4.3 %collective-permute-start.22 = (bf16[256,128]{1,0:T(8,128)(2,1)S(1)}, bf16[256,128]{1,0:T(8,128)(2,1)S(1)}, u32[]{:S(2)}, u32[]{:S(2)}) collective-permute-start(bf16[256,128]{1,0:T(8,128)(2,1)S(1)} %get-tuple-element.42), channel_id=1, source_target_pairs={{0,8},{8,0},{16,24},{24,16},{1,9},{9,1},{17,25},{25,17},{2,10},{10... | collective-permute-start | bytes 196616 | tf_op jit(solution)/shard_map/ppermute | solution.py:462
  37.6 4.5 %collective-permute-start.23 = (bf16[256,128]{1,0:T(8,128)(2,1)S(1)}, bf16[256,128]{1,0:T(8,128)(2,1)S(1)}, u32[]{:S(2)}, u32[]{:S(2)}) collective-permute-start(bf16[256,128]{1,0:T(8,128)(2,1)S(1)} %get-tuple-element.43), channel_id=1, source_target_pairs={{0,16},{8,24},{16,0},{24,8},{1,17},{9,25},{17,1},{25,9},{2,18},{10... | collective-permute-start | bytes 196616 | tf_op jit(solution)/shard_map/ppermute | solution.py:462
  40.6 5.2 %collective-permute-start.24 = (bf16[256,128]{1,0:T(8,128)(2,1)S(1)}, bf16[256,128]{1,0:T(8,128)(2,1)S(1)}, u32[]{:S(2)}, u32[]{:S(2)}) collective-permute-start(bf16[256,128]{1,0:T(8,128)(2,1)S(1)} %get-tuple-element.44), channel_id=1, source_target_pairs={{0,24},{8,16},{16,8},{24,0},{1,25},{9,17},{17,9},{25,1},{2,26},{10... | collective-permute-start | bytes 196616 | tf_op jit(solution)/shard_map/ppermute | solution.py:462
  45.7 18.2 %collective-permute-start.28 = (bf16[1024,128]{1,0:T(8,128)(2,1)S(1)}, bf16[1024,128]{1,0:T(8,128)(2,1)S(1)}, u32[]{:S(2)}, u32[]{:S(2)}) collective-permute-start(bf16[1024,128]{1,0:T(8,128)(2,1)S(1)} %constant_dynamic-update-slice_fusion.4.refs_0_), channel_id=1, source_target_pairs={{0,4},{1,5},{2,6},{3,7},{4,0},{5,1},{6,2},{7,3},{8,12},{9,13},{10,... | collective-permute-start | bytes 786440 | tf_op jit(solution)/shard_map/ppermute | solution.py:462
  48.5 49.7 %copy-start.12 = (f32[512]{0:T(512)S(1)}, f32[512]{0:T(512)}, u32[]{:S(2)}) copy-start(f32[512]{0:T(512)} %param.19) | copy-start | bytes 6148
  48.5 21.0 %collective-permute-start.12 = (bf16[1024,128]{1,0:T(8,128)(2,1)S(1)}, bf16[1024,128]{1,0:T(8,128)(2,1)S(1)}, u32[]{:S(2)}, u32[]{:S(2)}) collective-permute-start(bf16[1024,128]{1,0:T(8,128)(2,1)S(1)} %constant_dynamic-update-slice_fusion.refs_0_), channel_id=1, source_target_pairs={{0,4},{1,5},{2,6},{3,7},{4,0},{5,1},{6,2},{7,3},{8,12},{9,13},{10,... | collective-permute-start | bytes 786440 | tf_op jit(solution)/shard_map/ppermute | solution.py:462
  48.9 21.9 %collective-permute-start.14 = (bf16[1024,128]{1,0:T(8,128)(2,1)S(1)}, bf16[1024,128]{1,0:T(8,128)(2,1)S(1)}, u32[]{:S(2)}, u32[]{:S(2)}) collective-permute-start(bf16[1024,128]{1,0:T(8,128)(2,1)S(1)} %constant_dynamic-update-slice_fusion.refs_0_), channel_id=1, source_target_pairs={{2,4},{3,5},{4,2},{5,3},{10,12},{11,13},{12,10},{13,11},{18,20},{1... | collective-permute-start | bytes 786440 | tf_op jit(solution)/shard_map/ppermute | solution.py:462
  49.6 26.1 %collective-permute-start.26 = (bf16[1024,128]{1,0:T(8,128)(2,1)S(1)}, bf16[1024,128]{1,0:T(8,128)(2,1)S(1)}, u32[]{:S(2)}, u32[]{:S(2)}) collective-permute-start(bf16[1024,128]{1,0:T(8,128)(2,1)S(1)} %constant_dynamic-update-slice_fusion.4.refs_0_), channel_id=1, source_target_pairs={{0,2},{1,3},{2,0},{3,1},{4,6},{5,7},{6,4},{7,5},{8,10},{9,11},{10,... | collective-permute-start | bytes 786440 | tf_op jit(solution)/shard_map/ppermute | solution.py:462
  54.0 21.7 %collective-permute-start.30 = (bf16[1024,128]{1,0:T(8,128)(2,1)S(1)}, bf16[1024,128]{1,0:T(8,128)(2,1)S(1)}, u32[]{:S(2)}, u32[]{:S(2)}) collective-permute-start(bf16[1024,128]{1,0:T(8,128)(2,1)S(1)} %constant_dynamic-update-slice_fusion.4.refs_0_), channel_id=1, source_target_pairs={{2,4},{3,5},{4,2},{5,3},{10,12},{11,13},{12,10},{13,11},{18,20},{1... | collective-permute-start | bytes 786440 | tf_op jit(solution)/shard_map/ppermute | solution.py:462
  63.9 12.3 %collective-permute-start.31 = (bf16[1024,128]{1,0:T(8,128)(2,1)S(1)}, bf16[1024,128]{1,0:T(8,128)(2,1)S(1)}, u32[]{:S(2)}, u32[]{:S(2)}) collective-permute-start(bf16[1024,128]{1,0:T(8,128)(2,1)S(1)} %collective-permute-done.28.refs_4_), channel_id=1, source_target_pairs={{2,0},{3,1},{4,6},{5,7},{10,8},{11,9},{12,14},{13,15},{18,16},{19,... | collective-permute-start | bytes 786440 | tf_op jit(solution)/shard_map/ppermute | solution.py:462
  69.5 11.1 %collective-permute-start.15 = (bf16[1024,128]{1,0:T(8,128)(2,1)S(1)}, bf16[1024,128]{1,0:T(8,128)(2,1)S(1)}, u32[]{:S(2)}, u32[]{:S(2)}) collective-permute-start(bf16[1024,128]{1,0:T(8,128)(2,1)S(1)} %collective-permute-done.12.refs_4_), channel_id=1, source_target_pairs={{2,0},{3,1},{4,6},{5,7},{10,8},{11,9},{12,14},{13,15},{18,16},{19,... | collective-permute-start | bytes 786440 | tf_op jit(solution)/shard_map/ppermute | solution.py:462
  70.8 14.4 %collective-permute-start.10 = (bf16[1024,128]{1,0:T(8,128)(2,1)S(1)}, bf16[1024,128]{1,0:T(8,128)(2,1)S(1)}, u32[]{:S(2)}, u32[]{:S(2)}) collective-permute-start(bf16[1024,128]{1,0:T(8,128)(2,1)S(1)} %constant_dynamic-update-slice_fusion.refs_0_), channel_id=1, source_target_pairs={{0,2},{1,3},{2,0},{3,1},{4,6},{5,7},{6,4},{7,5},{8,10},{9,11},{10,... | collective-permute-start | bytes 786440 | tf_op jit(solution)/shard_map/ppermute | solution.py:462
  75.7 9.6 %collective-permute-start.25 = (bf16[1024,128]{1,0:T(8,128)(2,1)S(1)}, bf16[1024,128]{1,0:T(8,128)(2,1)S(1)}, u32[]{:S(2)}, u32[]{:S(2)}) collective-permute-start(bf16[1024,128]{1,0:T(8,128)(2,1)S(1)} %constant_dynamic-update-slice_fusion.4.refs_0_), channel_id=1, source_target_pairs={{0,1},{1,0},{2,3},{3,2},{4,5},{5,4},{6,7},{7,6},{8,9},{9,8},{10,11... | collective-permute-start | bytes 786440 | tf_op jit(solution)/shard_map/ppermute | solution.py:462
  75.7 10.1 %collective-permute-start.27 = (bf16[1024,128]{1,0:T(8,128)(2,1)S(1)}, bf16[1024,128]{1,0:T(8,128)(2,1)S(1)}, u32[]{:S(2)}, u32[]{:S(2)}) collective-permute-start(bf16[1024,128]{1,0:T(8,128)(2,1)S(1)} %collective-permute-done.26.refs_2_), channel_id=1, source_target_pairs={{0,1},{1,0},{2,3},{3,2},{4,5},{5,4},{6,7},{7,6},{8,9},{9,8},{10,11... | collective-permute-start | bytes 786440 | tf_op jit(solution)/shard_map/ppermute | solution.py:462
  76.2 9.6 %collective-permute-start.29 = (bf16[1024,128]{1,0:T(8,128)(2,1)S(1)}, bf16[1024,128]{1,0:T(8,128)(2,1)S(1)}, u32[]{:S(2)}, u32[]{:S(2)}) collective-permute-start(bf16[1024,128]{1,0:T(8,128)(2,1)S(1)} %collective-permute-done.28.refs_4_), channel_id=1, source_target_pairs={{0,1},{1,0},{2,3},{3,2},{4,5},{5,4},{6,7},{7,6},{8,9},{9,8},{10,11... | collective-permute-start | bytes 786440 | tf_op jit(solution)/shard_map/ppermute | solution.py:462
  80.7 5.6 %collective-permute-start.32 = (bf16[1024,128]{1,0:T(8,128)(2,1)S(1)}, bf16[1024,128]{1,0:T(8,128)(2,1)S(1)}, u32[]{:S(2)}, u32[]{:S(2)}) collective-permute-start(bf16[1024,128]{1,0:T(8,128)(2,1)S(1)} %add.28.refs_6_), channel_id=1, source_target_pairs={{0,1},{1,0},{2,3},{3,2},{4,5},{5,4},{6,7},{7,6},{8,9},{9,8},{10,11... | collective-permute-start | bytes 786440 | tf_op jit(solution)/shard_map/ppermute | solution.py:462
  85.2 15.9 %collective-permute-start.9 = (bf16[1024,128]{1,0:T(8,128)(2,1)S(1)}, bf16[1024,128]{1,0:T(8,128)(2,1)S(1)}, u32[]{:S(2)}, u32[]{:S(2)}) collective-permute-start(bf16[1024,128]{1,0:T(8,128)(2,1)S(1)} %constant_dynamic-update-slice_fusion.refs_0_), channel_id=1, source_target_pairs={{0,1},{1,0},{2,3},{3,2},{4,5},{5,4},{6,7},{7,6},{8,9},{9,8},{10,11... | collective-permute-start | bytes 786440 | tf_op jit(solution)/shard_map/ppermute | solution.py:462
  85.3 16.0 %collective-permute-start.13 = (bf16[1024,128]{1,0:T(8,128)(2,1)S(1)}, bf16[1024,128]{1,0:T(8,128)(2,1)S(1)}, u32[]{:S(2)}, u32[]{:S(2)}) collective-permute-start(bf16[1024,128]{1,0:T(8,128)(2,1)S(1)} %collective-permute-done.12.refs_4_), channel_id=1, source_target_pairs={{0,1},{1,0},{2,3},{3,2},{4,5},{5,4},{6,7},{7,6},{8,9},{9,8},{10,11... | collective-permute-start | bytes 786440 | tf_op jit(solution)/shard_map/ppermute | solution.py:462
  85.8 15.4 %collective-permute-start.11 = (bf16[1024,128]{1,0:T(8,128)(2,1)S(1)}, bf16[1024,128]{1,0:T(8,128)(2,1)S(1)}, u32[]{:S(2)}, u32[]{:S(2)}) collective-permute-start(bf16[1024,128]{1,0:T(8,128)(2,1)S(1)} %collective-permute-done.10.refs_2_), channel_id=1, source_target_pairs={{0,1},{1,0},{2,3},{3,2},{4,5},{5,4},{6,7},{7,6},{8,9},{9,8},{10,11... | collective-permute-start | bytes 786440 | tf_op jit(solution)/shard_map/ppermute | solution.py:462
  85.8 15.4 %collective-permute-start.16 = (bf16[1024,128]{1,0:T(8,128)(2,1)S(1)}, bf16[1024,128]{1,0:T(8,128)(2,1)S(1)}, u32[]{:S(2)}, u32[]{:S(2)}) collective-permute-start(bf16[1024,128]{1,0:T(8,128)(2,1)S(1)} %add.24.refs_6_), channel_id=1, source_target_pairs={{0,1},{1,0},{2,3},{3,2},{4,5},{5,4},{6,7},{7,6},{8,9},{9,8},{10,11... | collective-permute-start | bytes 786440 | tf_op jit(solution)/shard_map/ppermute | solution.py:462
  88.9 18.6 %copy-start.14 = (s32[512]{0:T(512)S(1)}, s32[512]{0:T(512)}, u32[]{:S(2)}) copy-start(s32[512]{0:T(512)} %param.21) | copy-start | bytes 6148
  88.9 23.1 %copy-start.1 = (bf16[512,256]{1,0:T(8,128)(2,1)S(1)}, bf16[512,256]{1,0:T(8,128)(2,1)}, u32[]{:S(2)}) copy-start(bf16[512,256]{1,0:T(8,128)(2,1)} %constant.16.clone.fh_ref.fh) | copy-start | bytes 786436
  88.9 23.1 %copy-start.2 = (bf16[512,256]{1,0:T(8,128)(2,1)S(1)}, bf16[512,256]{1,0:T(8,128)(2,1)}, u32[]{:S(2)}) copy-start(bf16[512,256]{1,0:T(8,128)(2,1)} %constant.17.clone.fl_ref.fl) | copy-start | bytes 786436
  88.9 23.1 %copy-start.9 = (bf16[512,256]{1,0:T(8,128)(2,1)S(1)}, bf16[512,256]{1,0:T(8,128)(2,1)}, u32[]{:S(2)}) copy-start(bf16[512,256]{1,0:T(8,128)(2,1)} %filters_ref.1) | copy-start | bytes 786436
  88.9 1.2 collective-permute-start.33
  90.1 3.6 %collective-permute-start.34 = (f32[1,256]{1,0:T(1,128)S(1)}, f32[1,256]{1,0:T(1,128)S(1)}, u32[]{:S(2)}, u32[]{:S(2)}) collective-permute-start(f32[1,256]{1,0:T(1,128)S(1)} %add.29), channel_id=1, source_target_pairs={{0,2},{1,3},{2,0},{3,1},{4,6},{5,7},{6,4},{7,5},{8,10},{9,11},{10,... | collective-permute-start | bytes 3080 | tf_op jit(solution)/shard_map/ppermute | solution.py:462
  93.7 4.5 %collective-permute-start.35 = (f32[1,256]{1,0:T(1,128)S(1)}, f32[1,256]{1,0:T(1,128)S(1)}, u32[]{:S(2)}, u32[]{:S(2)}) collective-permute-start(f32[1,256]{1,0:T(1,128)S(1)} %add.30), channel_id=1, source_target_pairs={{0,4},{1,5},{2,6},{3,7},{4,0},{5,1},{6,2},{7,3},{8,12},{9,13},{10,... | collective-permute-start | bytes 3080 | tf_op jit(solution)/shard_map/ppermute | solution.py:462
  98.3 17.4 %copy-start.7 = (bf16[256,512]{1,0:T(8,128)(2,1)S(1)}, bf16[256,512]{1,0:T(8,128)(2,1)}, u32[]{:S(2)}) copy-start(bf16[256,512]{1,0:T(8,128)(2,1)} %constant.18.clone.gh) | copy-start | bytes 786436
  98.3 17.4 %copy-start.8 = (bf16[256,512]{1,0:T(8,128)(2,1)S(1)}, bf16[256,512]{1,0:T(8,128)(2,1)}, u32[]{:S(2)}) copy-start(bf16[256,512]{1,0:T(8,128)(2,1)} %constant.19.clone.gl) | copy-start | bytes 786436
  98.3 17.4 %copy-start.13 = (f32[512]{0:T(512)S(1)}, f32[512]{0:T(512)}, u32[]{:S(2)}) copy-start(f32[512]{0:T(512)} %param.22) | copy-start | bytes 6148
  98.4 17.3 %collective-permute-start.36 = (bf16[256,512]{1,0:T(8,128)(2,1)S(1)}, bf16[256,512]{1,0:T(8,128)(2,1)S(1)}, u32[]{:S(2)}, u32[]{:S(2)}) collective-permute-start(bf16[256,512]{1,0:T(8,128)(2,1)S(1)} %shard_map.136.own_ref.low_ref), channel_id=1, source_target_pairs={{0,8},{8,16},{16,24},{1,9},{9,17},{17,25},{2,10},{10,18},{18,26},{... | collective-permute-start | bytes 786440 | tf_op jit(solution)/shard_map/ppermute | solution.py:462
  103.8 16.7 %collective-permute-start.20 = (bf16[256,512]{1,0:T(8,128)(2,1)}, bf16[256,512]{1,0:T(8,128)(2,1)S(1)}, u32[]{:S(2)}, u32[]{:S(2)}) collective-permute-start(bf16[256,512]{1,0:T(8,128)(2,1)} %get-tuple-element.40), channel_id=1, source_target_pairs={{8,0},{16,8},{24,16},{9,1},{17,9},{25,17},{10,2},{18,10},{26,18},{... | collective-permute-start | bytes 786440 | tf_op jit(solution)/shard_map/ppermute | solution.py:462
  105.1 1.2 collective-permute-start.17
  106.3 3.6 %collective-permute-start.18 = (f32[1,256]{1,0:T(1,128)S(1)}, f32[1,256]{1,0:T(1,128)S(1)}, u32[]{:S(2)}, u32[]{:S(2)}) collective-permute-start(f32[1,256]{1,0:T(1,128)S(1)} %add.25), channel_id=1, source_target_pairs={{0,2},{1,3},{2,0},{3,1},{4,6},{5,7},{6,4},{7,5},{8,10},{9,11},{10,... | collective-permute-start | bytes 3080 | tf_op jit(solution)/shard_map/ppermute | solution.py:462
  109.9 4.5 %collective-permute-start.19 = (f32[1,256]{1,0:T(1,128)S(1)}, f32[1,256]{1,0:T(1,128)S(1)}, u32[]{:S(2)}, u32[]{:S(2)}) collective-permute-start(f32[1,256]{1,0:T(1,128)S(1)} %add.26), channel_id=1, source_target_pairs={{0,4},{1,5},{2,6},{3,7},{4,0},{5,1},{6,2},{7,3},{8,12},{9,13},{10,... | collective-permute-start | bytes 3080 | tf_op jit(solution)/shard_map/ppermute | solution.py:462
  114.4 6.1 %collective-permute-start.21 = (f32[1,256]{1,0:T(1,128)S(1)}, f32[1,256]{1,0:T(1,128)S(1)}, u32[]{:S(2)}, u32[]{:S(2)}) collective-permute-start(f32[1,256]{1,0:T(1,128)S(1)} %add.27.sq_ref), channel_id=1, source_target_pairs={{8,0},{16,8},{24,16},{9,1},{17,9},{25,17},{10,2},{18,10},{26,18},{... | collective-permute-start | bytes 3080 | tf_op jit(solution)/shard_map/ppermute | solution.py:462

commit v3 on v2

--- a/solution.py
+++ b/solution.py
@@ -171,41 +171,43 @@
     return jnp.where(first_is_high, 1 - high, high).astype(jnp.int32)
 
 
-def pack_kernel(n, high, slots_ref, ids_ref, q_ref, k_ref, v_ref, *rest):
-    outs, sem = rest[:n], rest[n]
+def pack_kernel(n, slots_ref, ids_ref, q_ref, k_ref, v_ref, *rest):
+    outs, sem = rest[: 2 * n], rest[2 * n]
     rank = ids_ref[0]
     rows = outs[0].shape[0] // 3
     wide = outs[0].shape[1]
-    half = half_index(slots_ref, ids_ref, high)
-    source_rows = pl.ds(pl.multiple_of(half * rows, rows), rows)
     copies = []
-    for k in range(n):
-        cols = pl.ds(pl.multiple_of((rank ^ k) * wide, wide), wide)
-        for a, ref in enumerate((q_ref, k_ref, v_ref)):
-            copy = pltpu.make_async_copy(
-                ref.at[source_rows, cols],
-                outs[k].at[a * rows : (a + 1) * rows, :],
-                sem.at[k, a],
-            )
-            copy.start()
-            copies.append(copy)
+    for high in range(2):
+        half = half_index(slots_ref, ids_ref, high)
+        source_rows = pl.ds(pl.multiple_of(half * rows, rows), rows)
+        for k in range(n):
+            cols = pl.ds(pl.multiple_of((rank ^ k) * wide, wide), wide)
+            for a, ref in enumerate((q_ref, k_ref, v_ref)):
+                copy = pltpu.make_async_copy(
+                    ref.at[source_rows, cols],
+                    outs[high * n + k].at[a * rows : (a + 1) * rows, :],
+                    sem.at[high * n + k, a],
+                )
+                copy.start()
+                copies.append(copy)
     for copy in copies:
         copy.wait()
 
 
-def pack(n, high, slots, ids, q, k, v):
+def pack(n, slots, ids, q, k, v):
     rows, width = q.shape[0] // 2, q.shape[1]
     piece = jax.ShapeDtypeStruct((3 * rows, width // n), BF)
-    return pl.pallas_call(
-        functools.partial(pack_kernel, n, high),
-        out_shape=[piece] * n,
+    packed = pl.pallas_call(
+        functools.partial(pack_kernel, n),
+        out_shape=[piece] * (2 * n),
         in_specs=[sm(), sm()] + [pl.BlockSpec(memory_space=pltpu.HBM)] * 3,
-        out_specs=[vm()] * n,
-        scratch_shapes=[pltpu.SemaphoreType.DMA((n, 3))],
+        out_specs=[vm()] * (2 * n),
+        scratch_shapes=[pltpu.SemaphoreType.DMA((2 * n, 3))],
         compiler_params=params(8),
-        cost_estimate=cost(0, 12 * rows * width),
-        name="pack_high" if high else "pack_low",
-    )(slots, ids, q, k, v)
+        cost_estimate=cost(0, 24 * rows * width),
+        name="pack",
+    )(slots, ids, *(pltpu.with_memory_space_constraint(x, pltpu.HBM) for x in (q, k, v)))
+    return packed[:n], packed[n:]
 
 
 def attend_kernel(n, high, rows, ids_ref, *refs):
@@ -286,47 +288,51 @@
     )(ids, *pieces)
 
 
-def project_kernel(n, high, slots_ref, ids_ref, inc_ref, w_ref, *refs):
-    parts = refs[:-4]
-    res_ref, raw_ref, sq_ref, lhs = refs[-4:]
+def project_kernel(n, high, indices, slots_ref, ids_ref, base_ref, w_ref, *refs):
+    count = len(indices)
+    parts, outs, lhs = refs[:count], refs[count:-1], refs[-1]
     rank = ids_ref[0]
     me = ids_ref[1]
-    rows = res_ref.shape[0]
-    width = lhs.shape[1]
+    rows, width = lhs.shape
     wide = width // n
-    half = half_index(slots_ref, ids_ref, high)
-    total = inc_ref[pl.ds(pl.multiple_of(half * rows, rows), rows), :].astype(F32)
-    for index, part in enumerate(parts):
+    if base_ref.shape[0] == rows:
+        total = base_ref[...]
+    else:
+        half = half_index(slots_ref, ids_ref, high)
+        total = base_ref[pl.ds(pl.multiple_of(half * rows, rows), rows), :].astype(F32)
+    for index, part in zip(indices, parts):
         for k in range(n):
             cols = pl.ds(pl.multiple_of((rank ^ k) * wide, wide), wide)
             lhs[:, cols] = part[k * rows : (k + 1) * rows, :]
         depth = pl.ds(pl.multiple_of((me ^ index) * width, width), width)
         total = total + jnp.dot(lhs[...], w_ref[depth, :], preferred_element_type=F32)
-    res_ref[...] = total
-    raw_ref[...] = total.astype(BF)
+    outs[0][...] = total
+    if len(outs) == 1:
+        return
+    outs[1][...] = total.astype(BF)
     squares = total * total
     lanes = squares[:, 0:HD]
     for g in range(1, squares.shape[1] // HD):
         lanes = lanes + squares[:, g * HD : (g + 1) * HD]
-    sq_ref[...] = jnp.sum(lanes.T, axis=0, keepdims=True)
-
-
-def project(n, high, slots, ids, incoming, w_out, parts):
-    rows, width = incoming.shape[0] // 2, incoming.shape[1]
+    outs[2][...] = jnp.sum(lanes.T, axis=0, keepdims=True)
+
+
+def project(n, high, slots, ids, base, w_out, parts, indices, final):
+    rows = parts[0].shape[0] // n
+    width = w_out.shape[1]
+    shapes = [jax.ShapeDtypeStruct((rows, width), F32)]
+    if final:
+        shapes.append(jax.ShapeDtypeStruct((rows, width), BF))
+        shapes.append(jax.ShapeDtypeStruct((1, rows), F32))
     return pl.pallas_call(
-        functools.partial(project_kernel, n, high),
-        out_shape=[
-            jax.ShapeDtypeStruct((rows, width), F32),
-            jax.ShapeDtypeStruct((rows, width), BF),
-            jax.ShapeDtypeStruct((1, rows), F32),
-        ],
+        functools.partial(project_kernel, n, high, indices),
+        out_shape=shapes,
         in_specs=[sm(), sm()] + [vm()] * (2 + len(parts)),
-        out_specs=[vm()] * 3,
+        out_specs=[vm()] * len(shapes),
         scratch_shapes=[VMEM((rows, width), BF)],
         compiler_params=params(20),
-        cost_estimate=cost(2 * rows * width * w_out.shape[0], 2 * w_out.size * 1.5),
-        name="project_high" if high else "project_low",
-    )(slots, ids, incoming, w_out, *parts)
+        cost_estimate=cost(2 * rows * width * width * len(parts), 2 * w_out.size * 1.5),
+    )(slots, ids, base, w_out, *parts)
 
 
 def normed_rows(res, sq_row, gain, model_width):
@@ -404,58 +410,67 @@
     )(filters, filter_len.reshape(-1, 1), *forward)
 
 
-def conv_rows(before, own, fh, fl, gh, gl, spec):
+def two(a_high, a_low, b):
+    return jnp.dot(a_high, b, preferred_element_type=F32) + jnp.dot(
+        a_low, b, preferred_element_type=F32
+    )
+
+
+def frequency_signs(rows):
+    row_id = lax.broadcasted_iota(jnp.int32, (rows, 1), 0)
+    return row_id == 0, jnp.where(row_id % 2 == 0, 1.0, -1.0)
+
+
+def late_spectrum(own, fh, fl):
     rows = own.shape[0]
-
-    def two(a_high, a_low, b):
-        return jnp.dot(a_high, b, preferred_element_type=F32) + jnp.dot(
-            a_low, b, preferred_element_type=F32
-        )
-
-    row_id = lax.broadcasted_iota(jnp.int32, (rows, 1), 0)
-    sign = jnp.where(row_id % 2 == 0, 1.0, -1.0)
-    first = row_id == 0
-    spec_b = two(fh, fl, before)
-    spec_o = two(fh, fl, own)
-    x_re = spec_b[:rows] + sign * spec_o[:rows]
-    x_im = spec_b[rows:] + jnp.where(first, 1.0, sign) * spec_o[rows:]
+    first, sign = frequency_signs(rows)
+    plain = two(fh, fl, own)
+    return sign * plain[:rows], jnp.where(first, 1.0, sign) * plain[rows:]
+
+
+def filtered(x_re, x_im, gh, gl, spec):
+    rows = x_re.shape[0]
+    first, _ = frequency_signs(rows)
     h_re, h_im = spec[:rows], spec[rows:]
     h_cross = jnp.where(first, 0.0, h_im)
     h_own = jnp.where(first, h_im, h_re)
-    y_re = x_re * h_re - x_im * h_cross
-    y_im = x_re * h_cross + x_im * h_own
-    y = jnp.concatenate([y_re, y_im], axis=0)
+    y = jnp.concatenate([x_re * h_re - x_im * h_cross, x_re * h_cross + x_im * h_own], axis=0)
     y_high = y.astype(BF)
     y_low = (y - y_high.astype(F32)).astype(BF)
     return two(gh, gl, y_high) + jnp.dot(gh, y_low, preferred_element_type=F32)
 
 
-def finish(res, normed, conv, skip):
-    return (res + conv + skip * normed.astype(F32)).astype(BF)
-
-
 def conv_low_kernel(res_ref, own_ref, before_ref, spec_ref, skip_ref, fh, fl, gh, gl, out_ref):
-    conv = conv_rows(
-        before_ref[...], own_ref[...], fh[...], fl[...], gh[...], gl[...], spec_ref[...]
-    )
-    out_ref[...] = finish(res_ref[...], own_ref[...], conv, skip_ref[...])
+    rows = res_ref.shape[0]
+    own = own_ref[...]
+    late_re, late_im = late_spectrum(own, fh[...], fl[...])
+    early = two(fh[...], fl[...], before_ref[...])
+    conv = filtered(early[:rows] + late_re, early[rows:] + late_im, gh[...], gl[...], spec_ref[...])
+    out_ref[...] = (res_ref[...] + conv + skip_ref[...] * own.astype(F32)).astype(BF)
+
+
+def conv_own_kernel(
+    model_width, res_ref, sq_ref, spec_ref, gain_ref, skip_ref, fh, fl, gh, gl, out_ref
+):
+    own = normed_rows(res_ref[...], sq_ref[...], gain_ref[...], model_width)
+    late_re, late_im = late_spectrum(own, fh[...], fl[...])
+    conv = filtered(late_re, late_im, gh[...], gl[...], spec_ref[...])
+    out_ref[...] = res_ref[...] + conv + skip_ref[...] * own.astype(F32)
 
 
 def conv_high_kernel(
-    n, model_width, slots_ref, ids_ref, res_ref, sq_ref, raw_ref, raw_sq_ref, low_ref, done_ref,
-    spec_ref, gain_ref, skip_ref, fh, fl, gh, gl, out_ref,
+    n, model_width, slots_ref, ids_ref, part_ref, raw_ref, raw_sq_ref, low_ref, done_ref,
+    spec_ref, gain_ref, fh, fl, gh, gl, out_ref,
 ):
-    rows = res_ref.shape[0]
+    rows = part_ref.shape[0]
     last = ids_ref[0] == n - 1
-    own = normed_rows(res_ref[...], sq_ref[...], gain_ref[...], model_width)
     raw = normed_rows(raw_ref[...].astype(F32), raw_sq_ref[...], gain_ref[...], model_width)
     before = jnp.where(last, low_ref[...].astype(F32), raw.astype(F32)).astype(BF)
-    conv = conv_rows(before, own, fh[...], fl[...], gh[...], gl[...], spec_ref[...])
+    early = two(fh[...], fl[...], before)
+    conv = filtered(early[:rows], early[rows:], gh[...], gl[...], spec_ref[...])
     half = half_index(slots_ref, ids_ref, 1)
     out_ref[pl.ds(pl.multiple_of((1 - half) * rows, rows), rows), :] = done_ref[...]
-    out_ref[pl.ds(pl.multiple_of(half * rows, rows), rows), :] = finish(
-        res_ref[...], own, conv, skip_ref[...]
-    )
+    out_ref[pl.ds(pl.multiple_of(half * rows, rows), rows), :] = (part_ref[...] + conv).astype(BF)
 
 
 def moved(block, axis, route):
@@ -509,8 +524,9 @@
     def exchange(pieces):
         return [pieces[0]] + [moved(pieces[k], "seq", xor_route(n, k)) for k in range(1, n)]
 
-    low = exchange(pack(n, 0, slot_map, ids, queries, key_vecs, value_vecs))
-    high = exchange(pack(n, 1, slot_map, ids, queries, key_vecs, value_vecs))
+    packed_low, packed_high = pack(n, slot_map, ids, queries, key_vecs, value_vecs)
+    low = exchange(packed_low)
+    high = exchange(packed_high)
     spec = spectrum(filters, filter_len, forward)
 
     att_low = exchange(attend(n, 0, rows, ids, low))
@@ -518,9 +534,11 @@
     att_high = exchange(attend(n, 1, rows, ids, low + high))
     parts_high = gather_mp(jnp.concatenate(att_high, axis=0), mp_size)
 
-    res_low, _, sq_low = project(n, 0, slot_map, ids, incoming, w_out, parts_low)
+    every = tuple(range(mp_size))
+    res_low, _, sq_low = project(n, 0, slot_map, ids, incoming, w_out, parts_low, every, True)
     norm_low = norm(model_width, res_low, total_mp(sq_low, mp_size), gain)
     before_low = before_rows(norm_low, 1)
+    transforms = forward + backward
     done_low = pl.pallas_call(
         conv_low_kernel,
         out_shape=jax.ShapeDtypeStruct((rows, width), BF),
@@ -529,23 +547,37 @@
         compiler_params=params(20),
         cost_estimate=cost(14 * rows * rows * width, 12 * rows * width),
         name="conv_low",
-    )(res_low, norm_low, before_low, spec, skip, *forward, *backward)
-
-    res_high, raw_high, sq_high = project(n, 1, slot_map, ids, incoming, w_out, parts_high)
+    )(res_low, norm_low, before_low, spec, skip, *transforms)
+
+    most = mp_size - 2
+    (base_high,) = project(
+        n, 1, slot_map, ids, incoming, w_out, parts_high[:most], every[:most], False
+    )
+    res_high, raw_high, sq_high = project(
+        n, 1, slot_map, ids, base_high, w_out, parts_high[most:], every[most:], True
+    )
     raw_before = before_rows(raw_high, -1)
     sq_high = total_mp(sq_high, mp_size)
     sq_before = before_rows(sq_high, -1)
+    part_high = pl.pallas_call(
+        functools.partial(conv_own_kernel, model_width),
+        out_shape=jax.ShapeDtypeStruct((rows, width), F32),
+        in_specs=[vm()] * 9,
+        out_specs=vm(),
+        compiler_params=params(20),
+        cost_estimate=cost(10 * rows * rows * width, 12 * rows * width),
+        name="conv_own",
+    )(res_high, sq_high, spec, gain, skip, *transforms)
     return pl.pallas_call(
         functools.partial(conv_high_kernel, n, model_width),
         out_shape=jax.ShapeDtypeStruct((2 * rows, width), BF),
-        in_specs=[sm(), sm()] + [vm()] * 13,
+        in_specs=[sm(), sm()] + [vm()] * 11,
         out_specs=vm(),
         compiler_params=params(20),
-        cost_estimate=cost(14 * rows * rows * width, 12 * rows * width),
+        cost_estimate=cost(10 * rows * rows * width, 12 * rows * width),
         name="conv_high",
     )(
-        slot_map, ids, res_high, sq_high, raw_before, sq_before, norm_low, done_low, spec, gain,
-        skip, *forward, *backward,
+        slot_map, ids, part_high, raw_before, sq_before, norm_low, done_low, spec, gain, *transforms
     )
 
 

time: 124 us -> 130 us (1.048)
  waiting for transfers between devices: 54.3 us -> 64 us
  local copies, waits for them, and re-layouts: 4.07 us -> 0.95 us
  starting transfers between devices: 46.7 us -> 43.6 us
  Pallas kernels: 17.7 us -> 20.1 us
    ppermute x37, waiting for transfers between devices: 54.3 us -> 64 us  [moved(): return lax.ppermute(block, axis, route)]
    ppermute x37, starting transfers between devices: 46.7 us -> 43.6 us  [moved(): return lax.ppermute(block, axis, route)]
    unnamed x36 -> x30, local copies, waits for them, and re-layouts: 3.9 us -> 0.78 us
    pallas_call x4 -> x5, Pallas kernels: 6.83 us -> 9.58 us  [the longest x3 5.9 us: project(): pl.pallas_call(functools.partial(project_kernel, n, high, indices), out_s...]
  transfers between devices with their start and end apart: 37 -> 37, of which waited for: 16 -> 17; matrix products, arithmetic and copies ran while one was open for 0% -> 0% of each run, Pallas kernels for 8% -> 9%
where the time goes in v3:
time: 130 us; the launch traced here: 129 us
  waiting for transfers between devices  64 us (49%)
  starting transfers between devices  43.6 us (34%)
  Pallas kernels  20.1 us (15%)
    ppermute x37, waiting for transfers between devices, moved(): return lax.ppermute(block, axis, route)  64 us
    ppermute x37, starting transfers between devices, moved(): return lax.ppermute(block, axis, route)  43.6 us
    pallas_call x2, Pallas kernels, attend(): pl.pallas_call(functools.partial(attend_kernel, n, high, rows), out_shape...  5.91 us
    pallas_call x3, Pallas kernels, project(): pl.pallas_call(functools.partial(project_kernel, n, high, indices), out_s...  5.9 us
  transfers between devices with their start and end apart: 37, of which 17 were waited for; matrix products, arithmetic and copies ran while one was open for 0% of the time, Pallas kernels for 9%

profile of v3, /device:TPU:0, one launch (start us, length us, event | category | flops | bytes accessed | tf_op | source)
XLA Modules:
  0.0 129.3 jit_solution(3529680624789231)
XLA Ops:
  0.0 0.1 pad_add_fusion.ids_ref
  0.1 0.7 copy-done.8
  0.7 2.5 %pack.1 = (bf16[768,128]{1,0:T(8,128)(2,1)S(1)}, bf16[768,128]{1,0:T(8,128)(2,1)S(1)}, bf16[768,128]{1,0:T(8,128)(2,1)S(1)}, bf16[768,128]{1,0:T(8,128)(2,1)S(1)...) custom-call(s32[8]{0:T(128)S(1)} %copy-done.8, ...), custom_call_target="tpu_custom_call" | custom-call | bytes 3145728 | tf_op jit(solution)/shard_map/pack/pallas_call | solution.py:200
  3.2 3.0 %collective-permute-start = (bf16[768,128]{1,0:T(8,128)(2,1)S(1)}, bf16[768,128]{1,0:T(8,128)(2,1)S(1)}, u32[]{:S(2)}, u32[]{:S(2)}) collective-permute-start(bf16[768,128]{1,0:T(8,128)(2,1)S(1)} %get-tuple-element.27), channel_id=1, source_target_pairs={{0,8},{8,0},{16,24},{24,16},{1,9},{9,1},{17,25},{25,17},{2,10},{10... | collective-permute-start | bytes 589832 | tf_op jit(solution)/shard_map/ppermute | solution.py:477
  6.2 1.5 %collective-permute-start.1 = (bf16[768,128]{1,0:T(8,128)(2,1)S(1)}, bf16[768,128]{1,0:T(8,128)(2,1)S(1)}, u32[]{:S(2)}, u32[]{:S(2)}) collective-permute-start(bf16[768,128]{1,0:T(8,128)(2,1)S(1)} %get-tuple-element.28), channel_id=1, source_target_pairs={{0,16},{8,24},{16,0},{24,8},{1,17},{9,25},{17,1},{25,9},{2,18},{10... | collective-permute-start | bytes 589832 | tf_op jit(solution)/shard_map/ppermute | solution.py:477
  7.8 1.9 %collective-permute-start.3 = (bf16[768,128]{1,0:T(8,128)(2,1)S(1)}, bf16[768,128]{1,0:T(8,128)(2,1)S(1)}, u32[]{:S(2)}, u32[]{:S(2)}) collective-permute-start(bf16[768,128]{1,0:T(8,128)(2,1)S(1)} %get-tuple-element.31), channel_id=1, source_target_pairs={{0,8},{8,0},{16,24},{24,16},{1,9},{9,1},{17,25},{25,17},{2,10},{10... | collective-permute-start | bytes 589832 | tf_op jit(solution)/shard_map/ppermute | solution.py:477
  9.7 1.5 %collective-permute-start.4 = (bf16[768,128]{1,0:T(8,128)(2,1)S(1)}, bf16[768,128]{1,0:T(8,128)(2,1)S(1)}, u32[]{:S(2)}, u32[]{:S(2)}) collective-permute-start(bf16[768,128]{1,0:T(8,128)(2,1)S(1)} %get-tuple-element.32), channel_id=1, source_target_pairs={{0,16},{8,24},{16,0},{24,8},{1,17},{9,25},{17,1},{25,9},{2,18},{10... | collective-permute-start | bytes 589832 | tf_op jit(solution)/shard_map/ppermute | solution.py:477
  11.3 0.7 collective-permute-done.refs_1_
  12.0 3.0 %collective-permute-start.5 = (bf16[768,128]{1,0:T(8,128)(2,1)S(1)}, bf16[768,128]{1,0:T(8,128)(2,1)S(1)}, u32[]{:S(2)}, u32[]{:S(2)}) collective-permute-start(bf16[768,128]{1,0:T(8,128)(2,1)S(1)} %get-tuple-element.33), channel_id=1, source_target_pairs={{0,24},{8,16},{16,8},{24,0},{1,25},{9,17},{17,9},{25,1},{2,26},{10... | collective-permute-start | bytes 589832 | tf_op jit(solution)/shard_map/ppermute | solution.py:477
  15.0 3.3 %collective-permute-done.1.refs_2_ = bf16[768,128]{1,0:T(8,128)(2,1)S(1)} collective-permute-done((bf16[768,128]{1,0:T(8,128)(2,1)S(1)}, bf16[768,128]{1,0:T(8,128)(2,1)S(1)}, u32[]{:S(2)}, u32[]{:S(2)}) %collective-permute-start.1) | collective-permute-done | bytes 196640 | tf_op jit(solution)/shard_map/ppermute | solution.py:477
  18.2 2.2 %collective-permute-done.3.refs_5_ = bf16[768,128]{1,0:T(8,128)(2,1)S(1)} collective-permute-done((bf16[768,128]{1,0:T(8,128)(2,1)S(1)}, bf16[768,128]{1,0:T(8,128)(2,1)S(1)}, u32[]{:S(2)}, u32[]{:S(2)}) %collective-permute-start.3) | collective-permute-done | bytes 196640 | tf_op jit(solution)/shard_map/ppermute | solution.py:477
  20.5 4.8 %collective-permute-done.4.refs_6_ = bf16[768,128]{1,0:T(8,128)(2,1)S(1)} collective-permute-done((bf16[768,128]{1,0:T(8,128)(2,1)S(1)}, bf16[768,128]{1,0:T(8,128)(2,1)S(1)}, u32[]{:S(2)}, u32[]{:S(2)}) %collective-permute-start.4) | collective-permute-done | bytes 196640 | tf_op jit(solution)/shard_map/ppermute | solution.py:477
  25.3 3.6 %attend_high.1 = (bf16[256,128]{1,0:T(8,128)(2,1)S(1)}, bf16[256,128]{1,0:T(8,128)(2,1)S(1)}, bf16[256,128]{1,0:T(8,128)(2,1)S(1)}, bf16[256,128]{1,0:T(8,128)(2,1)S(1)}) custom-call(s32[2]{0:T(128)S(1)} %pad_add_fusion.ids_ref, bf16[768,128]{1,0:T(8,128)(2,1)S(1)} %get-tuple-element.26.refs_0_, bf16[768,128]{1,0:T(8,128)(2,1)S(1)} %collective-permute-done.refs_1_, ...), custom_call_target="tpu_custom_call" | custom-call | flops 872415232 | bytes 2097152 | tf_op jit(solution)/shard_map/attend_high/pallas_call | solution.py:274
  28.9 1.3 %collective-permute-start.6 = (bf16[256,128]{1,0:T(8,128)(2,1)S(1)}, bf16[256,128]{1,0:T(8,128)(2,1)S(1)}, u32[]{:S(2)}, u32[]{:S(2)}) collective-permute-start(bf16[256,128]{1,0:T(8,128)(2,1)S(1)} %get-tuple-element.35), channel_id=1, source_target_pairs={{0,8},{8,0},{16,24},{24,16},{1,9},{9,1},{17,25},{25,17},{2,10},{10... | collective-permute-start | bytes 196616 | tf_op jit(solution)/shard_map/ppermute | solution.py:477
  30.2 0.8 collective-permute-start.7
  31.0 1.4 %collective-permute-start.8 = (bf16[256,128]{1,0:T(8,128)(2,1)S(1)}, bf16[256,128]{1,0:T(8,128)(2,1)S(1)}, u32[]{:S(2)}, u32[]{:S(2)}) collective-permute-start(bf16[256,128]{1,0:T(8,128)(2,1)S(1)} %get-tuple-element.37), channel_id=1, source_target_pairs={{0,24},{8,16},{16,8},{24,0},{1,25},{9,17},{17,9},{25,1},{2,26},{10... | collective-permute-start | bytes 196616 | tf_op jit(solution)/shard_map/ppermute | solution.py:477
  32.4 2.3 %attend_low.1 = (bf16[256,128]{1,0:T(8,128)(2,1)S(1)}, bf16[256,128]{1,0:T(8,128)(2,1)S(1)}, bf16[256,128]{1,0:T(8,128)(2,1)S(1)}, bf16[256,128]{1,0:T(8,128)(2,1)S(1)}) custom-call(s32[2]{0:T(128)S(1)} %pad_add_fusion.ids_ref, bf16[768,128]{1,0:T(8,128)(2,1)S(1)} %get-tuple-element.26.refs_0_, bf16[768,128]{1,0:T(8,128)(2,1)S(1)} %collective-permute-done.refs_1_, ...), custom_call_target="tpu_custom_call" | custom-call | flops 335544320 | bytes 1048576 | tf_op jit(solution)/shard_map/attend_low/pallas_call | solution.py:274
  34.7 1.3 %collective-permute-start.22 = (bf16[256,128]{1,0:T(8,128)(2,1)S(1)}, bf16[256,128]{1,0:T(8,128)(2,1)S(1)}, u32[]{:S(2)}, u32[]{:S(2)}) collective-permute-start(bf16[256,128]{1,0:T(8,128)(2,1)S(1)} %get-tuple-element.42), channel_id=1, source_target_pairs={{0,8},{8,0},{16,24},{24,16},{1,9},{9,1},{17,25},{25,17},{2,10},{10... | collective-permute-start | bytes 196616 | tf_op jit(solution)/shard_map/ppermute | solution.py:477
  36.1 0.8 collective-permute-start.23
  36.9 2.2 %collective-permute-done.22 = bf16[256,128]{1,0:T(8,128)(2,1)S(1)} collective-permute-done((bf16[256,128]{1,0:T(8,128)(2,1)S(1)}, bf16[256,128]{1,0:T(8,128)(2,1)S(1)}, u32[]{:S(2)}, u32[]{:S(2)}) %collective-permute-start.22) | collective-permute-done | bytes 65568 | tf_op jit(solution)/shard_map/ppermute | solution.py:477
  39.1 1.5 %collective-permute-start.24 = (bf16[256,128]{1,0:T(8,128)(2,1)S(1)}, bf16[256,128]{1,0:T(8,128)(2,1)S(1)}, u32[]{:S(2)}, u32[]{:S(2)}) collective-permute-start(bf16[256,128]{1,0:T(8,128)(2,1)S(1)} %get-tuple-element.44), channel_id=1, source_target_pairs={{0,24},{8,16},{16,8},{24,0},{1,25},{9,17},{17,9},{25,1},{2,26},{10... | collective-permute-start | bytes 196616 | tf_op jit(solution)/shard_map/ppermute | solution.py:477
  40.6 3.6 %collective-permute-done.24 = bf16[256,128]{1,0:T(8,128)(2,1)S(1)} collective-permute-done((bf16[256,128]{1,0:T(8,128)(2,1)S(1)}, bf16[256,128]{1,0:T(8,128)(2,1)S(1)}, u32[]{:S(2)}, u32[]{:S(2)}) %collective-permute-start.24) | collective-permute-done | bytes 65568 | tf_op jit(solution)/shard_map/ppermute | solution.py:477
  44.2 0.7 collective-permute-start.30
  44.9 4.3 %collective-permute-start.28 = (bf16[1024,128]{1,0:T(8,128)(2,1)S(1)}, bf16[1024,128]{1,0:T(8,128)(2,1)S(1)}, u32[]{:S(2)}, u32[]{:S(2)}) collective-permute-start(bf16[1024,128]{1,0:T(8,128)(2,1)S(1)} %constant_dynamic-update-slice_fusion.4.refs_0_), channel_id=1, source_target_pairs={{0,4},{1,5},{2,6},{3,7},{4,0},{5,1},{6,2},{7,3},{8,12},{9,13},{10,... | collective-permute-start | bytes 786440 | tf_op jit(solution)/shard_map/ppermute | solution.py:477
  49.3 0.2 collective-permute-start.26
  49.5 0.1 collective-permute-start.25
  49.6 2.9 %collective-permute-start.12 = (bf16[1024,128]{1,0:T(8,128)(2,1)S(1)}, bf16[1024,128]{1,0:T(8,128)(2,1)S(1)}, u32[]{:S(2)}, u32[]{:S(2)}) collective-permute-start(bf16[1024,128]{1,0:T(8,128)(2,1)S(1)} %constant_dynamic-update-slice_fusion.refs_0_), channel_id=1, source_target_pairs={{0,4},{1,5},{2,6},{3,7},{4,0},{5,1},{6,2},{7,3},{8,12},{9,13},{10,... | collective-permute-start | bytes 786440 | tf_op jit(solution)/shard_map/ppermute | solution.py:477
  52.5 18.7 %collective-permute-done.28.refs_4_ = bf16[1024,128]{1,0:T(8,128)(2,1)S(1)} collective-permute-done((bf16[1024,128]{1,0:T(8,128)(2,1)S(1)}, bf16[1024,128]{1,0:T(8,128)(2,1)S(1)}, u32[]{:S(2)}, u32[]{:S(2)}) %collective-permute-start.28) | collective-permute-done | bytes 262176 | tf_op jit(solution)/shard_map/ppermute | solution.py:477
  71.2 1.3 collective-permute-start.31
  72.5 0.7 collective-permute-start.14
  73.2 4.6 %collective-permute-start.10 = (bf16[1024,128]{1,0:T(8,128)(2,1)S(1)}, bf16[1024,128]{1,0:T(8,128)(2,1)S(1)}, u32[]{:S(2)}, u32[]{:S(2)}) collective-permute-start(bf16[1024,128]{1,0:T(8,128)(2,1)S(1)} %constant_dynamic-update-slice_fusion.refs_0_), channel_id=1, source_target_pairs={{0,2},{1,3},{2,0},{3,1},{4,6},{5,7},{6,4},{7,5},{8,10},{9,11},{10,... | collective-permute-start | bytes 786440 | tf_op jit(solution)/shard_map/ppermute | solution.py:477
  77.9 1.3 collective-permute-start.15
  79.2 3.1 %collective-permute-done.31 = bf16[1024,128]{1,0:T(8,128)(2,1)S(1)} collective-permute-done((bf16[1024,128]{1,0:T(8,128)(2,1)S(1)}, bf16[1024,128]{1,0:T(8,128)(2,1)S(1)}, u32[]{:S(2)}, u32[]{:S(2)}) %collective-permute-start.31) | collective-permute-done | bytes 262176 | tf_op jit(solution)/shard_map/ppermute | solution.py:477
  82.3 0.1 add.28.refs_6_
  82.4 0.6 collective-permute-start.32
  83.0 5.0 %collective-permute-done.10.refs_2_ = bf16[1024,128]{1,0:T(8,128)(2,1)S(1)} collective-permute-done((bf16[1024,128]{1,0:T(8,128)(2,1)S(1)}, bf16[1024,128]{1,0:T(8,128)(2,1)S(1)}, u32[]{:S(2)}, u32[]{:S(2)}) %collective-permute-start.10) | collective-permute-done | bytes 262176 | tf_op jit(solution)/shard_map/ppermute | solution.py:477
  87.9 0.5 collective-permute-start.13
  88.4 2.9 %collective-permute-done.15 = bf16[1024,128]{1,0:T(8,128)(2,1)S(1)} collective-permute-done((bf16[1024,128]{1,0:T(8,128)(2,1)S(1)}, bf16[1024,128]{1,0:T(8,128)(2,1)S(1)}, u32[]{:S(2)}, u32[]{:S(2)}) %collective-permute-start.15) | collective-permute-done | bytes 262176 | tf_op jit(solution)/shard_map/ppermute | solution.py:477
  91.3 0.1 add.24.refs_0_
  91.4 0.6 collective-permute-start.16
  92.0 2.6 %shard_map.138 = (f32[256,512]{1,0:T(8,128)S(1)}, bf16[256,512]{1,0:T(8,128)(2,1)}, f32[1,256]{1,0:T(1,128)S(1)}) custom-call(s32[8]{0:T(128)S(1)} %copy-done.9, s32[2]{0:T(128)S(1)} %pad_add_fusion.ids_ref, bf16[512,512]{1,0:T(8,128)(2,1)S(1)} %copy-done.5, bf16[4096,512]{1,0:T(8,128)(2,1)S(1)} %copy-done, ...), custom_call_target="tpu_custom_call" | custom-call | flops 1073741824 | bytes 6291456 | tf_op jit(solution)/shard_map/pallas_call | solution.py:327
  94.6 0.0 collective-permute-start.33
  94.6 1.1 collective-permute-done.33
  95.8 3.6 %collective-permute-done.34 = f32[1,256]{1,0:T(1,128)S(1)} collective-permute-done((f32[1,256]{1,0:T(1,128)S(1)}, f32[1,256]{1,0:T(1,128)S(1)}, u32[]{:S(2)}, u32[]{:S(2)}) %collective-permute-start.34) | collective-permute-done | bytes 1056 | tf_op jit(solution)/shard_map/ppermute | solution.py:477
  99.3 1.0 collective-permute-start.35
  100.3 3.5 %collective-permute-done.35 = f32[1,256]{1,0:T(1,128)S(1)} collective-permute-done((f32[1,256]{1,0:T(1,128)S(1)}, f32[1,256]{1,0:T(1,128)S(1)}, u32[]{:S(2)}, u32[]{:S(2)}) %collective-permute-start.35) | collective-permute-done | bytes 1056 | tf_op jit(solution)/shard_map/ppermute | solution.py:477
  103.8 0.1 shard_map.139.own_ref.low_ref
  103.9 2.7 %collective-permute-start.36 = (bf16[256,512]{1,0:T(8,128)(2,1)S(1)}, bf16[256,512]{1,0:T(8,128)(2,1)S(1)}, u32[]{:S(2)}, u32[]{:S(2)}) collective-permute-start(bf16[256,512]{1,0:T(8,128)(2,1)S(1)} %shard_map.139.own_ref.low_ref), channel_id=1, source_target_pairs={{0,8},{8,16},{16,24},{1,9},{9,17},{17,25},{2,10},{10,18},{18,26},{... | collective-permute-start | bytes 786440 | tf_op jit(solution)/shard_map/ppermute | solution.py:477
  106.7 1.6 %shard_map.136.base_ref = f32[256,512]{1,0:T(8,128)S(1)} custom-call(s32[8]{0:T(128)S(1)} %copy-done.9, s32[2]{0:T(128)S(1)} %pad_add_fusion.ids_ref, bf16[512,512]{1,0:T(8,128)(2,1)S(1)} %copy-done.5, bf16[4096,512]{1,0:T(8,128)(2,1)S(1)} %copy-done, bf16[1024,128]{1,0:T(8,128)(2,1)S(1)} %constant_dynamic-update-slice_fusion.refs_0_, ...), custom_call_target="tpu_custom_call" | custom-call | flops 805306368 | bytes 6291456 | tf_op jit(solution)/shard_map/pallas_call | solution.py:327
  108.4 1.7 %shard_map.137 = (f32[256,512]{1,0:T(8,128)S(1)}, bf16[256,512]{1,0:T(8,128)(2,1)}, f32[1,256]{1,0:T(1,128)S(1)}) custom-call(s32[8]{0:T(128)S(1)} %copy-done.9, s32[2]{0:T(128)S(1)} %pad_add_fusion.ids_ref, f32[256,512]{1,0:T(8,128)S(1)} %shard_map.136.base_ref, bf16[4096,512]{1,0:T(8,128)(2,1)S(1)} %copy-done, bf16[1024,128]{1,0:T(8,128)(2,1)S(1)} %add.24.refs_0_, ...), custom_call_target="tpu_custom_call" | custom-call | flops 268435456 | bytes 6291456 | tf_op jit(solution)/shard_map/pallas_call | solution.py:327
  110.1 1.3 collective-permute-start.20
  111.4 0.1 collective-permute-start.17
  111.5 1.1 collective-permute-done.17
  112.6 0.1 collective-permute-start.18
  112.7 0.1 copy.15.len_ref
  112.9 3.3 %collective-permute-done.18 = f32[1,256]{1,0:T(1,128)S(1)} collective-permute-done((f32[1,256]{1,0:T(1,128)S(1)}, f32[1,256]{1,0:T(1,128)S(1)}, u32[]{:S(2)}, u32[]{:S(2)}) %collective-permute-start.18) | collective-permute-done | bytes 1056 | tf_op jit(solution)/shard_map/ppermute | solution.py:477
  116.2 1.0 collective-permute-start.19
  117.2 0.5 spectrum.1.spec_ref
  117.8 2.9 %collective-permute-done.19 = f32[1,256]{1,0:T(1,128)S(1)} collective-permute-done((f32[1,256]{1,0:T(1,128)S(1)}, f32[1,256]{1,0:T(1,128)S(1)}, u32[]{:S(2)}, u32[]{:S(2)}) %collective-permute-start.19) | collective-permute-done | bytes 1056 | tf_op jit(solution)/shard_map/ppermute | solution.py:477
  120.7 1.5 %collective-permute-start.21 = (f32[1,256]{1,0:T(1,128)S(1)}, f32[1,256]{1,0:T(1,128)S(1)}, u32[]{:S(2)}, u32[]{:S(2)}) collective-permute-start(f32[1,256]{1,0:T(1,128)S(1)} %add.27.sq_ref), channel_id=1, source_target_pairs={{8,0},{16,8},{24,16},{9,1},{17,9},{25,17},{10,2},{18,10},{26,18},{... | collective-permute-start | bytes 3080 | tf_op jit(solution)/shard_map/ppermute | solution.py:477
  122.2 1.2 conv_own.1.part_ref
  123.4 1.4 %conv_low.1.done_ref = bf16[256,512]{1,0:T(8,128)(2,1)S(1)} custom-call(f32[256,512]{1,0:T(8,128)S(1)} %get-tuple-element.45.res_ref, bf16[256,512]{1,0:T(8,128)(2,1)S(1)} %shard_map.139.own_ref.low_ref, bf16[256,512]{1,0:T(8,128)(2,1)S(1)} %collective-permute-done.36.before_ref, f32[512,512]{1,0:T(8,128)S(1)} %spectrum.1.spec_ref, f32[1,512]{1,0:T(1,128)S(1)} %bitcast.9, ...), custom_call_target="tpu_custom_call" | custom-call | flops 469762048 | bytes 1572864 | tf_op jit(solution)/shard_map/conv_low/pallas_call | solution.py:542
  124.8 1.9 %collective-permute-done.21.raw_sq_ref = f32[1,256]{1,0:T(1,128)S(1)} collective-permute-done((f32[1,256]{1,0:T(1,128)S(1)}, f32[1,256]{1,0:T(1,128)S(1)}, u32[]{:S(2)}, u32[]{:S(2)}) %collective-permute-start.21) | collective-permute-done | bytes 1056 | tf_op jit(solution)/shard_map/ppermute | solution.py:477
  126.7 2.5 %conv_high.1 = bf16[512,512]{1,0:T(8,128)(2,1)} custom-call(s32[8]{0:T(128)S(1)} %copy-done.9, s32[2]{0:T(128)S(1)} %pad_add_fusion.ids_ref, f32[256,512]{1,0:T(8,128)S(1)} %conv_own.1.part_ref, bf16[256,512]{1,0:T(8,128)(2,1)S(1)} %collective-permute-done.20.raw_ref, f32[1,256]{1,0:T(1,128)S(1)} %collective-permute-done.21.raw_sq_ref, ...), custom_call_target="tpu_custom_call" | custom-call | flops 335544320 | bytes 1572864 | tf_op jit(solution)/shard_map/conv_high/pallas_call | solution.py:571
  (63 shorter events, 0.3 us)
Async XLA Ops:
  0.1 0.7 copy-start.8
  0.7 91.2 %copy-start = (bf16[4096,512]{1,0:T(8,128)(2,1)S(1)}, bf16[4096,512]{1,0:T(8,128)(2,1)}, u32[]{:S(2)}) copy-start(bf16[4096,512]{1,0:T(8,128)(2,1)} %w_ref.5) | copy-start | bytes 12582916
  0.7 91.2 %copy-start.5 = (bf16[512,512]{1,0:T(8,128)(2,1)S(1)}, bf16[512,512]{1,0:T(8,128)(2,1)}, u32[]{:S(2)}) copy-start(bf16[512,512]{1,0:T(8,128)(2,1)} %base_ref.3) | copy-start | bytes 1572868
  0.7 91.3 %copy-start.9 = (s32[8]{0:T(128)S(1)}, s32[8]{0:T(128)}, u32[]{:S(2)}) copy-start(s32[8]{0:T(128)} %slots_ref.9) | copy-start | bytes 100
  3.2 8.8 %collective-permute-start = (bf16[768,128]{1,0:T(8,128)(2,1)S(1)}, bf16[768,128]{1,0:T(8,128)(2,1)S(1)}, u32[]{:S(2)}, u32[]{:S(2)}) collective-permute-start(bf16[768,128]{1,0:T(8,128)(2,1)S(1)} %get-tuple-element.27), channel_id=1, source_target_pairs={{0,8},{8,0},{16,24},{24,16},{1,9},{9,1},{17,25},{25,17},{2,10},{10... | collective-permute-start | bytes 589832 | tf_op jit(solution)/shard_map/ppermute | solution.py:477
  6.2 12.0 %collective-permute-start.1 = (bf16[768,128]{1,0:T(8,128)(2,1)S(1)}, bf16[768,128]{1,0:T(8,128)(2,1)S(1)}, u32[]{:S(2)}, u32[]{:S(2)}) collective-permute-start(bf16[768,128]{1,0:T(8,128)(2,1)S(1)} %get-tuple-element.28), channel_id=1, source_target_pairs={{0,16},{8,24},{16,0},{24,8},{1,17},{9,25},{17,1},{25,9},{2,18},{10... | collective-permute-start | bytes 589832 | tf_op jit(solution)/shard_map/ppermute | solution.py:477
  7.8 10.5 %collective-permute-start.2 = (bf16[768,128]{1,0:T(8,128)(2,1)S(1)}, bf16[768,128]{1,0:T(8,128)(2,1)S(1)}, u32[]{:S(2)}, u32[]{:S(2)}) collective-permute-start(bf16[768,128]{1,0:T(8,128)(2,1)S(1)} %get-tuple-element.29), channel_id=1, source_target_pairs={{0,24},{8,16},{16,8},{24,0},{1,25},{9,17},{17,9},{25,1},{2,26},{10... | collective-permute-start | bytes 589832 | tf_op jit(solution)/shard_map/ppermute | solution.py:477
  7.8 12.7 %collective-permute-start.3 = (bf16[768,128]{1,0:T(8,128)(2,1)S(1)}, bf16[768,128]{1,0:T(8,128)(2,1)S(1)}, u32[]{:S(2)}, u32[]{:S(2)}) collective-permute-start(bf16[768,128]{1,0:T(8,128)(2,1)S(1)} %get-tuple-element.31), channel_id=1, source_target_pairs={{0,8},{8,0},{16,24},{24,16},{1,9},{9,1},{17,25},{25,17},{2,10},{10... | collective-permute-start | bytes 589832 | tf_op jit(solution)/shard_map/ppermute | solution.py:477
  9.7 15.5 %collective-permute-start.4 = (bf16[768,128]{1,0:T(8,128)(2,1)S(1)}, bf16[768,128]{1,0:T(8,128)(2,1)S(1)}, u32[]{:S(2)}, u32[]{:S(2)}) collective-permute-start(bf16[768,128]{1,0:T(8,128)(2,1)S(1)} %get-tuple-element.32), channel_id=1, source_target_pairs={{0,16},{8,24},{16,0},{24,8},{1,17},{9,25},{17,1},{25,9},{2,18},{10... | collective-permute-start | bytes 589832 | tf_op jit(solution)/shard_map/ppermute | solution.py:477
  12.0 13.3 %collective-permute-start.5 = (bf16[768,128]{1,0:T(8,128)(2,1)S(1)}, bf16[768,128]{1,0:T(8,128)(2,1)S(1)}, u32[]{:S(2)}, u32[]{:S(2)}) collective-permute-start(bf16[768,128]{1,0:T(8,128)(2,1)S(1)} %get-tuple-element.33), channel_id=1, source_target_pairs={{0,24},{8,16},{16,8},{24,0},{1,25},{9,17},{17,9},{25,1},{2,26},{10... | collective-permute-start | bytes 589832 | tf_op jit(solution)/shard_map/ppermute | solution.py:477
  28.9 20.4 %collective-permute-start.6 = (bf16[256,128]{1,0:T(8,128)(2,1)S(1)}, bf16[256,128]{1,0:T(8,128)(2,1)S(1)}, u32[]{:S(2)}, u32[]{:S(2)}) collective-permute-start(bf16[256,128]{1,0:T(8,128)(2,1)S(1)} %get-tuple-element.35), channel_id=1, source_target_pairs={{0,8},{8,0},{16,24},{24,16},{1,9},{9,1},{17,25},{25,17},{2,10},{10... | collective-permute-start | bytes 196616 | tf_op jit(solution)/shard_map/ppermute | solution.py:477
  30.2 19.3 %collective-permute-start.7 = (bf16[256,128]{1,0:T(8,128)(2,1)S(1)}, bf16[256,128]{1,0:T(8,128)(2,1)S(1)}, u32[]{:S(2)}, u32[]{:S(2)}) collective-permute-start(bf16[256,128]{1,0:T(8,128)(2,1)S(1)} %get-tuple-element.36), channel_id=1, source_target_pairs={{0,16},{8,24},{16,0},{24,8},{1,17},{9,25},{17,1},{25,9},{2,18},{10... | collective-permute-start | bytes 196616 | tf_op jit(solution)/shard_map/ppermute | solution.py:477
  31.0 18.6 %collective-permute-start.8 = (bf16[256,128]{1,0:T(8,128)(2,1)S(1)}, bf16[256,128]{1,0:T(8,128)(2,1)S(1)}, u32[]{:S(2)}, u32[]{:S(2)}) collective-permute-start(bf16[256,128]{1,0:T(8,128)(2,1)S(1)} %get-tuple-element.37), channel_id=1, source_target_pairs={{0,24},{8,16},{16,8},{24,0},{1,25},{9,17},{17,9},{25,1},{2,26},{10... | collective-permute-start | bytes 196616 | tf_op jit(solution)/shard_map/ppermute | solution.py:477
  34.7 4.3 %collective-permute-start.22 = (bf16[256,128]{1,0:T(8,128)(2,1)S(1)}, bf16[256,128]{1,0:T(8,128)(2,1)S(1)}, u32[]{:S(2)}, u32[]{:S(2)}) collective-permute-start(bf16[256,128]{1,0:T(8,128)(2,1)S(1)} %get-tuple-element.42), channel_id=1, source_target_pairs={{0,8},{8,0},{16,24},{24,16},{1,9},{9,1},{17,25},{25,17},{2,10},{10... | collective-permute-start | bytes 196616 | tf_op jit(solution)/shard_map/ppermute | solution.py:477
  36.1 4.5 %collective-permute-start.23 = (bf16[256,128]{1,0:T(8,128)(2,1)S(1)}, bf16[256,128]{1,0:T(8,128)(2,1)S(1)}, u32[]{:S(2)}, u32[]{:S(2)}) collective-permute-start(bf16[256,128]{1,0:T(8,128)(2,1)S(1)} %get-tuple-element.43), channel_id=1, source_target_pairs={{0,16},{8,24},{16,0},{24,8},{1,17},{9,25},{17,1},{25,9},{2,18},{10... | collective-permute-start | bytes 196616 | tf_op jit(solution)/shard_map/ppermute | solution.py:477
  39.1 5.2 %collective-permute-start.24 = (bf16[256,128]{1,0:T(8,128)(2,1)S(1)}, bf16[256,128]{1,0:T(8,128)(2,1)S(1)}, u32[]{:S(2)}, u32[]{:S(2)}) collective-permute-start(bf16[256,128]{1,0:T(8,128)(2,1)S(1)} %get-tuple-element.44), channel_id=1, source_target_pairs={{0,24},{8,16},{16,8},{24,0},{1,25},{9,17},{17,9},{25,1},{2,26},{10... | collective-permute-start | bytes 196616 | tf_op jit(solution)/shard_map/ppermute | solution.py:477
  44.2 28.3 %collective-permute-start.30 = (bf16[1024,128]{1,0:T(8,128)(2,1)S(1)}, bf16[1024,128]{1,0:T(8,128)(2,1)S(1)}, u32[]{:S(2)}, u32[]{:S(2)}) collective-permute-start(bf16[1024,128]{1,0:T(8,128)(2,1)S(1)} %constant_dynamic-update-slice_fusion.4.refs_0_), channel_id=1, source_target_pairs={{2,4},{3,5},{4,2},{5,3},{10,12},{11,13},{12,10},{13,11},{18,20},{1... | collective-permute-start | bytes 786440 | tf_op jit(solution)/shard_map/ppermute | solution.py:477
  44.9 26.3 %collective-permute-start.28 = (bf16[1024,128]{1,0:T(8,128)(2,1)S(1)}, bf16[1024,128]{1,0:T(8,128)(2,1)S(1)}, u32[]{:S(2)}, u32[]{:S(2)}) collective-permute-start(bf16[1024,128]{1,0:T(8,128)(2,1)S(1)} %constant_dynamic-update-slice_fusion.4.refs_0_), channel_id=1, source_target_pairs={{0,4},{1,5},{2,6},{3,7},{4,0},{5,1},{6,2},{7,3},{8,12},{9,13},{10,... | collective-permute-start | bytes 786440 | tf_op jit(solution)/shard_map/ppermute | solution.py:477
  49.3 24.0 %collective-permute-start.26 = (bf16[1024,128]{1,0:T(8,128)(2,1)S(1)}, bf16[1024,128]{1,0:T(8,128)(2,1)S(1)}, u32[]{:S(2)}, u32[]{:S(2)}) collective-permute-start(bf16[1024,128]{1,0:T(8,128)(2,1)S(1)} %constant_dynamic-update-slice_fusion.4.refs_0_), channel_id=1, source_target_pairs={{0,2},{1,3},{2,0},{3,1},{4,6},{5,7},{6,4},{7,5},{8,10},{9,11},{10,... | collective-permute-start | bytes 786440 | tf_op jit(solution)/shard_map/ppermute | solution.py:477
  49.5 28.4 %collective-permute-start.25 = (bf16[1024,128]{1,0:T(8,128)(2,1)S(1)}, bf16[1024,128]{1,0:T(8,128)(2,1)S(1)}, u32[]{:S(2)}, u32[]{:S(2)}) collective-permute-start(bf16[1024,128]{1,0:T(8,128)(2,1)S(1)} %constant_dynamic-update-slice_fusion.4.refs_0_), channel_id=1, source_target_pairs={{0,1},{1,0},{2,3},{3,2},{4,5},{5,4},{6,7},{7,6},{8,9},{9,8},{10,11... | collective-permute-start | bytes 786440 | tf_op jit(solution)/shard_map/ppermute | solution.py:477
  49.6 54.2 %copy-start.7 = (f32[512]{0:T(512)S(1)}, f32[512]{0:T(512)}, u32[]{:S(2)}) copy-start(f32[512]{0:T(512)} %param.19) | copy-start | bytes 6148
  49.6 28.3 %collective-permute-start.12 = (bf16[1024,128]{1,0:T(8,128)(2,1)S(1)}, bf16[1024,128]{1,0:T(8,128)(2,1)S(1)}, u32[]{:S(2)}, u32[]{:S(2)}) collective-permute-start(bf16[1024,128]{1,0:T(8,128)(2,1)S(1)} %constant_dynamic-update-slice_fusion.refs_0_), channel_id=1, source_target_pairs={{0,4},{1,5},{2,6},{3,7},{4,0},{5,1},{6,2},{7,3},{8,12},{9,13},{10,... | collective-permute-start | bytes 786440 | tf_op jit(solution)/shard_map/ppermute | solution.py:477
  71.2 11.1 %collective-permute-start.31 = (bf16[1024,128]{1,0:T(8,128)(2,1)S(1)}, bf16[1024,128]{1,0:T(8,128)(2,1)S(1)}, u32[]{:S(2)}, u32[]{:S(2)}) collective-permute-start(bf16[1024,128]{1,0:T(8,128)(2,1)S(1)} %collective-permute-done.28.refs_4_), channel_id=1, source_target_pairs={{2,0},{3,1},{4,6},{5,7},{10,8},{11,9},{12,14},{13,15},{18,16},{19,... | collective-permute-start | bytes 786440 | tf_op jit(solution)/shard_map/ppermute | solution.py:477
  72.5 9.8 %collective-permute-start.14 = (bf16[1024,128]{1,0:T(8,128)(2,1)S(1)}, bf16[1024,128]{1,0:T(8,128)(2,1)S(1)}, u32[]{:S(2)}, u32[]{:S(2)}) collective-permute-start(bf16[1024,128]{1,0:T(8,128)(2,1)S(1)} %constant_dynamic-update-slice_fusion.refs_0_), channel_id=1, source_target_pairs={{2,4},{3,5},{4,2},{5,3},{10,12},{11,13},{12,10},{13,11},{18,20},{1... | collective-permute-start | bytes 786440 | tf_op jit(solution)/shard_map/ppermute | solution.py:477
  73.2 14.7 %collective-permute-start.10 = (bf16[1024,128]{1,0:T(8,128)(2,1)S(1)}, bf16[1024,128]{1,0:T(8,128)(2,1)S(1)}, u32[]{:S(2)}, u32[]{:S(2)}) collective-permute-start(bf16[1024,128]{1,0:T(8,128)(2,1)S(1)} %constant_dynamic-update-slice_fusion.refs_0_), channel_id=1, source_target_pairs={{0,2},{1,3},{2,0},{3,1},{4,6},{5,7},{6,4},{7,5},{8,10},{9,11},{10,... | collective-permute-start | bytes 786440 | tf_op jit(solution)/shard_map/ppermute | solution.py:477
  77.9 10.0 %collective-permute-start.29 = (bf16[1024,128]{1,0:T(8,128)(2,1)S(1)}, bf16[1024,128]{1,0:T(8,128)(2,1)S(1)}, u32[]{:S(2)}, u32[]{:S(2)}) collective-permute-start(bf16[1024,128]{1,0:T(8,128)(2,1)S(1)} %collective-permute-done.28.refs_4_), channel_id=1, source_target_pairs={{0,1},{1,0},{2,3},{3,2},{4,5},{5,4},{6,7},{7,6},{8,9},{9,8},{10,11... | collective-permute-start | bytes 786440 | tf_op jit(solution)/shard_map/ppermute | solution.py:477
  77.9 13.4 %collective-permute-start.15 = (bf16[1024,128]{1,0:T(8,128)(2,1)S(1)}, bf16[1024,128]{1,0:T(8,128)(2,1)S(1)}, u32[]{:S(2)}, u32[]{:S(2)}) collective-permute-start(bf16[1024,128]{1,0:T(8,128)(2,1)S(1)} %collective-permute-done.12.refs_4_), channel_id=1, source_target_pairs={{2,0},{3,1},{4,6},{5,7},{10,8},{11,9},{12,14},{13,15},{18,16},{19,... | collective-permute-start | bytes 786440 | tf_op jit(solution)/shard_map/ppermute | solution.py:477
  82.3 9.1 %collective-permute-start.27 = (bf16[1024,128]{1,0:T(8,128)(2,1)S(1)}, bf16[1024,128]{1,0:T(8,128)(2,1)S(1)}, u32[]{:S(2)}, u32[]{:S(2)}) collective-permute-start(bf16[1024,128]{1,0:T(8,128)(2,1)S(1)} %collective-permute-done.26.refs_2_), channel_id=1, source_target_pairs={{0,1},{1,0},{2,3},{3,2},{4,5},{5,4},{6,7},{7,6},{8,9},{9,8},{10,11... | collective-permute-start | bytes 786440 | tf_op jit(solution)/shard_map/ppermute | solution.py:477
  82.4 9.6 %collective-permute-start.32 = (bf16[1024,128]{1,0:T(8,128)(2,1)S(1)}, bf16[1024,128]{1,0:T(8,128)(2,1)S(1)}, u32[]{:S(2)}, u32[]{:S(2)}) collective-permute-start(bf16[1024,128]{1,0:T(8,128)(2,1)S(1)} %add.28.refs_6_), channel_id=1, source_target_pairs={{0,1},{1,0},{2,3},{3,2},{4,5},{5,4},{6,7},{7,6},{8,9},{9,8},{10,11... | collective-permute-start | bytes 786440 | tf_op jit(solution)/shard_map/ppermute | solution.py:477
  87.9 18.7 %collective-permute-start.9 = (bf16[1024,128]{1,0:T(8,128)(2,1)S(1)}, bf16[1024,128]{1,0:T(8,128)(2,1)S(1)}, u32[]{:S(2)}, u32[]{:S(2)}) collective-permute-start(bf16[1024,128]{1,0:T(8,128)(2,1)S(1)} %constant_dynamic-update-slice_fusion.refs_0_), channel_id=1, source_target_pairs={{0,1},{1,0},{2,3},{3,2},{4,5},{5,4},{6,7},{7,6},{8,9},{9,8},{10,11... | collective-permute-start | bytes 786440 | tf_op jit(solution)/shard_map/ppermute | solution.py:477
  87.9 18.7 %collective-permute-start.13 = (bf16[1024,128]{1,0:T(8,128)(2,1)S(1)}, bf16[1024,128]{1,0:T(8,128)(2,1)S(1)}, u32[]{:S(2)}, u32[]{:S(2)}) collective-permute-start(bf16[1024,128]{1,0:T(8,128)(2,1)S(1)} %collective-permute-done.12.refs_4_), channel_id=1, source_target_pairs={{0,1},{1,0},{2,3},{3,2},{4,5},{5,4},{6,7},{7,6},{8,9},{9,8},{10,11... | collective-permute-start | bytes 786440 | tf_op jit(solution)/shard_map/ppermute | solution.py:477
  91.3 15.3 %collective-permute-start.11 = (bf16[1024,128]{1,0:T(8,128)(2,1)S(1)}, bf16[1024,128]{1,0:T(8,128)(2,1)S(1)}, u32[]{:S(2)}, u32[]{:S(2)}) collective-permute-start(bf16[1024,128]{1,0:T(8,128)(2,1)S(1)} %collective-permute-done.10.refs_2_), channel_id=1, source_target_pairs={{0,1},{1,0},{2,3},{3,2},{4,5},{5,4},{6,7},{7,6},{8,9},{9,8},{10,11... | collective-permute-start | bytes 786440 | tf_op jit(solution)/shard_map/ppermute | solution.py:477
  91.4 16.9 %collective-permute-start.16 = (bf16[1024,128]{1,0:T(8,128)(2,1)S(1)}, bf16[1024,128]{1,0:T(8,128)(2,1)S(1)}, u32[]{:S(2)}, u32[]{:S(2)}) collective-permute-start(bf16[1024,128]{1,0:T(8,128)(2,1)S(1)} %add.24.refs_0_), channel_id=1, source_target_pairs={{0,1},{1,0},{2,3},{3,2},{4,5},{5,4},{6,7},{7,6},{8,9},{9,8},{10,11... | collective-permute-start | bytes 786440 | tf_op jit(solution)/shard_map/ppermute | solution.py:477
  94.6 1.2 collective-permute-start.33
  95.7 3.6 %collective-permute-start.34 = (f32[1,256]{1,0:T(1,128)S(1)}, f32[1,256]{1,0:T(1,128)S(1)}, u32[]{:S(2)}, u32[]{:S(2)}) collective-permute-start(f32[1,256]{1,0:T(1,128)S(1)} %add.29), channel_id=1, source_target_pairs={{0,2},{1,3},{2,0},{3,1},{4,6},{5,7},{6,4},{7,5},{8,10},{9,11},{10,... | collective-permute-start | bytes 3080 | tf_op jit(solution)/shard_map/ppermute | solution.py:477
  99.3 4.5 %collective-permute-start.35 = (f32[1,256]{1,0:T(1,128)S(1)}, f32[1,256]{1,0:T(1,128)S(1)}, u32[]{:S(2)}, u32[]{:S(2)}) collective-permute-start(f32[1,256]{1,0:T(1,128)S(1)} %add.30), channel_id=1, source_target_pairs={{0,4},{1,5},{2,6},{3,7},{4,0},{5,1},{6,2},{7,3},{8,12},{9,13},{10,... | collective-permute-start | bytes 3080 | tf_op jit(solution)/shard_map/ppermute | solution.py:477
  103.9 19.4 %collective-permute-start.36 = (bf16[256,512]{1,0:T(8,128)(2,1)S(1)}, bf16[256,512]{1,0:T(8,128)(2,1)S(1)}, u32[]{:S(2)}, u32[]{:S(2)}) collective-permute-start(bf16[256,512]{1,0:T(8,128)(2,1)S(1)} %shard_map.139.own_ref.low_ref), channel_id=1, source_target_pairs={{0,8},{8,16},{16,24},{1,9},{9,17},{17,25},{2,10},{10,18},{18,26},{... | collective-permute-start | bytes 786440 | tf_op jit(solution)/shard_map/ppermute | solution.py:477
  108.3 4.5 %copy-start.11 = (s32[512]{0:T(512)S(1)}, s32[512]{0:T(512)}, u32[]{:S(2)}) copy-start(s32[512]{0:T(512)} %param.21) | copy-start | bytes 6148
  108.3 8.9 %copy-start.1 = (bf16[512,256]{1,0:T(8,128)(2,1)S(1)}, bf16[512,256]{1,0:T(8,128)(2,1)}, u32[]{:S(2)}) copy-start(bf16[512,256]{1,0:T(8,128)(2,1)} %constant.17.clone.fl_ref.fl) | copy-start | bytes 786436
  108.3 8.9 %copy-start.2 = (bf16[512,256]{1,0:T(8,128)(2,1)S(1)}, bf16[512,256]{1,0:T(8,128)(2,1)}, u32[]{:S(2)}) copy-start(bf16[512,256]{1,0:T(8,128)(2,1)} %constant.16.clone.fh_ref.fh) | copy-start | bytes 786436
  108.3 8.9 %copy-start.6 = (bf16[512,256]{1,0:T(8,128)(2,1)S(1)}, bf16[512,256]{1,0:T(8,128)(2,1)}, u32[]{:S(2)}) copy-start(bf16[512,256]{1,0:T(8,128)(2,1)} %filters_ref.1) | copy-start | bytes 786436
  108.3 13.8 %copy-start.3 = (bf16[256,512]{1,0:T(8,128)(2,1)S(1)}, bf16[256,512]{1,0:T(8,128)(2,1)}, u32[]{:S(2)}) copy-start(bf16[256,512]{1,0:T(8,128)(2,1)} %constant.19.clone.gl) | copy-start | bytes 786436
  108.3 13.8 %copy-start.4 = (bf16[256,512]{1,0:T(8,128)(2,1)S(1)}, bf16[256,512]{1,0:T(8,128)(2,1)}, u32[]{:S(2)}) copy-start(bf16[256,512]{1,0:T(8,128)(2,1)} %constant.18.clone.gh) | copy-start | bytes 786436
  108.3 13.8 %copy-start.10 = (f32[512]{0:T(512)S(1)}, f32[512]{0:T(512)}, u32[]{:S(2)}) copy-start(f32[512]{0:T(512)} %param.22) | copy-start | bytes 6148
  110.1 16.7 %collective-permute-start.20 = (bf16[256,512]{1,0:T(8,128)(2,1)}, bf16[256,512]{1,0:T(8,128)(2,1)S(1)}, u32[]{:S(2)}, u32[]{:S(2)}) collective-permute-start(bf16[256,512]{1,0:T(8,128)(2,1)} %get-tuple-element.40), channel_id=1, source_target_pairs={{8,0},{16,8},{24,16},{9,1},{17,9},{25,17},{10,2},{18,10},{26,18},{... | collective-permute-start | bytes 786440 | tf_op jit(solution)/shard_map/ppermute | solution.py:477
  111.4 1.2 collective-permute-start.17
  112.6 3.6 %collective-permute-start.18 = (f32[1,256]{1,0:T(1,128)S(1)}, f32[1,256]{1,0:T(1,128)S(1)}, u32[]{:S(2)}, u32[]{:S(2)}) collective-permute-start(f32[1,256]{1,0:T(1,128)S(1)} %add.25), channel_id=1, source_target_pairs={{0,2},{1,3},{2,0},{3,1},{4,6},{5,7},{6,4},{7,5},{8,10},{9,11},{10,... | collective-permute-start | bytes 3080 | tf_op jit(solution)/shard_map/ppermute | solution.py:477
  116.2 4.5 %collective-permute-start.19 = (f32[1,256]{1,0:T(1,128)S(1)}, f32[1,256]{1,0:T(1,128)S(1)}, u32[]{:S(2)}, u32[]{:S(2)}) collective-permute-start(f32[1,256]{1,0:T(1,128)S(1)} %add.26), channel_id=1, source_target_pairs={{0,4},{1,5},{2,6},{3,7},{4,0},{5,1},{6,2},{7,3},{8,12},{9,13},{10,... | collective-permute-start | bytes 3080 | tf_op jit(solution)/shard_map/ppermute | solution.py:477
  120.7 6.1 %collective-permute-start.21 = (f32[1,256]{1,0:T(1,128)S(1)}, f32[1,256]{1,0:T(1,128)S(1)}, u32[]{:S(2)}, u32[]{:S(2)}) collective-permute-start(f32[1,256]{1,0:T(1,128)S(1)} %add.27.sq_ref), channel_id=1, source_target_pairs={{8,0},{16,8},{24,16},{9,1},{17,9},{25,17},{10,2},{18,10},{26,18},{... | collective-permute-start | bytes 3080 | tf_op jit(solution)/shard_map/ppermute | solution.py:477

commit v4 on v3

--- a/solution.py
+++ b/solution.py
@@ -478,17 +478,9 @@
 
 
 def gather_mp(own, size):
-    chips = size // 2
-    pieces = [own]
-    for k in range(1, chips - 1):
-        pieces.append(moved(own, "mp", xor_route(size, 2 * k)))
-    inner = [(i, i ^ (size - 2)) for i in range(2, size - 2)]
-    direct = moved(own, "mp", inner)
-    ends = [(2, 0), (3, 1), (size - 4, size - 2), (size - 3, size - 1)]
-    relayed = moved(pieces[chips - 2], "mp", ends)
-    pieces.append(direct + relayed)
     parts = []
-    for piece in pieces:
+    for k in range(size // 2):
+        piece = moved(own, "mp", xor_route(size, 2 * k)) if k else own
         parts.append(piece)
         parts.append(moved(piece, "mp", xor_route(size, 1)))
     return parts
@@ -595,7 +587,7 @@
         heads % n == 0
         and power_of_two(n)
         and power_of_two(size)
-        and size >= 8
+        and size >= 4
         and rows % 256 == 0
         and filters.shape[1] <= rows
     )

time: 130 us -> 129 us (level)
  starting transfers between devices: 43.6 us -> 54.6 us
  waiting for transfers between devices: 64 us -> 53.2 us
    ppermute x37 -> x35, starting transfers between devices: 43.6 us -> 54.6 us  [moved(): return lax.ppermute(block, axis, route)]
    ppermute x37 -> x35, waiting for transfers between devices: 64 us -> 53.2 us  [moved(): return lax.ppermute(block, axis, route)]
  transfers between devices with their start and end apart: 37 -> 35, of which waited for: 17 -> 17; matrix products, arithmetic and copies ran while one was open for 0% -> 0% of each run, Pallas kernels for 9% -> 9%
where the time goes in v4:
time: 129 us
  starting transfers between devices  54.6 us (42%)
  waiting for transfers between devices  53.2 us (41%)
  Pallas kernels  19.8 us (15%)
    ppermute x35, starting transfers between devices, moved(): return lax.ppermute(block, axis, route)  54.6 us
    ppermute x35, waiting for transfers between devices, moved(): return lax.ppermute(block, axis, route)  53.2 us
    pallas_call x3, Pallas kernels, project(): pl.pallas_call(functools.partial(project_kernel, n, high, indices), out_s...  5.9 us
    pallas_call x2, Pallas kernels, attend(): pl.pallas_call(functools.partial(attend_kernel, n, high, rows), out_shape...  5.9 us
  transfers between devices with their start and end apart: 35, of which 17 were waited for; matrix products, arithmetic and copies ran while one was open for 0% of the time, Pallas kernels for 9%

profile of v4, /device:TPU:0, one launch (start us, length us, event | category | flops | bytes accessed | tf_op | source)
XLA Modules:
  0.0 129.2 jit_solution(10532383224340673579)
XLA Ops:
  0.0 0.1 pad_add_fusion.ids_ref
  0.1 0.8 copy-done.8
  0.9 2.2 %pack.1 = (bf16[768,128]{1,0:T(8,128)(2,1)S(1)}, bf16[768,128]{1,0:T(8,128)(2,1)S(1)}, bf16[768,128]{1,0:T(8,128)(2,1)S(1)}, bf16[768,128]{1,0:T(8,128)(2,1)S(1)...) custom-call(s32[8]{0:T(128)S(1)} %copy-done.8, ...), custom_call_target="tpu_custom_call" | custom-call | bytes 3145728 | tf_op jit(solution)/shard_map/pack/pallas_call | solution.py:200
  3.1 3.0 %collective-permute-start = (bf16[768,128]{1,0:T(8,128)(2,1)S(1)}, bf16[768,128]{1,0:T(8,128)(2,1)S(1)}, u32[]{:S(2)}, u32[]{:S(2)}) collective-permute-start(bf16[768,128]{1,0:T(8,128)(2,1)S(1)} %get-tuple-element.27), channel_id=1, source_target_pairs={{0,8},{8,0},{16,24},{24,16},{1,9},{9,1},{17,25},{25,17},{2,10},{10... | collective-permute-start | bytes 589832 | tf_op jit(solution)/shard_map/ppermute | solution.py:477
  6.1 1.5 %collective-permute-start.1 = (bf16[768,128]{1,0:T(8,128)(2,1)S(1)}, bf16[768,128]{1,0:T(8,128)(2,1)S(1)}, u32[]{:S(2)}, u32[]{:S(2)}) collective-permute-start(bf16[768,128]{1,0:T(8,128)(2,1)S(1)} %get-tuple-element.28), channel_id=1, source_target_pairs={{0,16},{8,24},{16,0},{24,8},{1,17},{9,25},{17,1},{25,9},{2,18},{10... | collective-permute-start | bytes 589832 | tf_op jit(solution)/shard_map/ppermute | solution.py:477
  7.7 0.0 collective-permute-start.2
  7.7 1.9 %collective-permute-start.3 = (bf16[768,128]{1,0:T(8,128)(2,1)S(1)}, bf16[768,128]{1,0:T(8,128)(2,1)S(1)}, u32[]{:S(2)}, u32[]{:S(2)}) collective-permute-start(bf16[768,128]{1,0:T(8,128)(2,1)S(1)} %get-tuple-element.31), channel_id=1, source_target_pairs={{0,8},{8,0},{16,24},{24,16},{1,9},{9,1},{17,25},{25,17},{2,10},{10... | collective-permute-start | bytes 589832 | tf_op jit(solution)/shard_map/ppermute | solution.py:477
  9.6 1.5 %collective-permute-start.4 = (bf16[768,128]{1,0:T(8,128)(2,1)S(1)}, bf16[768,128]{1,0:T(8,128)(2,1)S(1)}, u32[]{:S(2)}, u32[]{:S(2)}) collective-permute-start(bf16[768,128]{1,0:T(8,128)(2,1)S(1)} %get-tuple-element.32), channel_id=1, source_target_pairs={{0,16},{8,24},{16,0},{24,8},{1,17},{9,25},{17,1},{25,9},{2,18},{10... | collective-permute-start | bytes 589832 | tf_op jit(solution)/shard_map/ppermute | solution.py:477
  11.2 0.7 collective-permute-done.refs_1_
  11.9 3.0 %collective-permute-start.5 = (bf16[768,128]{1,0:T(8,128)(2,1)S(1)}, bf16[768,128]{1,0:T(8,128)(2,1)S(1)}, u32[]{:S(2)}, u32[]{:S(2)}) collective-permute-start(bf16[768,128]{1,0:T(8,128)(2,1)S(1)} %get-tuple-element.33), channel_id=1, source_target_pairs={{0,24},{8,16},{16,8},{24,0},{1,25},{9,17},{17,9},{25,1},{2,26},{10... | collective-permute-start | bytes 589832 | tf_op jit(solution)/shard_map/ppermute | solution.py:477
  14.9 3.3 %collective-permute-done.1.refs_2_ = bf16[768,128]{1,0:T(8,128)(2,1)S(1)} collective-permute-done((bf16[768,128]{1,0:T(8,128)(2,1)S(1)}, bf16[768,128]{1,0:T(8,128)(2,1)S(1)}, u32[]{:S(2)}, u32[]{:S(2)}) %collective-permute-start.1) | collective-permute-done | bytes 196640 | tf_op jit(solution)/shard_map/ppermute | solution.py:477
  18.1 2.2 %collective-permute-done.3.refs_5_ = bf16[768,128]{1,0:T(8,128)(2,1)S(1)} collective-permute-done((bf16[768,128]{1,0:T(8,128)(2,1)S(1)}, bf16[768,128]{1,0:T(8,128)(2,1)S(1)}, u32[]{:S(2)}, u32[]{:S(2)}) %collective-permute-start.3) | collective-permute-done | bytes 196640 | tf_op jit(solution)/shard_map/ppermute | solution.py:477
  20.4 4.8 %collective-permute-done.4.refs_6_ = bf16[768,128]{1,0:T(8,128)(2,1)S(1)} collective-permute-done((bf16[768,128]{1,0:T(8,128)(2,1)S(1)}, bf16[768,128]{1,0:T(8,128)(2,1)S(1)}, u32[]{:S(2)}, u32[]{:S(2)}) %collective-permute-start.4) | collective-permute-done | bytes 196640 | tf_op jit(solution)/shard_map/ppermute | solution.py:477
  25.1 3.6 %attend_high.1 = (bf16[256,128]{1,0:T(8,128)(2,1)S(1)}, bf16[256,128]{1,0:T(8,128)(2,1)S(1)}, bf16[256,128]{1,0:T(8,128)(2,1)S(1)}, bf16[256,128]{1,0:T(8,128)(2,1)S(1)}) custom-call(s32[2]{0:T(128)S(1)} %pad_add_fusion.ids_ref, bf16[768,128]{1,0:T(8,128)(2,1)S(1)} %get-tuple-element.26.refs_0_, bf16[768,128]{1,0:T(8,128)(2,1)S(1)} %collective-permute-done.refs_1_, ...), custom_call_target="tpu_custom_call" | custom-call | flops 872415232 | bytes 2097152 | tf_op jit(solution)/shard_map/attend_high/pallas_call | solution.py:274
  28.8 1.3 %collective-permute-start.6 = (bf16[256,128]{1,0:T(8,128)(2,1)S(1)}, bf16[256,128]{1,0:T(8,128)(2,1)S(1)}, u32[]{:S(2)}, u32[]{:S(2)}) collective-permute-start(bf16[256,128]{1,0:T(8,128)(2,1)S(1)} %get-tuple-element.35), channel_id=1, source_target_pairs={{0,8},{8,0},{16,24},{24,16},{1,9},{9,1},{17,25},{25,17},{2,10},{10... | collective-permute-start | bytes 196616 | tf_op jit(solution)/shard_map/ppermute | solution.py:477
  30.1 0.8 collective-permute-start.7
  30.9 1.4 %collective-permute-start.8 = (bf16[256,128]{1,0:T(8,128)(2,1)S(1)}, bf16[256,128]{1,0:T(8,128)(2,1)S(1)}, u32[]{:S(2)}, u32[]{:S(2)}) collective-permute-start(bf16[256,128]{1,0:T(8,128)(2,1)S(1)} %get-tuple-element.37), channel_id=1, source_target_pairs={{0,24},{8,16},{16,8},{24,0},{1,25},{9,17},{17,9},{25,1},{2,26},{10... | collective-permute-start | bytes 196616 | tf_op jit(solution)/shard_map/ppermute | solution.py:477
  32.3 2.3 %attend_low.1 = (bf16[256,128]{1,0:T(8,128)(2,1)S(1)}, bf16[256,128]{1,0:T(8,128)(2,1)S(1)}, bf16[256,128]{1,0:T(8,128)(2,1)S(1)}, bf16[256,128]{1,0:T(8,128)(2,1)S(1)}) custom-call(s32[2]{0:T(128)S(1)} %pad_add_fusion.ids_ref, bf16[768,128]{1,0:T(8,128)(2,1)S(1)} %get-tuple-element.26.refs_0_, bf16[768,128]{1,0:T(8,128)(2,1)S(1)} %collective-permute-done.refs_1_, ...), custom_call_target="tpu_custom_call" | custom-call | flops 335544320 | bytes 1048576 | tf_op jit(solution)/shard_map/attend_low/pallas_call | solution.py:274
  34.6 1.3 %collective-permute-start.21 = (bf16[256,128]{1,0:T(8,128)(2,1)S(1)}, bf16[256,128]{1,0:T(8,128)(2,1)S(1)}, u32[]{:S(2)}, u32[]{:S(2)}) collective-permute-start(bf16[256,128]{1,0:T(8,128)(2,1)S(1)} %get-tuple-element.42), channel_id=1, source_target_pairs={{0,8},{8,0},{16,24},{24,16},{1,9},{9,1},{17,25},{25,17},{2,10},{10... | collective-permute-start | bytes 196616 | tf_op jit(solution)/shard_map/ppermute | solution.py:477
  36.0 0.8 collective-permute-start.22
  36.8 2.2 %collective-permute-done.21 = bf16[256,128]{1,0:T(8,128)(2,1)S(1)} collective-permute-done((bf16[256,128]{1,0:T(8,128)(2,1)S(1)}, bf16[256,128]{1,0:T(8,128)(2,1)S(1)}, u32[]{:S(2)}, u32[]{:S(2)}) %collective-permute-start.21) | collective-permute-done | bytes 65568 | tf_op jit(solution)/shard_map/ppermute | solution.py:477
  39.0 1.5 %collective-permute-start.23 = (bf16[256,128]{1,0:T(8,128)(2,1)S(1)}, bf16[256,128]{1,0:T(8,128)(2,1)S(1)}, u32[]{:S(2)}, u32[]{:S(2)}) collective-permute-start(bf16[256,128]{1,0:T(8,128)(2,1)S(1)} %get-tuple-element.44), channel_id=1, source_target_pairs={{0,24},{8,16},{16,8},{24,0},{1,25},{9,17},{17,9},{25,1},{2,26},{10... | collective-permute-start | bytes 196616 | tf_op jit(solution)/shard_map/ppermute | solution.py:477
  40.5 3.6 %collective-permute-done.23 = bf16[256,128]{1,0:T(8,128)(2,1)S(1)} collective-permute-done((bf16[256,128]{1,0:T(8,128)(2,1)S(1)}, bf16[256,128]{1,0:T(8,128)(2,1)S(1)}, u32[]{:S(2)}, u32[]{:S(2)}) %collective-permute-start.23) | collective-permute-done | bytes 65568 | tf_op jit(solution)/shard_map/ppermute | solution.py:477
  44.1 3.7 %collective-permute-start.29 = (bf16[1024,128]{1,0:T(8,128)(2,1)S(1)}, bf16[1024,128]{1,0:T(8,128)(2,1)S(1)}, u32[]{:S(2)}, u32[]{:S(2)}) collective-permute-start(bf16[1024,128]{1,0:T(8,128)(2,1)S(1)} %constant_dynamic-update-slice_fusion.4.refs_0_), channel_id=1, source_target_pairs={{0,6},{1,7},{2,4},{3,5},{4,2},{5,3},{6,0},{7,1},{8,14},{9,15},{10,... | collective-permute-start | bytes 786440 | tf_op jit(solution)/shard_map/ppermute | solution.py:477
  47.8 0.8 collective-permute-start.25
  48.6 0.1 collective-permute-start.24
  48.8 3.7 %collective-permute-start.14 = (bf16[1024,128]{1,0:T(8,128)(2,1)S(1)}, bf16[1024,128]{1,0:T(8,128)(2,1)S(1)}, u32[]{:S(2)}, u32[]{:S(2)}) collective-permute-start(bf16[1024,128]{1,0:T(8,128)(2,1)S(1)} %constant_dynamic-update-slice_fusion.refs_0_), channel_id=1, source_target_pairs={{0,6},{1,7},{2,4},{3,5},{4,2},{5,3},{6,0},{7,1},{8,14},{9,15},{10,... | collective-permute-start | bytes 786440 | tf_op jit(solution)/shard_map/ppermute | solution.py:477
  52.4 2.8 %collective-permute-done.29.refs_6_ = bf16[1024,128]{1,0:T(8,128)(2,1)S(1)} collective-permute-done((bf16[1024,128]{1,0:T(8,128)(2,1)S(1)}, bf16[1024,128]{1,0:T(8,128)(2,1)S(1)}, u32[]{:S(2)}, u32[]{:S(2)}) %collective-permute-start.29) | collective-permute-done | bytes 262176 | tf_op jit(solution)/shard_map/ppermute | solution.py:477
  55.2 18.2 %collective-permute-start.12 = (bf16[1024,128]{1,0:T(8,128)(2,1)S(1)}, bf16[1024,128]{1,0:T(8,128)(2,1)S(1)}, u32[]{:S(2)}, u32[]{:S(2)}) collective-permute-start(bf16[1024,128]{1,0:T(8,128)(2,1)S(1)} %constant_dynamic-update-slice_fusion.refs_0_), channel_id=1, source_target_pairs={{0,4},{1,5},{2,6},{3,7},{4,0},{5,1},{6,2},{7,3},{8,12},{9,13},{10,... | collective-permute-start | bytes 786440 | tf_op jit(solution)/shard_map/ppermute | solution.py:477
  73.4 5.7 %collective-permute-done.27.refs_4_ = bf16[1024,128]{1,0:T(8,128)(2,1)S(1)} collective-permute-done((bf16[1024,128]{1,0:T(8,128)(2,1)S(1)}, bf16[1024,128]{1,0:T(8,128)(2,1)S(1)}, u32[]{:S(2)}, u32[]{:S(2)}) %collective-permute-start.27) | collective-permute-done | bytes 262176 | tf_op jit(solution)/shard_map/ppermute | solution.py:477
  79.1 0.8 collective-permute-start.10
  79.9 0.5 collective-permute-start.28
  80.4 0.1 collective-permute-start.26
  80.5 9.0 %collective-permute-done.12.refs_4_ = bf16[1024,128]{1,0:T(8,128)(2,1)S(1)} collective-permute-done((bf16[1024,128]{1,0:T(8,128)(2,1)S(1)}, bf16[1024,128]{1,0:T(8,128)(2,1)S(1)}, u32[]{:S(2)}, u32[]{:S(2)}) %collective-permute-start.12) | collective-permute-done | bytes 262176 | tf_op jit(solution)/shard_map/ppermute | solution.py:477
  89.5 1.6 %collective-permute-done.10.refs_2_ = bf16[1024,128]{1,0:T(8,128)(2,1)S(1)} collective-permute-done((bf16[1024,128]{1,0:T(8,128)(2,1)S(1)}, bf16[1024,128]{1,0:T(8,128)(2,1)S(1)}, u32[]{:S(2)}, u32[]{:S(2)}) %collective-permute-start.10) | collective-permute-done | bytes 262176 | tf_op jit(solution)/shard_map/ppermute | solution.py:477
  91.1 0.5 collective-permute-start.11
  91.7 0.1 collective-permute-start.15
  91.8 2.6 %shard_map.138 = (f32[256,512]{1,0:T(8,128)S(1)}, bf16[256,512]{1,0:T(8,128)(2,1)}, f32[1,256]{1,0:T(1,128)S(1)}) custom-call(s32[8]{0:T(128)S(1)} %copy-done.9, s32[2]{0:T(128)S(1)} %pad_add_fusion.ids_ref, bf16[512,512]{1,0:T(8,128)(2,1)S(1)} %copy-done.5, bf16[4096,512]{1,0:T(8,128)(2,1)S(1)} %copy-done, ...), custom_call_target="tpu_custom_call" | custom-call | flops 1073741824 | bytes 6291456 | tf_op jit(solution)/shard_map/pallas_call | solution.py:327
  94.3 0.4 collective-permute-start.31
  94.8 0.8 collective-permute-done.31
  95.6 3.6 %collective-permute-done.32 = f32[1,256]{1,0:T(1,128)S(1)} collective-permute-done((f32[1,256]{1,0:T(1,128)S(1)}, f32[1,256]{1,0:T(1,128)S(1)}, u32[]{:S(2)}, u32[]{:S(2)}) %collective-permute-start.32) | collective-permute-done | bytes 1056 | tf_op jit(solution)/shard_map/ppermute | solution.py:477
  99.2 1.0 collective-permute-start.33
  100.2 3.4 %collective-permute-done.33 = f32[1,256]{1,0:T(1,128)S(1)} collective-permute-done((f32[1,256]{1,0:T(1,128)S(1)}, f32[1,256]{1,0:T(1,128)S(1)}, u32[]{:S(2)}, u32[]{:S(2)}) %collective-permute-start.33) | collective-permute-done | bytes 1056 | tf_op jit(solution)/shard_map/ppermute | solution.py:477
  103.7 0.1 shard_map.139.own_ref.low_ref
  103.8 2.7 %collective-permute-start.34 = (bf16[256,512]{1,0:T(8,128)(2,1)S(1)}, bf16[256,512]{1,0:T(8,128)(2,1)S(1)}, u32[]{:S(2)}, u32[]{:S(2)}) collective-permute-start(bf16[256,512]{1,0:T(8,128)(2,1)S(1)} %shard_map.139.own_ref.low_ref), channel_id=1, source_target_pairs={{0,8},{8,16},{16,24},{1,9},{9,17},{17,25},{2,10},{10,18},{18,26},{... | collective-permute-start | bytes 786440 | tf_op jit(solution)/shard_map/ppermute | solution.py:477
  106.5 1.6 %shard_map.136.base_ref = f32[256,512]{1,0:T(8,128)S(1)} custom-call(s32[8]{0:T(128)S(1)} %copy-done.9, s32[2]{0:T(128)S(1)} %pad_add_fusion.ids_ref, bf16[512,512]{1,0:T(8,128)(2,1)S(1)} %copy-done.5, bf16[4096,512]{1,0:T(8,128)(2,1)S(1)} %copy-done, bf16[1024,128]{1,0:T(8,128)(2,1)S(1)} %constant_dynamic-update-slice_fusion.refs_0_, ...), custom_call_target="tpu_custom_call" | custom-call | flops 805306368 | bytes 6291456 | tf_op jit(solution)/shard_map/pallas_call | solution.py:327
  108.1 0.0 copy-start.1
  108.2 0.0 copy-start.2
  108.2 0.0 copy-start.4
  108.2 1.7 %shard_map.137 = (f32[256,512]{1,0:T(8,128)S(1)}, bf16[256,512]{1,0:T(8,128)(2,1)}, f32[1,256]{1,0:T(1,128)S(1)}) custom-call(s32[8]{0:T(128)S(1)} %copy-done.9, s32[2]{0:T(128)S(1)} %pad_add_fusion.ids_ref, f32[256,512]{1,0:T(8,128)S(1)} %shard_map.136.base_ref, bf16[4096,512]{1,0:T(8,128)(2,1)S(1)} %copy-done, ...), custom_call_target="tpu_custom_call" | custom-call | flops 268435456 | bytes 6291456 | tf_op jit(solution)/shard_map/pallas_call | solution.py:327
  110.0 1.3 collective-permute-start.19
  111.3 0.1 collective-permute-start.16
  111.3 1.1 collective-permute-done.16
  112.5 0.1 collective-permute-start.17
  112.6 0.1 copy.15.len_ref
  112.8 3.3 %collective-permute-done.17 = f32[1,256]{1,0:T(1,128)S(1)} collective-permute-done((f32[1,256]{1,0:T(1,128)S(1)}, f32[1,256]{1,0:T(1,128)S(1)}, u32[]{:S(2)}, u32[]{:S(2)}) %collective-permute-start.17) | collective-permute-done | bytes 1056 | tf_op jit(solution)/shard_map/ppermute | solution.py:477
  116.1 1.0 collective-permute-start.18
  117.1 0.5 spectrum.1.spec_ref
  117.6 2.9 %collective-permute-done.18 = f32[1,256]{1,0:T(1,128)S(1)} collective-permute-done((f32[1,256]{1,0:T(1,128)S(1)}, f32[1,256]{1,0:T(1,128)S(1)}, u32[]{:S(2)}, u32[]{:S(2)}) %collective-permute-start.18) | collective-permute-done | bytes 1056 | tf_op jit(solution)/shard_map/ppermute | solution.py:477
  120.5 1.5 %collective-permute-start.20 = (f32[1,256]{1,0:T(1,128)S(1)}, f32[1,256]{1,0:T(1,128)S(1)}, u32[]{:S(2)}, u32[]{:S(2)}) collective-permute-start(f32[1,256]{1,0:T(1,128)S(1)} %add.20.sq_ref), channel_id=1, source_target_pairs={{8,0},{16,8},{24,16},{9,1},{17,9},{25,17},{10,2},{18,10},{26,18},{... | collective-permute-start | bytes 3080 | tf_op jit(solution)/shard_map/ppermute | solution.py:477
  122.0 1.2 conv_own.1.part_ref
  123.3 1.4 %conv_low.1.done_ref = bf16[256,512]{1,0:T(8,128)(2,1)S(1)} custom-call(f32[256,512]{1,0:T(8,128)S(1)} %get-tuple-element.45.res_ref, bf16[256,512]{1,0:T(8,128)(2,1)S(1)} %shard_map.139.own_ref.low_ref, bf16[256,512]{1,0:T(8,128)(2,1)S(1)} %collective-permute-done.34.before_ref, f32[512,512]{1,0:T(8,128)S(1)} %spectrum.1.spec_ref, f32[1,512]{1,0:T(1,128)S(1)} %bitcast.9, ...), custom_call_target="tpu_custom_call" | custom-call | flops 469762048 | bytes 1572864 | tf_op jit(solution)/shard_map/conv_low/pallas_call | solution.py:534
  124.7 1.9 %collective-permute-done.20.raw_sq_ref = f32[1,256]{1,0:T(1,128)S(1)} collective-permute-done((f32[1,256]{1,0:T(1,128)S(1)}, f32[1,256]{1,0:T(1,128)S(1)}, u32[]{:S(2)}, u32[]{:S(2)}) %collective-permute-start.20) | collective-permute-done | bytes 1056 | tf_op jit(solution)/shard_map/ppermute | solution.py:477
  126.6 2.5 %conv_high.1 = bf16[512,512]{1,0:T(8,128)(2,1)} custom-call(s32[8]{0:T(128)S(1)} %copy-done.9, s32[2]{0:T(128)S(1)} %pad_add_fusion.ids_ref, f32[256,512]{1,0:T(8,128)S(1)} %conv_own.1.part_ref, bf16[256,512]{1,0:T(8,128)(2,1)S(1)} %collective-permute-done.19.raw_ref, f32[1,256]{1,0:T(1,128)S(1)} %collective-permute-done.20.raw_sq_ref, ...), custom_call_target="tpu_custom_call" | custom-call | flops 335544320 | bytes 1572864 | tf_op jit(solution)/shard_map/conv_high/pallas_call | solution.py:563
  (57 shorter events, 0.2 us)
Async XLA Ops:
  0.0 91.7 %copy-start.5 = (bf16[512,512]{1,0:T(8,128)(2,1)S(1)}, bf16[512,512]{1,0:T(8,128)(2,1)}, u32[]{:S(2)}) copy-start(bf16[512,512]{1,0:T(8,128)(2,1)} %base_ref.3) | copy-start | bytes 1572868
  0.0 91.7 %copy-start = (bf16[4096,512]{1,0:T(8,128)(2,1)S(1)}, bf16[4096,512]{1,0:T(8,128)(2,1)}, u32[]{:S(2)}) copy-start(bf16[4096,512]{1,0:T(8,128)(2,1)} %w_ref.5) | copy-start | bytes 12582916
  0.1 0.8 copy-start.8
  0.9 90.9 %copy-start.9 = (s32[8]{0:T(128)S(1)}, s32[8]{0:T(128)}, u32[]{:S(2)}) copy-start(s32[8]{0:T(128)} %slots_ref.9) | copy-start | bytes 100
  3.1 8.8 %collective-permute-start = (bf16[768,128]{1,0:T(8,128)(2,1)S(1)}, bf16[768,128]{1,0:T(8,128)(2,1)S(1)}, u32[]{:S(2)}, u32[]{:S(2)}) collective-permute-start(bf16[768,128]{1,0:T(8,128)(2,1)S(1)} %get-tuple-element.27), channel_id=1, source_target_pairs={{0,8},{8,0},{16,24},{24,16},{1,9},{9,1},{17,25},{25,17},{2,10},{10... | collective-permute-start | bytes 589832 | tf_op jit(solution)/shard_map/ppermute | solution.py:477
  6.1 12.0 %collective-permute-start.1 = (bf16[768,128]{1,0:T(8,128)(2,1)S(1)}, bf16[768,128]{1,0:T(8,128)(2,1)S(1)}, u32[]{:S(2)}, u32[]{:S(2)}) collective-permute-start(bf16[768,128]{1,0:T(8,128)(2,1)S(1)} %get-tuple-element.28), channel_id=1, source_target_pairs={{0,16},{8,24},{16,0},{24,8},{1,17},{9,25},{17,1},{25,9},{2,18},{10... | collective-permute-start | bytes 589832 | tf_op jit(solution)/shard_map/ppermute | solution.py:477
  7.7 10.5 %collective-permute-start.2 = (bf16[768,128]{1,0:T(8,128)(2,1)S(1)}, bf16[768,128]{1,0:T(8,128)(2,1)S(1)}, u32[]{:S(2)}, u32[]{:S(2)}) collective-permute-start(bf16[768,128]{1,0:T(8,128)(2,1)S(1)} %get-tuple-element.29), channel_id=1, source_target_pairs={{0,24},{8,16},{16,8},{24,0},{1,25},{9,17},{17,9},{25,1},{2,26},{10... | collective-permute-start | bytes 589832 | tf_op jit(solution)/shard_map/ppermute | solution.py:477
  7.7 12.7 %collective-permute-start.3 = (bf16[768,128]{1,0:T(8,128)(2,1)S(1)}, bf16[768,128]{1,0:T(8,128)(2,1)S(1)}, u32[]{:S(2)}, u32[]{:S(2)}) collective-permute-start(bf16[768,128]{1,0:T(8,128)(2,1)S(1)} %get-tuple-element.31), channel_id=1, source_target_pairs={{0,8},{8,0},{16,24},{24,16},{1,9},{9,1},{17,25},{25,17},{2,10},{10... | collective-permute-start | bytes 589832 | tf_op jit(solution)/shard_map/ppermute | solution.py:477
  9.6 15.5 %collective-permute-start.4 = (bf16[768,128]{1,0:T(8,128)(2,1)S(1)}, bf16[768,128]{1,0:T(8,128)(2,1)S(1)}, u32[]{:S(2)}, u32[]{:S(2)}) collective-permute-start(bf16[768,128]{1,0:T(8,128)(2,1)S(1)} %get-tuple-element.32), channel_id=1, source_target_pairs={{0,16},{8,24},{16,0},{24,8},{1,17},{9,25},{17,1},{25,9},{2,18},{10... | collective-permute-start | bytes 589832 | tf_op jit(solution)/shard_map/ppermute | solution.py:477
  11.9 13.3 %collective-permute-start.5 = (bf16[768,128]{1,0:T(8,128)(2,1)S(1)}, bf16[768,128]{1,0:T(8,128)(2,1)S(1)}, u32[]{:S(2)}, u32[]{:S(2)}) collective-permute-start(bf16[768,128]{1,0:T(8,128)(2,1)S(1)} %get-tuple-element.33), channel_id=1, source_target_pairs={{0,24},{8,16},{16,8},{24,0},{1,25},{9,17},{17,9},{25,1},{2,26},{10... | collective-permute-start | bytes 589832 | tf_op jit(solution)/shard_map/ppermute | solution.py:477
  28.8 19.1 %collective-permute-start.6 = (bf16[256,128]{1,0:T(8,128)(2,1)S(1)}, bf16[256,128]{1,0:T(8,128)(2,1)S(1)}, u32[]{:S(2)}, u32[]{:S(2)}) collective-permute-start(bf16[256,128]{1,0:T(8,128)(2,1)S(1)} %get-tuple-element.35), channel_id=1, source_target_pairs={{0,8},{8,0},{16,24},{24,16},{1,9},{9,1},{17,25},{25,17},{2,10},{10... | collective-permute-start | bytes 196616 | tf_op jit(solution)/shard_map/ppermute | solution.py:477
  30.1 18.5 %collective-permute-start.7 = (bf16[256,128]{1,0:T(8,128)(2,1)S(1)}, bf16[256,128]{1,0:T(8,128)(2,1)S(1)}, u32[]{:S(2)}, u32[]{:S(2)}) collective-permute-start(bf16[256,128]{1,0:T(8,128)(2,1)S(1)} %get-tuple-element.36), channel_id=1, source_target_pairs={{0,16},{8,24},{16,0},{24,8},{1,17},{9,25},{17,1},{25,9},{2,18},{10... | collective-permute-start | bytes 196616 | tf_op jit(solution)/shard_map/ppermute | solution.py:477
  30.9 17.8 %collective-permute-start.8 = (bf16[256,128]{1,0:T(8,128)(2,1)S(1)}, bf16[256,128]{1,0:T(8,128)(2,1)S(1)}, u32[]{:S(2)}, u32[]{:S(2)}) collective-permute-start(bf16[256,128]{1,0:T(8,128)(2,1)S(1)} %get-tuple-element.37), channel_id=1, source_target_pairs={{0,24},{8,16},{16,8},{24,0},{1,25},{9,17},{17,9},{25,1},{2,26},{10... | collective-permute-start | bytes 196616 | tf_op jit(solution)/shard_map/ppermute | solution.py:477
  34.6 69.0 %copy-start.7 = (f32[512]{0:T(512)S(1)}, f32[512]{0:T(512)}, u32[]{:S(2)}) copy-start(f32[512]{0:T(512)} %param.19) | copy-start | bytes 6148
  34.6 4.3 %collective-permute-start.21 = (bf16[256,128]{1,0:T(8,128)(2,1)S(1)}, bf16[256,128]{1,0:T(8,128)(2,1)S(1)}, u32[]{:S(2)}, u32[]{:S(2)}) collective-permute-start(bf16[256,128]{1,0:T(8,128)(2,1)S(1)} %get-tuple-element.42), channel_id=1, source_target_pairs={{0,8},{8,0},{16,24},{24,16},{1,9},{9,1},{17,25},{25,17},{2,10},{10... | collective-permute-start | bytes 196616 | tf_op jit(solution)/shard_map/ppermute | solution.py:477
  36.0 4.5 %collective-permute-start.22 = (bf16[256,128]{1,0:T(8,128)(2,1)S(1)}, bf16[256,128]{1,0:T(8,128)(2,1)S(1)}, u32[]{:S(2)}, u32[]{:S(2)}) collective-permute-start(bf16[256,128]{1,0:T(8,128)(2,1)S(1)} %get-tuple-element.43), channel_id=1, source_target_pairs={{0,16},{8,24},{16,0},{24,8},{1,17},{9,25},{17,1},{25,9},{2,18},{10... | collective-permute-start | bytes 196616 | tf_op jit(solution)/shard_map/ppermute | solution.py:477
  39.0 5.2 %collective-permute-start.23 = (bf16[256,128]{1,0:T(8,128)(2,1)S(1)}, bf16[256,128]{1,0:T(8,128)(2,1)S(1)}, u32[]{:S(2)}, u32[]{:S(2)}) collective-permute-start(bf16[256,128]{1,0:T(8,128)(2,1)S(1)} %get-tuple-element.44), channel_id=1, source_target_pairs={{0,24},{8,16},{16,8},{24,0},{1,25},{9,17},{17,9},{25,1},{2,26},{10... | collective-permute-start | bytes 196616 | tf_op jit(solution)/shard_map/ppermute | solution.py:477
  44.1 11.0 %collective-permute-start.29 = (bf16[1024,128]{1,0:T(8,128)(2,1)S(1)}, bf16[1024,128]{1,0:T(8,128)(2,1)S(1)}, u32[]{:S(2)}, u32[]{:S(2)}) collective-permute-start(bf16[1024,128]{1,0:T(8,128)(2,1)S(1)} %constant_dynamic-update-slice_fusion.4.refs_0_), channel_id=1, source_target_pairs={{0,6},{1,7},{2,4},{3,5},{4,2},{5,3},{6,0},{7,1},{8,14},{9,15},{10,... | collective-permute-start | bytes 786440 | tf_op jit(solution)/shard_map/ppermute | solution.py:477
  47.8 31.3 %collective-permute-start.27 = (bf16[1024,128]{1,0:T(8,128)(2,1)S(1)}, bf16[1024,128]{1,0:T(8,128)(2,1)S(1)}, u32[]{:S(2)}, u32[]{:S(2)}) collective-permute-start(bf16[1024,128]{1,0:T(8,128)(2,1)S(1)} %constant_dynamic-update-slice_fusion.4.refs_0_), channel_id=1, source_target_pairs={{0,4},{1,5},{2,6},{3,7},{4,0},{5,1},{6,2},{7,3},{8,12},{9,13},{10,... | collective-permute-start | bytes 786440 | tf_op jit(solution)/shard_map/ppermute | solution.py:477
  47.8 32.0 %collective-permute-start.25 = (bf16[1024,128]{1,0:T(8,128)(2,1)S(1)}, bf16[1024,128]{1,0:T(8,128)(2,1)S(1)}, u32[]{:S(2)}, u32[]{:S(2)}) collective-permute-start(bf16[1024,128]{1,0:T(8,128)(2,1)S(1)} %constant_dynamic-update-slice_fusion.4.refs_0_), channel_id=1, source_target_pairs={{0,2},{1,3},{2,0},{3,1},{4,6},{5,7},{6,4},{7,5},{8,10},{9,11},{10,... | collective-permute-start | bytes 786440 | tf_op jit(solution)/shard_map/ppermute | solution.py:477
  48.6 31.3 %collective-permute-start.24 = (bf16[1024,128]{1,0:T(8,128)(2,1)S(1)}, bf16[1024,128]{1,0:T(8,128)(2,1)S(1)}, u32[]{:S(2)}, u32[]{:S(2)}) collective-permute-start(bf16[1024,128]{1,0:T(8,128)(2,1)S(1)} %constant_dynamic-update-slice_fusion.4.refs_0_), channel_id=1, source_target_pairs={{0,1},{1,0},{2,3},{3,2},{4,5},{5,4},{6,7},{7,6},{8,9},{9,8},{10,11... | collective-permute-start | bytes 786440 | tf_op jit(solution)/shard_map/ppermute | solution.py:477
  48.8 31.6 %collective-permute-start.14 = (bf16[1024,128]{1,0:T(8,128)(2,1)S(1)}, bf16[1024,128]{1,0:T(8,128)(2,1)S(1)}, u32[]{:S(2)}, u32[]{:S(2)}) collective-permute-start(bf16[1024,128]{1,0:T(8,128)(2,1)S(1)} %constant_dynamic-update-slice_fusion.refs_0_), channel_id=1, source_target_pairs={{0,6},{1,7},{2,4},{3,5},{4,2},{5,3},{6,0},{7,1},{8,14},{9,15},{10,... | collective-permute-start | bytes 786440 | tf_op jit(solution)/shard_map/ppermute | solution.py:477
  55.2 34.3 %collective-permute-start.12 = (bf16[1024,128]{1,0:T(8,128)(2,1)S(1)}, bf16[1024,128]{1,0:T(8,128)(2,1)S(1)}, u32[]{:S(2)}, u32[]{:S(2)}) collective-permute-start(bf16[1024,128]{1,0:T(8,128)(2,1)S(1)} %constant_dynamic-update-slice_fusion.refs_0_), channel_id=1, source_target_pairs={{0,4},{1,5},{2,6},{3,7},{4,0},{5,1},{6,2},{7,3},{8,12},{9,13},{10,... | collective-permute-start | bytes 786440 | tf_op jit(solution)/shard_map/ppermute | solution.py:477
  79.1 12.0 %collective-permute-start.10 = (bf16[1024,128]{1,0:T(8,128)(2,1)S(1)}, bf16[1024,128]{1,0:T(8,128)(2,1)S(1)}, u32[]{:S(2)}, u32[]{:S(2)}) collective-permute-start(bf16[1024,128]{1,0:T(8,128)(2,1)S(1)} %constant_dynamic-update-slice_fusion.refs_0_), channel_id=1, source_target_pairs={{0,2},{1,3},{2,0},{3,1},{4,6},{5,7},{6,4},{7,5},{8,10},{9,11},{10,... | collective-permute-start | bytes 786440 | tf_op jit(solution)/shard_map/ppermute | solution.py:477
  79.9 11.3 %collective-permute-start.30 = (bf16[1024,128]{1,0:T(8,128)(2,1)S(1)}, bf16[1024,128]{1,0:T(8,128)(2,1)S(1)}, u32[]{:S(2)}, u32[]{:S(2)}) collective-permute-start(bf16[1024,128]{1,0:T(8,128)(2,1)S(1)} %collective-permute-done.29.refs_6_), channel_id=1, source_target_pairs={{0,1},{1,0},{2,3},{3,2},{4,5},{5,4},{6,7},{7,6},{8,9},{9,8},{10,11... | collective-permute-start | bytes 786440 | tf_op jit(solution)/shard_map/ppermute | solution.py:477
  79.9 11.8 %collective-permute-start.28 = (bf16[1024,128]{1,0:T(8,128)(2,1)S(1)}, bf16[1024,128]{1,0:T(8,128)(2,1)S(1)}, u32[]{:S(2)}, u32[]{:S(2)}) collective-permute-start(bf16[1024,128]{1,0:T(8,128)(2,1)S(1)} %collective-permute-done.27.refs_4_), channel_id=1, source_target_pairs={{0,1},{1,0},{2,3},{3,2},{4,5},{5,4},{6,7},{7,6},{8,9},{9,8},{10,11... | collective-permute-start | bytes 786440 | tf_op jit(solution)/shard_map/ppermute | solution.py:477
  80.4 11.3 %collective-permute-start.26 = (bf16[1024,128]{1,0:T(8,128)(2,1)S(1)}, bf16[1024,128]{1,0:T(8,128)(2,1)S(1)}, u32[]{:S(2)}, u32[]{:S(2)}) collective-permute-start(bf16[1024,128]{1,0:T(8,128)(2,1)S(1)} %collective-permute-done.25.refs_2_), channel_id=1, source_target_pairs={{0,1},{1,0},{2,3},{3,2},{4,5},{5,4},{6,7},{7,6},{8,9},{9,8},{10,11... | collective-permute-start | bytes 786440 | tf_op jit(solution)/shard_map/ppermute | solution.py:477
  89.5 17.0 %collective-permute-start.9 = (bf16[1024,128]{1,0:T(8,128)(2,1)S(1)}, bf16[1024,128]{1,0:T(8,128)(2,1)S(1)}, u32[]{:S(2)}, u32[]{:S(2)}) collective-permute-start(bf16[1024,128]{1,0:T(8,128)(2,1)S(1)} %constant_dynamic-update-slice_fusion.refs_0_), channel_id=1, source_target_pairs={{0,1},{1,0},{2,3},{3,2},{4,5},{5,4},{6,7},{7,6},{8,9},{9,8},{10,11... | collective-permute-start | bytes 786440 | tf_op jit(solution)/shard_map/ppermute | solution.py:477
  91.1 15.4 %collective-permute-start.13 = (bf16[1024,128]{1,0:T(8,128)(2,1)S(1)}, bf16[1024,128]{1,0:T(8,128)(2,1)S(1)}, u32[]{:S(2)}, u32[]{:S(2)}) collective-permute-start(bf16[1024,128]{1,0:T(8,128)(2,1)S(1)} %collective-permute-done.12.refs_4_), channel_id=1, source_target_pairs={{0,1},{1,0},{2,3},{3,2},{4,5},{5,4},{6,7},{7,6},{8,9},{9,8},{10,11... | collective-permute-start | bytes 786440 | tf_op jit(solution)/shard_map/ppermute | solution.py:477
  91.1 15.4 %collective-permute-start.11 = (bf16[1024,128]{1,0:T(8,128)(2,1)S(1)}, bf16[1024,128]{1,0:T(8,128)(2,1)S(1)}, u32[]{:S(2)}, u32[]{:S(2)}) collective-permute-start(bf16[1024,128]{1,0:T(8,128)(2,1)S(1)} %collective-permute-done.10.refs_2_), channel_id=1, source_target_pairs={{0,1},{1,0},{2,3},{3,2},{4,5},{5,4},{6,7},{7,6},{8,9},{9,8},{10,11... | collective-permute-start | bytes 786440 | tf_op jit(solution)/shard_map/ppermute | solution.py:477
  91.7 16.6 %collective-permute-start.15 = (bf16[1024,128]{1,0:T(8,128)(2,1)S(1)}, bf16[1024,128]{1,0:T(8,128)(2,1)S(1)}, u32[]{:S(2)}, u32[]{:S(2)}) collective-permute-start(bf16[1024,128]{1,0:T(8,128)(2,1)S(1)} %collective-permute-done.14.refs_0_), channel_id=1, source_target_pairs={{0,1},{1,0},{2,3},{3,2},{4,5},{5,4},{6,7},{7,6},{8,9},{9,8},{10,11... | collective-permute-start | bytes 786440 | tf_op jit(solution)/shard_map/ppermute | solution.py:477
  94.3 1.3 collective-permute-start.31
  95.6 3.6 %collective-permute-start.32 = (f32[1,256]{1,0:T(1,128)S(1)}, f32[1,256]{1,0:T(1,128)S(1)}, u32[]{:S(2)}, u32[]{:S(2)}) collective-permute-start(f32[1,256]{1,0:T(1,128)S(1)} %add.21), channel_id=1, source_target_pairs={{0,2},{1,3},{2,0},{3,1},{4,6},{5,7},{6,4},{7,5},{8,10},{9,11},{10,... | collective-permute-start | bytes 3080 | tf_op jit(solution)/shard_map/ppermute | solution.py:477
  99.2 4.5 %collective-permute-start.33 = (f32[1,256]{1,0:T(1,128)S(1)}, f32[1,256]{1,0:T(1,128)S(1)}, u32[]{:S(2)}, u32[]{:S(2)}) collective-permute-start(f32[1,256]{1,0:T(1,128)S(1)} %add.22), channel_id=1, source_target_pairs={{0,4},{1,5},{2,6},{3,7},{4,0},{5,1},{6,2},{7,3},{8,12},{9,13},{10,... | collective-permute-start | bytes 3080 | tf_op jit(solution)/shard_map/ppermute | solution.py:477
  103.8 19.5 %collective-permute-start.34 = (bf16[256,512]{1,0:T(8,128)(2,1)S(1)}, bf16[256,512]{1,0:T(8,128)(2,1)S(1)}, u32[]{:S(2)}, u32[]{:S(2)}) collective-permute-start(bf16[256,512]{1,0:T(8,128)(2,1)S(1)} %shard_map.139.own_ref.low_ref), channel_id=1, source_target_pairs={{0,8},{8,16},{16,24},{1,9},{9,17},{17,25},{2,10},{10,18},{18,26},{... | collective-permute-start | bytes 786440 | tf_op jit(solution)/shard_map/ppermute | solution.py:477
  108.1 4.5 %copy-start.11 = (s32[512]{0:T(512)S(1)}, s32[512]{0:T(512)}, u32[]{:S(2)}) copy-start(s32[512]{0:T(512)} %param.21) | copy-start | bytes 6148
  108.1 8.9 %copy-start.1 = (bf16[512,256]{1,0:T(8,128)(2,1)S(1)}, bf16[512,256]{1,0:T(8,128)(2,1)}, u32[]{:S(2)}) copy-start(bf16[512,256]{1,0:T(8,128)(2,1)} %constant.17.clone.fl_ref.fl) | copy-start | bytes 786436
  108.2 8.9 %copy-start.2 = (bf16[512,256]{1,0:T(8,128)(2,1)S(1)}, bf16[512,256]{1,0:T(8,128)(2,1)}, u32[]{:S(2)}) copy-start(bf16[512,256]{1,0:T(8,128)(2,1)} %constant.16.clone.fh_ref.fh) | copy-start | bytes 786436
  108.2 8.9 %copy-start.6 = (bf16[512,256]{1,0:T(8,128)(2,1)S(1)}, bf16[512,256]{1,0:T(8,128)(2,1)}, u32[]{:S(2)}) copy-start(bf16[512,256]{1,0:T(8,128)(2,1)} %filters_ref.1) | copy-start | bytes 786436
  108.2 13.8 %copy-start.3 = (bf16[256,512]{1,0:T(8,128)(2,1)S(1)}, bf16[256,512]{1,0:T(8,128)(2,1)}, u32[]{:S(2)}) copy-start(bf16[256,512]{1,0:T(8,128)(2,1)} %constant.19.clone.gl) | copy-start | bytes 786436
  108.2 13.8 %copy-start.4 = (bf16[256,512]{1,0:T(8,128)(2,1)S(1)}, bf16[256,512]{1,0:T(8,128)(2,1)}, u32[]{:S(2)}) copy-start(bf16[256,512]{1,0:T(8,128)(2,1)} %constant.18.clone.gh) | copy-start | bytes 786436
  108.2 13.8 %copy-start.10 = (f32[512]{0:T(512)S(1)}, f32[512]{0:T(512)}, u32[]{:S(2)}) copy-start(f32[512]{0:T(512)} %param.22) | copy-start | bytes 6148
  110.0 16.7 %collective-permute-start.19 = (bf16[256,512]{1,0:T(8,128)(2,1)}, bf16[256,512]{1,0:T(8,128)(2,1)S(1)}, u32[]{:S(2)}, u32[]{:S(2)}) collective-permute-start(bf16[256,512]{1,0:T(8,128)(2,1)} %get-tuple-element.40), channel_id=1, source_target_pairs={{8,0},{16,8},{24,16},{9,1},{17,9},{25,17},{10,2},{18,10},{26,18},{... | collective-permute-start | bytes 786440 | tf_op jit(solution)/shard_map/ppermute | solution.py:477
  111.3 1.2 collective-permute-start.16
  112.5 3.6 %collective-permute-start.17 = (f32[1,256]{1,0:T(1,128)S(1)}, f32[1,256]{1,0:T(1,128)S(1)}, u32[]{:S(2)}, u32[]{:S(2)}) collective-permute-start(f32[1,256]{1,0:T(1,128)S(1)} %add.18), channel_id=1, source_target_pairs={{0,2},{1,3},{2,0},{3,1},{4,6},{5,7},{6,4},{7,5},{8,10},{9,11},{10,... | collective-permute-start | bytes 3080 | tf_op jit(solution)/shard_map/ppermute | solution.py:477
  116.1 4.5 %collective-permute-start.18 = (f32[1,256]{1,0:T(1,128)S(1)}, f32[1,256]{1,0:T(1,128)S(1)}, u32[]{:S(2)}, u32[]{:S(2)}) collective-permute-start(f32[1,256]{1,0:T(1,128)S(1)} %add.19), channel_id=1, source_target_pairs={{0,4},{1,5},{2,6},{3,7},{4,0},{5,1},{6,2},{7,3},{8,12},{9,13},{10,... | collective-permute-start | bytes 3080 | tf_op jit(solution)/shard_map/ppermute | solution.py:477
  120.5 6.1 %collective-permute-start.20 = (f32[1,256]{1,0:T(1,128)S(1)}, f32[1,256]{1,0:T(1,128)S(1)}, u32[]{:S(2)}, u32[]{:S(2)}) collective-permute-start(f32[1,256]{1,0:T(1,128)S(1)} %add.20.sq_ref), channel_id=1, source_target_pairs={{8,0},{16,8},{24,16},{9,1},{17,9},{25,17},{10,2},{18,10},{26,18},{... | collective-permute-start | bytes 3080 | tf_op jit(solution)/shard_map/ppermute | solution.py:477

commit v5 on v3

--- a/solution.py
+++ b/solution.py
@@ -288,51 +288,57 @@
     )(ids, *pieces)
 
 
-def project_kernel(n, high, indices, slots_ref, ids_ref, base_ref, w_ref, *refs):
+def project_kernel(n, indices, slots_ref, ids_ref, base_ref, w_ref, *refs):
     count = len(indices)
-    parts, outs, lhs = refs[:count], refs[count:-1], refs[-1]
+    chunks, outs, lhs = (refs[:count], refs[count : 2 * count]), refs[2 * count : -1], refs[-1]
     rank = ids_ref[0]
     me = ids_ref[1]
-    rows, width = lhs.shape
+    size, width = lhs.shape
+    rows = size // 2
     wide = width // n
-    if base_ref.shape[0] == rows:
+    if base_ref.dtype == F32:
         total = base_ref[...]
     else:
-        half = half_index(slots_ref, ids_ref, high)
-        total = base_ref[pl.ds(pl.multiple_of(half * rows, rows), rows), :].astype(F32)
-    for index, part in zip(indices, parts):
-        for k in range(n):
-            cols = pl.ds(pl.multiple_of((rank ^ k) * wide, wide), wide)
-            lhs[:, cols] = part[k * rows : (k + 1) * rows, :]
+        halves = [half_index(slots_ref, ids_ref, high) * rows for high in range(2)]
+        total = jnp.concatenate(
+            [base_ref[pl.ds(pl.multiple_of(h, rows), rows), :] for h in halves], axis=0
+        ).astype(F32)
+    for j, index in enumerate(indices):
+        for high in range(2):
+            for k in range(n):
+                cols = pl.ds(pl.multiple_of((rank ^ k) * wide, wide), wide)
+                lhs[high * rows : (high + 1) * rows, cols] = chunks[high][j][
+                    k * rows : (k + 1) * rows, :
+                ]
         depth = pl.ds(pl.multiple_of((me ^ index) * width, width), width)
         total = total + jnp.dot(lhs[...], w_ref[depth, :], preferred_element_type=F32)
     outs[0][...] = total
     if len(outs) == 1:
         return
-    outs[1][...] = total.astype(BF)
+    outs[1][...] = total[:rows].astype(BF)
+    outs[2][...] = total[rows:].astype(BF)
     squares = total * total
     lanes = squares[:, 0:HD]
     for g in range(1, squares.shape[1] // HD):
         lanes = lanes + squares[:, g * HD : (g + 1) * HD]
-    outs[2][...] = jnp.sum(lanes.T, axis=0, keepdims=True)
-
-
-def project(n, high, slots, ids, base, w_out, parts, indices, final):
-    rows = parts[0].shape[0] // n
-    width = w_out.shape[1]
-    shapes = [jax.ShapeDtypeStruct((rows, width), F32)]
+    outs[3][...] = jnp.sum(lanes.T, axis=0, keepdims=True)
+
+
+def project(n, slots, ids, base, w_out, low, high, indices, final):
+    size, width = base.shape
+    shapes = [jax.ShapeDtypeStruct((size, width), F32)]
     if final:
-        shapes.append(jax.ShapeDtypeStruct((rows, width), BF))
-        shapes.append(jax.ShapeDtypeStruct((1, rows), F32))
+        shapes += [jax.ShapeDtypeStruct((size // 2, width), BF)] * 2
+        shapes.append(jax.ShapeDtypeStruct((1, size), F32))
     return pl.pallas_call(
-        functools.partial(project_kernel, n, high, indices),
+        functools.partial(project_kernel, n, indices),
         out_shape=shapes,
-        in_specs=[sm(), sm()] + [vm()] * (2 + len(parts)),
+        in_specs=[sm(), sm()] + [vm()] * (2 + 2 * len(indices)),
         out_specs=[vm()] * len(shapes),
-        scratch_shapes=[VMEM((rows, width), BF)],
+        scratch_shapes=[VMEM((size, width), BF)],
         compiler_params=params(20),
-        cost_estimate=cost(2 * rows * width * width * len(parts), 2 * w_out.size * 1.5),
-    )(slots, ids, base, w_out, *parts)
+        cost_estimate=cost(2 * size * width * width * len(indices), 2 * w_out.size * 1.5),
+    )(slots, ids, base, w_out, *low, *high)
 
 
 def normed_rows(res, sq_row, gain, model_width):
@@ -344,21 +350,6 @@
         for g in range(width // HD)
     ]
     return jnp.concatenate(parts, axis=1)
-
-
-def norm_kernel(model_width, res_ref, sq_ref, gain_ref, out_ref):
-    out_ref[...] = normed_rows(res_ref[...], sq_ref[...], gain_ref[...], model_width)
-
-
-def norm(model_width, res, sq, gain):
-    return pl.pallas_call(
-        functools.partial(norm_kernel, model_width),
-        out_shape=jax.ShapeDtypeStruct(res.shape, BF),
-        in_specs=[vm()] * 3,
-        out_specs=vm(),
-        compiler_params=params(8),
-        cost_estimate=cost(4 * res.size, 6 * res.size),
-    )(res, sq, gain)
 
 
 def split(array):
@@ -440,41 +431,49 @@
     return two(gh, gl, y_high) + jnp.dot(gh, y_low, preferred_element_type=F32)
 
 
-def conv_low_kernel(res_ref, own_ref, before_ref, spec_ref, skip_ref, fh, fl, gh, gl, out_ref):
-    rows = res_ref.shape[0]
-    own = own_ref[...]
-    late_re, late_im = late_spectrum(own, fh[...], fl[...])
-    early = two(fh[...], fl[...], before_ref[...])
-    conv = filtered(early[:rows] + late_re, early[rows:] + late_im, gh[...], gl[...], spec_ref[...])
-    out_ref[...] = (res_ref[...] + conv + skip_ref[...] * own.astype(F32)).astype(BF)
-
-
 def conv_own_kernel(
-    model_width, res_ref, sq_ref, spec_ref, gain_ref, skip_ref, fh, fl, gh, gl, out_ref
+    model_width, res_ref, sq_ref, spec_ref, gain_ref, skip_ref, fh, fl, gh, gl, out_ref, low_ref
 ):
-    own = normed_rows(res_ref[...], sq_ref[...], gain_ref[...], model_width)
-    late_re, late_im = late_spectrum(own, fh[...], fl[...])
-    conv = filtered(late_re, late_im, gh[...], gl[...], spec_ref[...])
-    out_ref[...] = res_ref[...] + conv + skip_ref[...] * own.astype(F32)
-
-
-def conv_high_kernel(
-    n, model_width, slots_ref, ids_ref, part_ref, raw_ref, raw_sq_ref, low_ref, done_ref,
+    rows = spec_ref.shape[0] // 2
+    for high in range(2):
+        part = slice(high * rows, (high + 1) * rows)
+        res = res_ref[part, :]
+        own = normed_rows(res, sq_ref[:, part], gain_ref[...], model_width)
+        if not high:
+            low_ref[...] = own
+        late_re, late_im = late_spectrum(own, fh[...], fl[...])
+        conv = filtered(late_re, late_im, gh[...], gl[...], spec_ref[...])
+        out_ref[part, :] = res + conv + skip_ref[...] * own.astype(F32)
+
+
+def conv_last_kernel(
+    n, model_width, slots_ref, ids_ref, part_ref, low_ref, raw_low, raw_high, sq_low, sq_high,
     spec_ref, gain_ref, fh, fl, gh, gl, out_ref,
 ):
-    rows = part_ref.shape[0]
+    rows = low_ref.shape[0]
     last = ids_ref[0] == n - 1
-    raw = normed_rows(raw_ref[...].astype(F32), raw_sq_ref[...], gain_ref[...], model_width)
-    before = jnp.where(last, low_ref[...].astype(F32), raw.astype(F32)).astype(BF)
-    early = two(fh[...], fl[...], before)
-    conv = filtered(early[:rows], early[rows:], gh[...], gl[...], spec_ref[...])
-    half = half_index(slots_ref, ids_ref, 1)
-    out_ref[pl.ds(pl.multiple_of((1 - half) * rows, rows), rows), :] = done_ref[...]
-    out_ref[pl.ds(pl.multiple_of(half * rows, rows), rows), :] = (part_ref[...] + conv).astype(BF)
+    gain = gain_ref[...]
+    for high, raw_ref, sq_ref in ((0, raw_low, sq_low), (1, raw_high, sq_high)):
+        before = normed_rows(raw_ref[...].astype(F32), sq_ref[...], gain, model_width)
+        if high:
+            before = jnp.where(last, low_ref[...].astype(F32), before.astype(F32)).astype(BF)
+        early = two(fh[...], fl[...], before)
+        conv = filtered(early[:rows], early[rows:], gh[...], gl[...], spec_ref[...])
+        half = half_index(slots_ref, ids_ref, high)
+        out_ref[pl.ds(pl.multiple_of(half * rows, rows), rows), :] = (
+            part_ref[high * rows : (high + 1) * rows, :] + conv
+        ).astype(BF)
 
 
 def moved(block, axis, route):
     return lax.ppermute(block, axis, route)
+
+
+def far_piece(own, near, size):
+    inner = [(i, i ^ (size - 2)) for i in range(2, size - 2)]
+    direct = moved(own, "mp", inner)
+    ends = [(2, 0), (3, 1), (size - 4, size - 2), (size - 3, size - 1)]
+    return direct + moved(near, "mp", ends)
 
 
 def gather_mp(own, size):
@@ -482,11 +481,7 @@
     pieces = [own]
     for k in range(1, chips - 1):
         pieces.append(moved(own, "mp", xor_route(size, 2 * k)))
-    inner = [(i, i ^ (size - 2)) for i in range(2, size - 2)]
-    direct = moved(own, "mp", inner)
-    ends = [(2, 0), (3, 1), (size - 4, size - 2), (size - 3, size - 1)]
-    relayed = moved(pieces[chips - 2], "mp", ends)
-    pieces.append(direct + relayed)
+    pieces.append(far_piece(own, pieces[chips - 2], size))
     parts = []
     for piece in pieces:
         parts.append(piece)
@@ -534,50 +529,44 @@
     att_high = exchange(attend(n, 1, rows, ids, low + high))
     parts_high = gather_mp(jnp.concatenate(att_high, axis=0), mp_size)
 
-    every = tuple(range(mp_size))
-    res_low, _, sq_low = project(n, 0, slot_map, ids, incoming, w_out, parts_low, every, True)
-    norm_low = norm(model_width, res_low, total_mp(sq_low, mp_size), gain)
-    before_low = before_rows(norm_low, 1)
+    most = mp_size - 2
+    first, last = tuple(range(most)), tuple(range(most, mp_size))
+    (base,) = project(
+        n, slot_map, ids, incoming, w_out,
+        parts_low[:most], parts_high[:most], first, False,
+    )
+    res, raw_low, raw_high, squares = project(
+        n, slot_map, ids, base, w_out,
+        parts_low[most:], parts_high[most:], last, True,
+    )
+    raw_low = before_rows(raw_low, 1)
+    raw_high = before_rows(raw_high, -1)
+    squares = total_mp(squares, mp_size)
+    sq_low = before_rows(squares[:, :rows], 1)
+    sq_high = before_rows(squares[:, rows:], -1)
     transforms = forward + backward
-    done_low = pl.pallas_call(
-        conv_low_kernel,
-        out_shape=jax.ShapeDtypeStruct((rows, width), BF),
+    part, norm_low = pl.pallas_call(
+        functools.partial(conv_own_kernel, model_width),
+        out_shape=[
+            jax.ShapeDtypeStruct((2 * rows, width), F32),
+            jax.ShapeDtypeStruct((rows, width), BF),
+        ],
         in_specs=[vm()] * 9,
+        out_specs=[vm()] * 2,
+        compiler_params=params(20),
+        cost_estimate=cost(20 * rows * rows * width, 24 * rows * width),
+        name="conv_own",
+    )(res, squares, spec, gain, skip, *transforms)
+    return pl.pallas_call(
+        functools.partial(conv_last_kernel, n, model_width),
+        out_shape=jax.ShapeDtypeStruct((2 * rows, width), BF),
+        in_specs=[sm(), sm()] + [vm()] * 12,
         out_specs=vm(),
         compiler_params=params(20),
-        cost_estimate=cost(14 * rows * rows * width, 12 * rows * width),
-        name="conv_low",
-    )(res_low, norm_low, before_low, spec, skip, *transforms)
-
-    most = mp_size - 2
-    (base_high,) = project(
-        n, 1, slot_map, ids, incoming, w_out, parts_high[:most], every[:most], False
-    )
-    res_high, raw_high, sq_high = project(
-        n, 1, slot_map, ids, base_high, w_out, parts_high[most:], every[most:], True
-    )
-    raw_before = before_rows(raw_high, -1)
-    sq_high = total_mp(sq_high, mp_size)
-    sq_before = before_rows(sq_high, -1)
-    part_high = pl.pallas_call(
-        functools.partial(conv_own_kernel, model_width),
-        out_shape=jax.ShapeDtypeStruct((rows, width), F32),
-        in_specs=[vm()] * 9,
-        out_specs=vm(),
-        compiler_params=params(20),
-        cost_estimate=cost(10 * rows * rows * width, 12 * rows * width),
-        name="conv_own",
-    )(res_high, sq_high, spec, gain, skip, *transforms)
-    return pl.pallas_call(
-        functools.partial(conv_high_kernel, n, model_width),
-        out_shape=jax.ShapeDtypeStruct((2 * rows, width), BF),
-        in_specs=[sm(), sm()] + [vm()] * 11,
-        out_specs=vm(),
-        compiler_params=params(20),
-        cost_estimate=cost(10 * rows * rows * width, 12 * rows * width),
-        name="conv_high",
+        cost_estimate=cost(20 * rows * rows * width, 24 * rows * width),
+        name="conv_last",
     )(
-        slot_map, ids, part_high, raw_before, sq_before, norm_low, done_low, spec, gain, *transforms
+        slot_map, ids, part, norm_low, raw_low, raw_high, sq_low, sq_high, spec, gain, *transforms
     )
 
 

time: 130 us -> 106 us (0.82)
  waiting for transfers between devices: 64 us -> 36.6 us
  starting transfers between devices: 43.6 us -> 48.7 us
  Pallas kernels: 20.1 us -> 18.5 us
    ppermute x37 -> x35, waiting for transfers between devices: 64 us -> 36.6 us  [moved(): return lax.ppermute(block, axis, route)]
    ppermute x37 -> x35, starting transfers between devices: 43.6 us -> 48.7 us  [moved(): return lax.ppermute(block, axis, route)]
    pallas_call x6 -> x3, Pallas kernels: 9.96 us -> 7.44 us  [the longest x2 3.96 us: project(): pl.pallas_call(functools.partial(project_kernel, n, indices), out_shape=s...]
  transfers between devices with their start and end apart: 37 -> 35, of which waited for: 17 -> 13; matrix products, arithmetic and copies ran while one was open for 0% -> 0% of each run, Pallas kernels for 9% -> 11%
where the time goes in v5:
time: 106 us; the launch traced here: 105 us
  starting transfers between devices  48.7 us (46%)
  waiting for transfers between devices  36.6 us (35%)
  Pallas kernels  18.5 us (17%)
    ppermute x35, starting transfers between devices, moved(): return lax.ppermute(block, axis, route)  48.7 us
    ppermute x35, waiting for transfers between devices, moved(): return lax.ppermute(block, axis, route)  36.6 us
    pallas_call x2, Pallas kernels, attend(): pl.pallas_call(functools.partial(attend_kernel, n, high, rows), out_shape...  5.91 us
    pallas_call x2, Pallas kernels, project(): pl.pallas_call(functools.partial(project_kernel, n, indices), out_shape=s...  3.96 us
    pallas_call x1, Pallas kernels, fast_device(): pl.pallas_call(functools.partial(conv_last_kernel, n, model_width), out_s...  3.48 us
    pallas_call x1, Pallas kernels, pack(): pl.pallas_call(functools.partial(pack_kernel, n), out_shape=[piece] * (2...  2.47 us
    pallas_call x1, Pallas kernels, fast_device(): pl.pallas_call(functools.partial(conv_own_kernel, model_width), out_shape...  2.16 us
  transfers between devices with their start and end apart: 35, of which 13 were waited for; matrix products, arithmetic and copies ran while one was open for 0% of the time, Pallas kernels for 11%

profile of v5, /device:TPU:0, one launch (start us, length us, event | category | flops | bytes accessed | tf_op | source)
XLA Modules:
  0.0 105.4 jit_solution(8428619218548955880)
XLA Ops:
  0.0 0.1 pad_add_fusion.ids_ref
  0.1 0.7 copy-done.8
  0.7 2.5 %pack.1 = (bf16[768,128]{1,0:T(8,128)(2,1)S(1)}, bf16[768,128]{1,0:T(8,128)(2,1)S(1)}, bf16[768,128]{1,0:T(8,128)(2,1)S(1)}, bf16[768,128]{1,0:T(8,128)(2,1)S(1)...) custom-call(s32[8]{0:T(128)S(1)} %copy-done.8, ...), custom_call_target="tpu_custom_call" | custom-call | bytes 3145728 | tf_op jit(solution)/shard_map/pack/pallas_call | solution.py:200
  3.2 3.0 %collective-permute-start = (bf16[768,128]{1,0:T(8,128)(2,1)S(1)}, bf16[768,128]{1,0:T(8,128)(2,1)S(1)}, u32[]{:S(2)}, u32[]{:S(2)}) collective-permute-start(bf16[768,128]{1,0:T(8,128)(2,1)S(1)} %get-tuple-element.28), channel_id=1, source_target_pairs={{0,8},{8,0},{16,24},{24,16},{1,9},{9,1},{17,25},{25,17},{2,10},{10... | collective-permute-start | bytes 589832 | tf_op jit(solution)/shard_map/ppermute | solution.py:469
  6.2 1.5 %collective-permute-start.1 = (bf16[768,128]{1,0:T(8,128)(2,1)S(1)}, bf16[768,128]{1,0:T(8,128)(2,1)S(1)}, u32[]{:S(2)}, u32[]{:S(2)}) collective-permute-start(bf16[768,128]{1,0:T(8,128)(2,1)S(1)} %get-tuple-element.29), channel_id=1, source_target_pairs={{0,16},{8,24},{16,0},{24,8},{1,17},{9,25},{17,1},{25,9},{2,18},{10... | collective-permute-start | bytes 589832 | tf_op jit(solution)/shard_map/ppermute | solution.py:469
  7.8 0.0 collective-permute-start.2
  7.8 1.9 %collective-permute-start.11 = (bf16[768,128]{1,0:T(8,128)(2,1)S(1)}, bf16[768,128]{1,0:T(8,128)(2,1)S(1)}, u32[]{:S(2)}, u32[]{:S(2)}) collective-permute-start(bf16[768,128]{1,0:T(8,128)(2,1)S(1)} %get-tuple-element.36), channel_id=1, source_target_pairs={{0,8},{8,0},{16,24},{24,16},{1,9},{9,1},{17,25},{25,17},{2,10},{10... | collective-permute-start | bytes 589832 | tf_op jit(solution)/shard_map/ppermute | solution.py:469
  9.7 1.5 %collective-permute-start.12 = (bf16[768,128]{1,0:T(8,128)(2,1)S(1)}, bf16[768,128]{1,0:T(8,128)(2,1)S(1)}, u32[]{:S(2)}, u32[]{:S(2)}) collective-permute-start(bf16[768,128]{1,0:T(8,128)(2,1)S(1)} %get-tuple-element.37), channel_id=1, source_target_pairs={{0,16},{8,24},{16,0},{24,8},{1,17},{9,25},{17,1},{25,9},{2,18},{10... | collective-permute-start | bytes 589832 | tf_op jit(solution)/shard_map/ppermute | solution.py:469
  11.3 0.7 collective-permute-done.refs_1_
  12.0 3.0 %collective-permute-start.13 = (bf16[768,128]{1,0:T(8,128)(2,1)S(1)}, bf16[768,128]{1,0:T(8,128)(2,1)S(1)}, u32[]{:S(2)}, u32[]{:S(2)}) collective-permute-start(bf16[768,128]{1,0:T(8,128)(2,1)S(1)} %get-tuple-element.38), channel_id=1, source_target_pairs={{0,24},{8,16},{16,8},{24,0},{1,25},{9,17},{17,9},{25,1},{2,26},{10... | collective-permute-start | bytes 589832 | tf_op jit(solution)/shard_map/ppermute | solution.py:469
  15.0 3.3 %collective-permute-done.1.refs_2_ = bf16[768,128]{1,0:T(8,128)(2,1)S(1)} collective-permute-done((bf16[768,128]{1,0:T(8,128)(2,1)S(1)}, bf16[768,128]{1,0:T(8,128)(2,1)S(1)}, u32[]{:S(2)}, u32[]{:S(2)}) %collective-permute-start.1) | collective-permute-done | bytes 196640 | tf_op jit(solution)/shard_map/ppermute | solution.py:469
  18.2 2.3 %attend_low.1 = (bf16[256,128]{1,0:T(8,128)(2,1)S(1)}, bf16[256,128]{1,0:T(8,128)(2,1)S(1)}, bf16[256,128]{1,0:T(8,128)(2,1)S(1)}, bf16[256,128]{1,0:T(8,128)(2,1)S(1)}) custom-call(s32[2]{0:T(128)S(1)} %pad_add_fusion.ids_ref, bf16[768,128]{1,0:T(8,128)(2,1)S(1)} %get-tuple-element.27.refs_0_, bf16[768,128]{1,0:T(8,128)(2,1)S(1)} %collective-permute-done.refs_1_, ...), custom_call_target="tpu_custom_call" | custom-call | flops 335544320 | bytes 1048576 | tf_op jit(solution)/shard_map/attend_low/pallas_call | solution.py:274
  20.5 1.1 %collective-permute-start.3 = (bf16[256,128]{1,0:T(8,128)(2,1)S(1)}, bf16[256,128]{1,0:T(8,128)(2,1)S(1)}, u32[]{:S(2)}, u32[]{:S(2)}) collective-permute-start(bf16[256,128]{1,0:T(8,128)(2,1)S(1)} %get-tuple-element.32), channel_id=1, source_target_pairs={{0,8},{8,0},{16,24},{24,16},{1,9},{9,1},{17,25},{25,17},{2,10},{10... | collective-permute-start | bytes 196616 | tf_op jit(solution)/shard_map/ppermute | solution.py:469
  21.6 1.1 %collective-permute-start.4 = (bf16[256,128]{1,0:T(8,128)(2,1)S(1)}, bf16[256,128]{1,0:T(8,128)(2,1)S(1)}, u32[]{:S(2)}, u32[]{:S(2)}) collective-permute-start(bf16[256,128]{1,0:T(8,128)(2,1)S(1)} %get-tuple-element.33), channel_id=1, source_target_pairs={{0,16},{8,24},{16,0},{24,8},{1,17},{9,25},{17,1},{25,9},{2,18},{10... | collective-permute-start | bytes 196616 | tf_op jit(solution)/shard_map/ppermute | solution.py:469
  22.7 1.5 %collective-permute-start.5 = (bf16[256,128]{1,0:T(8,128)(2,1)S(1)}, bf16[256,128]{1,0:T(8,128)(2,1)S(1)}, u32[]{:S(2)}, u32[]{:S(2)}) collective-permute-start(bf16[256,128]{1,0:T(8,128)(2,1)S(1)} %get-tuple-element.34), channel_id=1, source_target_pairs={{0,24},{8,16},{16,8},{24,0},{1,25},{9,17},{17,9},{25,1},{2,26},{10... | collective-permute-start | bytes 196616 | tf_op jit(solution)/shard_map/ppermute | solution.py:469
  24.2 1.5 %collective-permute-done.12.refs_6_ = bf16[768,128]{1,0:T(8,128)(2,1)S(1)} collective-permute-done((bf16[768,128]{1,0:T(8,128)(2,1)S(1)}, bf16[768,128]{1,0:T(8,128)(2,1)S(1)}, u32[]{:S(2)}, u32[]{:S(2)}) %collective-permute-start.12) | collective-permute-done | bytes 196640 | tf_op jit(solution)/shard_map/ppermute | solution.py:469
  25.7 0.5 collective-permute-done.13.refs_7_
  26.2 3.6 %attend_high.1 = (bf16[256,128]{1,0:T(8,128)(2,1)S(1)}, bf16[256,128]{1,0:T(8,128)(2,1)S(1)}, bf16[256,128]{1,0:T(8,128)(2,1)S(1)}, bf16[256,128]{1,0:T(8,128)(2,1)S(1)}) custom-call(s32[2]{0:T(128)S(1)} %pad_add_fusion.ids_ref, bf16[768,128]{1,0:T(8,128)(2,1)S(1)} %get-tuple-element.27.refs_0_, bf16[768,128]{1,0:T(8,128)(2,1)S(1)} %collective-permute-done.refs_1_, ...), custom_call_target="tpu_custom_call" | custom-call | flops 872415232 | bytes 2097152 | tf_op jit(solution)/shard_map/attend_high/pallas_call | solution.py:274
  29.8 1.5 %collective-permute-start.14 = (bf16[256,128]{1,0:T(8,128)(2,1)S(1)}, bf16[256,128]{1,0:T(8,128)(2,1)S(1)}, u32[]{:S(2)}, u32[]{:S(2)}) collective-permute-start(bf16[256,128]{1,0:T(8,128)(2,1)S(1)} %get-tuple-element.40), channel_id=1, source_target_pairs={{0,8},{8,0},{16,24},{24,16},{1,9},{9,1},{17,25},{25,17},{2,10},{10... | collective-permute-start | bytes 196616 | tf_op jit(solution)/shard_map/ppermute | solution.py:469
  31.4 1.0 collective-permute-start.15
  32.4 1.1 %collective-permute-start.16 = (bf16[256,128]{1,0:T(8,128)(2,1)S(1)}, bf16[256,128]{1,0:T(8,128)(2,1)S(1)}, u32[]{:S(2)}, u32[]{:S(2)}) collective-permute-start(bf16[256,128]{1,0:T(8,128)(2,1)S(1)} %get-tuple-element.42), channel_id=1, source_target_pairs={{0,24},{8,16},{16,8},{24,0},{1,25},{9,17},{17,9},{25,1},{2,26},{10... | collective-permute-start | bytes 196616 | tf_op jit(solution)/shard_map/ppermute | solution.py:469
  33.5 0.1 collective-permute-start.6
  33.6 1.6 %collective-permute-start.7 = (bf16[1024,128]{1,0:T(8,128)(2,1)S(1)}, bf16[1024,128]{1,0:T(8,128)(2,1)S(1)}, u32[]{:S(2)}, u32[]{:S(2)}) collective-permute-start(bf16[1024,128]{1,0:T(8,128)(2,1)S(1)} %constant_dynamic-update-slice_fusion.refs_0_), channel_id=1, source_target_pairs={{0,2},{1,3},{2,0},{3,1},{4,6},{5,7},{6,4},{7,5},{8,10},{9,11},{10,... | collective-permute-start | bytes 786440 | tf_op jit(solution)/shard_map/ppermute | solution.py:469
  35.3 2.6 %collective-permute-start.9 = (bf16[1024,128]{1,0:T(8,128)(2,1)S(1)}, bf16[1024,128]{1,0:T(8,128)(2,1)S(1)}, u32[]{:S(2)}, u32[]{:S(2)}) collective-permute-start(bf16[1024,128]{1,0:T(8,128)(2,1)S(1)} %constant_dynamic-update-slice_fusion.refs_0_), channel_id=1, source_target_pairs={{0,4},{1,5},{2,6},{3,7},{4,0},{5,1},{6,2},{7,3},{8,12},{9,13},{10,... | collective-permute-start | bytes 786440 | tf_op jit(solution)/shard_map/ppermute | solution.py:469
  37.9 2.3 %collective-permute-start.20 = (bf16[1024,128]{1,0:T(8,128)(2,1)S(1)}, bf16[1024,128]{1,0:T(8,128)(2,1)S(1)}, u32[]{:S(2)}, u32[]{:S(2)}) collective-permute-start(bf16[1024,128]{1,0:T(8,128)(2,1)S(1)} %constant_dynamic-update-slice_fusion.4.refs_6_), channel_id=1, source_target_pairs={{0,4},{1,5},{2,6},{3,7},{4,0},{5,1},{6,2},{7,3},{8,12},{9,13},{10,... | collective-permute-start | bytes 786440 | tf_op jit(solution)/shard_map/ppermute | solution.py:469
  40.2 1.6 %collective-permute-start.18 = (bf16[1024,128]{1,0:T(8,128)(2,1)S(1)}, bf16[1024,128]{1,0:T(8,128)(2,1)S(1)}, u32[]{:S(2)}, u32[]{:S(2)}) collective-permute-start(bf16[1024,128]{1,0:T(8,128)(2,1)S(1)} %constant_dynamic-update-slice_fusion.4.refs_6_), channel_id=1, source_target_pairs={{0,2},{1,3},{2,0},{3,1},{4,6},{5,7},{6,4},{7,5},{8,10},{9,11},{10,... | collective-permute-start | bytes 786440 | tf_op jit(solution)/shard_map/ppermute | solution.py:469
  41.8 0.7 collective-permute-start.22
  42.5 5.9 %collective-permute-done.7.refs_2_ = bf16[1024,128]{1,0:T(8,128)(2,1)S(1)} collective-permute-done((bf16[1024,128]{1,0:T(8,128)(2,1)S(1)}, bf16[1024,128]{1,0:T(8,128)(2,1)S(1)}, u32[]{:S(2)}, u32[]{:S(2)}) %collective-permute-start.7) | collective-permute-done | bytes 262176 | tf_op jit(solution)/shard_map/ppermute | solution.py:469
  48.4 0.7 collective-permute-start.25
  49.0 7.7 %collective-permute-done.9.refs_4_ = bf16[1024,128]{1,0:T(8,128)(2,1)S(1)} collective-permute-done((bf16[1024,128]{1,0:T(8,128)(2,1)S(1)}, bf16[1024,128]{1,0:T(8,128)(2,1)S(1)}, u32[]{:S(2)}, u32[]{:S(2)}) %collective-permute-start.9) | collective-permute-done | bytes 262176 | tf_op jit(solution)/shard_map/ppermute | solution.py:469
  56.7 1.3 %collective-permute-start.23 = (bf16[1024,128]{1,0:T(8,128)(2,1)S(1)}, bf16[1024,128]{1,0:T(8,128)(2,1)S(1)}, u32[]{:S(2)}, u32[]{:S(2)}) collective-permute-start(bf16[1024,128]{1,0:T(8,128)(2,1)S(1)} %collective-permute-done.9.refs_4_), channel_id=1, source_target_pairs={{2,0},{3,1},{4,6},{5,7},{10,8},{11,9},{12,14},{13,15},{18,16},{19,... | collective-permute-start | bytes 786440 | tf_op jit(solution)/shard_map/ppermute | solution.py:469
  58.0 4.3 %collective-permute-done.20.refs_10_ = bf16[1024,128]{1,0:T(8,128)(2,1)S(1)} collective-permute-done((bf16[1024,128]{1,0:T(8,128)(2,1)S(1)}, bf16[1024,128]{1,0:T(8,128)(2,1)S(1)}, u32[]{:S(2)}, u32[]{:S(2)}) %collective-permute-start.20) | collective-permute-done | bytes 262176 | tf_op jit(solution)/shard_map/ppermute | solution.py:469
  62.3 1.3 %collective-permute-start.26 = (bf16[1024,128]{1,0:T(8,128)(2,1)S(1)}, bf16[1024,128]{1,0:T(8,128)(2,1)S(1)}, u32[]{:S(2)}, u32[]{:S(2)}) collective-permute-start(bf16[1024,128]{1,0:T(8,128)(2,1)S(1)} %collective-permute-done.20.refs_10_), channel_id=1, source_target_pairs={{2,0},{3,1},{4,6},{5,7},{10,8},{11,9},{12,14},{13,15},{18,16},{19,... | collective-permute-start | bytes 786440 | tf_op jit(solution)/shard_map/ppermute | solution.py:469
  63.6 0.1 collective-permute-start.17
  63.7 0.5 collective-permute-start.8
  64.2 0.1 collective-permute-start.10
  64.3 0.8 collective-permute-done.23
  65.0 5.8 %collective-permute-done.26 = bf16[1024,128]{1,0:T(8,128)(2,1)S(1)} collective-permute-done((bf16[1024,128]{1,0:T(8,128)(2,1)S(1)}, bf16[1024,128]{1,0:T(8,128)(2,1)S(1)}, u32[]{:S(2)}, u32[]{:S(2)}) %collective-permute-start.26) | collective-permute-done | bytes 262176 | tf_op jit(solution)/shard_map/ppermute | solution.py:469
  70.9 0.1 add.15.refs_0_
  70.9 0.1 add.16.refs_2_
  71.0 0.6 collective-permute-start.24
  71.6 0.1 collective-permute-start.27
  71.7 0.7 collective-permute-done.21.refs_11_
  72.4 2.5 %shard_map.136.base_ref = f32[512,512]{1,0:T(8,128)S(1)} custom-call(s32[8]{0:T(128)S(1)} %copy-done.9, s32[2]{0:T(128)S(1)} %pad_add_fusion.ids_ref, bf16[512,512]{1,0:T(8,128)(2,1)S(1)} %copy-done.5, bf16[4096,512]{1,0:T(8,128)(2,1)S(1)} %copy-done, bf16[1024,128]{1,0:T(8,128)(2,1)S(1)} %constant_dynamic-update-slice_fusion.refs_0_, ...), custom_call_target="tpu_custom_call" | custom-call | flops 1610612736 | bytes 6291456 | tf_op jit(solution)/shard_map/pallas_call | solution.py:333
  74.9 0.0 copy-start.1
  74.9 0.0 copy-start.2
  75.0 0.0 copy-start.6
  75.0 0.0 copy-start.3
  75.0 0.0 copy-start.4
  75.0 1.4 %shard_map.137 = (f32[512,512]{1,0:T(8,128)S(1)}, bf16[256,512]{1,0:T(8,128)(2,1)S(1)}, bf16[256,512]{1,0:T(8,128)(2,1)S(1)}, f32[1,512]{1,0:T(1,128)S(1)}) custom-call(s32[8]{0:T(128)S(1)} %copy-done.9, s32[2]{0:T(128)S(1)} %pad_add_fusion.ids_ref, f32[512,512]{1,0:T(8,128)S(1)} %shard_map.136.base_ref, bf16[4096,512]{1,0:T(8,128)(2,1)S(1)} %copy-done, ...), custom_call_target="tpu_custom_call" | custom-call | flops 536870912 | bytes 6291456 | tf_op jit(solution)/shard_map/pallas_call | solution.py:333
  76.5 0.2 collective-permute-start.28
  76.7 1.0 collective-permute-done.28
  77.7 3.2 %collective-permute-start.29 = (f32[1,512]{1,0:T(1,128)S(1)}, f32[1,512]{1,0:T(1,128)S(1)}, u32[]{:S(2)}, u32[]{:S(2)}) collective-permute-start(f32[1,512]{1,0:T(1,128)S(1)} %add.17), channel_id=1, source_target_pairs={{0,2},{1,3},{2,0},{3,1},{4,6},{5,7},{6,4},{7,5},{8,10},{9,11},{10,... | collective-permute-start | bytes 6152 | tf_op jit(solution)/shard_map/ppermute | solution.py:469
  80.9 0.1 copy.15.len_ref
  81.0 1.4 %collective-permute-done.29 = f32[1,512]{1,0:T(1,128)S(1)} collective-permute-done((f32[1,512]{1,0:T(1,128)S(1)}, f32[1,512]{1,0:T(1,128)S(1)}, u32[]{:S(2)}, u32[]{:S(2)}) %collective-permute-start.29) | collective-permute-done | bytes 2080 | tf_op jit(solution)/shard_map/ppermute | solution.py:469
  82.4 3.0 %collective-permute-start.30 = (f32[1,512]{1,0:T(1,128)S(1)}, f32[1,512]{1,0:T(1,128)S(1)}, u32[]{:S(2)}, u32[]{:S(2)}) collective-permute-start(f32[1,512]{1,0:T(1,128)S(1)} %add.18), channel_id=1, source_target_pairs={{0,4},{1,5},{2,6},{3,7},{4,0},{5,1},{6,2},{7,3},{8,12},{9,13},{10,... | collective-permute-start | bytes 6152 | tf_op jit(solution)/shard_map/ppermute | solution.py:469
  85.4 0.5 spectrum.1.spec_ref
  86.0 3.4 %collective-permute-start.31 = (bf16[256,512]{1,0:T(8,128)(2,1)S(1)}, bf16[256,512]{1,0:T(8,128)(2,1)S(1)}, u32[]{:S(2)}, u32[]{:S(2)}) collective-permute-start(bf16[256,512]{1,0:T(8,128)(2,1)S(1)} %get-tuple-element.47), channel_id=1, source_target_pairs={{0,8},{8,16},{16,24},{1,9},{9,17},{17,25},{2,10},{10,18},{18,26},{... | collective-permute-start | bytes 786440 | tf_op jit(solution)/shard_map/ppermute | solution.py:469
  89.4 1.3 %collective-permute-start.32 = (bf16[256,512]{1,0:T(8,128)(2,1)S(1)}, bf16[256,512]{1,0:T(8,128)(2,1)S(1)}, u32[]{:S(2)}, u32[]{:S(2)}) collective-permute-start(bf16[256,512]{1,0:T(8,128)(2,1)S(1)} %get-tuple-element.48), channel_id=1, source_target_pairs={{8,0},{16,8},{24,16},{9,1},{17,9},{25,17},{10,2},{18,10},{26,18},{... | collective-permute-start | bytes 786440 | tf_op jit(solution)/shard_map/ppermute | solution.py:469
  90.8 4.5 %collective-permute-start.33 = (f32[1,256]{1,0:T(1,128)S(1)}, f32[1,256]{1,0:T(1,128)S(1)}, u32[]{:S(2)}, u32[]{:S(2)}) collective-permute-start(f32[1,256]{1,0:T(1,128)S(1)} %get-tuple-element.50), channel_id=1, source_target_pairs={{0,8},{8,16},{16,24},{1,9},{9,17},{17,25},{2,10},{10,18},{18,26},{... | collective-permute-start | bytes 3080 | tf_op jit(solution)/shard_map/ppermute | solution.py:469
  95.3 1.5 %collective-permute-start.34 = (f32[1,256]{1,0:T(1,128)S(1)}, f32[1,256]{1,0:T(1,128)S(1)}, u32[]{:S(2)}, u32[]{:S(2)}) collective-permute-start(f32[1,256]{1,0:T(1,128)S(1)} %get-tuple-element.49), channel_id=1, source_target_pairs={{8,0},{16,8},{24,16},{9,1},{17,9},{25,17},{10,2},{18,10},{26,18},{... | collective-permute-start | bytes 3080 | tf_op jit(solution)/shard_map/ppermute | solution.py:469
  96.8 2.2 %conv_own.1 = (f32[512,512]{1,0:T(8,128)S(1)}, bf16[256,512]{1,0:T(8,128)(2,1)S(1)}) custom-call(f32[512,512]{1,0:T(8,128)S(1)} %get-tuple-element.43.res_ref, f32[1,512]{1,0:T(1,128)S(1)} %add.19.sq_ref, f32[512,512]{1,0:T(8,128)S(1)} %spectrum.1.spec_ref, f32[1,512]{1,0:T(1,128)S(1)} %bitcast.5, f32[1,512]{1,0:T(1,128)S(1)} %bitcast.7, ...), custom_call_target="tpu_custom_call" | custom-call | flops 671088640 | bytes 3145728 | tf_op jit(solution)/shard_map/conv_own/pallas_call | solution.py:548
  99.0 2.9 %collective-permute-done.34.sq_high = f32[1,256]{1,0:T(1,128)S(1)} collective-permute-done((f32[1,256]{1,0:T(1,128)S(1)}, f32[1,256]{1,0:T(1,128)S(1)}, u32[]{:S(2)}, u32[]{:S(2)}) %collective-permute-start.34) | collective-permute-done | bytes 1056 | tf_op jit(solution)/shard_map/ppermute | solution.py:469
  102.0 3.5 %conv_last.1 = bf16[512,512]{1,0:T(8,128)(2,1)} custom-call(s32[8]{0:T(128)S(1)} %copy-done.9, s32[2]{0:T(128)S(1)} %pad_add_fusion.ids_ref, f32[512,512]{1,0:T(8,128)S(1)} %get-tuple-element.45.part_ref, bf16[256,512]{1,0:T(8,128)(2,1)S(1)} %get-tuple-element.46.low_ref, bf16[256,512]{1,0:T(8,128)(2,1)S(1)} %collective-permute-done.31.raw_low, ...), custom_call_target="tpu_custom_call" | custom-call | flops 671088640 | bytes 3145728 | tf_op jit(solution)/shard_map/conv_last/pallas_call | solution.py:560
  (54 shorter events, 0.2 us)
Async XLA Ops:
  0.1 0.7 copy-start.8
  0.7 71.7 %copy-start = (bf16[4096,512]{1,0:T(8,128)(2,1)S(1)}, bf16[4096,512]{1,0:T(8,128)(2,1)}, u32[]{:S(2)}) copy-start(bf16[4096,512]{1,0:T(8,128)(2,1)} %w_ref.3) | copy-start | bytes 12582916
  0.7 71.7 %copy-start.5 = (bf16[512,512]{1,0:T(8,128)(2,1)S(1)}, bf16[512,512]{1,0:T(8,128)(2,1)}, u32[]{:S(2)}) copy-start(bf16[512,512]{1,0:T(8,128)(2,1)} %base_ref.1) | copy-start | bytes 1572868
  0.7 71.7 %copy-start.9 = (s32[8]{0:T(128)S(1)}, s32[8]{0:T(128)}, u32[]{:S(2)}) copy-start(s32[8]{0:T(128)} %slots_ref.7) | copy-start | bytes 100
  3.2 8.8 %collective-permute-start = (bf16[768,128]{1,0:T(8,128)(2,1)S(1)}, bf16[768,128]{1,0:T(8,128)(2,1)S(1)}, u32[]{:S(2)}, u32[]{:S(2)}) collective-permute-start(bf16[768,128]{1,0:T(8,128)(2,1)S(1)} %get-tuple-element.28), channel_id=1, source_target_pairs={{0,8},{8,0},{16,24},{24,16},{1,9},{9,1},{17,25},{25,17},{2,10},{10... | collective-permute-start | bytes 589832 | tf_op jit(solution)/shard_map/ppermute | solution.py:469
  6.2 12.0 %collective-permute-start.1 = (bf16[768,128]{1,0:T(8,128)(2,1)S(1)}, bf16[768,128]{1,0:T(8,128)(2,1)S(1)}, u32[]{:S(2)}, u32[]{:S(2)}) collective-permute-start(bf16[768,128]{1,0:T(8,128)(2,1)S(1)} %get-tuple-element.29), channel_id=1, source_target_pairs={{0,16},{8,24},{16,0},{24,8},{1,17},{9,25},{17,1},{25,9},{2,18},{10... | collective-permute-start | bytes 589832 | tf_op jit(solution)/shard_map/ppermute | solution.py:469
  7.8 10.5 %collective-permute-start.2 = (bf16[768,128]{1,0:T(8,128)(2,1)S(1)}, bf16[768,128]{1,0:T(8,128)(2,1)S(1)}, u32[]{:S(2)}, u32[]{:S(2)}) collective-permute-start(bf16[768,128]{1,0:T(8,128)(2,1)S(1)} %get-tuple-element.30), channel_id=1, source_target_pairs={{0,24},{8,16},{16,8},{24,0},{1,25},{9,17},{17,9},{25,1},{2,26},{10... | collective-permute-start | bytes 589832 | tf_op jit(solution)/shard_map/ppermute | solution.py:469
  7.8 14.9 %collective-permute-start.11 = (bf16[768,128]{1,0:T(8,128)(2,1)S(1)}, bf16[768,128]{1,0:T(8,128)(2,1)S(1)}, u32[]{:S(2)}, u32[]{:S(2)}) collective-permute-start(bf16[768,128]{1,0:T(8,128)(2,1)S(1)} %get-tuple-element.36), channel_id=1, source_target_pairs={{0,8},{8,0},{16,24},{24,16},{1,9},{9,1},{17,25},{25,17},{2,10},{10... | collective-permute-start | bytes 589832 | tf_op jit(solution)/shard_map/ppermute | solution.py:469
  9.7 16.0 %collective-permute-start.12 = (bf16[768,128]{1,0:T(8,128)(2,1)S(1)}, bf16[768,128]{1,0:T(8,128)(2,1)S(1)}, u32[]{:S(2)}, u32[]{:S(2)}) collective-permute-start(bf16[768,128]{1,0:T(8,128)(2,1)S(1)} %get-tuple-element.37), channel_id=1, source_target_pairs={{0,16},{8,24},{16,0},{24,8},{1,17},{9,25},{17,1},{25,9},{2,18},{10... | collective-permute-start | bytes 589832 | tf_op jit(solution)/shard_map/ppermute | solution.py:469
  12.0 14.2 %collective-permute-start.13 = (bf16[768,128]{1,0:T(8,128)(2,1)S(1)}, bf16[768,128]{1,0:T(8,128)(2,1)S(1)}, u32[]{:S(2)}, u32[]{:S(2)}) collective-permute-start(bf16[768,128]{1,0:T(8,128)(2,1)S(1)} %get-tuple-element.38), channel_id=1, source_target_pairs={{0,24},{8,16},{16,8},{24,0},{1,25},{9,17},{17,9},{25,1},{2,26},{10... | collective-permute-start | bytes 589832 | tf_op jit(solution)/shard_map/ppermute | solution.py:469
  20.5 11.8 %collective-permute-start.3 = (bf16[256,128]{1,0:T(8,128)(2,1)S(1)}, bf16[256,128]{1,0:T(8,128)(2,1)S(1)}, u32[]{:S(2)}, u32[]{:S(2)}) collective-permute-start(bf16[256,128]{1,0:T(8,128)(2,1)S(1)} %get-tuple-element.32), channel_id=1, source_target_pairs={{0,8},{8,0},{16,24},{24,16},{1,9},{9,1},{17,25},{25,17},{2,10},{10... | collective-permute-start | bytes 196616 | tf_op jit(solution)/shard_map/ppermute | solution.py:469
  21.6 11.9 %collective-permute-start.4 = (bf16[256,128]{1,0:T(8,128)(2,1)S(1)}, bf16[256,128]{1,0:T(8,128)(2,1)S(1)}, u32[]{:S(2)}, u32[]{:S(2)}) collective-permute-start(bf16[256,128]{1,0:T(8,128)(2,1)S(1)} %get-tuple-element.33), channel_id=1, source_target_pairs={{0,16},{8,24},{16,0},{24,8},{1,17},{9,25},{17,1},{25,9},{2,18},{10... | collective-permute-start | bytes 196616 | tf_op jit(solution)/shard_map/ppermute | solution.py:469
  22.7 10.8 %collective-permute-start.5 = (bf16[256,128]{1,0:T(8,128)(2,1)S(1)}, bf16[256,128]{1,0:T(8,128)(2,1)S(1)}, u32[]{:S(2)}, u32[]{:S(2)}) collective-permute-start(bf16[256,128]{1,0:T(8,128)(2,1)S(1)} %get-tuple-element.34), channel_id=1, source_target_pairs={{0,24},{8,16},{16,8},{24,0},{1,25},{9,17},{17,9},{25,1},{2,26},{10... | collective-permute-start | bytes 196616 | tf_op jit(solution)/shard_map/ppermute | solution.py:469
  29.8 5.4 %collective-permute-start.14 = (bf16[256,128]{1,0:T(8,128)(2,1)S(1)}, bf16[256,128]{1,0:T(8,128)(2,1)S(1)}, u32[]{:S(2)}, u32[]{:S(2)}) collective-permute-start(bf16[256,128]{1,0:T(8,128)(2,1)S(1)} %get-tuple-element.40), channel_id=1, source_target_pairs={{0,8},{8,0},{16,24},{24,16},{1,9},{9,1},{17,25},{25,17},{2,10},{10... | collective-permute-start | bytes 196616 | tf_op jit(solution)/shard_map/ppermute | solution.py:469
  31.4 6.5 %collective-permute-start.15 = (bf16[256,128]{1,0:T(8,128)(2,1)S(1)}, bf16[256,128]{1,0:T(8,128)(2,1)S(1)}, u32[]{:S(2)}, u32[]{:S(2)}) collective-permute-start(bf16[256,128]{1,0:T(8,128)(2,1)S(1)} %get-tuple-element.41), channel_id=1, source_target_pairs={{0,16},{8,24},{16,0},{24,8},{1,17},{9,25},{17,1},{25,9},{2,18},{10... | collective-permute-start | bytes 196616 | tf_op jit(solution)/shard_map/ppermute | solution.py:469
  32.4 5.5 %collective-permute-start.16 = (bf16[256,128]{1,0:T(8,128)(2,1)S(1)}, bf16[256,128]{1,0:T(8,128)(2,1)S(1)}, u32[]{:S(2)}, u32[]{:S(2)}) collective-permute-start(bf16[256,128]{1,0:T(8,128)(2,1)S(1)} %get-tuple-element.42), channel_id=1, source_target_pairs={{0,24},{8,16},{16,8},{24,0},{1,25},{9,17},{17,9},{25,1},{2,26},{10... | collective-permute-start | bytes 196616 | tf_op jit(solution)/shard_map/ppermute | solution.py:469
  33.5 8.3 %collective-permute-start.6 = (bf16[1024,128]{1,0:T(8,128)(2,1)S(1)}, bf16[1024,128]{1,0:T(8,128)(2,1)S(1)}, u32[]{:S(2)}, u32[]{:S(2)}) collective-permute-start(bf16[1024,128]{1,0:T(8,128)(2,1)S(1)} %constant_dynamic-update-slice_fusion.refs_0_), channel_id=1, source_target_pairs={{0,1},{1,0},{2,3},{3,2},{4,5},{5,4},{6,7},{7,6},{8,9},{9,8},{10,11... | collective-permute-start | bytes 786440 | tf_op jit(solution)/shard_map/ppermute | solution.py:469
  33.6 14.7 %collective-permute-start.7 = (bf16[1024,128]{1,0:T(8,128)(2,1)S(1)}, bf16[1024,128]{1,0:T(8,128)(2,1)S(1)}, u32[]{:S(2)}, u32[]{:S(2)}) collective-permute-start(bf16[1024,128]{1,0:T(8,128)(2,1)S(1)} %constant_dynamic-update-slice_fusion.refs_0_), channel_id=1, source_target_pairs={{0,2},{1,3},{2,0},{3,1},{4,6},{5,7},{6,4},{7,5},{8,10},{9,11},{10,... | collective-permute-start | bytes 786440 | tf_op jit(solution)/shard_map/ppermute | solution.py:469
  35.3 21.5 %collective-permute-start.9 = (bf16[1024,128]{1,0:T(8,128)(2,1)S(1)}, bf16[1024,128]{1,0:T(8,128)(2,1)S(1)}, u32[]{:S(2)}, u32[]{:S(2)}) collective-permute-start(bf16[1024,128]{1,0:T(8,128)(2,1)S(1)} %constant_dynamic-update-slice_fusion.refs_0_), channel_id=1, source_target_pairs={{0,4},{1,5},{2,6},{3,7},{4,0},{5,1},{6,2},{7,3},{8,12},{9,13},{10,... | collective-permute-start | bytes 786440 | tf_op jit(solution)/shard_map/ppermute | solution.py:469
  37.9 24.4 %collective-permute-start.20 = (bf16[1024,128]{1,0:T(8,128)(2,1)S(1)}, bf16[1024,128]{1,0:T(8,128)(2,1)S(1)}, u32[]{:S(2)}, u32[]{:S(2)}) collective-permute-start(bf16[1024,128]{1,0:T(8,128)(2,1)S(1)} %constant_dynamic-update-slice_fusion.4.refs_6_), channel_id=1, source_target_pairs={{0,4},{1,5},{2,6},{3,7},{4,0},{5,1},{6,2},{7,3},{8,12},{9,13},{10,... | collective-permute-start | bytes 786440 | tf_op jit(solution)/shard_map/ppermute | solution.py:469
  40.2 23.3 %collective-permute-start.18 = (bf16[1024,128]{1,0:T(8,128)(2,1)S(1)}, bf16[1024,128]{1,0:T(8,128)(2,1)S(1)}, u32[]{:S(2)}, u32[]{:S(2)}) collective-permute-start(bf16[1024,128]{1,0:T(8,128)(2,1)S(1)} %constant_dynamic-update-slice_fusion.4.refs_6_), channel_id=1, source_target_pairs={{0,2},{1,3},{2,0},{3,1},{4,6},{5,7},{6,4},{7,5},{8,10},{9,11},{10,... | collective-permute-start | bytes 786440 | tf_op jit(solution)/shard_map/ppermute | solution.py:469
  41.8 21.8 %collective-permute-start.22 = (bf16[1024,128]{1,0:T(8,128)(2,1)S(1)}, bf16[1024,128]{1,0:T(8,128)(2,1)S(1)}, u32[]{:S(2)}, u32[]{:S(2)}) collective-permute-start(bf16[1024,128]{1,0:T(8,128)(2,1)S(1)} %constant_dynamic-update-slice_fusion.refs_0_), channel_id=1, source_target_pairs={{2,4},{3,5},{4,2},{5,3},{10,12},{11,13},{12,10},{13,11},{18,20},{1... | collective-permute-start | bytes 786440 | tf_op jit(solution)/shard_map/ppermute | solution.py:469
  48.4 15.8 %collective-permute-start.25 = (bf16[1024,128]{1,0:T(8,128)(2,1)S(1)}, bf16[1024,128]{1,0:T(8,128)(2,1)S(1)}, u32[]{:S(2)}, u32[]{:S(2)}) collective-permute-start(bf16[1024,128]{1,0:T(8,128)(2,1)S(1)} %constant_dynamic-update-slice_fusion.4.refs_6_), channel_id=1, source_target_pairs={{2,4},{3,5},{4,2},{5,3},{10,12},{11,13},{12,10},{13,11},{18,20},{1... | collective-permute-start | bytes 786440 | tf_op jit(solution)/shard_map/ppermute | solution.py:469
  56.7 8.3 %collective-permute-start.23 = (bf16[1024,128]{1,0:T(8,128)(2,1)S(1)}, bf16[1024,128]{1,0:T(8,128)(2,1)S(1)}, u32[]{:S(2)}, u32[]{:S(2)}) collective-permute-start(bf16[1024,128]{1,0:T(8,128)(2,1)S(1)} %collective-permute-done.9.refs_4_), channel_id=1, source_target_pairs={{2,0},{3,1},{4,6},{5,7},{10,8},{11,9},{12,14},{13,15},{18,16},{19,... | collective-permute-start | bytes 786440 | tf_op jit(solution)/shard_map/ppermute | solution.py:469
  62.3 8.6 %collective-permute-start.26 = (bf16[1024,128]{1,0:T(8,128)(2,1)S(1)}, bf16[1024,128]{1,0:T(8,128)(2,1)S(1)}, u32[]{:S(2)}, u32[]{:S(2)}) collective-permute-start(bf16[1024,128]{1,0:T(8,128)(2,1)S(1)} %collective-permute-done.20.refs_10_), channel_id=1, source_target_pairs={{2,0},{3,1},{4,6},{5,7},{10,8},{11,9},{12,14},{13,15},{18,16},{19,... | collective-permute-start | bytes 786440 | tf_op jit(solution)/shard_map/ppermute | solution.py:469
  63.6 7.4 %collective-permute-start.17 = (bf16[1024,128]{1,0:T(8,128)(2,1)S(1)}, bf16[1024,128]{1,0:T(8,128)(2,1)S(1)}, u32[]{:S(2)}, u32[]{:S(2)}) collective-permute-start(bf16[1024,128]{1,0:T(8,128)(2,1)S(1)} %constant_dynamic-update-slice_fusion.4.refs_6_), channel_id=1, source_target_pairs={{0,1},{1,0},{2,3},{3,2},{4,5},{5,4},{6,7},{7,6},{8,9},{9,8},{10,11... | collective-permute-start | bytes 786440 | tf_op jit(solution)/shard_map/ppermute | solution.py:469
  63.7 7.9 %collective-permute-start.8 = (bf16[1024,128]{1,0:T(8,128)(2,1)S(1)}, bf16[1024,128]{1,0:T(8,128)(2,1)S(1)}, u32[]{:S(2)}, u32[]{:S(2)}) collective-permute-start(bf16[1024,128]{1,0:T(8,128)(2,1)S(1)} %collective-permute-done.7.refs_2_), channel_id=1, source_target_pairs={{0,1},{1,0},{2,3},{3,2},{4,5},{5,4},{6,7},{7,6},{8,9},{9,8},{10,11... | collective-permute-start | bytes 786440 | tf_op jit(solution)/shard_map/ppermute | solution.py:469
  64.2 7.5 %collective-permute-start.10 = (bf16[1024,128]{1,0:T(8,128)(2,1)S(1)}, bf16[1024,128]{1,0:T(8,128)(2,1)S(1)}, u32[]{:S(2)}, u32[]{:S(2)}) collective-permute-start(bf16[1024,128]{1,0:T(8,128)(2,1)S(1)} %collective-permute-done.9.refs_4_), channel_id=1, source_target_pairs={{0,1},{1,0},{2,3},{3,2},{4,5},{5,4},{6,7},{7,6},{8,9},{9,8},{10,11... | collective-permute-start | bytes 786440 | tf_op jit(solution)/shard_map/ppermute | solution.py:469
  65.0 6.7 %collective-permute-start.19 = (bf16[1024,128]{1,0:T(8,128)(2,1)S(1)}, bf16[1024,128]{1,0:T(8,128)(2,1)S(1)}, u32[]{:S(2)}, u32[]{:S(2)}) collective-permute-start(bf16[1024,128]{1,0:T(8,128)(2,1)S(1)} %collective-permute-done.18.refs_8_), channel_id=1, source_target_pairs={{0,1},{1,0},{2,3},{3,2},{4,5},{5,4},{6,7},{7,6},{8,9},{9,8},{10,11... | collective-permute-start | bytes 786440 | tf_op jit(solution)/shard_map/ppermute | solution.py:469
  70.9 1.5 %collective-permute-start.21 = (bf16[1024,128]{1,0:T(8,128)(2,1)S(1)}, bf16[1024,128]{1,0:T(8,128)(2,1)S(1)}, u32[]{:S(2)}, u32[]{:S(2)}) collective-permute-start(bf16[1024,128]{1,0:T(8,128)(2,1)S(1)} %collective-permute-done.20.refs_10_), channel_id=1, source_target_pairs={{0,1},{1,0},{2,3},{3,2},{4,5},{5,4},{6,7},{7,6},{8,9},{9,8},{10,11... | collective-permute-start | bytes 786440 | tf_op jit(solution)/shard_map/ppermute | solution.py:469
  71.0 4.0 %collective-permute-start.24 = (bf16[1024,128]{1,0:T(8,128)(2,1)S(1)}, bf16[1024,128]{1,0:T(8,128)(2,1)S(1)}, u32[]{:S(2)}, u32[]{:S(2)}) collective-permute-start(bf16[1024,128]{1,0:T(8,128)(2,1)S(1)} %add.15.refs_0_), channel_id=1, source_target_pairs={{0,1},{1,0},{2,3},{3,2},{4,5},{5,4},{6,7},{7,6},{8,9},{9,8},{10,11... | collective-permute-start | bytes 786440 | tf_op jit(solution)/shard_map/ppermute | solution.py:469
  71.6 3.4 %collective-permute-start.27 = (bf16[1024,128]{1,0:T(8,128)(2,1)S(1)}, bf16[1024,128]{1,0:T(8,128)(2,1)S(1)}, u32[]{:S(2)}, u32[]{:S(2)}) collective-permute-start(bf16[1024,128]{1,0:T(8,128)(2,1)S(1)} %add.16.refs_2_), channel_id=1, source_target_pairs={{0,1},{1,0},{2,3},{3,2},{4,5},{5,4},{6,7},{7,6},{8,9},{9,8},{10,11... | collective-permute-start | bytes 786440 | tf_op jit(solution)/shard_map/ppermute | solution.py:469
  74.9 6.0 %copy-start.11 = (s32[512]{0:T(512)S(1)}, s32[512]{0:T(512)}, u32[]{:S(2)}) copy-start(s32[512]{0:T(512)} %param.21) | copy-start | bytes 6148
  74.9 10.5 %copy-start.1 = (bf16[512,256]{1,0:T(8,128)(2,1)S(1)}, bf16[512,256]{1,0:T(8,128)(2,1)}, u32[]{:S(2)}) copy-start(bf16[512,256]{1,0:T(8,128)(2,1)} %constant.16.clone.fh_ref.fh) | copy-start | bytes 786436
  74.9 10.5 %copy-start.2 = (bf16[512,256]{1,0:T(8,128)(2,1)S(1)}, bf16[512,256]{1,0:T(8,128)(2,1)}, u32[]{:S(2)}) copy-start(bf16[512,256]{1,0:T(8,128)(2,1)} %constant.17.clone.fl_ref.fl) | copy-start | bytes 786436
  75.0 10.5 %copy-start.6 = (bf16[512,256]{1,0:T(8,128)(2,1)S(1)}, bf16[512,256]{1,0:T(8,128)(2,1)}, u32[]{:S(2)}) copy-start(bf16[512,256]{1,0:T(8,128)(2,1)} %filters_ref.1) | copy-start | bytes 786436
  75.0 21.8 %copy-start.3 = (bf16[256,512]{1,0:T(8,128)(2,1)S(1)}, bf16[256,512]{1,0:T(8,128)(2,1)}, u32[]{:S(2)}) copy-start(bf16[256,512]{1,0:T(8,128)(2,1)} %constant.18.clone.gh) | copy-start | bytes 786436
  75.0 21.8 %copy-start.4 = (bf16[256,512]{1,0:T(8,128)(2,1)S(1)}, bf16[256,512]{1,0:T(8,128)(2,1)}, u32[]{:S(2)}) copy-start(bf16[256,512]{1,0:T(8,128)(2,1)} %constant.19.clone.gl) | copy-start | bytes 786436
  75.0 21.8 %copy-start.7 = (f32[512]{0:T(512)S(1)}, f32[512]{0:T(512)}, u32[]{:S(2)}) copy-start(f32[512]{0:T(512)} %param.19) | copy-start | bytes 6148
  75.0 21.8 %copy-start.10 = (f32[512]{0:T(512)S(1)}, f32[512]{0:T(512)}, u32[]{:S(2)}) copy-start(f32[512]{0:T(512)} %param.22) | copy-start | bytes 6148
  76.5 1.2 %collective-permute-start.28 = (f32[1,512]{1,0:T(1,128)S(1)}, f32[1,512]{1,0:T(1,128)S(1)}, u32[]{:S(2)}, u32[]{:S(2)}) collective-permute-start(f32[1,512]{1,0:T(1,128)S(1)} %get-tuple-element.44), channel_id=1, source_target_pairs={{0,1},{1,0},{2,3},{3,2},{4,5},{5,4},{6,7},{7,6},{8,9},{9,8},{10,11... | collective-permute-start | bytes 6152 | tf_op jit(solution)/shard_map/ppermute | solution.py:469
  77.7 4.7 %collective-permute-start.29 = (f32[1,512]{1,0:T(1,128)S(1)}, f32[1,512]{1,0:T(1,128)S(1)}, u32[]{:S(2)}, u32[]{:S(2)}) collective-permute-start(f32[1,512]{1,0:T(1,128)S(1)} %add.17), channel_id=1, source_target_pairs={{0,2},{1,3},{2,0},{3,1},{4,6},{5,7},{6,4},{7,5},{8,10},{9,11},{10,... | collective-permute-start | bytes 6152 | tf_op jit(solution)/shard_map/ppermute | solution.py:469
  82.4 8.3 %collective-permute-start.30 = (f32[1,512]{1,0:T(1,128)S(1)}, f32[1,512]{1,0:T(1,128)S(1)}, u32[]{:S(2)}, u32[]{:S(2)}) collective-permute-start(f32[1,512]{1,0:T(1,128)S(1)} %add.18), channel_id=1, source_target_pairs={{0,4},{1,5},{2,6},{3,7},{4,0},{5,1},{6,2},{7,3},{8,12},{9,13},{10,... | collective-permute-start | bytes 6152 | tf_op jit(solution)/shard_map/ppermute | solution.py:469
  86.0 16.0 %collective-permute-start.31 = (bf16[256,512]{1,0:T(8,128)(2,1)S(1)}, bf16[256,512]{1,0:T(8,128)(2,1)S(1)}, u32[]{:S(2)}, u32[]{:S(2)}) collective-permute-start(bf16[256,512]{1,0:T(8,128)(2,1)S(1)} %get-tuple-element.47), channel_id=1, source_target_pairs={{0,8},{8,16},{16,24},{1,9},{9,17},{17,25},{2,10},{10,18},{18,26},{... | collective-permute-start | bytes 786440 | tf_op jit(solution)/shard_map/ppermute | solution.py:469
  89.4 12.5 %collective-permute-start.32 = (bf16[256,512]{1,0:T(8,128)(2,1)S(1)}, bf16[256,512]{1,0:T(8,128)(2,1)S(1)}, u32[]{:S(2)}, u32[]{:S(2)}) collective-permute-start(bf16[256,512]{1,0:T(8,128)(2,1)S(1)} %get-tuple-element.48), channel_id=1, source_target_pairs={{8,0},{16,8},{24,16},{9,1},{17,9},{25,17},{10,2},{18,10},{26,18},{... | collective-permute-start | bytes 786440 | tf_op jit(solution)/shard_map/ppermute | solution.py:469
  90.8 8.2 %collective-permute-start.33 = (f32[1,256]{1,0:T(1,128)S(1)}, f32[1,256]{1,0:T(1,128)S(1)}, u32[]{:S(2)}, u32[]{:S(2)}) collective-permute-start(f32[1,256]{1,0:T(1,128)S(1)} %get-tuple-element.50), channel_id=1, source_target_pairs={{0,8},{8,16},{16,24},{1,9},{9,17},{17,25},{2,10},{10,18},{18,26},{... | collective-permute-start | bytes 3080 | tf_op jit(solution)/shard_map/ppermute | solution.py:469
  95.3 6.6 %collective-permute-start.34 = (f32[1,256]{1,0:T(1,128)S(1)}, f32[1,256]{1,0:T(1,128)S(1)}, u32[]{:S(2)}, u32[]{:S(2)}) collective-permute-start(f32[1,256]{1,0:T(1,128)S(1)} %get-tuple-element.49), channel_id=1, source_target_pairs={{8,0},{16,8},{24,16},{9,1},{17,9},{25,17},{10,2},{18,10},{26,18},{... | collective-permute-start | bytes 3080 | tf_op jit(solution)/shard_map/ppermute | solution.py:469

commit v6 on v3

--- a/solution.py
+++ b/solution.py
@@ -477,16 +477,21 @@
     return lax.ppermute(block, axis, route)
 
 
-def gather_mp(own, size):
-    chips = size // 2
-    pieces = [own]
-    for k in range(1, chips - 1):
-        pieces.append(moved(own, "mp", xor_route(size, 2 * k)))
+def relayed_piece(own, near, size):
     inner = [(i, i ^ (size - 2)) for i in range(2, size - 2)]
     direct = moved(own, "mp", inner)
     ends = [(2, 0), (3, 1), (size - 4, size - 2), (size - 3, size - 1)]
-    relayed = moved(pieces[chips - 2], "mp", ends)
-    pieces.append(direct + relayed)
+    return direct + moved(near, "mp", ends)
+
+
+def gather_mp(own, size, relay):
+    chips = size // 2
+    pieces = [own]
+    for k in range(1, chips):
+        if relay and k == chips - 1:
+            pieces.append(relayed_piece(own, pieces[k - 1], size))
+        else:
+            pieces.append(moved(own, "mp", xor_route(size, 2 * k)))
     parts = []
     for piece in pieces:
         parts.append(piece)
@@ -530,9 +535,9 @@
     spec = spectrum(filters, filter_len, forward)
 
     att_low = exchange(attend(n, 0, rows, ids, low))
-    parts_low = gather_mp(jnp.concatenate(att_low, axis=0), mp_size)
+    parts_low = gather_mp(jnp.concatenate(att_low, axis=0), mp_size, True)
     att_high = exchange(attend(n, 1, rows, ids, low + high))
-    parts_high = gather_mp(jnp.concatenate(att_high, axis=0), mp_size)
+    parts_high = gather_mp(jnp.concatenate(att_high, axis=0), mp_size, False)
 
     every = tuple(range(mp_size))
     res_low, _, sq_low = project(n, 0, slot_map, ids, incoming, w_out, parts_low, every, True)

time: 130 us -> 123 us (0.946)
  waiting for transfers between devices: 64 us -> 50 us
  starting transfers between devices: 43.6 us -> 51.2 us
    ppermute x37 -> x36, waiting for transfers between devices: 64 us -> 50 us  [moved(): return lax.ppermute(block, axis, route)]
    ppermute x37 -> x36, starting transfers between devices: 43.6 us -> 51.2 us  [moved(): return lax.ppermute(block, axis, route)]
  transfers between devices with their start and end apart: 37 -> 36, of which waited for: 17 -> 16; matrix products, arithmetic and copies ran while one was open for 0% -> 0% of each run, Pallas kernels for 9% -> 9%
where the time goes in v6:
time: 123 us
  starting transfers between devices  51.2 us (42%)
  waiting for transfers between devices  50 us (41%)
  Pallas kernels  19.8 us (16%)
    ppermute x36, starting transfers between devices, moved(): return lax.ppermute(block, axis, route)  51.2 us
    ppermute x36, waiting for transfers between devices, moved(): return lax.ppermute(block, axis, route)  50 us
    pallas_call x2, Pallas kernels, attend(): pl.pallas_call(functools.partial(attend_kernel, n, high, rows), out_shape...  5.9 us
    pallas_call x3, Pallas kernels, project(): pl.pallas_call(functools.partial(project_kernel, n, high, indices), out_s...  5.9 us
    pallas_call x1, Pallas kernels, fast_device(): pl.pallas_call(functools.partial(conv_high_kernel, n, model_width), out_s...  2.53 us
  transfers between devices with their start and end apart: 36, of which 16 were waited for; matrix products, arithmetic and copies ran while one was open for 0% of the time, Pallas kernels for 9%

profile of v6, /device:TPU:0, one launch (start us, length us, event | category | flops | bytes accessed | tf_op | source)
XLA Modules:
  0.0 122.7 jit_solution(3564410722071224211)
XLA Ops:
  0.0 0.1 pad_add_fusion.ids_ref
  0.1 0.8 copy-done.8
  0.9 2.2 %pack.1 = (bf16[768,128]{1,0:T(8,128)(2,1)S(1)}, bf16[768,128]{1,0:T(8,128)(2,1)S(1)}, bf16[768,128]{1,0:T(8,128)(2,1)S(1)}, bf16[768,128]{1,0:T(8,128)(2,1)S(1)...) custom-call(s32[8]{0:T(128)S(1)} %copy-done.8, ...), custom_call_target="tpu_custom_call" | custom-call | bytes 3145728 | tf_op jit(solution)/shard_map/pack/pallas_call | solution.py:200
  3.1 3.0 %collective-permute-start = (bf16[768,128]{1,0:T(8,128)(2,1)S(1)}, bf16[768,128]{1,0:T(8,128)(2,1)S(1)}, u32[]{:S(2)}, u32[]{:S(2)}) collective-permute-start(bf16[768,128]{1,0:T(8,128)(2,1)S(1)} %get-tuple-element.27), channel_id=1, source_target_pairs={{0,8},{8,0},{16,24},{24,16},{1,9},{9,1},{17,25},{25,17},{2,10},{10... | collective-permute-start | bytes 589832 | tf_op jit(solution)/shard_map/ppermute | solution.py:477
  6.1 1.5 %collective-permute-start.1 = (bf16[768,128]{1,0:T(8,128)(2,1)S(1)}, bf16[768,128]{1,0:T(8,128)(2,1)S(1)}, u32[]{:S(2)}, u32[]{:S(2)}) collective-permute-start(bf16[768,128]{1,0:T(8,128)(2,1)S(1)} %get-tuple-element.28), channel_id=1, source_target_pairs={{0,16},{8,24},{16,0},{24,8},{1,17},{9,25},{17,1},{25,9},{2,18},{10... | collective-permute-start | bytes 589832 | tf_op jit(solution)/shard_map/ppermute | solution.py:477
  7.7 0.0 collective-permute-start.2
  7.7 1.9 %collective-permute-start.3 = (bf16[768,128]{1,0:T(8,128)(2,1)S(1)}, bf16[768,128]{1,0:T(8,128)(2,1)S(1)}, u32[]{:S(2)}, u32[]{:S(2)}) collective-permute-start(bf16[768,128]{1,0:T(8,128)(2,1)S(1)} %get-tuple-element.31), channel_id=1, source_target_pairs={{0,8},{8,0},{16,24},{24,16},{1,9},{9,1},{17,25},{25,17},{2,10},{10... | collective-permute-start | bytes 589832 | tf_op jit(solution)/shard_map/ppermute | solution.py:477
  9.6 1.5 %collective-permute-start.4 = (bf16[768,128]{1,0:T(8,128)(2,1)S(1)}, bf16[768,128]{1,0:T(8,128)(2,1)S(1)}, u32[]{:S(2)}, u32[]{:S(2)}) collective-permute-start(bf16[768,128]{1,0:T(8,128)(2,1)S(1)} %get-tuple-element.32), channel_id=1, source_target_pairs={{0,16},{8,24},{16,0},{24,8},{1,17},{9,25},{17,1},{25,9},{2,18},{10... | collective-permute-start | bytes 589832 | tf_op jit(solution)/shard_map/ppermute | solution.py:477
  11.2 0.7 collective-permute-done.refs_1_
  11.9 3.0 %collective-permute-start.5 = (bf16[768,128]{1,0:T(8,128)(2,1)S(1)}, bf16[768,128]{1,0:T(8,128)(2,1)S(1)}, u32[]{:S(2)}, u32[]{:S(2)}) collective-permute-start(bf16[768,128]{1,0:T(8,128)(2,1)S(1)} %get-tuple-element.33), channel_id=1, source_target_pairs={{0,24},{8,16},{16,8},{24,0},{1,25},{9,17},{17,9},{25,1},{2,26},{10... | collective-permute-start | bytes 589832 | tf_op jit(solution)/shard_map/ppermute | solution.py:477
  14.9 3.3 %collective-permute-done.1.refs_2_ = bf16[768,128]{1,0:T(8,128)(2,1)S(1)} collective-permute-done((bf16[768,128]{1,0:T(8,128)(2,1)S(1)}, bf16[768,128]{1,0:T(8,128)(2,1)S(1)}, u32[]{:S(2)}, u32[]{:S(2)}) %collective-permute-start.1) | collective-permute-done | bytes 196640 | tf_op jit(solution)/shard_map/ppermute | solution.py:477
  18.1 2.2 %collective-permute-done.3.refs_5_ = bf16[768,128]{1,0:T(8,128)(2,1)S(1)} collective-permute-done((bf16[768,128]{1,0:T(8,128)(2,1)S(1)}, bf16[768,128]{1,0:T(8,128)(2,1)S(1)}, u32[]{:S(2)}, u32[]{:S(2)}) %collective-permute-start.3) | collective-permute-done | bytes 196640 | tf_op jit(solution)/shard_map/ppermute | solution.py:477
  20.4 4.8 %collective-permute-done.4.refs_6_ = bf16[768,128]{1,0:T(8,128)(2,1)S(1)} collective-permute-done((bf16[768,128]{1,0:T(8,128)(2,1)S(1)}, bf16[768,128]{1,0:T(8,128)(2,1)S(1)}, u32[]{:S(2)}, u32[]{:S(2)}) %collective-permute-start.4) | collective-permute-done | bytes 196640 | tf_op jit(solution)/shard_map/ppermute | solution.py:477
  25.1 3.6 %attend_high.1 = (bf16[256,128]{1,0:T(8,128)(2,1)S(1)}, bf16[256,128]{1,0:T(8,128)(2,1)S(1)}, bf16[256,128]{1,0:T(8,128)(2,1)S(1)}, bf16[256,128]{1,0:T(8,128)(2,1)S(1)}) custom-call(s32[2]{0:T(128)S(1)} %pad_add_fusion.ids_ref, bf16[768,128]{1,0:T(8,128)(2,1)S(1)} %get-tuple-element.26.refs_0_, bf16[768,128]{1,0:T(8,128)(2,1)S(1)} %collective-permute-done.refs_1_, ...), custom_call_target="tpu_custom_call" | custom-call | flops 872415232 | bytes 2097152 | tf_op jit(solution)/shard_map/attend_high/pallas_call | solution.py:274
  28.8 1.3 %collective-permute-start.6 = (bf16[256,128]{1,0:T(8,128)(2,1)S(1)}, bf16[256,128]{1,0:T(8,128)(2,1)S(1)}, u32[]{:S(2)}, u32[]{:S(2)}) collective-permute-start(bf16[256,128]{1,0:T(8,128)(2,1)S(1)} %get-tuple-element.35), channel_id=1, source_target_pairs={{0,8},{8,0},{16,24},{24,16},{1,9},{9,1},{17,25},{25,17},{2,10},{10... | collective-permute-start | bytes 196616 | tf_op jit(solution)/shard_map/ppermute | solution.py:477
  30.1 0.8 collective-permute-start.7
  30.9 1.4 %collective-permute-start.8 = (bf16[256,128]{1,0:T(8,128)(2,1)S(1)}, bf16[256,128]{1,0:T(8,128)(2,1)S(1)}, u32[]{:S(2)}, u32[]{:S(2)}) collective-permute-start(bf16[256,128]{1,0:T(8,128)(2,1)S(1)} %get-tuple-element.37), channel_id=1, source_target_pairs={{0,24},{8,16},{16,8},{24,0},{1,25},{9,17},{17,9},{25,1},{2,26},{10... | collective-permute-start | bytes 196616 | tf_op jit(solution)/shard_map/ppermute | solution.py:477
  32.3 2.3 %attend_low.1 = (bf16[256,128]{1,0:T(8,128)(2,1)S(1)}, bf16[256,128]{1,0:T(8,128)(2,1)S(1)}, bf16[256,128]{1,0:T(8,128)(2,1)S(1)}, bf16[256,128]{1,0:T(8,128)(2,1)S(1)}) custom-call(s32[2]{0:T(128)S(1)} %pad_add_fusion.ids_ref, bf16[768,128]{1,0:T(8,128)(2,1)S(1)} %get-tuple-element.26.refs_0_, bf16[768,128]{1,0:T(8,128)(2,1)S(1)} %collective-permute-done.refs_1_, ...), custom_call_target="tpu_custom_call" | custom-call | flops 335544320 | bytes 1048576 | tf_op jit(solution)/shard_map/attend_low/pallas_call | solution.py:274
  34.6 1.3 %collective-permute-start.21 = (bf16[256,128]{1,0:T(8,128)(2,1)S(1)}, bf16[256,128]{1,0:T(8,128)(2,1)S(1)}, u32[]{:S(2)}, u32[]{:S(2)}) collective-permute-start(bf16[256,128]{1,0:T(8,128)(2,1)S(1)} %get-tuple-element.42), channel_id=1, source_target_pairs={{0,8},{8,0},{16,24},{24,16},{1,9},{9,1},{17,25},{25,17},{2,10},{10... | collective-permute-start | bytes 196616 | tf_op jit(solution)/shard_map/ppermute | solution.py:477
  36.0 0.8 collective-permute-start.22
  36.8 2.2 %collective-permute-done.21 = bf16[256,128]{1,0:T(8,128)(2,1)S(1)} collective-permute-done((bf16[256,128]{1,0:T(8,128)(2,1)S(1)}, bf16[256,128]{1,0:T(8,128)(2,1)S(1)}, u32[]{:S(2)}, u32[]{:S(2)}) %collective-permute-start.21) | collective-permute-done | bytes 65568 | tf_op jit(solution)/shard_map/ppermute | solution.py:477
  39.0 1.5 %collective-permute-start.23 = (bf16[256,128]{1,0:T(8,128)(2,1)S(1)}, bf16[256,128]{1,0:T(8,128)(2,1)S(1)}, u32[]{:S(2)}, u32[]{:S(2)}) collective-permute-start(bf16[256,128]{1,0:T(8,128)(2,1)S(1)} %get-tuple-element.44), channel_id=1, source_target_pairs={{0,24},{8,16},{16,8},{24,0},{1,25},{9,17},{17,9},{25,1},{2,26},{10... | collective-permute-start | bytes 196616 | tf_op jit(solution)/shard_map/ppermute | solution.py:477
  40.5 3.6 %collective-permute-done.23 = bf16[256,128]{1,0:T(8,128)(2,1)S(1)} collective-permute-done((bf16[256,128]{1,0:T(8,128)(2,1)S(1)}, bf16[256,128]{1,0:T(8,128)(2,1)S(1)}, u32[]{:S(2)}, u32[]{:S(2)}) %collective-permute-start.23) | collective-permute-done | bytes 65568 | tf_op jit(solution)/shard_map/ppermute | solution.py:477
  44.1 2.7 %collective-permute-start.27 = (bf16[1024,128]{1,0:T(8,128)(2,1)S(1)}, bf16[1024,128]{1,0:T(8,128)(2,1)S(1)}, u32[]{:S(2)}, u32[]{:S(2)}) collective-permute-start(bf16[1024,128]{1,0:T(8,128)(2,1)S(1)} %constant_dynamic-update-slice_fusion.4.refs_0_), channel_id=1, source_target_pairs={{0,4},{1,5},{2,6},{3,7},{4,0},{5,1},{6,2},{7,3},{8,12},{9,13},{10,... | collective-permute-start | bytes 786440 | tf_op jit(solution)/shard_map/ppermute | solution.py:477
  46.8 0.7 collective-permute-start.29
  47.5 2.9 %collective-permute-start.25 = (bf16[1024,128]{1,0:T(8,128)(2,1)S(1)}, bf16[1024,128]{1,0:T(8,128)(2,1)S(1)}, u32[]{:S(2)}, u32[]{:S(2)}) collective-permute-start(bf16[1024,128]{1,0:T(8,128)(2,1)S(1)} %constant_dynamic-update-slice_fusion.4.refs_0_), channel_id=1, source_target_pairs={{0,2},{1,3},{2,0},{3,1},{4,6},{5,7},{6,4},{7,5},{8,10},{9,11},{10,... | collective-permute-start | bytes 786440 | tf_op jit(solution)/shard_map/ppermute | solution.py:477
  50.4 0.1 collective-permute-start.24
  50.5 6.6 %collective-permute-done.27.refs_4_ = bf16[1024,128]{1,0:T(8,128)(2,1)S(1)} collective-permute-done((bf16[1024,128]{1,0:T(8,128)(2,1)S(1)}, bf16[1024,128]{1,0:T(8,128)(2,1)S(1)}, u32[]{:S(2)}, u32[]{:S(2)}) %collective-permute-start.27) | collective-permute-done | bytes 262176 | tf_op jit(solution)/shard_map/ppermute | solution.py:477
  57.1 1.3 %collective-permute-start.30 = (bf16[1024,128]{1,0:T(8,128)(2,1)S(1)}, bf16[1024,128]{1,0:T(8,128)(2,1)S(1)}, u32[]{:S(2)}, u32[]{:S(2)}) collective-permute-start(bf16[1024,128]{1,0:T(8,128)(2,1)S(1)} %collective-permute-done.27.refs_4_), channel_id=1, source_target_pairs={{2,0},{3,1},{4,6},{5,7},{10,8},{11,9},{12,14},{13,15},{18,16},{19,... | collective-permute-start | bytes 786440 | tf_op jit(solution)/shard_map/ppermute | solution.py:477
  58.4 3.6 %collective-permute-start.14 = (bf16[1024,128]{1,0:T(8,128)(2,1)S(1)}, bf16[1024,128]{1,0:T(8,128)(2,1)S(1)}, u32[]{:S(2)}, u32[]{:S(2)}) collective-permute-start(bf16[1024,128]{1,0:T(8,128)(2,1)S(1)} %constant_dynamic-update-slice_fusion.refs_0_), channel_id=1, source_target_pairs={{0,6},{1,7},{2,4},{3,5},{4,2},{5,3},{6,0},{7,1},{8,14},{9,15},{10,... | collective-permute-start | bytes 786440 | tf_op jit(solution)/shard_map/ppermute | solution.py:477
  62.0 11.5 %collective-permute-start.12 = (bf16[1024,128]{1,0:T(8,128)(2,1)S(1)}, bf16[1024,128]{1,0:T(8,128)(2,1)S(1)}, u32[]{:S(2)}, u32[]{:S(2)}) collective-permute-start(bf16[1024,128]{1,0:T(8,128)(2,1)S(1)} %constant_dynamic-update-slice_fusion.refs_0_), channel_id=1, source_target_pairs={{0,4},{1,5},{2,6},{3,7},{4,0},{5,1},{6,2},{7,3},{8,12},{9,13},{10,... | collective-permute-start | bytes 786440 | tf_op jit(solution)/shard_map/ppermute | solution.py:477
  73.5 0.1 collective-permute-start.28
  73.6 0.5 collective-permute-start.26
  74.1 0.1 add.24.refs_6_
  74.2 0.2 collective-permute-start.31
  74.3 9.4 %collective-permute-done.12.refs_4_ = bf16[1024,128]{1,0:T(8,128)(2,1)S(1)} collective-permute-done((bf16[1024,128]{1,0:T(8,128)(2,1)S(1)}, bf16[1024,128]{1,0:T(8,128)(2,1)S(1)}, u32[]{:S(2)}, u32[]{:S(2)}) %collective-permute-start.12) | collective-permute-done | bytes 262176 | tf_op jit(solution)/shard_map/ppermute | solution.py:477
  83.8 0.9 collective-permute-done.10.refs_2_
  84.7 0.5 collective-permute-start.11
  85.2 0.1 collective-permute-start.15
  85.3 2.6 %shard_map.138 = (f32[256,512]{1,0:T(8,128)S(1)}, bf16[256,512]{1,0:T(8,128)(2,1)}, f32[1,256]{1,0:T(1,128)S(1)}) custom-call(s32[8]{0:T(128)S(1)} %copy-done.9, s32[2]{0:T(128)S(1)} %pad_add_fusion.ids_ref, bf16[512,512]{1,0:T(8,128)(2,1)S(1)} %copy-done.5, bf16[4096,512]{1,0:T(8,128)(2,1)S(1)} %copy-done, ...), custom_call_target="tpu_custom_call" | custom-call | flops 1073741824 | bytes 6291456 | tf_op jit(solution)/shard_map/pallas_call | solution.py:327
  87.9 0.4 collective-permute-start.32
  88.4 0.8 collective-permute-done.32
  89.2 3.6 %collective-permute-done.33 = f32[1,256]{1,0:T(1,128)S(1)} collective-permute-done((f32[1,256]{1,0:T(1,128)S(1)}, f32[1,256]{1,0:T(1,128)S(1)}, u32[]{:S(2)}, u32[]{:S(2)}) %collective-permute-start.33) | collective-permute-done | bytes 1056 | tf_op jit(solution)/shard_map/ppermute | solution.py:477
  92.8 1.3 %collective-permute-start.34 = (f32[1,256]{1,0:T(1,128)S(1)}, f32[1,256]{1,0:T(1,128)S(1)}, u32[]{:S(2)}, u32[]{:S(2)}) collective-permute-start(f32[1,256]{1,0:T(1,128)S(1)} %add.26), channel_id=1, source_target_pairs={{0,4},{1,5},{2,6},{3,7},{4,0},{5,1},{6,2},{7,3},{8,12},{9,13},{10,... | collective-permute-start | bytes 3080 | tf_op jit(solution)/shard_map/ppermute | solution.py:477
  94.1 3.1 %collective-permute-done.34 = f32[1,256]{1,0:T(1,128)S(1)} collective-permute-done((f32[1,256]{1,0:T(1,128)S(1)}, f32[1,256]{1,0:T(1,128)S(1)}, u32[]{:S(2)}, u32[]{:S(2)}) %collective-permute-start.34) | collective-permute-done | bytes 1056 | tf_op jit(solution)/shard_map/ppermute | solution.py:477
  97.2 0.1 shard_map.139.own_ref.low_ref
  97.4 2.7 %collective-permute-start.35 = (bf16[256,512]{1,0:T(8,128)(2,1)S(1)}, bf16[256,512]{1,0:T(8,128)(2,1)S(1)}, u32[]{:S(2)}, u32[]{:S(2)}) collective-permute-start(bf16[256,512]{1,0:T(8,128)(2,1)S(1)} %shard_map.139.own_ref.low_ref), channel_id=1, source_target_pairs={{0,8},{8,16},{16,24},{1,9},{9,17},{17,25},{2,10},{10,18},{18,26},{... | collective-permute-start | bytes 786440 | tf_op jit(solution)/shard_map/ppermute | solution.py:477
  100.1 1.6 %shard_map.136.base_ref = f32[256,512]{1,0:T(8,128)S(1)} custom-call(s32[8]{0:T(128)S(1)} %copy-done.9, s32[2]{0:T(128)S(1)} %pad_add_fusion.ids_ref, bf16[512,512]{1,0:T(8,128)(2,1)S(1)} %copy-done.5, bf16[4096,512]{1,0:T(8,128)(2,1)S(1)} %copy-done, bf16[1024,128]{1,0:T(8,128)(2,1)S(1)} %constant_dynamic-update-slice_fusion.refs_0_, ...), custom_call_target="tpu_custom_call" | custom-call | flops 805306368 | bytes 6291456 | tf_op jit(solution)/shard_map/pallas_call | solution.py:327
  101.7 0.0 copy-start.1
  101.8 1.7 %shard_map.137 = (f32[256,512]{1,0:T(8,128)S(1)}, bf16[256,512]{1,0:T(8,128)(2,1)}, f32[1,256]{1,0:T(1,128)S(1)}) custom-call(s32[8]{0:T(128)S(1)} %copy-done.9, s32[2]{0:T(128)S(1)} %pad_add_fusion.ids_ref, f32[256,512]{1,0:T(8,128)S(1)} %shard_map.136.base_ref, bf16[4096,512]{1,0:T(8,128)(2,1)S(1)} %copy-done, ...), custom_call_target="tpu_custom_call" | custom-call | flops 268435456 | bytes 6291456 | tf_op jit(solution)/shard_map/pallas_call | solution.py:327
  103.5 1.3 %collective-permute-start.19 = (bf16[256,512]{1,0:T(8,128)(2,1)}, bf16[256,512]{1,0:T(8,128)(2,1)S(1)}, u32[]{:S(2)}, u32[]{:S(2)}) collective-permute-start(bf16[256,512]{1,0:T(8,128)(2,1)} %get-tuple-element.40), channel_id=1, source_target_pairs={{8,0},{16,8},{24,16},{9,1},{17,9},{25,17},{10,2},{18,10},{26,18},{... | collective-permute-start | bytes 786440 | tf_op jit(solution)/shard_map/ppermute | solution.py:477
  104.8 0.1 collective-permute-start.16
  104.9 1.1 collective-permute-done.16
  106.0 0.5 collective-permute-start.17
  106.5 0.1 copy.15.len_ref
  106.7 3.0 %collective-permute-done.17 = f32[1,256]{1,0:T(1,128)S(1)} collective-permute-done((f32[1,256]{1,0:T(1,128)S(1)}, f32[1,256]{1,0:T(1,128)S(1)}, u32[]{:S(2)}, u32[]{:S(2)}) %collective-permute-start.17) | collective-permute-done | bytes 1056 | tf_op jit(solution)/shard_map/ppermute | solution.py:477
  109.6 1.4 %collective-permute-start.18 = (f32[1,256]{1,0:T(1,128)S(1)}, f32[1,256]{1,0:T(1,128)S(1)}, u32[]{:S(2)}, u32[]{:S(2)}) collective-permute-start(f32[1,256]{1,0:T(1,128)S(1)} %add.22), channel_id=1, source_target_pairs={{0,4},{1,5},{2,6},{3,7},{4,0},{5,1},{6,2},{7,3},{8,12},{9,13},{10,... | collective-permute-start | bytes 3080 | tf_op jit(solution)/shard_map/ppermute | solution.py:477
  111.0 0.5 spectrum.1.spec_ref
  111.5 2.6 %collective-permute-done.18 = f32[1,256]{1,0:T(1,128)S(1)} collective-permute-done((f32[1,256]{1,0:T(1,128)S(1)}, f32[1,256]{1,0:T(1,128)S(1)}, u32[]{:S(2)}, u32[]{:S(2)}) %collective-permute-start.18) | collective-permute-done | bytes 1056 | tf_op jit(solution)/shard_map/ppermute | solution.py:477
  114.1 1.5 %collective-permute-start.20 = (f32[1,256]{1,0:T(1,128)S(1)}, f32[1,256]{1,0:T(1,128)S(1)}, u32[]{:S(2)}, u32[]{:S(2)}) collective-permute-start(f32[1,256]{1,0:T(1,128)S(1)} %add.23.sq_ref), channel_id=1, source_target_pairs={{8,0},{16,8},{24,16},{9,1},{17,9},{25,17},{10,2},{18,10},{26,18},{... | collective-permute-start | bytes 3080 | tf_op jit(solution)/shard_map/ppermute | solution.py:477
  115.6 1.2 conv_own.1.part_ref
  116.8 1.4 %conv_low.1.done_ref = bf16[256,512]{1,0:T(8,128)(2,1)S(1)} custom-call(f32[256,512]{1,0:T(8,128)S(1)} %get-tuple-element.45.res_ref, bf16[256,512]{1,0:T(8,128)(2,1)S(1)} %shard_map.139.own_ref.low_ref, bf16[256,512]{1,0:T(8,128)(2,1)S(1)} %collective-permute-done.35.before_ref, f32[512,512]{1,0:T(8,128)S(1)} %spectrum.1.spec_ref, f32[1,512]{1,0:T(1,128)S(1)} %bitcast.9, ...), custom_call_target="tpu_custom_call" | custom-call | flops 469762048 | bytes 1572864 | tf_op jit(solution)/shard_map/conv_low/pallas_call | solution.py:547
  118.3 1.9 %collective-permute-done.20.raw_sq_ref = f32[1,256]{1,0:T(1,128)S(1)} collective-permute-done((f32[1,256]{1,0:T(1,128)S(1)}, f32[1,256]{1,0:T(1,128)S(1)}, u32[]{:S(2)}, u32[]{:S(2)}) %collective-permute-start.20) | collective-permute-done | bytes 1056 | tf_op jit(solution)/shard_map/ppermute | solution.py:477
  120.2 2.5 %conv_high.1 = bf16[512,512]{1,0:T(8,128)(2,1)} custom-call(s32[8]{0:T(128)S(1)} %copy-done.9, s32[2]{0:T(128)S(1)} %pad_add_fusion.ids_ref, f32[256,512]{1,0:T(8,128)S(1)} %conv_own.1.part_ref, bf16[256,512]{1,0:T(8,128)(2,1)S(1)} %collective-permute-done.19.raw_ref, f32[1,256]{1,0:T(1,128)S(1)} %collective-permute-done.20.raw_sq_ref, ...), custom_call_target="tpu_custom_call" | custom-call | flops 335544320 | bytes 1572864 | tf_op jit(solution)/shard_map/conv_high/pallas_call | solution.py:576
  (60 shorter events, 0.2 us)
Async XLA Ops:
  0.0 85.3 %copy-start.5 = (bf16[512,512]{1,0:T(8,128)(2,1)S(1)}, bf16[512,512]{1,0:T(8,128)(2,1)}, u32[]{:S(2)}) copy-start(bf16[512,512]{1,0:T(8,128)(2,1)} %base_ref.3) | copy-start | bytes 1572868
  0.0 85.3 %copy-start = (bf16[4096,512]{1,0:T(8,128)(2,1)S(1)}, bf16[4096,512]{1,0:T(8,128)(2,1)}, u32[]{:S(2)}) copy-start(bf16[4096,512]{1,0:T(8,128)(2,1)} %w_ref.5) | copy-start | bytes 12582916
  0.1 0.8 copy-start.8
  0.9 84.4 %copy-start.9 = (s32[8]{0:T(128)S(1)}, s32[8]{0:T(128)}, u32[]{:S(2)}) copy-start(s32[8]{0:T(128)} %slots_ref.9) | copy-start | bytes 100
  3.1 8.8 %collective-permute-start = (bf16[768,128]{1,0:T(8,128)(2,1)S(1)}, bf16[768,128]{1,0:T(8,128)(2,1)S(1)}, u32[]{:S(2)}, u32[]{:S(2)}) collective-permute-start(bf16[768,128]{1,0:T(8,128)(2,1)S(1)} %get-tuple-element.27), channel_id=1, source_target_pairs={{0,8},{8,0},{16,24},{24,16},{1,9},{9,1},{17,25},{25,17},{2,10},{10... | collective-permute-start | bytes 589832 | tf_op jit(solution)/shard_map/ppermute | solution.py:477
  6.1 12.0 %collective-permute-start.1 = (bf16[768,128]{1,0:T(8,128)(2,1)S(1)}, bf16[768,128]{1,0:T(8,128)(2,1)S(1)}, u32[]{:S(2)}, u32[]{:S(2)}) collective-permute-start(bf16[768,128]{1,0:T(8,128)(2,1)S(1)} %get-tuple-element.28), channel_id=1, source_target_pairs={{0,16},{8,24},{16,0},{24,8},{1,17},{9,25},{17,1},{25,9},{2,18},{10... | collective-permute-start | bytes 589832 | tf_op jit(solution)/shard_map/ppermute | solution.py:477
  7.7 10.5 %collective-permute-start.2 = (bf16[768,128]{1,0:T(8,128)(2,1)S(1)}, bf16[768,128]{1,0:T(8,128)(2,1)S(1)}, u32[]{:S(2)}, u32[]{:S(2)}) collective-permute-start(bf16[768,128]{1,0:T(8,128)(2,1)S(1)} %get-tuple-element.29), channel_id=1, source_target_pairs={{0,24},{8,16},{16,8},{24,0},{1,25},{9,17},{17,9},{25,1},{2,26},{10... | collective-permute-start | bytes 589832 | tf_op jit(solution)/shard_map/ppermute | solution.py:477
  7.7 12.7 %collective-permute-start.3 = (bf16[768,128]{1,0:T(8,128)(2,1)S(1)}, bf16[768,128]{1,0:T(8,128)(2,1)S(1)}, u32[]{:S(2)}, u32[]{:S(2)}) collective-permute-start(bf16[768,128]{1,0:T(8,128)(2,1)S(1)} %get-tuple-element.31), channel_id=1, source_target_pairs={{0,8},{8,0},{16,24},{24,16},{1,9},{9,1},{17,25},{25,17},{2,10},{10... | collective-permute-start | bytes 589832 | tf_op jit(solution)/shard_map/ppermute | solution.py:477
  9.6 15.5 %collective-permute-start.4 = (bf16[768,128]{1,0:T(8,128)(2,1)S(1)}, bf16[768,128]{1,0:T(8,128)(2,1)S(1)}, u32[]{:S(2)}, u32[]{:S(2)}) collective-permute-start(bf16[768,128]{1,0:T(8,128)(2,1)S(1)} %get-tuple-element.32), channel_id=1, source_target_pairs={{0,16},{8,24},{16,0},{24,8},{1,17},{9,25},{17,1},{25,9},{2,18},{10... | collective-permute-start | bytes 589832 | tf_op jit(solution)/shard_map/ppermute | solution.py:477
  11.9 13.3 %collective-permute-start.5 = (bf16[768,128]{1,0:T(8,128)(2,1)S(1)}, bf16[768,128]{1,0:T(8,128)(2,1)S(1)}, u32[]{:S(2)}, u32[]{:S(2)}) collective-permute-start(bf16[768,128]{1,0:T(8,128)(2,1)S(1)} %get-tuple-element.33), channel_id=1, source_target_pairs={{0,24},{8,16},{16,8},{24,0},{1,25},{9,17},{17,9},{25,1},{2,26},{10... | collective-permute-start | bytes 589832 | tf_op jit(solution)/shard_map/ppermute | solution.py:477
  28.8 18.7 %collective-permute-start.6 = (bf16[256,128]{1,0:T(8,128)(2,1)S(1)}, bf16[256,128]{1,0:T(8,128)(2,1)S(1)}, u32[]{:S(2)}, u32[]{:S(2)}) collective-permute-start(bf16[256,128]{1,0:T(8,128)(2,1)S(1)} %get-tuple-element.35), channel_id=1, source_target_pairs={{0,8},{8,0},{16,24},{24,16},{1,9},{9,1},{17,25},{25,17},{2,10},{10... | collective-permute-start | bytes 196616 | tf_op jit(solution)/shard_map/ppermute | solution.py:477
  30.1 20.3 %collective-permute-start.7 = (bf16[256,128]{1,0:T(8,128)(2,1)S(1)}, bf16[256,128]{1,0:T(8,128)(2,1)S(1)}, u32[]{:S(2)}, u32[]{:S(2)}) collective-permute-start(bf16[256,128]{1,0:T(8,128)(2,1)S(1)} %get-tuple-element.36), channel_id=1, source_target_pairs={{0,16},{8,24},{16,0},{24,8},{1,17},{9,25},{17,1},{25,9},{2,18},{10... | collective-permute-start | bytes 196616 | tf_op jit(solution)/shard_map/ppermute | solution.py:477
  30.9 27.5 %collective-permute-start.8 = (bf16[256,128]{1,0:T(8,128)(2,1)S(1)}, bf16[256,128]{1,0:T(8,128)(2,1)S(1)}, u32[]{:S(2)}, u32[]{:S(2)}) collective-permute-start(bf16[256,128]{1,0:T(8,128)(2,1)S(1)} %get-tuple-element.37), channel_id=1, source_target_pairs={{0,24},{8,16},{16,8},{24,0},{1,25},{9,17},{17,9},{25,1},{2,26},{10... | collective-permute-start | bytes 196616 | tf_op jit(solution)/shard_map/ppermute | solution.py:477
  34.6 4.3 %collective-permute-start.21 = (bf16[256,128]{1,0:T(8,128)(2,1)S(1)}, bf16[256,128]{1,0:T(8,128)(2,1)S(1)}, u32[]{:S(2)}, u32[]{:S(2)}) collective-permute-start(bf16[256,128]{1,0:T(8,128)(2,1)S(1)} %get-tuple-element.42), channel_id=1, source_target_pairs={{0,8},{8,0},{16,24},{24,16},{1,9},{9,1},{17,25},{25,17},{2,10},{10... | collective-permute-start | bytes 196616 | tf_op jit(solution)/shard_map/ppermute | solution.py:477
  36.0 4.5 %collective-permute-start.22 = (bf16[256,128]{1,0:T(8,128)(2,1)S(1)}, bf16[256,128]{1,0:T(8,128)(2,1)S(1)}, u32[]{:S(2)}, u32[]{:S(2)}) collective-permute-start(bf16[256,128]{1,0:T(8,128)(2,1)S(1)} %get-tuple-element.43), channel_id=1, source_target_pairs={{0,16},{8,24},{16,0},{24,8},{1,17},{9,25},{17,1},{25,9},{2,18},{10... | collective-permute-start | bytes 196616 | tf_op jit(solution)/shard_map/ppermute | solution.py:477
  39.0 5.2 %collective-permute-start.23 = (bf16[256,128]{1,0:T(8,128)(2,1)S(1)}, bf16[256,128]{1,0:T(8,128)(2,1)S(1)}, u32[]{:S(2)}, u32[]{:S(2)}) collective-permute-start(bf16[256,128]{1,0:T(8,128)(2,1)S(1)} %get-tuple-element.44), channel_id=1, source_target_pairs={{0,24},{8,16},{16,8},{24,0},{1,25},{9,17},{17,9},{25,1},{2,26},{10... | collective-permute-start | bytes 196616 | tf_op jit(solution)/shard_map/ppermute | solution.py:477
  40.5 56.8 %copy-start.7 = (f32[512]{0:T(512)S(1)}, f32[512]{0:T(512)}, u32[]{:S(2)}) copy-start(f32[512]{0:T(512)} %param.19) | copy-start | bytes 6148
  44.1 13.0 %collective-permute-start.27 = (bf16[1024,128]{1,0:T(8,128)(2,1)S(1)}, bf16[1024,128]{1,0:T(8,128)(2,1)S(1)}, u32[]{:S(2)}, u32[]{:S(2)}) collective-permute-start(bf16[1024,128]{1,0:T(8,128)(2,1)S(1)} %constant_dynamic-update-slice_fusion.4.refs_0_), channel_id=1, source_target_pairs={{0,4},{1,5},{2,6},{3,7},{4,0},{5,1},{6,2},{7,3},{8,12},{9,13},{10,... | collective-permute-start | bytes 786440 | tf_op jit(solution)/shard_map/ppermute | solution.py:477
  46.8 15.2 %collective-permute-start.29 = (bf16[1024,128]{1,0:T(8,128)(2,1)S(1)}, bf16[1024,128]{1,0:T(8,128)(2,1)S(1)}, u32[]{:S(2)}, u32[]{:S(2)}) collective-permute-start(bf16[1024,128]{1,0:T(8,128)(2,1)S(1)} %constant_dynamic-update-slice_fusion.4.refs_0_), channel_id=1, source_target_pairs={{2,4},{3,5},{4,2},{5,3},{10,12},{11,13},{12,10},{13,11},{18,20},{1... | collective-permute-start | bytes 786440 | tf_op jit(solution)/shard_map/ppermute | solution.py:477
  47.5 26.0 %collective-permute-start.25 = (bf16[1024,128]{1,0:T(8,128)(2,1)S(1)}, bf16[1024,128]{1,0:T(8,128)(2,1)S(1)}, u32[]{:S(2)}, u32[]{:S(2)}) collective-permute-start(bf16[1024,128]{1,0:T(8,128)(2,1)S(1)} %constant_dynamic-update-slice_fusion.4.refs_0_), channel_id=1, source_target_pairs={{0,2},{1,3},{2,0},{3,1},{4,6},{5,7},{6,4},{7,5},{8,10},{9,11},{10,... | collective-permute-start | bytes 786440 | tf_op jit(solution)/shard_map/ppermute | solution.py:477
  50.4 23.1 %collective-permute-start.24 = (bf16[1024,128]{1,0:T(8,128)(2,1)S(1)}, bf16[1024,128]{1,0:T(8,128)(2,1)S(1)}, u32[]{:S(2)}, u32[]{:S(2)}) collective-permute-start(bf16[1024,128]{1,0:T(8,128)(2,1)S(1)} %constant_dynamic-update-slice_fusion.4.refs_0_), channel_id=1, source_target_pairs={{0,1},{1,0},{2,3},{3,2},{4,5},{5,4},{6,7},{7,6},{8,9},{9,8},{10,11... | collective-permute-start | bytes 786440 | tf_op jit(solution)/shard_map/ppermute | solution.py:477
  57.1 16.5 %collective-permute-start.30 = (bf16[1024,128]{1,0:T(8,128)(2,1)S(1)}, bf16[1024,128]{1,0:T(8,128)(2,1)S(1)}, u32[]{:S(2)}, u32[]{:S(2)}) collective-permute-start(bf16[1024,128]{1,0:T(8,128)(2,1)S(1)} %collective-permute-done.27.refs_4_), channel_id=1, source_target_pairs={{2,0},{3,1},{4,6},{5,7},{10,8},{11,9},{12,14},{13,15},{18,16},{19,... | collective-permute-start | bytes 786440 | tf_op jit(solution)/shard_map/ppermute | solution.py:477
  58.4 15.7 %collective-permute-start.14 = (bf16[1024,128]{1,0:T(8,128)(2,1)S(1)}, bf16[1024,128]{1,0:T(8,128)(2,1)S(1)}, u32[]{:S(2)}, u32[]{:S(2)}) collective-permute-start(bf16[1024,128]{1,0:T(8,128)(2,1)S(1)} %constant_dynamic-update-slice_fusion.refs_0_), channel_id=1, source_target_pairs={{0,6},{1,7},{2,4},{3,5},{4,2},{5,3},{6,0},{7,1},{8,14},{9,15},{10,... | collective-permute-start | bytes 786440 | tf_op jit(solution)/shard_map/ppermute | solution.py:477
  62.0 21.8 %collective-permute-start.12 = (bf16[1024,128]{1,0:T(8,128)(2,1)S(1)}, bf16[1024,128]{1,0:T(8,128)(2,1)S(1)}, u32[]{:S(2)}, u32[]{:S(2)}) collective-permute-start(bf16[1024,128]{1,0:T(8,128)(2,1)S(1)} %constant_dynamic-update-slice_fusion.refs_0_), channel_id=1, source_target_pairs={{0,4},{1,5},{2,6},{3,7},{4,0},{5,1},{6,2},{7,3},{8,12},{9,13},{10,... | collective-permute-start | bytes 786440 | tf_op jit(solution)/shard_map/ppermute | solution.py:477
  73.5 11.2 %collective-permute-start.10 = (bf16[1024,128]{1,0:T(8,128)(2,1)S(1)}, bf16[1024,128]{1,0:T(8,128)(2,1)S(1)}, u32[]{:S(2)}, u32[]{:S(2)}) collective-permute-start(bf16[1024,128]{1,0:T(8,128)(2,1)S(1)} %constant_dynamic-update-slice_fusion.refs_0_), channel_id=1, source_target_pairs={{0,2},{1,3},{2,0},{3,1},{4,6},{5,7},{6,4},{7,5},{8,10},{9,11},{10,... | collective-permute-start | bytes 786440 | tf_op jit(solution)/shard_map/ppermute | solution.py:477
  73.5 11.2 %collective-permute-start.28 = (bf16[1024,128]{1,0:T(8,128)(2,1)S(1)}, bf16[1024,128]{1,0:T(8,128)(2,1)S(1)}, u32[]{:S(2)}, u32[]{:S(2)}) collective-permute-start(bf16[1024,128]{1,0:T(8,128)(2,1)S(1)} %collective-permute-done.27.refs_4_), channel_id=1, source_target_pairs={{0,1},{1,0},{2,3},{3,2},{4,5},{5,4},{6,7},{7,6},{8,9},{9,8},{10,11... | collective-permute-start | bytes 786440 | tf_op jit(solution)/shard_map/ppermute | solution.py:477
  73.6 11.6 %collective-permute-start.26 = (bf16[1024,128]{1,0:T(8,128)(2,1)S(1)}, bf16[1024,128]{1,0:T(8,128)(2,1)S(1)}, u32[]{:S(2)}, u32[]{:S(2)}) collective-permute-start(bf16[1024,128]{1,0:T(8,128)(2,1)S(1)} %collective-permute-done.25.refs_2_), channel_id=1, source_target_pairs={{0,1},{1,0},{2,3},{3,2},{4,5},{5,4},{6,7},{7,6},{8,9},{9,8},{10,11... | collective-permute-start | bytes 786440 | tf_op jit(solution)/shard_map/ppermute | solution.py:477
  74.2 11.1 %collective-permute-start.31 = (bf16[1024,128]{1,0:T(8,128)(2,1)S(1)}, bf16[1024,128]{1,0:T(8,128)(2,1)S(1)}, u32[]{:S(2)}, u32[]{:S(2)}) collective-permute-start(bf16[1024,128]{1,0:T(8,128)(2,1)S(1)} %add.24.refs_6_), channel_id=1, source_target_pairs={{0,1},{1,0},{2,3},{3,2},{4,5},{5,4},{6,7},{7,6},{8,9},{9,8},{10,11... | collective-permute-start | bytes 786440 | tf_op jit(solution)/shard_map/ppermute | solution.py:477
  83.8 16.3 %collective-permute-start.9 = (bf16[1024,128]{1,0:T(8,128)(2,1)S(1)}, bf16[1024,128]{1,0:T(8,128)(2,1)S(1)}, u32[]{:S(2)}, u32[]{:S(2)}) collective-permute-start(bf16[1024,128]{1,0:T(8,128)(2,1)S(1)} %constant_dynamic-update-slice_fusion.refs_0_), channel_id=1, source_target_pairs={{0,1},{1,0},{2,3},{3,2},{4,5},{5,4},{6,7},{7,6},{8,9},{9,8},{10,11... | collective-permute-start | bytes 786440 | tf_op jit(solution)/shard_map/ppermute | solution.py:477
  84.7 15.4 %collective-permute-start.13 = (bf16[1024,128]{1,0:T(8,128)(2,1)S(1)}, bf16[1024,128]{1,0:T(8,128)(2,1)S(1)}, u32[]{:S(2)}, u32[]{:S(2)}) collective-permute-start(bf16[1024,128]{1,0:T(8,128)(2,1)S(1)} %collective-permute-done.12.refs_4_), channel_id=1, source_target_pairs={{0,1},{1,0},{2,3},{3,2},{4,5},{5,4},{6,7},{7,6},{8,9},{9,8},{10,11... | collective-permute-start | bytes 786440 | tf_op jit(solution)/shard_map/ppermute | solution.py:477
  84.7 15.4 %collective-permute-start.11 = (bf16[1024,128]{1,0:T(8,128)(2,1)S(1)}, bf16[1024,128]{1,0:T(8,128)(2,1)S(1)}, u32[]{:S(2)}, u32[]{:S(2)}) collective-permute-start(bf16[1024,128]{1,0:T(8,128)(2,1)S(1)} %collective-permute-done.10.refs_2_), channel_id=1, source_target_pairs={{0,1},{1,0},{2,3},{3,2},{4,5},{5,4},{6,7},{7,6},{8,9},{9,8},{10,11... | collective-permute-start | bytes 786440 | tf_op jit(solution)/shard_map/ppermute | solution.py:477
  85.2 16.5 %collective-permute-start.15 = (bf16[1024,128]{1,0:T(8,128)(2,1)S(1)}, bf16[1024,128]{1,0:T(8,128)(2,1)S(1)}, u32[]{:S(2)}, u32[]{:S(2)}) collective-permute-start(bf16[1024,128]{1,0:T(8,128)(2,1)S(1)} %collective-permute-done.14.refs_0_), channel_id=1, source_target_pairs={{0,1},{1,0},{2,3},{3,2},{4,5},{5,4},{6,7},{7,6},{8,9},{9,8},{10,11... | collective-permute-start | bytes 786440 | tf_op jit(solution)/shard_map/ppermute | solution.py:477
  87.9 1.3 %collective-permute-start.32 = (f32[1,256]{1,0:T(1,128)S(1)}, f32[1,256]{1,0:T(1,128)S(1)}, u32[]{:S(2)}, u32[]{:S(2)}) collective-permute-start(f32[1,256]{1,0:T(1,128)S(1)} %get-tuple-element.46), channel_id=1, source_target_pairs={{0,1},{1,0},{2,3},{3,2},{4,5},{5,4},{6,7},{7,6},{8,9},{9,8},{10,11... | collective-permute-start | bytes 3080 | tf_op jit(solution)/shard_map/ppermute | solution.py:477
  89.2 3.6 %collective-permute-start.33 = (f32[1,256]{1,0:T(1,128)S(1)}, f32[1,256]{1,0:T(1,128)S(1)}, u32[]{:S(2)}, u32[]{:S(2)}) collective-permute-start(f32[1,256]{1,0:T(1,128)S(1)} %add.25), channel_id=1, source_target_pairs={{0,2},{1,3},{2,0},{3,1},{4,6},{5,7},{6,4},{7,5},{8,10},{9,11},{10,... | collective-permute-start | bytes 3080 | tf_op jit(solution)/shard_map/ppermute | solution.py:477
  92.8 4.5 %collective-permute-start.34 = (f32[1,256]{1,0:T(1,128)S(1)}, f32[1,256]{1,0:T(1,128)S(1)}, u32[]{:S(2)}, u32[]{:S(2)}) collective-permute-start(f32[1,256]{1,0:T(1,128)S(1)} %add.26), channel_id=1, source_target_pairs={{0,4},{1,5},{2,6},{3,7},{4,0},{5,1},{6,2},{7,3},{8,12},{9,13},{10,... | collective-permute-start | bytes 3080 | tf_op jit(solution)/shard_map/ppermute | solution.py:477
  97.4 19.5 %collective-permute-start.35 = (bf16[256,512]{1,0:T(8,128)(2,1)S(1)}, bf16[256,512]{1,0:T(8,128)(2,1)S(1)}, u32[]{:S(2)}, u32[]{:S(2)}) collective-permute-start(bf16[256,512]{1,0:T(8,128)(2,1)S(1)} %shard_map.139.own_ref.low_ref), channel_id=1, source_target_pairs={{0,8},{8,16},{16,24},{1,9},{9,17},{17,25},{2,10},{10,18},{18,26},{... | collective-permute-start | bytes 786440 | tf_op jit(solution)/shard_map/ppermute | solution.py:477
  101.7 4.8 %copy-start.11 = (s32[512]{0:T(512)S(1)}, s32[512]{0:T(512)}, u32[]{:S(2)}) copy-start(s32[512]{0:T(512)} %param.21) | copy-start | bytes 6148
  101.7 9.3 %copy-start.1 = (bf16[512,256]{1,0:T(8,128)(2,1)S(1)}, bf16[512,256]{1,0:T(8,128)(2,1)}, u32[]{:S(2)}) copy-start(bf16[512,256]{1,0:T(8,128)(2,1)} %constant.17.clone.fl_ref.fl) | copy-start | bytes 786436
  101.7 9.3 %copy-start.2 = (bf16[512,256]{1,0:T(8,128)(2,1)S(1)}, bf16[512,256]{1,0:T(8,128)(2,1)}, u32[]{:S(2)}) copy-start(bf16[512,256]{1,0:T(8,128)(2,1)} %constant.16.clone.fh_ref.fh) | copy-start | bytes 786436
  101.7 9.3 %copy-start.6 = (bf16[512,256]{1,0:T(8,128)(2,1)S(1)}, bf16[512,256]{1,0:T(8,128)(2,1)}, u32[]{:S(2)}) copy-start(bf16[512,256]{1,0:T(8,128)(2,1)} %filters_ref.1) | copy-start | bytes 786436
  101.7 13.8 %copy-start.3 = (bf16[256,512]{1,0:T(8,128)(2,1)S(1)}, bf16[256,512]{1,0:T(8,128)(2,1)}, u32[]{:S(2)}) copy-start(bf16[256,512]{1,0:T(8,128)(2,1)} %constant.19.clone.gl) | copy-start | bytes 786436
  101.8 13.8 %copy-start.4 = (bf16[256,512]{1,0:T(8,128)(2,1)S(1)}, bf16[256,512]{1,0:T(8,128)(2,1)}, u32[]{:S(2)}) copy-start(bf16[256,512]{1,0:T(8,128)(2,1)} %constant.18.clone.gh) | copy-start | bytes 786436
  101.8 13.8 %copy-start.10 = (f32[512]{0:T(512)S(1)}, f32[512]{0:T(512)}, u32[]{:S(2)}) copy-start(f32[512]{0:T(512)} %param.22) | copy-start | bytes 6148
  103.5 16.7 %collective-permute-start.19 = (bf16[256,512]{1,0:T(8,128)(2,1)}, bf16[256,512]{1,0:T(8,128)(2,1)S(1)}, u32[]{:S(2)}, u32[]{:S(2)}) collective-permute-start(bf16[256,512]{1,0:T(8,128)(2,1)} %get-tuple-element.40), channel_id=1, source_target_pairs={{8,0},{16,8},{24,16},{9,1},{17,9},{25,17},{10,2},{18,10},{26,18},{... | collective-permute-start | bytes 786440 | tf_op jit(solution)/shard_map/ppermute | solution.py:477
  104.8 1.2 %collective-permute-start.16 = (f32[1,256]{1,0:T(1,128)S(1)}, f32[1,256]{1,0:T(1,128)S(1)}, u32[]{:S(2)}, u32[]{:S(2)}) collective-permute-start(f32[1,256]{1,0:T(1,128)S(1)} %get-tuple-element.39), channel_id=1, source_target_pairs={{0,1},{1,0},{2,3},{3,2},{4,5},{5,4},{6,7},{7,6},{8,9},{9,8},{10,11... | collective-permute-start | bytes 3080 | tf_op jit(solution)/shard_map/ppermute | solution.py:477
  106.0 3.6 %collective-permute-start.17 = (f32[1,256]{1,0:T(1,128)S(1)}, f32[1,256]{1,0:T(1,128)S(1)}, u32[]{:S(2)}, u32[]{:S(2)}) collective-permute-start(f32[1,256]{1,0:T(1,128)S(1)} %add.21), channel_id=1, source_target_pairs={{0,2},{1,3},{2,0},{3,1},{4,6},{5,7},{6,4},{7,5},{8,10},{9,11},{10,... | collective-permute-start | bytes 3080 | tf_op jit(solution)/shard_map/ppermute | solution.py:477
  109.6 4.5 %collective-permute-start.18 = (f32[1,256]{1,0:T(1,128)S(1)}, f32[1,256]{1,0:T(1,128)S(1)}, u32[]{:S(2)}, u32[]{:S(2)}) collective-permute-start(f32[1,256]{1,0:T(1,128)S(1)} %add.22), channel_id=1, source_target_pairs={{0,4},{1,5},{2,6},{3,7},{4,0},{5,1},{6,2},{7,3},{8,12},{9,13},{10,... | collective-permute-start | bytes 3080 | tf_op jit(solution)/shard_map/ppermute | solution.py:477
  114.1 6.1 %collective-permute-start.20 = (f32[1,256]{1,0:T(1,128)S(1)}, f32[1,256]{1,0:T(1,128)S(1)}, u32[]{:S(2)}, u32[]{:S(2)}) collective-permute-start(f32[1,256]{1,0:T(1,128)S(1)} %add.23.sq_ref), channel_id=1, source_target_pairs={{8,0},{16,8},{24,16},{9,1},{17,9},{25,17},{10,2},{18,10},{26,18},{... | collective-permute-start | bytes 3080 | tf_op jit(solution)/shard_map/ppermute | solution.py:477

commit v7 on v5

--- a/solution.py
+++ b/solution.py
@@ -171,43 +171,40 @@
     return jnp.where(first_is_high, 1 - high, high).astype(jnp.int32)
 
 
-def pack_kernel(n, slots_ref, ids_ref, q_ref, k_ref, v_ref, *rest):
-    outs, sem = rest[: 2 * n], rest[2 * n]
+def pack_kernel(n, high, slots_ref, ids_ref, q_ref, k_ref, v_ref, *rest):
+    outs, sem = rest[:n], rest[n]
     rank = ids_ref[0]
     rows = outs[0].shape[0] // 3
     wide = outs[0].shape[1]
+    half = half_index(slots_ref, ids_ref, high)
+    source_rows = pl.ds(pl.multiple_of(half * rows, rows), rows)
     copies = []
-    for high in range(2):
-        half = half_index(slots_ref, ids_ref, high)
-        source_rows = pl.ds(pl.multiple_of(half * rows, rows), rows)
-        for k in range(n):
-            cols = pl.ds(pl.multiple_of((rank ^ k) * wide, wide), wide)
-            for a, ref in enumerate((q_ref, k_ref, v_ref)):
-                copy = pltpu.make_async_copy(
-                    ref.at[source_rows, cols],
-                    outs[high * n + k].at[a * rows : (a + 1) * rows, :],
-                    sem.at[high * n + k, a],
-                )
-                copy.start()
-                copies.append(copy)
+    for k in range(n):
+        cols = pl.ds(pl.multiple_of((rank ^ k) * wide, wide), wide)
+        for a, ref in enumerate((q_ref, k_ref, v_ref)):
+            copy = pltpu.make_async_copy(
+                ref.at[source_rows, cols],
+                outs[k].at[a * rows : (a + 1) * rows, :],
+                sem.at[k, a],
+            )
+            copy.start()
+            copies.append(copy)
     for copy in copies:
         copy.wait()
 
 
-def pack(n, slots, ids, q, k, v):
-    rows, width = q.shape[0] // 2, q.shape[1]
+def pack(n, high, slots, ids, arrays):
+    rows, width = arrays[0].shape[0] // 2, arrays[0].shape[1]
     piece = jax.ShapeDtypeStruct((3 * rows, width // n), BF)
-    packed = pl.pallas_call(
-        functools.partial(pack_kernel, n),
-        out_shape=[piece] * (2 * n),
+    return pl.pallas_call(
+        functools.partial(pack_kernel, n, high),
+        out_shape=[piece] * n,
         in_specs=[sm(), sm()] + [pl.BlockSpec(memory_space=pltpu.HBM)] * 3,
-        out_specs=[vm()] * (2 * n),
-        scratch_shapes=[pltpu.SemaphoreType.DMA((2 * n, 3))],
+        out_specs=[vm()] * n,
+        scratch_shapes=[pltpu.SemaphoreType.DMA((n, 3))],
         compiler_params=params(8),
-        cost_estimate=cost(0, 24 * rows * width),
-        name="pack",
-    )(slots, ids, *(pltpu.with_memory_space_constraint(x, pltpu.HBM) for x in (q, k, v)))
-    return packed[:n], packed[n:]
+        cost_estimate=cost(0, 12 * rows * width),
+    )(slots, ids, *(pltpu.with_memory_space_constraint(x, pltpu.HBM) for x in arrays))
 
 
 def attend_kernel(n, high, rows, ids_ref, *refs):
@@ -469,21 +466,10 @@
     return lax.ppermute(block, axis, route)
 
 
-def far_piece(own, near, size):
-    inner = [(i, i ^ (size - 2)) for i in range(2, size - 2)]
-    direct = moved(own, "mp", inner)
-    ends = [(2, 0), (3, 1), (size - 4, size - 2), (size - 3, size - 1)]
-    return direct + moved(near, "mp", ends)
-
-
 def gather_mp(own, size):
-    chips = size // 2
-    pieces = [own]
-    for k in range(1, chips - 1):
-        pieces.append(moved(own, "mp", xor_route(size, 2 * k)))
-    pieces.append(far_piece(own, pieces[chips - 2], size))
     parts = []
-    for piece in pieces:
+    for k in range(size // 2):
+        piece = moved(own, "mp", xor_route(size, 2 * k)) if k else own
         parts.append(piece)
         parts.append(moved(piece, "mp", xor_route(size, 1)))
     return parts
@@ -519,9 +505,9 @@
     def exchange(pieces):
         return [pieces[0]] + [moved(pieces[k], "seq", xor_route(n, k)) for k in range(1, n)]
 
-    packed_low, packed_high = pack(n, slot_map, ids, queries, key_vecs, value_vecs)
-    low = exchange(packed_low)
-    high = exchange(packed_high)
+    inputs = (queries, key_vecs, value_vecs)
+    low = exchange(pack(n, 0, slot_map, ids, inputs))
+    high = exchange(pack(n, 1, slot_map, ids, inputs))
     spec = spectrum(filters, filter_len, forward)
 
     att_low = exchange(attend(n, 0, rows, ids, low))
@@ -529,7 +515,7 @@
     att_high = exchange(attend(n, 1, rows, ids, low + high))
     parts_high = gather_mp(jnp.concatenate(att_high, axis=0), mp_size)
 
-    most = mp_size - 2
+    most = mp_size // 2
     first, last = tuple(range(most)), tuple(range(most, mp_size))
     (base,) = project(
         n, slot_map, ids, incoming, w_out,
@@ -584,7 +570,7 @@
         heads % n == 0
         and power_of_two(n)
         and power_of_two(size)
-        and size >= 8
+        and size >= 4
         and rows % 256 == 0
         and filters.shape[1] <= rows
     )

time: 106 us -> 122 us (1.15)
  waiting for transfers between devices: 36.6 us -> 48.3 us
  starting transfers between devices: 48.7 us -> 52.5 us
  Pallas kernels: 18.5 us -> 20 us
    ppermute x35 -> x33, waiting for transfers between devices: 36.6 us -> 48.3 us  [moved(): return lax.ppermute(block, axis, route)]
    ppermute x35 -> x33, starting transfers between devices: 48.7 us -> 52.5 us  [moved(): return lax.ppermute(block, axis, route)]
    pallas_call x1 -> x2, Pallas kernels: 2.47 us -> 3.94 us  [pack(): pl.pallas_call(functools.partial(pack_kernel, n, high), out_shape=[piece]...]
  transfers between devices with their start and end apart: 35 -> 33, of which waited for: 13 -> 10; matrix products, arithmetic and copies ran while one was open for 0% -> 0% of each run, Pallas kernels for 11% -> 7%
where the time goes in v7:
time: 122 us
  starting transfers between devices  52.5 us (43%)
  waiting for transfers between devices  48.3 us (40%)
  Pallas kernels  20 us (16%)
    ppermute x33, starting transfers between devices, moved(): return lax.ppermute(block, axis, route)  52.5 us
    ppermute x33, waiting for transfers between devices, moved(): return lax.ppermute(block, axis, route)  48.3 us
    pallas_call x2, Pallas kernels, attend(): pl.pallas_call(functools.partial(attend_kernel, n, high, rows), out_shape...  5.9 us
    pallas_call x2, Pallas kernels, project(): pl.pallas_call(functools.partial(project_kernel, n, indices), out_shape=s...  3.96 us
    pallas_call x2, Pallas kernels, pack(): pl.pallas_call(functools.partial(pack_kernel, n, high), out_shape=[piece]...  3.94 us
    pallas_call x1, Pallas kernels, fast_device(): pl.pallas_call(functools.partial(conv_last_kernel, n, model_width), out_s...  3.48 us
  transfers between devices with their start and end apart: 33, of which 10 were waited for; matrix products, arithmetic and copies ran while one was open for 0% of the time, Pallas kernels for 7%

profile of v7, /device:TPU:0, one launch (start us, length us, event | category | flops | bytes accessed | tf_op | source)
XLA Modules:
  0.0 122.2 jit_solution(10327349690875202253)
XLA Ops:
  0.0 0.1 pad_add_fusion.ids_ref
  0.1 0.7 copy-done.7
  0.7 2.1 %shard_map.136 = (bf16[768,128]{1,0:T(8,128)(2,1)S(1)}, bf16[768,128]{1,0:T(8,128)(2,1)S(1)}, bf16[768,128]{1,0:T(8,128)(2,1)S(1)}, bf16[768,128]{1,0:T(8,128)(2,1)S(1)}) custom-call(s32[8]{0:T(128)S(1)} %copy-done.7, s32[2]{0:T(128)S(1)} %pad_add_fusion.ids_ref, bf16[512,512]{1,0:T(8,128)(2,1)} %q_ref.3, bf16[512,512]{1,0:T(8,128)(2,1)} %k_ref.3, ...), custom_call_target="tpu_custom_call" | custom-call | bytes 1572864 | tf_op jit(solution)/shard_map/pallas_call | solution.py:199
  2.8 3.0 %collective-permute-start = (bf16[768,128]{1,0:T(8,128)(2,1)S(1)}, bf16[768,128]{1,0:T(8,128)(2,1)S(1)}, u32[]{:S(2)}, u32[]{:S(2)}) collective-permute-start(bf16[768,128]{1,0:T(8,128)(2,1)S(1)} %get-tuple-element.28), channel_id=1, source_target_pairs={{0,8},{8,0},{16,24},{24,16},{1,9},{9,1},{17,25},{25,17},{2,10},{10... | collective-permute-start | bytes 589832 | tf_op jit(solution)/shard_map/ppermute | solution.py:466
  5.9 1.5 %collective-permute-start.1 = (bf16[768,128]{1,0:T(8,128)(2,1)S(1)}, bf16[768,128]{1,0:T(8,128)(2,1)S(1)}, u32[]{:S(2)}, u32[]{:S(2)}) collective-permute-start(bf16[768,128]{1,0:T(8,128)(2,1)S(1)} %get-tuple-element.29), channel_id=1, source_target_pairs={{0,16},{8,24},{16,0},{24,8},{1,17},{9,25},{17,1},{25,9},{2,18},{10... | collective-permute-start | bytes 589832 | tf_op jit(solution)/shard_map/ppermute | solution.py:466
  7.4 0.0 collective-permute-start.2
  7.4 1.8 %shard_map.137 = (bf16[768,128]{1,0:T(8,128)(2,1)S(1)}, bf16[768,128]{1,0:T(8,128)(2,1)S(1)}, bf16[768,128]{1,0:T(8,128)(2,1)S(1)}, bf16[768,128]{1,0:T(8,128)(2,1)S(1)}) custom-call(s32[8]{0:T(128)S(1)} %copy-done.7, s32[2]{0:T(128)S(1)} %pad_add_fusion.ids_ref, bf16[512,512]{1,0:T(8,128)(2,1)} %q_ref.3, bf16[512,512]{1,0:T(8,128)(2,1)} %k_ref.3, ...), custom_call_target="tpu_custom_call" | custom-call | bytes 1572864 | tf_op jit(solution)/shard_map/pallas_call | solution.py:199
  9.3 2.0 %collective-permute-start.10 = (bf16[768,128]{1,0:T(8,128)(2,1)S(1)}, bf16[768,128]{1,0:T(8,128)(2,1)S(1)}, u32[]{:S(2)}, u32[]{:S(2)}) collective-permute-start(bf16[768,128]{1,0:T(8,128)(2,1)S(1)} %get-tuple-element.37), channel_id=1, source_target_pairs={{0,16},{8,24},{16,0},{24,8},{1,17},{9,25},{17,1},{25,9},{2,18},{10... | collective-permute-start | bytes 589832 | tf_op jit(solution)/shard_map/ppermute | solution.py:466
  11.3 1.4 %collective-permute-start.11 = (bf16[768,128]{1,0:T(8,128)(2,1)S(1)}, bf16[768,128]{1,0:T(8,128)(2,1)S(1)}, u32[]{:S(2)}, u32[]{:S(2)}) collective-permute-start(bf16[768,128]{1,0:T(8,128)(2,1)S(1)} %get-tuple-element.38), channel_id=1, source_target_pairs={{0,24},{8,16},{16,8},{24,0},{1,25},{9,17},{17,9},{25,1},{2,26},{10... | collective-permute-start | bytes 589832 | tf_op jit(solution)/shard_map/ppermute | solution.py:466
  12.7 0.0 collective-permute-done.refs_1_
  12.7 0.9 collective-permute-start.9
  13.7 8.2 %collective-permute-done.1.refs_2_ = bf16[768,128]{1,0:T(8,128)(2,1)S(1)} collective-permute-done((bf16[768,128]{1,0:T(8,128)(2,1)S(1)}, bf16[768,128]{1,0:T(8,128)(2,1)S(1)}, u32[]{:S(2)}, u32[]{:S(2)}) %collective-permute-start.1) | collective-permute-done | bytes 196640 | tf_op jit(solution)/shard_map/ppermute | solution.py:466
  21.9 0.0 collective-permute-done.2.refs_3_
  21.9 3.0 %collective-permute-done.10.refs_6_ = bf16[768,128]{1,0:T(8,128)(2,1)S(1)} collective-permute-done((bf16[768,128]{1,0:T(8,128)(2,1)S(1)}, bf16[768,128]{1,0:T(8,128)(2,1)S(1)}, u32[]{:S(2)}, u32[]{:S(2)}) %collective-permute-start.10) | collective-permute-done | bytes 196640 | tf_op jit(solution)/shard_map/ppermute | solution.py:466
  24.9 3.6 %attend_high.1 = (bf16[256,128]{1,0:T(8,128)(2,1)S(1)}, bf16[256,128]{1,0:T(8,128)(2,1)S(1)}, bf16[256,128]{1,0:T(8,128)(2,1)S(1)}, bf16[256,128]{1,0:T(8,128)(2,1)S(1)}) custom-call(s32[2]{0:T(128)S(1)} %pad_add_fusion.ids_ref, bf16[768,128]{1,0:T(8,128)(2,1)S(1)} %get-tuple-element.27.refs_0_, bf16[768,128]{1,0:T(8,128)(2,1)S(1)} %collective-permute-done.refs_1_, ...), custom_call_target="tpu_custom_call" | custom-call | flops 872415232 | bytes 2097152 | tf_op jit(solution)/shard_map/attend_high/pallas_call | solution.py:271
  28.5 0.4 collective-permute-start.12
  28.9 1.7 %collective-permute-start.13 = (bf16[256,128]{1,0:T(8,128)(2,1)S(1)}, bf16[256,128]{1,0:T(8,128)(2,1)S(1)}, u32[]{:S(2)}, u32[]{:S(2)}) collective-permute-start(bf16[256,128]{1,0:T(8,128)(2,1)S(1)} %get-tuple-element.41), channel_id=1, source_target_pairs={{0,16},{8,24},{16,0},{24,8},{1,17},{9,25},{17,1},{25,9},{2,18},{10... | collective-permute-start | bytes 196616 | tf_op jit(solution)/shard_map/ppermute | solution.py:466
  30.6 1.4 %collective-permute-start.14 = (bf16[256,128]{1,0:T(8,128)(2,1)S(1)}, bf16[256,128]{1,0:T(8,128)(2,1)S(1)}, u32[]{:S(2)}, u32[]{:S(2)}) collective-permute-start(bf16[256,128]{1,0:T(8,128)(2,1)S(1)} %get-tuple-element.42), channel_id=1, source_target_pairs={{0,24},{8,16},{16,8},{24,0},{1,25},{9,17},{17,9},{25,1},{2,26},{10... | collective-permute-start | bytes 196616 | tf_op jit(solution)/shard_map/ppermute | solution.py:466
  32.1 2.3 %attend_low.1 = (bf16[256,128]{1,0:T(8,128)(2,1)S(1)}, bf16[256,128]{1,0:T(8,128)(2,1)S(1)}, bf16[256,128]{1,0:T(8,128)(2,1)S(1)}, bf16[256,128]{1,0:T(8,128)(2,1)S(1)}) custom-call(s32[2]{0:T(128)S(1)} %pad_add_fusion.ids_ref, bf16[768,128]{1,0:T(8,128)(2,1)S(1)} %get-tuple-element.27.refs_0_, bf16[768,128]{1,0:T(8,128)(2,1)S(1)} %collective-permute-done.refs_1_, ...), custom_call_target="tpu_custom_call" | custom-call | flops 335544320 | bytes 1048576 | tf_op jit(solution)/shard_map/attend_low/pallas_call | solution.py:271
  34.4 0.4 collective-permute-start.3
  34.8 1.7 %collective-permute-start.4 = (bf16[256,128]{1,0:T(8,128)(2,1)S(1)}, bf16[256,128]{1,0:T(8,128)(2,1)S(1)}, u32[]{:S(2)}, u32[]{:S(2)}) collective-permute-start(bf16[256,128]{1,0:T(8,128)(2,1)S(1)} %get-tuple-element.33), channel_id=1, source_target_pairs={{0,16},{8,24},{16,0},{24,8},{1,17},{9,25},{17,1},{25,9},{2,18},{10... | collective-permute-start | bytes 196616 | tf_op jit(solution)/shard_map/ppermute | solution.py:466
  36.5 1.5 %collective-permute-start.5 = (bf16[256,128]{1,0:T(8,128)(2,1)S(1)}, bf16[256,128]{1,0:T(8,128)(2,1)S(1)}, u32[]{:S(2)}, u32[]{:S(2)}) collective-permute-start(bf16[256,128]{1,0:T(8,128)(2,1)S(1)} %get-tuple-element.34), channel_id=1, source_target_pairs={{0,24},{8,16},{16,8},{24,0},{1,25},{9,17},{17,9},{25,1},{2,26},{10... | collective-permute-start | bytes 196616 | tf_op jit(solution)/shard_map/ppermute | solution.py:466
  38.0 0.0 collective-permute-done.13
  38.0 0.0 collective-permute-done.14
  38.1 1.6 %collective-permute-start.16 = (bf16[1024,128]{1,0:T(8,128)(2,1)S(1)}, bf16[1024,128]{1,0:T(8,128)(2,1)S(1)}, u32[]{:S(2)}, u32[]{:S(2)}) collective-permute-start(bf16[1024,128]{1,0:T(8,128)(2,1)S(1)} %constant_dynamic-update-slice_fusion.4.refs_4_), channel_id=1, source_target_pairs={{0,2},{1,3},{2,0},{3,1},{4,6},{5,7},{6,4},{7,5},{8,10},{9,11},{10,... | collective-permute-start | bytes 786440 | tf_op jit(solution)/shard_map/ppermute | solution.py:466
  39.7 0.0 collective-permute-start.15
  39.7 0.0 collective-permute-done.4
  39.8 2.0 %collective-permute-done.5 = bf16[256,128]{1,0:T(8,128)(2,1)S(1)} collective-permute-done((bf16[256,128]{1,0:T(8,128)(2,1)S(1)}, bf16[256,128]{1,0:T(8,128)(2,1)S(1)}, u32[]{:S(2)}, u32[]{:S(2)}) %collective-permute-start.5) | collective-permute-done | bytes 65568 | tf_op jit(solution)/shard_map/ppermute | solution.py:466
  41.8 1.6 %collective-permute-start.7 = (bf16[1024,128]{1,0:T(8,128)(2,1)S(1)}, bf16[1024,128]{1,0:T(8,128)(2,1)S(1)}, u32[]{:S(2)}, u32[]{:S(2)}) collective-permute-start(bf16[1024,128]{1,0:T(8,128)(2,1)S(1)} %constant_dynamic-update-slice_fusion.refs_0_), channel_id=1, source_target_pairs={{0,2},{1,3},{2,0},{3,1},{4,6},{5,7},{6,4},{7,5},{8,10},{9,11},{10,... | collective-permute-start | bytes 786440 | tf_op jit(solution)/shard_map/ppermute | solution.py:466
  43.4 0.0 collective-permute-start.6
  43.4 2.6 %collective-permute-start.22 = (bf16[1024,128]{1,0:T(8,128)(2,1)S(1)}, bf16[1024,128]{1,0:T(8,128)(2,1)S(1)}, u32[]{:S(2)}, u32[]{:S(2)}) collective-permute-start(bf16[1024,128]{1,0:T(8,128)(2,1)S(1)} %constant_dynamic-update-slice_fusion.4.refs_4_), channel_id=1, source_target_pairs={{0,4},{1,5},{2,6},{3,7},{4,0},{5,1},{6,2},{7,3},{8,12},{9,13},{10,... | collective-permute-start | bytes 786440 | tf_op jit(solution)/shard_map/ppermute | solution.py:466
  46.0 0.3 collective-permute-done.16.refs_6_
  46.3 6.4 %collective-permute-start.24 = (bf16[1024,128]{1,0:T(8,128)(2,1)S(1)}, bf16[1024,128]{1,0:T(8,128)(2,1)S(1)}, u32[]{:S(2)}, u32[]{:S(2)}) collective-permute-start(bf16[1024,128]{1,0:T(8,128)(2,1)S(1)} %constant_dynamic-update-slice_fusion.4.refs_4_), channel_id=1, source_target_pairs={{0,6},{1,7},{2,4},{3,5},{4,2},{5,3},{6,0},{7,1},{8,14},{9,15},{10,... | collective-permute-start | bytes 786440 | tf_op jit(solution)/shard_map/ppermute | solution.py:466
  52.7 2.3 %collective-permute-done.7.refs_2_ = bf16[1024,128]{1,0:T(8,128)(2,1)S(1)} collective-permute-done((bf16[1024,128]{1,0:T(8,128)(2,1)S(1)}, bf16[1024,128]{1,0:T(8,128)(2,1)S(1)}, u32[]{:S(2)}, u32[]{:S(2)}) %collective-permute-start.7) | collective-permute-done | bytes 262176 | tf_op jit(solution)/shard_map/ppermute | solution.py:466
  55.0 3.3 %collective-permute-start.20 = (bf16[1024,128]{1,0:T(8,128)(2,1)S(1)}, bf16[1024,128]{1,0:T(8,128)(2,1)S(1)}, u32[]{:S(2)}, u32[]{:S(2)}) collective-permute-start(bf16[1024,128]{1,0:T(8,128)(2,1)S(1)} %constant_dynamic-update-slice_fusion.refs_0_), channel_id=1, source_target_pairs={{0,6},{1,7},{2,4},{3,5},{4,2},{5,3},{6,0},{7,1},{8,14},{9,15},{10,... | collective-permute-start | bytes 786440 | tf_op jit(solution)/shard_map/ppermute | solution.py:466
  58.3 17.7 %collective-permute-done.22.refs_4_ = bf16[1024,128]{1,0:T(8,128)(2,1)S(1)} collective-permute-done((bf16[1024,128]{1,0:T(8,128)(2,1)S(1)}, bf16[1024,128]{1,0:T(8,128)(2,1)S(1)}, u32[]{:S(2)}, u32[]{:S(2)}) %collective-permute-start.22) | collective-permute-done | bytes 262176 | tf_op jit(solution)/shard_map/ppermute | solution.py:466
  76.0 0.5 collective-permute-start.23
  76.5 10.7 %collective-permute-done.18.refs_0_ = bf16[1024,128]{1,0:T(8,128)(2,1)S(1)} collective-permute-done((bf16[1024,128]{1,0:T(8,128)(2,1)S(1)}, bf16[1024,128]{1,0:T(8,128)(2,1)S(1)}, u32[]{:S(2)}, u32[]{:S(2)}) %collective-permute-start.18) | collective-permute-done | bytes 262176 | tf_op jit(solution)/shard_map/ppermute | solution.py:466
  87.2 0.5 collective-permute-start.19
  87.7 0.1 collective-permute-start.21
  87.8 1.9 %shard_map.138.base_ref = f32[512,512]{1,0:T(8,128)S(1)} custom-call(s32[8]{0:T(128)S(1)} %copy-done.8, s32[2]{0:T(128)S(1)} %pad_add_fusion.ids_ref, bf16[512,512]{1,0:T(8,128)(2,1)S(1)} %copy-done.5, bf16[4096,512]{1,0:T(8,128)(2,1)S(1)} %copy-done, bf16[1024,128]{1,0:T(8,128)(2,1)S(1)} %constant_dynamic-update-slice_fusion.refs_0_, ...), custom_call_target="tpu_custom_call" | custom-call | flops 1073741824 | bytes 6291456 | tf_op jit(solution)/shard_map/pallas_call | solution.py:330
  89.8 0.0 copy-start.11
  89.8 0.0 copy-start.1
  89.8 0.0 copy-start.2
  89.8 0.0 copy-start.6
  89.8 0.0 copy-start.3
  89.8 0.0 copy-start.4
  89.9 0.0 copy-start.9
  89.9 0.0 copy-start.10
  89.9 2.0 %shard_map.139 = (f32[512,512]{1,0:T(8,128)S(1)}, bf16[256,512]{1,0:T(8,128)(2,1)S(1)}, bf16[256,512]{1,0:T(8,128)(2,1)S(1)}, f32[1,512]{1,0:T(1,128)S(1)}) custom-call(s32[8]{0:T(128)S(1)} %copy-done.8, s32[2]{0:T(128)S(1)} %pad_add_fusion.ids_ref, f32[512,512]{1,0:T(8,128)S(1)} %shard_map.138.base_ref, bf16[4096,512]{1,0:T(8,128)(2,1)S(1)} %copy-done, ...), custom_call_target="tpu_custom_call" | custom-call | flops 1073741824 | bytes 6291456 | tf_op jit(solution)/shard_map/pallas_call | solution.py:330
  91.9 0.5 collective-permute-start.26
  92.4 0.8 collective-permute-done.26
  93.3 5.6 %collective-permute-start.27 = (f32[1,512]{1,0:T(1,128)S(1)}, f32[1,512]{1,0:T(1,128)S(1)}, u32[]{:S(2)}, u32[]{:S(2)}) collective-permute-start(f32[1,512]{1,0:T(1,128)S(1)} %add.9), channel_id=1, source_target_pairs={{0,2},{1,3},{2,0},{3,1},{4,6},{5,7},{6,4},{7,5},{8,10},{9,11},{10,... | collective-permute-start | bytes 6152 | tf_op jit(solution)/shard_map/ppermute | solution.py:466
  98.8 0.1 copy.15.len_ref
  99.0 1.4 %collective-permute-done.27 = f32[1,512]{1,0:T(1,128)S(1)} collective-permute-done((f32[1,512]{1,0:T(1,128)S(1)}, f32[1,512]{1,0:T(1,128)S(1)}, u32[]{:S(2)}, u32[]{:S(2)}) %collective-permute-start.27) | collective-permute-done | bytes 2080 | tf_op jit(solution)/shard_map/ppermute | solution.py:466
  100.4 3.0 %collective-permute-start.28 = (f32[1,512]{1,0:T(1,128)S(1)}, f32[1,512]{1,0:T(1,128)S(1)}, u32[]{:S(2)}, u32[]{:S(2)}) collective-permute-start(f32[1,512]{1,0:T(1,128)S(1)} %add.10), channel_id=1, source_target_pairs={{0,4},{1,5},{2,6},{3,7},{4,0},{5,1},{6,2},{7,3},{8,12},{9,13},{10,... | collective-permute-start | bytes 6152 | tf_op jit(solution)/shard_map/ppermute | solution.py:466
  103.4 0.6 spectrum.1.spec_ref
  104.0 3.4 %collective-permute-start.29 = (bf16[256,512]{1,0:T(8,128)(2,1)S(1)}, bf16[256,512]{1,0:T(8,128)(2,1)S(1)}, u32[]{:S(2)}, u32[]{:S(2)}) collective-permute-start(bf16[256,512]{1,0:T(8,128)(2,1)S(1)} %get-tuple-element.47), channel_id=1, source_target_pairs={{0,8},{8,16},{16,24},{1,9},{9,17},{17,25},{2,10},{10,18},{18,26},{... | collective-permute-start | bytes 786440 | tf_op jit(solution)/shard_map/ppermute | solution.py:466
  107.4 1.3 %collective-permute-start.30 = (bf16[256,512]{1,0:T(8,128)(2,1)S(1)}, bf16[256,512]{1,0:T(8,128)(2,1)S(1)}, u32[]{:S(2)}, u32[]{:S(2)}) collective-permute-start(bf16[256,512]{1,0:T(8,128)(2,1)S(1)} %get-tuple-element.48), channel_id=1, source_target_pairs={{8,0},{16,8},{24,16},{9,1},{17,9},{25,17},{10,2},{18,10},{26,18},{... | collective-permute-start | bytes 786440 | tf_op jit(solution)/shard_map/ppermute | solution.py:466
  108.7 4.5 %collective-permute-start.31 = (f32[1,256]{1,0:T(1,128)S(1)}, f32[1,256]{1,0:T(1,128)S(1)}, u32[]{:S(2)}, u32[]{:S(2)}) collective-permute-start(f32[1,256]{1,0:T(1,128)S(1)} %get-tuple-element.50), channel_id=1, source_target_pairs={{0,8},{8,16},{16,24},{1,9},{9,17},{17,25},{2,10},{10,18},{18,26},{... | collective-permute-start | bytes 3080 | tf_op jit(solution)/shard_map/ppermute | solution.py:466
  113.3 1.5 %collective-permute-start.32 = (f32[1,256]{1,0:T(1,128)S(1)}, f32[1,256]{1,0:T(1,128)S(1)}, u32[]{:S(2)}, u32[]{:S(2)}) collective-permute-start(f32[1,256]{1,0:T(1,128)S(1)} %get-tuple-element.49), channel_id=1, source_target_pairs={{8,0},{16,8},{24,16},{9,1},{17,9},{25,17},{10,2},{18,10},{26,18},{... | collective-permute-start | bytes 3080 | tf_op jit(solution)/shard_map/ppermute | solution.py:466
  114.8 2.2 %conv_own.1 = (f32[512,512]{1,0:T(8,128)S(1)}, bf16[256,512]{1,0:T(8,128)(2,1)S(1)}) custom-call(f32[512,512]{1,0:T(8,128)S(1)} %get-tuple-element.43.res_ref, f32[1,512]{1,0:T(1,128)S(1)} %add.11.sq_ref, f32[512,512]{1,0:T(8,128)S(1)} %spectrum.1.spec_ref, f32[1,512]{1,0:T(1,128)S(1)} %bitcast.5, f32[1,512]{1,0:T(1,128)S(1)} %bitcast.7, ...), custom_call_target="tpu_custom_call" | custom-call | flops 671088640 | bytes 3145728 | tf_op jit(solution)/shard_map/conv_own/pallas_call | solution.py:534
  117.0 1.8 %collective-permute-done.32.sq_high = f32[1,256]{1,0:T(1,128)S(1)} collective-permute-done((f32[1,256]{1,0:T(1,128)S(1)}, f32[1,256]{1,0:T(1,128)S(1)}, u32[]{:S(2)}, u32[]{:S(2)}) %collective-permute-start.32) | collective-permute-done | bytes 1056 | tf_op jit(solution)/shard_map/ppermute | solution.py:466
  118.8 3.5 %conv_last.1 = bf16[512,512]{1,0:T(8,128)(2,1)} custom-call(s32[8]{0:T(128)S(1)} %copy-done.8, s32[2]{0:T(128)S(1)} %pad_add_fusion.ids_ref, f32[512,512]{1,0:T(8,128)S(1)} %get-tuple-element.45.part_ref, bf16[256,512]{1,0:T(8,128)(2,1)S(1)} %get-tuple-element.46.low_ref, bf16[256,512]{1,0:T(8,128)(2,1)S(1)} %collective-permute-done.29.raw_low, ...), custom_call_target="tpu_custom_call" | custom-call | flops 671088640 | bytes 3145728 | tf_op jit(solution)/shard_map/conv_last/pallas_call | solution.py:546
  (49 shorter events, 0.2 us)
Async XLA Ops:
  0.1 0.7 copy-start.7
  0.7 87.1 %copy-start = (bf16[4096,512]{1,0:T(8,128)(2,1)S(1)}, bf16[4096,512]{1,0:T(8,128)(2,1)}, u32[]{:S(2)}) copy-start(bf16[4096,512]{1,0:T(8,128)(2,1)} %w_ref.3) | copy-start | bytes 12582916
  0.7 87.1 %copy-start.5 = (bf16[512,512]{1,0:T(8,128)(2,1)S(1)}, bf16[512,512]{1,0:T(8,128)(2,1)}, u32[]{:S(2)}) copy-start(bf16[512,512]{1,0:T(8,128)(2,1)} %base_ref.1) | copy-start | bytes 1572868
  0.7 87.1 %copy-start.8 = (s32[8]{0:T(128)S(1)}, s32[8]{0:T(128)}, u32[]{:S(2)}) copy-start(s32[8]{0:T(128)} %slots_ref.9) | copy-start | bytes 100
  2.8 9.9 %collective-permute-start = (bf16[768,128]{1,0:T(8,128)(2,1)S(1)}, bf16[768,128]{1,0:T(8,128)(2,1)S(1)}, u32[]{:S(2)}, u32[]{:S(2)}) collective-permute-start(bf16[768,128]{1,0:T(8,128)(2,1)S(1)} %get-tuple-element.28), channel_id=1, source_target_pairs={{0,8},{8,0},{16,24},{24,16},{1,9},{9,1},{17,25},{25,17},{2,10},{10... | collective-permute-start | bytes 589832 | tf_op jit(solution)/shard_map/ppermute | solution.py:466
  5.9 16.0 %collective-permute-start.1 = (bf16[768,128]{1,0:T(8,128)(2,1)S(1)}, bf16[768,128]{1,0:T(8,128)(2,1)S(1)}, u32[]{:S(2)}, u32[]{:S(2)}) collective-permute-start(bf16[768,128]{1,0:T(8,128)(2,1)S(1)} %get-tuple-element.29), channel_id=1, source_target_pairs={{0,16},{8,24},{16,0},{24,8},{1,17},{9,25},{17,1},{25,9},{2,18},{10... | collective-permute-start | bytes 589832 | tf_op jit(solution)/shard_map/ppermute | solution.py:466
  7.4 14.5 %collective-permute-start.2 = (bf16[768,128]{1,0:T(8,128)(2,1)S(1)}, bf16[768,128]{1,0:T(8,128)(2,1)S(1)}, u32[]{:S(2)}, u32[]{:S(2)}) collective-permute-start(bf16[768,128]{1,0:T(8,128)(2,1)S(1)} %get-tuple-element.30), channel_id=1, source_target_pairs={{0,24},{8,16},{16,8},{24,0},{1,25},{9,17},{17,9},{25,1},{2,26},{10... | collective-permute-start | bytes 589832 | tf_op jit(solution)/shard_map/ppermute | solution.py:466
  9.3 15.6 %collective-permute-start.10 = (bf16[768,128]{1,0:T(8,128)(2,1)S(1)}, bf16[768,128]{1,0:T(8,128)(2,1)S(1)}, u32[]{:S(2)}, u32[]{:S(2)}) collective-permute-start(bf16[768,128]{1,0:T(8,128)(2,1)S(1)} %get-tuple-element.37), channel_id=1, source_target_pairs={{0,16},{8,24},{16,0},{24,8},{1,17},{9,25},{17,1},{25,9},{2,18},{10... | collective-permute-start | bytes 589832 | tf_op jit(solution)/shard_map/ppermute | solution.py:466
  11.3 13.6 %collective-permute-start.11 = (bf16[768,128]{1,0:T(8,128)(2,1)S(1)}, bf16[768,128]{1,0:T(8,128)(2,1)S(1)}, u32[]{:S(2)}, u32[]{:S(2)}) collective-permute-start(bf16[768,128]{1,0:T(8,128)(2,1)S(1)} %get-tuple-element.38), channel_id=1, source_target_pairs={{0,24},{8,16},{16,8},{24,0},{1,25},{9,17},{17,9},{25,1},{2,26},{10... | collective-permute-start | bytes 589832 | tf_op jit(solution)/shard_map/ppermute | solution.py:466
  12.7 12.1 %collective-permute-start.9 = (bf16[768,128]{1,0:T(8,128)(2,1)S(1)}, bf16[768,128]{1,0:T(8,128)(2,1)S(1)}, u32[]{:S(2)}, u32[]{:S(2)}) collective-permute-start(bf16[768,128]{1,0:T(8,128)(2,1)S(1)} %get-tuple-element.36), channel_id=1, source_target_pairs={{0,8},{8,0},{16,24},{24,16},{1,9},{9,1},{17,25},{25,17},{2,10},{10... | collective-permute-start | bytes 589832 | tf_op jit(solution)/shard_map/ppermute | solution.py:466
  28.5 8.0 %collective-permute-start.12 = (bf16[256,128]{1,0:T(8,128)(2,1)S(1)}, bf16[256,128]{1,0:T(8,128)(2,1)S(1)}, u32[]{:S(2)}, u32[]{:S(2)}) collective-permute-start(bf16[256,128]{1,0:T(8,128)(2,1)S(1)} %get-tuple-element.40), channel_id=1, source_target_pairs={{0,8},{8,0},{16,24},{24,16},{1,9},{9,1},{17,25},{25,17},{2,10},{10... | collective-permute-start | bytes 196616 | tf_op jit(solution)/shard_map/ppermute | solution.py:466
  28.9 9.1 %collective-permute-start.13 = (bf16[256,128]{1,0:T(8,128)(2,1)S(1)}, bf16[256,128]{1,0:T(8,128)(2,1)S(1)}, u32[]{:S(2)}, u32[]{:S(2)}) collective-permute-start(bf16[256,128]{1,0:T(8,128)(2,1)S(1)} %get-tuple-element.41), channel_id=1, source_target_pairs={{0,16},{8,24},{16,0},{24,8},{1,17},{9,25},{17,1},{25,9},{2,18},{10... | collective-permute-start | bytes 196616 | tf_op jit(solution)/shard_map/ppermute | solution.py:466
  30.6 7.4 %collective-permute-start.14 = (bf16[256,128]{1,0:T(8,128)(2,1)S(1)}, bf16[256,128]{1,0:T(8,128)(2,1)S(1)}, u32[]{:S(2)}, u32[]{:S(2)}) collective-permute-start(bf16[256,128]{1,0:T(8,128)(2,1)S(1)} %get-tuple-element.42), channel_id=1, source_target_pairs={{0,24},{8,16},{16,8},{24,0},{1,25},{9,17},{17,9},{25,1},{2,26},{10... | collective-permute-start | bytes 196616 | tf_op jit(solution)/shard_map/ppermute | solution.py:466
  34.4 5.4 %collective-permute-start.3 = (bf16[256,128]{1,0:T(8,128)(2,1)S(1)}, bf16[256,128]{1,0:T(8,128)(2,1)S(1)}, u32[]{:S(2)}, u32[]{:S(2)}) collective-permute-start(bf16[256,128]{1,0:T(8,128)(2,1)S(1)} %get-tuple-element.32), channel_id=1, source_target_pairs={{0,8},{8,0},{16,24},{24,16},{1,9},{9,1},{17,25},{25,17},{2,10},{10... | collective-permute-start | bytes 196616 | tf_op jit(solution)/shard_map/ppermute | solution.py:466
  34.8 4.9 %collective-permute-start.4 = (bf16[256,128]{1,0:T(8,128)(2,1)S(1)}, bf16[256,128]{1,0:T(8,128)(2,1)S(1)}, u32[]{:S(2)}, u32[]{:S(2)}) collective-permute-start(bf16[256,128]{1,0:T(8,128)(2,1)S(1)} %get-tuple-element.33), channel_id=1, source_target_pairs={{0,16},{8,24},{16,0},{24,8},{1,17},{9,25},{17,1},{25,9},{2,18},{10... | collective-permute-start | bytes 196616 | tf_op jit(solution)/shard_map/ppermute | solution.py:466
  36.5 5.2 %collective-permute-start.5 = (bf16[256,128]{1,0:T(8,128)(2,1)S(1)}, bf16[256,128]{1,0:T(8,128)(2,1)S(1)}, u32[]{:S(2)}, u32[]{:S(2)}) collective-permute-start(bf16[256,128]{1,0:T(8,128)(2,1)S(1)} %get-tuple-element.34), channel_id=1, source_target_pairs={{0,24},{8,16},{16,8},{24,0},{1,25},{9,17},{17,9},{25,1},{2,26},{10... | collective-permute-start | bytes 196616 | tf_op jit(solution)/shard_map/ppermute | solution.py:466
  38.1 8.2 %collective-permute-start.16 = (bf16[1024,128]{1,0:T(8,128)(2,1)S(1)}, bf16[1024,128]{1,0:T(8,128)(2,1)S(1)}, u32[]{:S(2)}, u32[]{:S(2)}) collective-permute-start(bf16[1024,128]{1,0:T(8,128)(2,1)S(1)} %constant_dynamic-update-slice_fusion.4.refs_4_), channel_id=1, source_target_pairs={{0,2},{1,3},{2,0},{3,1},{4,6},{5,7},{6,4},{7,5},{8,10},{9,11},{10,... | collective-permute-start | bytes 786440 | tf_op jit(solution)/shard_map/ppermute | solution.py:466
  39.7 12.9 %collective-permute-start.15 = (bf16[1024,128]{1,0:T(8,128)(2,1)S(1)}, bf16[1024,128]{1,0:T(8,128)(2,1)S(1)}, u32[]{:S(2)}, u32[]{:S(2)}) collective-permute-start(bf16[1024,128]{1,0:T(8,128)(2,1)S(1)} %constant_dynamic-update-slice_fusion.4.refs_4_), channel_id=1, source_target_pairs={{0,1},{1,0},{2,3},{3,2},{4,5},{5,4},{6,7},{7,6},{8,9},{9,8},{10,11... | collective-permute-start | bytes 786440 | tf_op jit(solution)/shard_map/ppermute | solution.py:466
  41.8 13.2 %collective-permute-start.7 = (bf16[1024,128]{1,0:T(8,128)(2,1)S(1)}, bf16[1024,128]{1,0:T(8,128)(2,1)S(1)}, u32[]{:S(2)}, u32[]{:S(2)}) collective-permute-start(bf16[1024,128]{1,0:T(8,128)(2,1)S(1)} %constant_dynamic-update-slice_fusion.refs_0_), channel_id=1, source_target_pairs={{0,2},{1,3},{2,0},{3,1},{4,6},{5,7},{6,4},{7,5},{8,10},{9,11},{10,... | collective-permute-start | bytes 786440 | tf_op jit(solution)/shard_map/ppermute | solution.py:466
  43.4 14.9 %collective-permute-start.6 = (bf16[1024,128]{1,0:T(8,128)(2,1)S(1)}, bf16[1024,128]{1,0:T(8,128)(2,1)S(1)}, u32[]{:S(2)}, u32[]{:S(2)}) collective-permute-start(bf16[1024,128]{1,0:T(8,128)(2,1)S(1)} %constant_dynamic-update-slice_fusion.refs_0_), channel_id=1, source_target_pairs={{0,1},{1,0},{2,3},{3,2},{4,5},{5,4},{6,7},{7,6},{8,9},{9,8},{10,11... | collective-permute-start | bytes 786440 | tf_op jit(solution)/shard_map/ppermute | solution.py:466
  43.4 32.6 %collective-permute-start.22 = (bf16[1024,128]{1,0:T(8,128)(2,1)S(1)}, bf16[1024,128]{1,0:T(8,128)(2,1)S(1)}, u32[]{:S(2)}, u32[]{:S(2)}) collective-permute-start(bf16[1024,128]{1,0:T(8,128)(2,1)S(1)} %constant_dynamic-update-slice_fusion.4.refs_4_), channel_id=1, source_target_pairs={{0,4},{1,5},{2,6},{3,7},{4,0},{5,1},{6,2},{7,3},{8,12},{9,13},{10,... | collective-permute-start | bytes 786440 | tf_op jit(solution)/shard_map/ppermute | solution.py:466
  46.3 29.7 %collective-permute-start.24 = (bf16[1024,128]{1,0:T(8,128)(2,1)S(1)}, bf16[1024,128]{1,0:T(8,128)(2,1)S(1)}, u32[]{:S(2)}, u32[]{:S(2)}) collective-permute-start(bf16[1024,128]{1,0:T(8,128)(2,1)S(1)} %constant_dynamic-update-slice_fusion.4.refs_4_), channel_id=1, source_target_pairs={{0,6},{1,7},{2,4},{3,5},{4,2},{5,3},{6,0},{7,1},{8,14},{9,15},{10,... | collective-permute-start | bytes 786440 | tf_op jit(solution)/shard_map/ppermute | solution.py:466
  52.6 34.6 %collective-permute-start.18 = (bf16[1024,128]{1,0:T(8,128)(2,1)S(1)}, bf16[1024,128]{1,0:T(8,128)(2,1)S(1)}, u32[]{:S(2)}, u32[]{:S(2)}) collective-permute-start(bf16[1024,128]{1,0:T(8,128)(2,1)S(1)} %constant_dynamic-update-slice_fusion.refs_0_), channel_id=1, source_target_pairs={{0,4},{1,5},{2,6},{3,7},{4,0},{5,1},{6,2},{7,3},{8,12},{9,13},{10,... | collective-permute-start | bytes 786440 | tf_op jit(solution)/shard_map/ppermute | solution.py:466
  55.0 32.3 %collective-permute-start.20 = (bf16[1024,128]{1,0:T(8,128)(2,1)S(1)}, bf16[1024,128]{1,0:T(8,128)(2,1)S(1)}, u32[]{:S(2)}, u32[]{:S(2)}) collective-permute-start(bf16[1024,128]{1,0:T(8,128)(2,1)S(1)} %constant_dynamic-update-slice_fusion.refs_0_), channel_id=1, source_target_pairs={{0,6},{1,7},{2,4},{3,5},{4,2},{5,3},{6,0},{7,1},{8,14},{9,15},{10,... | collective-permute-start | bytes 786440 | tf_op jit(solution)/shard_map/ppermute | solution.py:466
  58.2 29.5 %collective-permute-start.17 = (bf16[1024,128]{1,0:T(8,128)(2,1)S(1)}, bf16[1024,128]{1,0:T(8,128)(2,1)S(1)}, u32[]{:S(2)}, u32[]{:S(2)}) collective-permute-start(bf16[1024,128]{1,0:T(8,128)(2,1)S(1)} %collective-permute-done.16.refs_6_), channel_id=1, source_target_pairs={{0,1},{1,0},{2,3},{3,2},{4,5},{5,4},{6,7},{7,6},{8,9},{9,8},{10,11... | collective-permute-start | bytes 786440 | tf_op jit(solution)/shard_map/ppermute | solution.py:466
  76.0 11.8 %collective-permute-start.8 = (bf16[1024,128]{1,0:T(8,128)(2,1)S(1)}, bf16[1024,128]{1,0:T(8,128)(2,1)S(1)}, u32[]{:S(2)}, u32[]{:S(2)}) collective-permute-start(bf16[1024,128]{1,0:T(8,128)(2,1)S(1)} %collective-permute-done.7.refs_2_), channel_id=1, source_target_pairs={{0,1},{1,0},{2,3},{3,2},{4,5},{5,4},{6,7},{7,6},{8,9},{9,8},{10,11... | collective-permute-start | bytes 786440 | tf_op jit(solution)/shard_map/ppermute | solution.py:466
  76.0 13.9 %collective-permute-start.23 = (bf16[1024,128]{1,0:T(8,128)(2,1)S(1)}, bf16[1024,128]{1,0:T(8,128)(2,1)S(1)}, u32[]{:S(2)}, u32[]{:S(2)}) collective-permute-start(bf16[1024,128]{1,0:T(8,128)(2,1)S(1)} %collective-permute-done.22.refs_4_), channel_id=1, source_target_pairs={{0,1},{1,0},{2,3},{3,2},{4,5},{5,4},{6,7},{7,6},{8,9},{9,8},{10,11... | collective-permute-start | bytes 786440 | tf_op jit(solution)/shard_map/ppermute | solution.py:466
  87.2 2.7 %collective-permute-start.25 = (bf16[1024,128]{1,0:T(8,128)(2,1)S(1)}, bf16[1024,128]{1,0:T(8,128)(2,1)S(1)}, u32[]{:S(2)}, u32[]{:S(2)}) collective-permute-start(bf16[1024,128]{1,0:T(8,128)(2,1)S(1)} %collective-permute-done.24.refs_6_), channel_id=1, source_target_pairs={{0,1},{1,0},{2,3},{3,2},{4,5},{5,4},{6,7},{7,6},{8,9},{9,8},{10,11... | collective-permute-start | bytes 786440 | tf_op jit(solution)/shard_map/ppermute | solution.py:466
  87.2 2.7 %collective-permute-start.19 = (bf16[1024,128]{1,0:T(8,128)(2,1)S(1)}, bf16[1024,128]{1,0:T(8,128)(2,1)S(1)}, u32[]{:S(2)}, u32[]{:S(2)}) collective-permute-start(bf16[1024,128]{1,0:T(8,128)(2,1)S(1)} %collective-permute-done.18.refs_0_), channel_id=1, source_target_pairs={{0,1},{1,0},{2,3},{3,2},{4,5},{5,4},{6,7},{7,6},{8,9},{9,8},{10,11... | collective-permute-start | bytes 786440 | tf_op jit(solution)/shard_map/ppermute | solution.py:466
  87.7 2.2 %collective-permute-start.21 = (bf16[1024,128]{1,0:T(8,128)(2,1)S(1)}, bf16[1024,128]{1,0:T(8,128)(2,1)S(1)}, u32[]{:S(2)}, u32[]{:S(2)}) collective-permute-start(bf16[1024,128]{1,0:T(8,128)(2,1)S(1)} %collective-permute-done.20.refs_2_), channel_id=1, source_target_pairs={{0,1},{1,0},{2,3},{3,2},{4,5},{5,4},{6,7},{7,6},{8,9},{9,8},{10,11... | collective-permute-start | bytes 786440 | tf_op jit(solution)/shard_map/ppermute | solution.py:466
  89.8 9.0 %copy-start.11 = (s32[512]{0:T(512)S(1)}, s32[512]{0:T(512)}, u32[]{:S(2)}) copy-start(s32[512]{0:T(512)} %param.21) | copy-start | bytes 6148
  89.8 13.6 %copy-start.1 = (bf16[512,256]{1,0:T(8,128)(2,1)S(1)}, bf16[512,256]{1,0:T(8,128)(2,1)}, u32[]{:S(2)}) copy-start(bf16[512,256]{1,0:T(8,128)(2,1)} %constant.16.clone.fh_ref.fh) | copy-start | bytes 786436
  89.8 13.6 %copy-start.2 = (bf16[512,256]{1,0:T(8,128)(2,1)S(1)}, bf16[512,256]{1,0:T(8,128)(2,1)}, u32[]{:S(2)}) copy-start(bf16[512,256]{1,0:T(8,128)(2,1)} %constant.17.clone.fl_ref.fl) | copy-start | bytes 786436
  89.8 13.6 %copy-start.6 = (bf16[512,256]{1,0:T(8,128)(2,1)S(1)}, bf16[512,256]{1,0:T(8,128)(2,1)}, u32[]{:S(2)}) copy-start(bf16[512,256]{1,0:T(8,128)(2,1)} %filters_ref.1) | copy-start | bytes 786436
  89.8 24.9 %copy-start.3 = (bf16[256,512]{1,0:T(8,128)(2,1)S(1)}, bf16[256,512]{1,0:T(8,128)(2,1)}, u32[]{:S(2)}) copy-start(bf16[256,512]{1,0:T(8,128)(2,1)} %constant.18.clone.gh) | copy-start | bytes 786436
  89.8 24.9 %copy-start.4 = (bf16[256,512]{1,0:T(8,128)(2,1)S(1)}, bf16[256,512]{1,0:T(8,128)(2,1)}, u32[]{:S(2)}) copy-start(bf16[256,512]{1,0:T(8,128)(2,1)} %constant.19.clone.gl) | copy-start | bytes 786436
  89.9 24.9 %copy-start.9 = (f32[512]{0:T(512)S(1)}, f32[512]{0:T(512)}, u32[]{:S(2)}) copy-start(f32[512]{0:T(512)} %param.19) | copy-start | bytes 6148
  89.9 24.9 %copy-start.10 = (f32[512]{0:T(512)S(1)}, f32[512]{0:T(512)}, u32[]{:S(2)}) copy-start(f32[512]{0:T(512)} %param.22) | copy-start | bytes 6148
  91.9 1.3 %collective-permute-start.26 = (f32[1,512]{1,0:T(1,128)S(1)}, f32[1,512]{1,0:T(1,128)S(1)}, u32[]{:S(2)}, u32[]{:S(2)}) collective-permute-start(f32[1,512]{1,0:T(1,128)S(1)} %get-tuple-element.44), channel_id=1, source_target_pairs={{0,1},{1,0},{2,3},{3,2},{4,5},{5,4},{6,7},{7,6},{8,9},{9,8},{10,11... | collective-permute-start | bytes 6152 | tf_op jit(solution)/shard_map/ppermute | solution.py:466
  93.3 7.1 %collective-permute-start.27 = (f32[1,512]{1,0:T(1,128)S(1)}, f32[1,512]{1,0:T(1,128)S(1)}, u32[]{:S(2)}, u32[]{:S(2)}) collective-permute-start(f32[1,512]{1,0:T(1,128)S(1)} %add.9), channel_id=1, source_target_pairs={{0,2},{1,3},{2,0},{3,1},{4,6},{5,7},{6,4},{7,5},{8,10},{9,11},{10,... | collective-permute-start | bytes 6152 | tf_op jit(solution)/shard_map/ppermute | solution.py:466
  100.4 8.3 %collective-permute-start.28 = (f32[1,512]{1,0:T(1,128)S(1)}, f32[1,512]{1,0:T(1,128)S(1)}, u32[]{:S(2)}, u32[]{:S(2)}) collective-permute-start(f32[1,512]{1,0:T(1,128)S(1)} %add.10), channel_id=1, source_target_pairs={{0,4},{1,5},{2,6},{3,7},{4,0},{5,1},{6,2},{7,3},{8,12},{9,13},{10,... | collective-permute-start | bytes 6152 | tf_op jit(solution)/shard_map/ppermute | solution.py:466
  104.0 14.8 %collective-permute-start.29 = (bf16[256,512]{1,0:T(8,128)(2,1)S(1)}, bf16[256,512]{1,0:T(8,128)(2,1)S(1)}, u32[]{:S(2)}, u32[]{:S(2)}) collective-permute-start(bf16[256,512]{1,0:T(8,128)(2,1)S(1)} %get-tuple-element.47), channel_id=1, source_target_pairs={{0,8},{8,16},{16,24},{1,9},{9,17},{17,25},{2,10},{10,18},{18,26},{... | collective-permute-start | bytes 786440 | tf_op jit(solution)/shard_map/ppermute | solution.py:466
  107.4 11.4 %collective-permute-start.30 = (bf16[256,512]{1,0:T(8,128)(2,1)S(1)}, bf16[256,512]{1,0:T(8,128)(2,1)S(1)}, u32[]{:S(2)}, u32[]{:S(2)}) collective-permute-start(bf16[256,512]{1,0:T(8,128)(2,1)S(1)} %get-tuple-element.48), channel_id=1, source_target_pairs={{8,0},{16,8},{24,16},{9,1},{17,9},{25,17},{10,2},{18,10},{26,18},{... | collective-permute-start | bytes 786440 | tf_op jit(solution)/shard_map/ppermute | solution.py:466
  108.7 8.3 %collective-permute-start.31 = (f32[1,256]{1,0:T(1,128)S(1)}, f32[1,256]{1,0:T(1,128)S(1)}, u32[]{:S(2)}, u32[]{:S(2)}) collective-permute-start(f32[1,256]{1,0:T(1,128)S(1)} %get-tuple-element.50), channel_id=1, source_target_pairs={{0,8},{8,16},{16,24},{1,9},{9,17},{17,25},{2,10},{10,18},{18,26},{... | collective-permute-start | bytes 3080 | tf_op jit(solution)/shard_map/ppermute | solution.py:466
  113.3 5.5 %collective-permute-start.32 = (f32[1,256]{1,0:T(1,128)S(1)}, f32[1,256]{1,0:T(1,128)S(1)}, u32[]{:S(2)}, u32[]{:S(2)}) collective-permute-start(f32[1,256]{1,0:T(1,128)S(1)} %get-tuple-element.49), channel_id=1, source_target_pairs={{8,0},{16,8},{24,16},{9,1},{17,9},{25,17},{10,2},{18,10},{26,18},{... | collective-permute-start | bytes 3080 | tf_op jit(solution)/shard_map/ppermute | solution.py:466

commit v8 on v3

--- a/solution.py
+++ b/solution.py
@@ -171,43 +171,40 @@
     return jnp.where(first_is_high, 1 - high, high).astype(jnp.int32)
 
 
-def pack_kernel(n, slots_ref, ids_ref, q_ref, k_ref, v_ref, *rest):
-    outs, sem = rest[: 2 * n], rest[2 * n]
+def pack_kernel(n, high, slots_ref, ids_ref, q_ref, k_ref, v_ref, *rest):
+    outs, sem = rest[:n], rest[n]
     rank = ids_ref[0]
     rows = outs[0].shape[0] // 3
     wide = outs[0].shape[1]
+    half = half_index(slots_ref, ids_ref, high)
+    source_rows = pl.ds(pl.multiple_of(half * rows, rows), rows)
     copies = []
-    for high in range(2):
-        half = half_index(slots_ref, ids_ref, high)
-        source_rows = pl.ds(pl.multiple_of(half * rows, rows), rows)
-        for k in range(n):
-            cols = pl.ds(pl.multiple_of((rank ^ k) * wide, wide), wide)
-            for a, ref in enumerate((q_ref, k_ref, v_ref)):
-                copy = pltpu.make_async_copy(
-                    ref.at[source_rows, cols],
-                    outs[high * n + k].at[a * rows : (a + 1) * rows, :],
-                    sem.at[high * n + k, a],
-                )
-                copy.start()
-                copies.append(copy)
+    for k in range(n):
+        cols = pl.ds(pl.multiple_of((rank ^ k) * wide, wide), wide)
+        for a, ref in enumerate((q_ref, k_ref, v_ref)):
+            copy = pltpu.make_async_copy(
+                ref.at[source_rows, cols],
+                outs[k].at[a * rows : (a + 1) * rows, :],
+                sem.at[k, a],
+            )
+            copy.start()
+            copies.append(copy)
     for copy in copies:
         copy.wait()
 
 
-def pack(n, slots, ids, q, k, v):
-    rows, width = q.shape[0] // 2, q.shape[1]
+def pack(n, high, slots, ids, arrays):
+    rows, width = arrays[0].shape[0] // 2, arrays[0].shape[1]
     piece = jax.ShapeDtypeStruct((3 * rows, width // n), BF)
-    packed = pl.pallas_call(
-        functools.partial(pack_kernel, n),
-        out_shape=[piece] * (2 * n),
+    return pl.pallas_call(
+        functools.partial(pack_kernel, n, high),
+        out_shape=[piece] * n,
         in_specs=[sm(), sm()] + [pl.BlockSpec(memory_space=pltpu.HBM)] * 3,
-        out_specs=[vm()] * (2 * n),
-        scratch_shapes=[pltpu.SemaphoreType.DMA((2 * n, 3))],
+        out_specs=[vm()] * n,
+        scratch_shapes=[pltpu.SemaphoreType.DMA((n, 3))],
         compiler_params=params(8),
-        cost_estimate=cost(0, 24 * rows * width),
-        name="pack",
-    )(slots, ids, *(pltpu.with_memory_space_constraint(x, pltpu.HBM) for x in (q, k, v)))
-    return packed[:n], packed[n:]
+        cost_estimate=cost(0, 12 * rows * width),
+    )(slots, ids, *(pltpu.with_memory_space_constraint(x, pltpu.HBM) for x in arrays))
 
 
 def attend_kernel(n, high, rows, ids_ref, *refs):
@@ -524,9 +521,9 @@
     def exchange(pieces):
         return [pieces[0]] + [moved(pieces[k], "seq", xor_route(n, k)) for k in range(1, n)]
 
-    packed_low, packed_high = pack(n, slot_map, ids, queries, key_vecs, value_vecs)
-    low = exchange(packed_low)
-    high = exchange(packed_high)
+    inputs = (queries, key_vecs, value_vecs)
+    low = exchange(pack(n, 0, slot_map, ids, inputs))
+    high = exchange(pack(n, 1, slot_map, ids, inputs))
     spec = spectrum(filters, filter_len, forward)
 
     att_low = exchange(attend(n, 0, rows, ids, low))

time: 130 us -> 114 us (0.88)
  waiting for transfers between devices: 64 us -> 33.2 us
  starting transfers between devices: 43.6 us -> 56.9 us
  Pallas kernels: 20.1 us -> 21.6 us
    ppermute x37, waiting for transfers between devices: 64 us -> 33.2 us  [moved(): return lax.ppermute(block, axis, route)]
    ppermute x37, starting transfers between devices: 43.6 us -> 56.9 us  [moved(): return lax.ppermute(block, axis, route)]
    pallas_call x1 -> x2, Pallas kernels: 2.47 us -> 3.96 us  [pack(): pl.pallas_call(functools.partial(pack_kernel, n, high), out_shape=[piece]...]
  transfers between devices with their start and end apart: 37 -> 37, of which waited for: 17 -> 16; matrix products, arithmetic and copies ran while one was open for 0% -> 0% of each run, Pallas kernels for 9% -> 15%
where the time goes in v8:
time: 114 us; the launch traced here: 113 us
  starting transfers between devices  56.9 us (50%)
  waiting for transfers between devices  33.2 us (29%)
  Pallas kernels  21.6 us (19%)
    ppermute x37, starting transfers between devices, moved(): return lax.ppermute(block, axis, route)  56.9 us
    ppermute x37, waiting for transfers between devices, moved(): return lax.ppermute(block, axis, route)  33.2 us
    pallas_call x2, Pallas kernels, attend(): pl.pallas_call(functools.partial(attend_kernel, n, high, rows), out_shape...  5.9 us
    pallas_call x3, Pallas kernels, project(): pl.pallas_call(functools.partial(project_kernel, n, high, indices), out_s...  5.89 us
    pallas_call x2, Pallas kernels, pack(): pl.pallas_call(functools.partial(pack_kernel, n, high), out_shape=[piece]...  3.96 us
    pallas_call x1, Pallas kernels, fast_device(): pl.pallas_call(functools.partial(conv_high_kernel, n, model_width), out_s...  2.53 us
  transfers between devices with their start and end apart: 37, of which 16 were waited for; matrix products, arithmetic and copies ran while one was open for 0% of the time, Pallas kernels for 15%

profile of v8, /device:TPU:0, one launch (start us, length us, event | category | flops | bytes accessed | tf_op | source)
XLA Modules:
  0.0 113.3 jit_solution(5469082698303529235)
XLA Ops:
  0.0 0.1 pad_add_fusion.ids_ref
  0.1 0.7 copy-done.7
  0.7 1.8 %shard_map.136 = (bf16[768,128]{1,0:T(8,128)(2,1)S(1)}, bf16[768,128]{1,0:T(8,128)(2,1)S(1)}, bf16[768,128]{1,0:T(8,128)(2,1)S(1)}, bf16[768,128]{1,0:T(8,128)(2,1)S(1)}) custom-call(s32[8]{0:T(128)S(1)} %copy-done.7, s32[2]{0:T(128)S(1)} %pad_add_fusion.ids_ref, bf16[512,512]{1,0:T(8,128)(2,1)} %q_ref.3, bf16[512,512]{1,0:T(8,128)(2,1)} %k_ref.3, ...), custom_call_target="tpu_custom_call" | custom-call | bytes 1572864 | tf_op jit(solution)/shard_map/pallas_call | solution.py:199
  2.6 3.0 %collective-permute-start = (bf16[768,128]{1,0:T(8,128)(2,1)S(1)}, bf16[768,128]{1,0:T(8,128)(2,1)S(1)}, u32[]{:S(2)}, u32[]{:S(2)}) collective-permute-start(bf16[768,128]{1,0:T(8,128)(2,1)S(1)} %get-tuple-element.27), channel_id=1, source_target_pairs={{0,8},{8,0},{16,24},{24,16},{1,9},{9,1},{17,25},{25,17},{2,10},{10... | collective-permute-start | bytes 589832 | tf_op jit(solution)/shard_map/ppermute | solution.py:474
  5.6 1.5 %collective-permute-start.1 = (bf16[768,128]{1,0:T(8,128)(2,1)S(1)}, bf16[768,128]{1,0:T(8,128)(2,1)S(1)}, u32[]{:S(2)}, u32[]{:S(2)}) collective-permute-start(bf16[768,128]{1,0:T(8,128)(2,1)S(1)} %get-tuple-element.28), channel_id=1, source_target_pairs={{0,16},{8,24},{16,0},{24,8},{1,17},{9,25},{17,1},{25,9},{2,18},{10... | collective-permute-start | bytes 589832 | tf_op jit(solution)/shard_map/ppermute | solution.py:474
  7.1 0.1 collective-permute-start.2
  7.2 2.1 %shard_map.137 = (bf16[768,128]{1,0:T(8,128)(2,1)S(1)}, bf16[768,128]{1,0:T(8,128)(2,1)S(1)}, bf16[768,128]{1,0:T(8,128)(2,1)S(1)}, bf16[768,128]{1,0:T(8,128)(2,1)S(1)}) custom-call(s32[8]{0:T(128)S(1)} %copy-done.7, s32[2]{0:T(128)S(1)} %pad_add_fusion.ids_ref, bf16[512,512]{1,0:T(8,128)(2,1)} %q_ref.3, bf16[512,512]{1,0:T(8,128)(2,1)} %k_ref.3, ...), custom_call_target="tpu_custom_call" | custom-call | bytes 1572864 | tf_op jit(solution)/shard_map/pallas_call | solution.py:199
  9.3 1.7 %collective-permute-start.3 = (bf16[768,128]{1,0:T(8,128)(2,1)S(1)}, bf16[768,128]{1,0:T(8,128)(2,1)S(1)}, u32[]{:S(2)}, u32[]{:S(2)}) collective-permute-start(bf16[768,128]{1,0:T(8,128)(2,1)S(1)} %get-tuple-element.31), channel_id=1, source_target_pairs={{0,8},{8,0},{16,24},{24,16},{1,9},{9,1},{17,25},{25,17},{2,10},{10... | collective-permute-start | bytes 589832 | tf_op jit(solution)/shard_map/ppermute | solution.py:474
  11.0 1.5 %collective-permute-start.4 = (bf16[768,128]{1,0:T(8,128)(2,1)S(1)}, bf16[768,128]{1,0:T(8,128)(2,1)S(1)}, u32[]{:S(2)}, u32[]{:S(2)}) collective-permute-start(bf16[768,128]{1,0:T(8,128)(2,1)S(1)} %get-tuple-element.32), channel_id=1, source_target_pairs={{0,16},{8,24},{16,0},{24,8},{1,17},{9,25},{17,1},{25,9},{2,18},{10... | collective-permute-start | bytes 589832 | tf_op jit(solution)/shard_map/ppermute | solution.py:474
  12.5 1.8 %collective-permute-start.5 = (bf16[768,128]{1,0:T(8,128)(2,1)S(1)}, bf16[768,128]{1,0:T(8,128)(2,1)S(1)}, u32[]{:S(2)}, u32[]{:S(2)}) collective-permute-start(bf16[768,128]{1,0:T(8,128)(2,1)S(1)} %get-tuple-element.33), channel_id=1, source_target_pairs={{0,24},{8,16},{16,8},{24,0},{1,25},{9,17},{17,9},{25,1},{2,26},{10... | collective-permute-start | bytes 589832 | tf_op jit(solution)/shard_map/ppermute | solution.py:474
  14.3 2.3 %collective-permute-done.1.refs_2_ = bf16[768,128]{1,0:T(8,128)(2,1)S(1)} collective-permute-done((bf16[768,128]{1,0:T(8,128)(2,1)S(1)}, bf16[768,128]{1,0:T(8,128)(2,1)S(1)}, u32[]{:S(2)}, u32[]{:S(2)}) %collective-permute-start.1) | collective-permute-done | bytes 196640 | tf_op jit(solution)/shard_map/ppermute | solution.py:474
  16.6 0.5 collective-permute-done.2.refs_3_
  17.1 2.3 %attend_low.1 = (bf16[256,128]{1,0:T(8,128)(2,1)S(1)}, bf16[256,128]{1,0:T(8,128)(2,1)S(1)}, bf16[256,128]{1,0:T(8,128)(2,1)S(1)}, bf16[256,128]{1,0:T(8,128)(2,1)S(1)}) custom-call(s32[2]{0:T(128)S(1)} %pad_add_fusion.ids_ref, bf16[768,128]{1,0:T(8,128)(2,1)S(1)} %get-tuple-element.26.refs_0_, bf16[768,128]{1,0:T(8,128)(2,1)S(1)} %collective-permute-done.refs_1_, ...), custom_call_target="tpu_custom_call" | custom-call | flops 335544320 | bytes 1048576 | tf_op jit(solution)/shard_map/attend_low/pallas_call | solution.py:271
  19.4 1.6 %collective-permute-start.22 = (bf16[256,128]{1,0:T(8,128)(2,1)S(1)}, bf16[256,128]{1,0:T(8,128)(2,1)S(1)}, u32[]{:S(2)}, u32[]{:S(2)}) collective-permute-start(bf16[256,128]{1,0:T(8,128)(2,1)S(1)} %get-tuple-element.42), channel_id=1, source_target_pairs={{0,8},{8,0},{16,24},{24,16},{1,9},{9,1},{17,25},{25,17},{2,10},{10... | collective-permute-start | bytes 196616 | tf_op jit(solution)/shard_map/ppermute | solution.py:474
  21.0 0.6 collective-permute-start.23
  21.6 1.5 %collective-permute-start.24 = (bf16[256,128]{1,0:T(8,128)(2,1)S(1)}, bf16[256,128]{1,0:T(8,128)(2,1)S(1)}, u32[]{:S(2)}, u32[]{:S(2)}) collective-permute-start(bf16[256,128]{1,0:T(8,128)(2,1)S(1)} %get-tuple-element.44), channel_id=1, source_target_pairs={{0,24},{8,16},{16,8},{24,0},{1,25},{9,17},{17,9},{25,1},{2,26},{10... | collective-permute-start | bytes 196616 | tf_op jit(solution)/shard_map/ppermute | solution.py:474
  23.0 2.0 %collective-permute-done.4.refs_6_ = bf16[768,128]{1,0:T(8,128)(2,1)S(1)} collective-permute-done((bf16[768,128]{1,0:T(8,128)(2,1)S(1)}, bf16[768,128]{1,0:T(8,128)(2,1)S(1)}, u32[]{:S(2)}, u32[]{:S(2)}) %collective-permute-start.4) | collective-permute-done | bytes 196640 | tf_op jit(solution)/shard_map/ppermute | solution.py:474
  25.1 0.5 collective-permute-done.5.refs_7_
  25.6 3.6 %attend_high.1 = (bf16[256,128]{1,0:T(8,128)(2,1)S(1)}, bf16[256,128]{1,0:T(8,128)(2,1)S(1)}, bf16[256,128]{1,0:T(8,128)(2,1)S(1)}, bf16[256,128]{1,0:T(8,128)(2,1)S(1)}) custom-call(s32[2]{0:T(128)S(1)} %pad_add_fusion.ids_ref, bf16[768,128]{1,0:T(8,128)(2,1)S(1)} %get-tuple-element.26.refs_0_, bf16[768,128]{1,0:T(8,128)(2,1)S(1)} %collective-permute-done.refs_1_, ...), custom_call_target="tpu_custom_call" | custom-call | flops 872415232 | bytes 2097152 | tf_op jit(solution)/shard_map/attend_high/pallas_call | solution.py:271
  29.2 1.6 %collective-permute-start.6 = (bf16[256,128]{1,0:T(8,128)(2,1)S(1)}, bf16[256,128]{1,0:T(8,128)(2,1)S(1)}, u32[]{:S(2)}, u32[]{:S(2)}) collective-permute-start(bf16[256,128]{1,0:T(8,128)(2,1)S(1)} %get-tuple-element.35), channel_id=1, source_target_pairs={{0,8},{8,0},{16,24},{24,16},{1,9},{9,1},{17,25},{25,17},{2,10},{10... | collective-permute-start | bytes 196616 | tf_op jit(solution)/shard_map/ppermute | solution.py:474
  30.7 0.6 collective-permute-start.7
  31.4 1.4 %collective-permute-start.8 = (bf16[256,128]{1,0:T(8,128)(2,1)S(1)}, bf16[256,128]{1,0:T(8,128)(2,1)S(1)}, u32[]{:S(2)}, u32[]{:S(2)}) collective-permute-start(bf16[256,128]{1,0:T(8,128)(2,1)S(1)} %get-tuple-element.37), channel_id=1, source_target_pairs={{0,24},{8,16},{16,8},{24,0},{1,25},{9,17},{17,9},{25,1},{2,26},{10... | collective-permute-start | bytes 196616 | tf_op jit(solution)/shard_map/ppermute | solution.py:474
  32.9 2.7 %collective-permute-start.28 = (bf16[1024,128]{1,0:T(8,128)(2,1)S(1)}, bf16[1024,128]{1,0:T(8,128)(2,1)S(1)}, u32[]{:S(2)}, u32[]{:S(2)}) collective-permute-start(bf16[1024,128]{1,0:T(8,128)(2,1)S(1)} %constant_dynamic-update-slice_fusion.4.refs_0_), channel_id=1, source_target_pairs={{0,4},{1,5},{2,6},{3,7},{4,0},{5,1},{6,2},{7,3},{8,12},{9,13},{10,... | collective-permute-start | bytes 786440 | tf_op jit(solution)/shard_map/ppermute | solution.py:474
  35.5 0.7 collective-permute-start.30
  36.2 2.9 %collective-permute-start.26 = (bf16[1024,128]{1,0:T(8,128)(2,1)S(1)}, bf16[1024,128]{1,0:T(8,128)(2,1)S(1)}, u32[]{:S(2)}, u32[]{:S(2)}) collective-permute-start(bf16[1024,128]{1,0:T(8,128)(2,1)S(1)} %constant_dynamic-update-slice_fusion.4.refs_0_), channel_id=1, source_target_pairs={{0,2},{1,3},{2,0},{3,1},{4,6},{5,7},{6,4},{7,5},{8,10},{9,11},{10,... | collective-permute-start | bytes 786440 | tf_op jit(solution)/shard_map/ppermute | solution.py:474
  39.1 0.1 collective-permute-start.25
  39.3 1.5 %collective-permute-start.12 = (bf16[1024,128]{1,0:T(8,128)(2,1)S(1)}, bf16[1024,128]{1,0:T(8,128)(2,1)S(1)}, u32[]{:S(2)}, u32[]{:S(2)}) collective-permute-start(bf16[1024,128]{1,0:T(8,128)(2,1)S(1)} %constant_dynamic-update-slice_fusion.refs_0_), channel_id=1, source_target_pairs={{0,4},{1,5},{2,6},{3,7},{4,0},{5,1},{6,2},{7,3},{8,12},{9,13},{10,... | collective-permute-start | bytes 786440 | tf_op jit(solution)/shard_map/ppermute | solution.py:474
  40.8 6.4 %collective-permute-done.28.refs_4_ = bf16[1024,128]{1,0:T(8,128)(2,1)S(1)} collective-permute-done((bf16[1024,128]{1,0:T(8,128)(2,1)S(1)}, bf16[1024,128]{1,0:T(8,128)(2,1)S(1)}, u32[]{:S(2)}, u32[]{:S(2)}) %collective-permute-start.28) | collective-permute-done | bytes 262176 | tf_op jit(solution)/shard_map/ppermute | solution.py:474
  47.2 1.3 %collective-permute-start.31 = (bf16[1024,128]{1,0:T(8,128)(2,1)S(1)}, bf16[1024,128]{1,0:T(8,128)(2,1)S(1)}, u32[]{:S(2)}, u32[]{:S(2)}) collective-permute-start(bf16[1024,128]{1,0:T(8,128)(2,1)S(1)} %collective-permute-done.28.refs_4_), channel_id=1, source_target_pairs={{2,0},{3,1},{4,6},{5,7},{10,8},{11,9},{12,14},{13,15},{18,16},{19,... | collective-permute-start | bytes 786440 | tf_op jit(solution)/shard_map/ppermute | solution.py:474
  48.5 0.7 collective-permute-start.14
  49.2 13.0 %collective-permute-start.10 = (bf16[1024,128]{1,0:T(8,128)(2,1)S(1)}, bf16[1024,128]{1,0:T(8,128)(2,1)S(1)}, u32[]{:S(2)}, u32[]{:S(2)}) collective-permute-start(bf16[1024,128]{1,0:T(8,128)(2,1)S(1)} %constant_dynamic-update-slice_fusion.refs_0_), channel_id=1, source_target_pairs={{0,2},{1,3},{2,0},{3,1},{4,6},{5,7},{6,4},{7,5},{8,10},{9,11},{10,... | collective-permute-start | bytes 786440 | tf_op jit(solution)/shard_map/ppermute | solution.py:474
  62.3 0.5 collective-permute-done.12.refs_4_
  62.8 1.3 %collective-permute-start.15 = (bf16[1024,128]{1,0:T(8,128)(2,1)S(1)}, bf16[1024,128]{1,0:T(8,128)(2,1)S(1)}, u32[]{:S(2)}, u32[]{:S(2)}) collective-permute-start(bf16[1024,128]{1,0:T(8,128)(2,1)S(1)} %collective-permute-done.12.refs_4_), channel_id=1, source_target_pairs={{2,0},{3,1},{4,6},{5,7},{10,8},{11,9},{12,14},{13,15},{18,16},{19,... | collective-permute-start | bytes 786440 | tf_op jit(solution)/shard_map/ppermute | solution.py:474
  64.1 0.7 collective-permute-done.31
  64.8 0.1 add.28.refs_6_
  64.9 0.6 collective-permute-start.32
  65.5 5.0 %collective-permute-done.10.refs_2_ = bf16[1024,128]{1,0:T(8,128)(2,1)S(1)} collective-permute-done((bf16[1024,128]{1,0:T(8,128)(2,1)S(1)}, bf16[1024,128]{1,0:T(8,128)(2,1)S(1)}, u32[]{:S(2)}, u32[]{:S(2)}) %collective-permute-start.10) | collective-permute-done | bytes 262176 | tf_op jit(solution)/shard_map/ppermute | solution.py:474
  70.4 0.5 collective-permute-start.11
  70.9 3.5 %collective-permute-done.15 = bf16[1024,128]{1,0:T(8,128)(2,1)S(1)} collective-permute-done((bf16[1024,128]{1,0:T(8,128)(2,1)S(1)}, bf16[1024,128]{1,0:T(8,128)(2,1)S(1)}, u32[]{:S(2)}, u32[]{:S(2)}) %collective-permute-start.15) | collective-permute-done | bytes 262176 | tf_op jit(solution)/shard_map/ppermute | solution.py:474
  74.5 0.1 add.24.refs_0_
  74.6 0.6 collective-permute-start.16
  75.2 2.6 %shard_map.140 = (f32[256,512]{1,0:T(8,128)S(1)}, bf16[256,512]{1,0:T(8,128)(2,1)}, f32[1,256]{1,0:T(1,128)S(1)}) custom-call(s32[8]{0:T(128)S(1)} %copy-done.8, s32[2]{0:T(128)S(1)} %pad_add_fusion.ids_ref, bf16[512,512]{1,0:T(8,128)(2,1)S(1)} %copy-done.5, bf16[4096,512]{1,0:T(8,128)(2,1)S(1)} %copy-done, ...), custom_call_target="tpu_custom_call" | custom-call | flops 1073741824 | bytes 6291456 | tf_op jit(solution)/shard_map/pallas_call | solution.py:324
  77.8 1.1 collective-permute-done.33
  78.9 3.6 %collective-permute-done.34 = f32[1,256]{1,0:T(1,128)S(1)} collective-permute-done((f32[1,256]{1,0:T(1,128)S(1)}, f32[1,256]{1,0:T(1,128)S(1)}, u32[]{:S(2)}, u32[]{:S(2)}) %collective-permute-start.34) | collective-permute-done | bytes 1056 | tf_op jit(solution)/shard_map/ppermute | solution.py:474
  82.5 3.1 %collective-permute-start.35 = (f32[1,256]{1,0:T(1,128)S(1)}, f32[1,256]{1,0:T(1,128)S(1)}, u32[]{:S(2)}, u32[]{:S(2)}) collective-permute-start(f32[1,256]{1,0:T(1,128)S(1)} %add.30), channel_id=1, source_target_pairs={{0,4},{1,5},{2,6},{3,7},{4,0},{5,1},{6,2},{7,3},{8,12},{9,13},{10,... | collective-permute-start | bytes 3080 | tf_op jit(solution)/shard_map/ppermute | solution.py:474
  85.6 1.6 %collective-permute-done.35 = f32[1,256]{1,0:T(1,128)S(1)} collective-permute-done((f32[1,256]{1,0:T(1,128)S(1)}, f32[1,256]{1,0:T(1,128)S(1)}, u32[]{:S(2)}, u32[]{:S(2)}) %collective-permute-start.35) | collective-permute-done | bytes 1056 | tf_op jit(solution)/shard_map/ppermute | solution.py:474
  87.1 0.1 shard_map.141.own_ref.low_ref
  87.3 3.4 %collective-permute-start.36 = (bf16[256,512]{1,0:T(8,128)(2,1)S(1)}, bf16[256,512]{1,0:T(8,128)(2,1)S(1)}, u32[]{:S(2)}, u32[]{:S(2)}) collective-permute-start(bf16[256,512]{1,0:T(8,128)(2,1)S(1)} %shard_map.141.own_ref.low_ref), channel_id=1, source_target_pairs={{0,8},{8,16},{16,24},{1,9},{9,17},{17,25},{2,10},{10,18},{18,26},{... | collective-permute-start | bytes 786440 | tf_op jit(solution)/shard_map/ppermute | solution.py:474
  90.7 1.6 %shard_map.138.base_ref = f32[256,512]{1,0:T(8,128)S(1)} custom-call(s32[8]{0:T(128)S(1)} %copy-done.8, s32[2]{0:T(128)S(1)} %pad_add_fusion.ids_ref, bf16[512,512]{1,0:T(8,128)(2,1)S(1)} %copy-done.5, bf16[4096,512]{1,0:T(8,128)(2,1)S(1)} %copy-done, bf16[1024,128]{1,0:T(8,128)(2,1)S(1)} %constant_dynamic-update-slice_fusion.refs_0_, ...), custom_call_target="tpu_custom_call" | custom-call | flops 805306368 | bytes 6291456 | tf_op jit(solution)/shard_map/pallas_call | solution.py:324
  92.4 1.7 %shard_map.139 = (f32[256,512]{1,0:T(8,128)S(1)}, bf16[256,512]{1,0:T(8,128)(2,1)}, f32[1,256]{1,0:T(1,128)S(1)}) custom-call(s32[8]{0:T(128)S(1)} %copy-done.8, s32[2]{0:T(128)S(1)} %pad_add_fusion.ids_ref, f32[256,512]{1,0:T(8,128)S(1)} %shard_map.138.base_ref, bf16[4096,512]{1,0:T(8,128)(2,1)S(1)} %copy-done, bf16[1024,128]{1,0:T(8,128)(2,1)S(1)} %add.24.refs_0_, ...), custom_call_target="tpu_custom_call" | custom-call | flops 268435456 | bytes 6291456 | tf_op jit(solution)/shard_map/pallas_call | solution.py:324
  94.1 1.3 %collective-permute-start.20 = (bf16[256,512]{1,0:T(8,128)(2,1)}, bf16[256,512]{1,0:T(8,128)(2,1)S(1)}, u32[]{:S(2)}, u32[]{:S(2)}) collective-permute-start(bf16[256,512]{1,0:T(8,128)(2,1)} %get-tuple-element.40), channel_id=1, source_target_pairs={{8,0},{16,8},{24,16},{9,1},{17,9},{25,17},{10,2},{18,10},{26,18},{... | collective-permute-start | bytes 786440 | tf_op jit(solution)/shard_map/ppermute | solution.py:474
  95.4 0.1 collective-permute-start.17
  95.5 1.1 %collective-permute-done.17 = f32[1,256]{1,0:T(1,128)S(1)} collective-permute-done((f32[1,256]{1,0:T(1,128)S(1)}, f32[1,256]{1,0:T(1,128)S(1)}, u32[]{:S(2)}, u32[]{:S(2)}) %collective-permute-start.17) | collective-permute-done | bytes 1056 | tf_op jit(solution)/shard_map/ppermute | solution.py:474
  96.7 2.0 %collective-permute-start.18 = (f32[1,256]{1,0:T(1,128)S(1)}, f32[1,256]{1,0:T(1,128)S(1)}, u32[]{:S(2)}, u32[]{:S(2)}) collective-permute-start(f32[1,256]{1,0:T(1,128)S(1)} %add.25), channel_id=1, source_target_pairs={{0,2},{1,3},{2,0},{3,1},{4,6},{5,7},{6,4},{7,5},{8,10},{9,11},{10,... | collective-permute-start | bytes 3080 | tf_op jit(solution)/shard_map/ppermute | solution.py:474
  98.7 0.1 copy.15.len_ref
  98.8 1.4 %collective-permute-done.18 = f32[1,256]{1,0:T(1,128)S(1)} collective-permute-done((f32[1,256]{1,0:T(1,128)S(1)}, f32[1,256]{1,0:T(1,128)S(1)}, u32[]{:S(2)}, u32[]{:S(2)}) %collective-permute-start.18) | collective-permute-done | bytes 1056 | tf_op jit(solution)/shard_map/ppermute | solution.py:474
  100.2 2.9 %collective-permute-start.19 = (f32[1,256]{1,0:T(1,128)S(1)}, f32[1,256]{1,0:T(1,128)S(1)}, u32[]{:S(2)}, u32[]{:S(2)}) collective-permute-start(f32[1,256]{1,0:T(1,128)S(1)} %add.26), channel_id=1, source_target_pairs={{0,4},{1,5},{2,6},{3,7},{4,0},{5,1},{6,2},{7,3},{8,12},{9,13},{10,... | collective-permute-start | bytes 3080 | tf_op jit(solution)/shard_map/ppermute | solution.py:474
  103.2 0.5 spectrum.1.spec_ref
  103.7 1.0 collective-permute-done.19
  104.7 1.5 %collective-permute-start.21 = (f32[1,256]{1,0:T(1,128)S(1)}, f32[1,256]{1,0:T(1,128)S(1)}, u32[]{:S(2)}, u32[]{:S(2)}) collective-permute-start(f32[1,256]{1,0:T(1,128)S(1)} %add.27.sq_ref), channel_id=1, source_target_pairs={{8,0},{16,8},{24,16},{9,1},{17,9},{25,17},{10,2},{18,10},{26,18},{... | collective-permute-start | bytes 3080 | tf_op jit(solution)/shard_map/ppermute | solution.py:474
  106.2 1.2 %conv_own.1.part_ref = f32[256,512]{1,0:T(8,128)S(1)} custom-call(f32[256,512]{1,0:T(8,128)S(1)} %get-tuple-element.38.res_ref, f32[1,256]{1,0:T(1,128)S(1)} %add.27.sq_ref, f32[512,512]{1,0:T(8,128)S(1)} %spectrum.1.spec_ref, f32[1,512]{1,0:T(1,128)S(1)} %bitcast.6, f32[1,512]{1,0:T(1,128)S(1)} %bitcast.8, bf16[512,256]{1,0:T(8,128)(2,1)S(1)} %copy-done.1, ...), custom_call_target="tpu_custom_call" | custom-call | flops 335544320 | bytes 1572864 | tf_op jit(solution)/shard_map/conv_own/pallas_call | solution.py:559
  107.5 1.4 %conv_low.1.done_ref = bf16[256,512]{1,0:T(8,128)(2,1)S(1)} custom-call(f32[256,512]{1,0:T(8,128)S(1)} %get-tuple-element.45.res_ref, bf16[256,512]{1,0:T(8,128)(2,1)S(1)} %shard_map.141.own_ref.low_ref, bf16[256,512]{1,0:T(8,128)(2,1)S(1)} %collective-permute-done.36.before_ref, f32[512,512]{1,0:T(8,128)S(1)} %spectrum.1.spec_ref, f32[1,512]{1,0:T(1,128)S(1)} %bitcast.9, ...), custom_call_target="tpu_custom_call" | custom-call | flops 469762048 | bytes 1572864 | tf_op jit(solution)/shard_map/conv_low/pallas_call | solution.py:539
  108.9 1.9 %collective-permute-done.21.raw_sq_ref = f32[1,256]{1,0:T(1,128)S(1)} collective-permute-done((f32[1,256]{1,0:T(1,128)S(1)}, f32[1,256]{1,0:T(1,128)S(1)}, u32[]{:S(2)}, u32[]{:S(2)}) %collective-permute-start.21) | collective-permute-done | bytes 1056 | tf_op jit(solution)/shard_map/ppermute | solution.py:474
  110.8 2.5 %conv_high.1 = bf16[512,512]{1,0:T(8,128)(2,1)} custom-call(s32[8]{0:T(128)S(1)} %copy-done.8, s32[2]{0:T(128)S(1)} %pad_add_fusion.ids_ref, f32[256,512]{1,0:T(8,128)S(1)} %conv_own.1.part_ref, bf16[256,512]{1,0:T(8,128)(2,1)S(1)} %collective-permute-done.20.raw_ref, f32[1,256]{1,0:T(1,128)S(1)} %collective-permute-done.21.raw_sq_ref, ...), custom_call_target="tpu_custom_call" | custom-call | flops 335544320 | bytes 1572864 | tf_op jit(solution)/shard_map/conv_high/pallas_call | solution.py:568
  (64 shorter events, 0.3 us)
Async XLA Ops:
  0.1 0.7 copy-start.7
  2.6 10.0 %collective-permute-start = (bf16[768,128]{1,0:T(8,128)(2,1)S(1)}, bf16[768,128]{1,0:T(8,128)(2,1)S(1)}, u32[]{:S(2)}, u32[]{:S(2)}) collective-permute-start(bf16[768,128]{1,0:T(8,128)(2,1)S(1)} %get-tuple-element.27), channel_id=1, source_target_pairs={{0,8},{8,0},{16,24},{24,16},{1,9},{9,1},{17,25},{25,17},{2,10},{10... | collective-permute-start | bytes 589832 | tf_op jit(solution)/shard_map/ppermute | solution.py:474
  5.6 11.0 %collective-permute-start.1 = (bf16[768,128]{1,0:T(8,128)(2,1)S(1)}, bf16[768,128]{1,0:T(8,128)(2,1)S(1)}, u32[]{:S(2)}, u32[]{:S(2)}) collective-permute-start(bf16[768,128]{1,0:T(8,128)(2,1)S(1)} %get-tuple-element.28), channel_id=1, source_target_pairs={{0,16},{8,24},{16,0},{24,8},{1,17},{9,25},{17,1},{25,9},{2,18},{10... | collective-permute-start | bytes 589832 | tf_op jit(solution)/shard_map/ppermute | solution.py:474
  7.1 68.0 %copy-start = (bf16[4096,512]{1,0:T(8,128)(2,1)S(1)}, bf16[4096,512]{1,0:T(8,128)(2,1)}, u32[]{:S(2)}) copy-start(bf16[4096,512]{1,0:T(8,128)(2,1)} %w_ref.5) | copy-start | bytes 12582916
  7.1 68.0 %copy-start.5 = (bf16[512,512]{1,0:T(8,128)(2,1)S(1)}, bf16[512,512]{1,0:T(8,128)(2,1)}, u32[]{:S(2)}) copy-start(bf16[512,512]{1,0:T(8,128)(2,1)} %base_ref.3) | copy-start | bytes 1572868
  7.1 68.0 %copy-start.8 = (s32[8]{0:T(128)S(1)}, s32[8]{0:T(128)}, u32[]{:S(2)}) copy-start(s32[8]{0:T(128)} %slots_ref.11) | copy-start | bytes 100
  7.1 10.0 %collective-permute-start.2 = (bf16[768,128]{1,0:T(8,128)(2,1)S(1)}, bf16[768,128]{1,0:T(8,128)(2,1)S(1)}, u32[]{:S(2)}, u32[]{:S(2)}) collective-permute-start(bf16[768,128]{1,0:T(8,128)(2,1)S(1)} %get-tuple-element.29), channel_id=1, source_target_pairs={{0,24},{8,16},{16,8},{24,0},{1,25},{9,17},{17,9},{25,1},{2,26},{10... | collective-permute-start | bytes 589832 | tf_op jit(solution)/shard_map/ppermute | solution.py:474
  9.3 12.3 %collective-permute-start.3 = (bf16[768,128]{1,0:T(8,128)(2,1)S(1)}, bf16[768,128]{1,0:T(8,128)(2,1)S(1)}, u32[]{:S(2)}, u32[]{:S(2)}) collective-permute-start(bf16[768,128]{1,0:T(8,128)(2,1)S(1)} %get-tuple-element.31), channel_id=1, source_target_pairs={{0,8},{8,0},{16,24},{24,16},{1,9},{9,1},{17,25},{25,17},{2,10},{10... | collective-permute-start | bytes 589832 | tf_op jit(solution)/shard_map/ppermute | solution.py:474
  11.0 14.0 %collective-permute-start.4 = (bf16[768,128]{1,0:T(8,128)(2,1)S(1)}, bf16[768,128]{1,0:T(8,128)(2,1)S(1)}, u32[]{:S(2)}, u32[]{:S(2)}) collective-permute-start(bf16[768,128]{1,0:T(8,128)(2,1)S(1)} %get-tuple-element.32), channel_id=1, source_target_pairs={{0,16},{8,24},{16,0},{24,8},{1,17},{9,25},{17,1},{25,9},{2,18},{10... | collective-permute-start | bytes 589832 | tf_op jit(solution)/shard_map/ppermute | solution.py:474
  12.5 13.0 %collective-permute-start.5 = (bf16[768,128]{1,0:T(8,128)(2,1)S(1)}, bf16[768,128]{1,0:T(8,128)(2,1)S(1)}, u32[]{:S(2)}, u32[]{:S(2)}) collective-permute-start(bf16[768,128]{1,0:T(8,128)(2,1)S(1)} %get-tuple-element.33), channel_id=1, source_target_pairs={{0,24},{8,16},{16,8},{24,0},{1,25},{9,17},{17,9},{25,1},{2,26},{10... | collective-permute-start | bytes 589832 | tf_op jit(solution)/shard_map/ppermute | solution.py:474
  19.4 12.0 %collective-permute-start.22 = (bf16[256,128]{1,0:T(8,128)(2,1)S(1)}, bf16[256,128]{1,0:T(8,128)(2,1)S(1)}, u32[]{:S(2)}, u32[]{:S(2)}) collective-permute-start(bf16[256,128]{1,0:T(8,128)(2,1)S(1)} %get-tuple-element.42), channel_id=1, source_target_pairs={{0,8},{8,0},{16,24},{24,16},{1,9},{9,1},{17,25},{25,17},{2,10},{10... | collective-permute-start | bytes 196616 | tf_op jit(solution)/shard_map/ppermute | solution.py:474
  21.0 11.9 %collective-permute-start.23 = (bf16[256,128]{1,0:T(8,128)(2,1)S(1)}, bf16[256,128]{1,0:T(8,128)(2,1)S(1)}, u32[]{:S(2)}, u32[]{:S(2)}) collective-permute-start(bf16[256,128]{1,0:T(8,128)(2,1)S(1)} %get-tuple-element.43), channel_id=1, source_target_pairs={{0,16},{8,24},{16,0},{24,8},{1,17},{9,25},{17,1},{25,9},{2,18},{10... | collective-permute-start | bytes 196616 | tf_op jit(solution)/shard_map/ppermute | solution.py:474
  21.6 11.3 %collective-permute-start.24 = (bf16[256,128]{1,0:T(8,128)(2,1)S(1)}, bf16[256,128]{1,0:T(8,128)(2,1)S(1)}, u32[]{:S(2)}, u32[]{:S(2)}) collective-permute-start(bf16[256,128]{1,0:T(8,128)(2,1)S(1)} %get-tuple-element.44), channel_id=1, source_target_pairs={{0,24},{8,16},{16,8},{24,0},{1,25},{9,17},{17,9},{25,1},{2,26},{10... | collective-permute-start | bytes 196616 | tf_op jit(solution)/shard_map/ppermute | solution.py:474
  29.2 7.0 %collective-permute-start.6 = (bf16[256,128]{1,0:T(8,128)(2,1)S(1)}, bf16[256,128]{1,0:T(8,128)(2,1)S(1)}, u32[]{:S(2)}, u32[]{:S(2)}) collective-permute-start(bf16[256,128]{1,0:T(8,128)(2,1)S(1)} %get-tuple-element.35), channel_id=1, source_target_pairs={{0,8},{8,0},{16,24},{24,16},{1,9},{9,1},{17,25},{25,17},{2,10},{10... | collective-permute-start | bytes 196616 | tf_op jit(solution)/shard_map/ppermute | solution.py:474
  30.7 8.4 %collective-permute-start.7 = (bf16[256,128]{1,0:T(8,128)(2,1)S(1)}, bf16[256,128]{1,0:T(8,128)(2,1)S(1)}, u32[]{:S(2)}, u32[]{:S(2)}) collective-permute-start(bf16[256,128]{1,0:T(8,128)(2,1)S(1)} %get-tuple-element.36), channel_id=1, source_target_pairs={{0,16},{8,24},{16,0},{24,8},{1,17},{9,25},{17,1},{25,9},{2,18},{10... | collective-permute-start | bytes 196616 | tf_op jit(solution)/shard_map/ppermute | solution.py:474
  31.4 7.9 %collective-permute-start.8 = (bf16[256,128]{1,0:T(8,128)(2,1)S(1)}, bf16[256,128]{1,0:T(8,128)(2,1)S(1)}, u32[]{:S(2)}, u32[]{:S(2)}) collective-permute-start(bf16[256,128]{1,0:T(8,128)(2,1)S(1)} %get-tuple-element.37), channel_id=1, source_target_pairs={{0,24},{8,16},{16,8},{24,0},{1,25},{9,17},{17,9},{25,1},{2,26},{10... | collective-permute-start | bytes 196616 | tf_op jit(solution)/shard_map/ppermute | solution.py:474
  32.9 14.3 %collective-permute-start.28 = (bf16[1024,128]{1,0:T(8,128)(2,1)S(1)}, bf16[1024,128]{1,0:T(8,128)(2,1)S(1)}, u32[]{:S(2)}, u32[]{:S(2)}) collective-permute-start(bf16[1024,128]{1,0:T(8,128)(2,1)S(1)} %constant_dynamic-update-slice_fusion.4.refs_0_), channel_id=1, source_target_pairs={{0,4},{1,5},{2,6},{3,7},{4,0},{5,1},{6,2},{7,3},{8,12},{9,13},{10,... | collective-permute-start | bytes 786440 | tf_op jit(solution)/shard_map/ppermute | solution.py:474
  35.5 13.0 %collective-permute-start.30 = (bf16[1024,128]{1,0:T(8,128)(2,1)S(1)}, bf16[1024,128]{1,0:T(8,128)(2,1)S(1)}, u32[]{:S(2)}, u32[]{:S(2)}) collective-permute-start(bf16[1024,128]{1,0:T(8,128)(2,1)S(1)} %constant_dynamic-update-slice_fusion.4.refs_0_), channel_id=1, source_target_pairs={{2,4},{3,5},{4,2},{5,3},{10,12},{11,13},{12,10},{13,11},{18,20},{1... | collective-permute-start | bytes 786440 | tf_op jit(solution)/shard_map/ppermute | solution.py:474
  36.2 13.0 %collective-permute-start.26 = (bf16[1024,128]{1,0:T(8,128)(2,1)S(1)}, bf16[1024,128]{1,0:T(8,128)(2,1)S(1)}, u32[]{:S(2)}, u32[]{:S(2)}) collective-permute-start(bf16[1024,128]{1,0:T(8,128)(2,1)S(1)} %constant_dynamic-update-slice_fusion.4.refs_0_), channel_id=1, source_target_pairs={{0,2},{1,3},{2,0},{3,1},{4,6},{5,7},{6,4},{7,5},{8,10},{9,11},{10,... | collective-permute-start | bytes 786440 | tf_op jit(solution)/shard_map/ppermute | solution.py:474
  39.1 23.1 %collective-permute-start.25 = (bf16[1024,128]{1,0:T(8,128)(2,1)S(1)}, bf16[1024,128]{1,0:T(8,128)(2,1)S(1)}, u32[]{:S(2)}, u32[]{:S(2)}) collective-permute-start(bf16[1024,128]{1,0:T(8,128)(2,1)S(1)} %constant_dynamic-update-slice_fusion.4.refs_0_), channel_id=1, source_target_pairs={{0,1},{1,0},{2,3},{3,2},{4,5},{5,4},{6,7},{7,6},{8,9},{9,8},{10,11... | collective-permute-start | bytes 786440 | tf_op jit(solution)/shard_map/ppermute | solution.py:474
  39.3 47.9 %copy-start.9 = (f32[512]{0:T(512)S(1)}, f32[512]{0:T(512)}, u32[]{:S(2)}) copy-start(f32[512]{0:T(512)} %param.19) | copy-start | bytes 6148
  39.3 23.5 %collective-permute-start.12 = (bf16[1024,128]{1,0:T(8,128)(2,1)S(1)}, bf16[1024,128]{1,0:T(8,128)(2,1)S(1)}, u32[]{:S(2)}, u32[]{:S(2)}) collective-permute-start(bf16[1024,128]{1,0:T(8,128)(2,1)S(1)} %constant_dynamic-update-slice_fusion.refs_0_), channel_id=1, source_target_pairs={{0,4},{1,5},{2,6},{3,7},{4,0},{5,1},{6,2},{7,3},{8,12},{9,13},{10,... | collective-permute-start | bytes 786440 | tf_op jit(solution)/shard_map/ppermute | solution.py:474
  47.2 17.6 %collective-permute-start.31 = (bf16[1024,128]{1,0:T(8,128)(2,1)S(1)}, bf16[1024,128]{1,0:T(8,128)(2,1)S(1)}, u32[]{:S(2)}, u32[]{:S(2)}) collective-permute-start(bf16[1024,128]{1,0:T(8,128)(2,1)S(1)} %collective-permute-done.28.refs_4_), channel_id=1, source_target_pairs={{2,0},{3,1},{4,6},{5,7},{10,8},{11,9},{12,14},{13,15},{18,16},{19,... | collective-permute-start | bytes 786440 | tf_op jit(solution)/shard_map/ppermute | solution.py:474
  48.5 16.4 %collective-permute-start.14 = (bf16[1024,128]{1,0:T(8,128)(2,1)S(1)}, bf16[1024,128]{1,0:T(8,128)(2,1)S(1)}, u32[]{:S(2)}, u32[]{:S(2)}) collective-permute-start(bf16[1024,128]{1,0:T(8,128)(2,1)S(1)} %constant_dynamic-update-slice_fusion.refs_0_), channel_id=1, source_target_pairs={{2,4},{3,5},{4,2},{5,3},{10,12},{11,13},{12,10},{13,11},{18,20},{1... | collective-permute-start | bytes 786440 | tf_op jit(solution)/shard_map/ppermute | solution.py:474
  49.2 21.2 %collective-permute-start.10 = (bf16[1024,128]{1,0:T(8,128)(2,1)S(1)}, bf16[1024,128]{1,0:T(8,128)(2,1)S(1)}, u32[]{:S(2)}, u32[]{:S(2)}) collective-permute-start(bf16[1024,128]{1,0:T(8,128)(2,1)S(1)} %constant_dynamic-update-slice_fusion.refs_0_), channel_id=1, source_target_pairs={{0,2},{1,3},{2,0},{3,1},{4,6},{5,7},{6,4},{7,5},{8,10},{9,11},{10,... | collective-permute-start | bytes 786440 | tf_op jit(solution)/shard_map/ppermute | solution.py:474
  62.3 8.2 %collective-permute-start.27 = (bf16[1024,128]{1,0:T(8,128)(2,1)S(1)}, bf16[1024,128]{1,0:T(8,128)(2,1)S(1)}, u32[]{:S(2)}, u32[]{:S(2)}) collective-permute-start(bf16[1024,128]{1,0:T(8,128)(2,1)S(1)} %collective-permute-done.26.refs_2_), channel_id=1, source_target_pairs={{0,1},{1,0},{2,3},{3,2},{4,5},{5,4},{6,7},{7,6},{8,9},{9,8},{10,11... | collective-permute-start | bytes 786440 | tf_op jit(solution)/shard_map/ppermute | solution.py:474
  62.8 11.7 %collective-permute-start.15 = (bf16[1024,128]{1,0:T(8,128)(2,1)S(1)}, bf16[1024,128]{1,0:T(8,128)(2,1)S(1)}, u32[]{:S(2)}, u32[]{:S(2)}) collective-permute-start(bf16[1024,128]{1,0:T(8,128)(2,1)S(1)} %collective-permute-done.12.refs_4_), channel_id=1, source_target_pairs={{2,0},{3,1},{4,6},{5,7},{10,8},{11,9},{12,14},{13,15},{18,16},{19,... | collective-permute-start | bytes 786440 | tf_op jit(solution)/shard_map/ppermute | solution.py:474
  64.8 9.8 %collective-permute-start.29 = (bf16[1024,128]{1,0:T(8,128)(2,1)S(1)}, bf16[1024,128]{1,0:T(8,128)(2,1)S(1)}, u32[]{:S(2)}, u32[]{:S(2)}) collective-permute-start(bf16[1024,128]{1,0:T(8,128)(2,1)S(1)} %collective-permute-done.28.refs_4_), channel_id=1, source_target_pairs={{0,1},{1,0},{2,3},{3,2},{4,5},{5,4},{6,7},{7,6},{8,9},{9,8},{10,11... | collective-permute-start | bytes 786440 | tf_op jit(solution)/shard_map/ppermute | solution.py:474
  64.9 10.3 %collective-permute-start.32 = (bf16[1024,128]{1,0:T(8,128)(2,1)S(1)}, bf16[1024,128]{1,0:T(8,128)(2,1)S(1)}, u32[]{:S(2)}, u32[]{:S(2)}) collective-permute-start(bf16[1024,128]{1,0:T(8,128)(2,1)S(1)} %add.28.refs_6_), channel_id=1, source_target_pairs={{0,1},{1,0},{2,3},{3,2},{4,5},{5,4},{6,7},{7,6},{8,9},{9,8},{10,11... | collective-permute-start | bytes 786440 | tf_op jit(solution)/shard_map/ppermute | solution.py:474
  70.4 20.3 %collective-permute-start.9 = (bf16[1024,128]{1,0:T(8,128)(2,1)S(1)}, bf16[1024,128]{1,0:T(8,128)(2,1)S(1)}, u32[]{:S(2)}, u32[]{:S(2)}) collective-permute-start(bf16[1024,128]{1,0:T(8,128)(2,1)S(1)} %constant_dynamic-update-slice_fusion.refs_0_), channel_id=1, source_target_pairs={{0,1},{1,0},{2,3},{3,2},{4,5},{5,4},{6,7},{7,6},{8,9},{9,8},{10,11... | collective-permute-start | bytes 786440 | tf_op jit(solution)/shard_map/ppermute | solution.py:474
  70.4 20.3 %collective-permute-start.11 = (bf16[1024,128]{1,0:T(8,128)(2,1)S(1)}, bf16[1024,128]{1,0:T(8,128)(2,1)S(1)}, u32[]{:S(2)}, u32[]{:S(2)}) collective-permute-start(bf16[1024,128]{1,0:T(8,128)(2,1)S(1)} %collective-permute-done.10.refs_2_), channel_id=1, source_target_pairs={{0,1},{1,0},{2,3},{3,2},{4,5},{5,4},{6,7},{7,6},{8,9},{9,8},{10,11... | collective-permute-start | bytes 786440 | tf_op jit(solution)/shard_map/ppermute | solution.py:474
  74.5 16.2 %collective-permute-start.13 = (bf16[1024,128]{1,0:T(8,128)(2,1)S(1)}, bf16[1024,128]{1,0:T(8,128)(2,1)S(1)}, u32[]{:S(2)}, u32[]{:S(2)}) collective-permute-start(bf16[1024,128]{1,0:T(8,128)(2,1)S(1)} %collective-permute-done.12.refs_4_), channel_id=1, source_target_pairs={{0,1},{1,0},{2,3},{3,2},{4,5},{5,4},{6,7},{7,6},{8,9},{9,8},{10,11... | collective-permute-start | bytes 786440 | tf_op jit(solution)/shard_map/ppermute | solution.py:474
  74.6 17.8 %collective-permute-start.16 = (bf16[1024,128]{1,0:T(8,128)(2,1)S(1)}, bf16[1024,128]{1,0:T(8,128)(2,1)S(1)}, u32[]{:S(2)}, u32[]{:S(2)}) collective-permute-start(bf16[1024,128]{1,0:T(8,128)(2,1)S(1)} %add.24.refs_0_), channel_id=1, source_target_pairs={{0,1},{1,0},{2,3},{3,2},{4,5},{5,4},{6,7},{7,6},{8,9},{9,8},{10,11... | collective-permute-start | bytes 786440 | tf_op jit(solution)/shard_map/ppermute | solution.py:474
  77.8 1.2 %collective-permute-start.33 = (f32[1,256]{1,0:T(1,128)S(1)}, f32[1,256]{1,0:T(1,128)S(1)}, u32[]{:S(2)}, u32[]{:S(2)}) collective-permute-start(f32[1,256]{1,0:T(1,128)S(1)} %get-tuple-element.46), channel_id=1, source_target_pairs={{0,1},{1,0},{2,3},{3,2},{4,5},{5,4},{6,7},{7,6},{8,9},{9,8},{10,11... | collective-permute-start | bytes 3080 | tf_op jit(solution)/shard_map/ppermute | solution.py:474
  78.9 3.6 %collective-permute-start.34 = (f32[1,256]{1,0:T(1,128)S(1)}, f32[1,256]{1,0:T(1,128)S(1)}, u32[]{:S(2)}, u32[]{:S(2)}) collective-permute-start(f32[1,256]{1,0:T(1,128)S(1)} %add.29), channel_id=1, source_target_pairs={{0,2},{1,3},{2,0},{3,1},{4,6},{5,7},{6,4},{7,5},{8,10},{9,11},{10,... | collective-permute-start | bytes 3080 | tf_op jit(solution)/shard_map/ppermute | solution.py:474
  82.5 4.6 %collective-permute-start.35 = (f32[1,256]{1,0:T(1,128)S(1)}, f32[1,256]{1,0:T(1,128)S(1)}, u32[]{:S(2)}, u32[]{:S(2)}) collective-permute-start(f32[1,256]{1,0:T(1,128)S(1)} %add.30), channel_id=1, source_target_pairs={{0,4},{1,5},{2,6},{3,7},{4,0},{5,1},{6,2},{7,3},{8,12},{9,13},{10,... | collective-permute-start | bytes 3080 | tf_op jit(solution)/shard_map/ppermute | solution.py:474
  87.3 20.2 %collective-permute-start.36 = (bf16[256,512]{1,0:T(8,128)(2,1)S(1)}, bf16[256,512]{1,0:T(8,128)(2,1)S(1)}, u32[]{:S(2)}, u32[]{:S(2)}) collective-permute-start(bf16[256,512]{1,0:T(8,128)(2,1)S(1)} %shard_map.141.own_ref.low_ref), channel_id=1, source_target_pairs={{0,8},{8,16},{16,24},{1,9},{9,17},{17,25},{2,10},{10,18},{18,26},{... | collective-permute-start | bytes 786440 | tf_op jit(solution)/shard_map/ppermute | solution.py:474
  92.3 6.4 %copy-start.11 = (s32[512]{0:T(512)S(1)}, s32[512]{0:T(512)}, u32[]{:S(2)}) copy-start(s32[512]{0:T(512)} %param.21) | copy-start | bytes 6148
  92.3 10.9 %copy-start.1 = (bf16[512,256]{1,0:T(8,128)(2,1)S(1)}, bf16[512,256]{1,0:T(8,128)(2,1)}, u32[]{:S(2)}) copy-start(bf16[512,256]{1,0:T(8,128)(2,1)} %constant.16.clone.fh_ref.fh) | copy-start | bytes 786436
  92.3 10.8 %copy-start.2 = (bf16[512,256]{1,0:T(8,128)(2,1)S(1)}, bf16[512,256]{1,0:T(8,128)(2,1)}, u32[]{:S(2)}) copy-start(bf16[512,256]{1,0:T(8,128)(2,1)} %constant.17.clone.fl_ref.fl) | copy-start | bytes 786436
  92.3 10.8 %copy-start.6 = (bf16[512,256]{1,0:T(8,128)(2,1)S(1)}, bf16[512,256]{1,0:T(8,128)(2,1)}, u32[]{:S(2)}) copy-start(bf16[512,256]{1,0:T(8,128)(2,1)} %filters_ref.1) | copy-start | bytes 786436
  92.4 13.8 %copy-start.3 = (bf16[256,512]{1,0:T(8,128)(2,1)S(1)}, bf16[256,512]{1,0:T(8,128)(2,1)}, u32[]{:S(2)}) copy-start(bf16[256,512]{1,0:T(8,128)(2,1)} %constant.18.clone.gh) | copy-start | bytes 786436
  92.4 13.8 %copy-start.4 = (bf16[256,512]{1,0:T(8,128)(2,1)S(1)}, bf16[256,512]{1,0:T(8,128)(2,1)}, u32[]{:S(2)}) copy-start(bf16[256,512]{1,0:T(8,128)(2,1)} %constant.19.clone.gl) | copy-start | bytes 786436
  92.4 13.8 %copy-start.10 = (f32[512]{0:T(512)S(1)}, f32[512]{0:T(512)}, u32[]{:S(2)}) copy-start(f32[512]{0:T(512)} %param.22) | copy-start | bytes 6148
  94.1 16.7 %collective-permute-start.20 = (bf16[256,512]{1,0:T(8,128)(2,1)}, bf16[256,512]{1,0:T(8,128)(2,1)S(1)}, u32[]{:S(2)}, u32[]{:S(2)}) collective-permute-start(bf16[256,512]{1,0:T(8,128)(2,1)} %get-tuple-element.40), channel_id=1, source_target_pairs={{8,0},{16,8},{24,16},{9,1},{17,9},{25,17},{10,2},{18,10},{26,18},{... | collective-permute-start | bytes 786440 | tf_op jit(solution)/shard_map/ppermute | solution.py:474
  95.4 1.2 %collective-permute-start.17 = (f32[1,256]{1,0:T(1,128)S(1)}, f32[1,256]{1,0:T(1,128)S(1)}, u32[]{:S(2)}, u32[]{:S(2)}) collective-permute-start(f32[1,256]{1,0:T(1,128)S(1)} %get-tuple-element.39), channel_id=1, source_target_pairs={{0,1},{1,0},{2,3},{3,2},{4,5},{5,4},{6,7},{7,6},{8,9},{9,8},{10,11... | collective-permute-start | bytes 3080 | tf_op jit(solution)/shard_map/ppermute | solution.py:474
  96.7 3.6 %collective-permute-start.18 = (f32[1,256]{1,0:T(1,128)S(1)}, f32[1,256]{1,0:T(1,128)S(1)}, u32[]{:S(2)}, u32[]{:S(2)}) collective-permute-start(f32[1,256]{1,0:T(1,128)S(1)} %add.25), channel_id=1, source_target_pairs={{0,2},{1,3},{2,0},{3,1},{4,6},{5,7},{6,4},{7,5},{8,10},{9,11},{10,... | collective-permute-start | bytes 3080 | tf_op jit(solution)/shard_map/ppermute | solution.py:474
  100.2 4.5 %collective-permute-start.19 = (f32[1,256]{1,0:T(1,128)S(1)}, f32[1,256]{1,0:T(1,128)S(1)}, u32[]{:S(2)}, u32[]{:S(2)}) collective-permute-start(f32[1,256]{1,0:T(1,128)S(1)} %add.26), channel_id=1, source_target_pairs={{0,4},{1,5},{2,6},{3,7},{4,0},{5,1},{6,2},{7,3},{8,12},{9,13},{10,... | collective-permute-start | bytes 3080 | tf_op jit(solution)/shard_map/ppermute | solution.py:474
  104.7 6.1 %collective-permute-start.21 = (f32[1,256]{1,0:T(1,128)S(1)}, f32[1,256]{1,0:T(1,128)S(1)}, u32[]{:S(2)}, u32[]{:S(2)}) collective-permute-start(f32[1,256]{1,0:T(1,128)S(1)} %add.27.sq_ref), channel_id=1, source_target_pairs={{8,0},{16,8},{24,16},{9,1},{17,9},{25,17},{10,2},{18,10},{26,18},{... | collective-permute-start | bytes 3080 | tf_op jit(solution)/shard_map/ppermute | solution.py:474

commit v9 on v7

--- a/solution.py
+++ b/solution.py
@@ -312,8 +312,13 @@
     outs[0][...] = total
     if len(outs) == 1:
         return
-    outs[1][...] = total[:rows].astype(BF)
-    outs[2][...] = total[rows:].astype(BF)
+    for parity in range(2):
+
+        @pl.when(rank % 2 == parity)
+        def _():
+            outs[1 + parity][...] = total[:rows].astype(BF)
+            outs[2 - parity][...] = total[rows:].astype(BF)
+
     squares = total * total
     lanes = squares[:, 0:HD]
     for g in range(1, squares.shape[1] // HD):
@@ -416,13 +421,17 @@
     return sign * plain[:rows], jnp.where(first, 1.0, sign) * plain[rows:]
 
 
-def filtered(x_re, x_im, gh, gl, spec):
+def filtered_spectrum(x_re, x_im, spec):
     rows = x_re.shape[0]
     first, _ = frequency_signs(rows)
     h_re, h_im = spec[:rows], spec[rows:]
     h_cross = jnp.where(first, 0.0, h_im)
     h_own = jnp.where(first, h_im, h_re)
-    y = jnp.concatenate([x_re * h_re - x_im * h_cross, x_re * h_cross + x_im * h_own], axis=0)
+    return jnp.concatenate([x_re * h_re - x_im * h_cross, x_re * h_cross + x_im * h_own], axis=0)
+
+
+def filtered(x_re, x_im, gh, gl, spec):
+    y = filtered_spectrum(x_re, x_im, spec)
     y_high = y.astype(BF)
     y_low = (y - y_high.astype(F32)).astype(BF)
     return two(gh, gl, y_high) + jnp.dot(gh, y_low, preferred_element_type=F32)
@@ -444,48 +453,67 @@
 
 
 def conv_last_kernel(
-    n, model_width, slots_ref, ids_ref, part_ref, low_ref, raw_low, raw_high, sq_low, sq_high,
-    spec_ref, gain_ref, fh, fl, gh, gl, out_ref,
+    n, model_width, slots_ref, ids_ref, part_ref, low_ref, raw_a, raw_b, sq_a, sq_b,
+    spec_ref, gain_ref, fh, gh, out_ref,
 ):
     rows = low_ref.shape[0]
-    last = ids_ref[0] == n - 1
+    rank = ids_ref[0]
+    odd = rank % 2 == 1
     gain = gain_ref[...]
-    for high, raw_ref, sq_ref in ((0, raw_low, sq_low), (1, raw_high, sq_high)):
-        before = normed_rows(raw_ref[...].astype(F32), sq_ref[...], gain, model_width)
+    for high in range(2):
+        from_a = odd != (high == 1)
+        raw = jnp.where(from_a, raw_a[...].astype(F32), raw_b[...].astype(F32))
+        part = slice(high * rows, (high + 1) * rows)
+        squares = jnp.where(from_a, sq_a[:, part], sq_b[:, part])
+        before = normed_rows(raw, squares, gain, model_width)
         if high:
+            last = rank == n - 1
             before = jnp.where(last, low_ref[...].astype(F32), before.astype(F32)).astype(BF)
-        early = two(fh[...], fl[...], before)
-        conv = filtered(early[:rows], early[rows:], gh[...], gl[...], spec_ref[...])
+        early = jnp.dot(fh[...], before, preferred_element_type=F32)
+        y = filtered_spectrum(early[:rows], early[rows:], spec_ref[...]).astype(BF)
+        conv = jnp.dot(gh[...], y, preferred_element_type=F32)
         half = half_index(slots_ref, ids_ref, high)
-        out_ref[pl.ds(pl.multiple_of(half * rows, rows), rows), :] = (
-            part_ref[high * rows : (high + 1) * rows, :] + conv
-        ).astype(BF)
-
-
-def moved(block, axis, route):
-    return lax.ppermute(block, axis, route)
-
-
-def gather_mp(own, size):
+        out_ref[pl.ds(pl.multiple_of(half * rows, rows), rows), :] = (part_ref[part, :] + conv).astype(
+            BF
+        )
+
+
+def relayed_piece(own, near, size):
+    inner = [(i, i ^ (size - 2)) for i in range(2, size - 2)]
+    direct = lax.ppermute(own, "mp", inner)
+    ends = [(2, 0), (3, 1), (size - 4, size - 2), (size - 3, size - 1)]
+    return direct + lax.ppermute(near, "mp", ends)
+
+
+def gather_mp(own, size, relay):
+    chips = size // 2
+    pieces = [own]
+    for k in range(1, chips):
+        if relay and k == chips - 1:
+            pieces.append(relayed_piece(own, pieces[k - 1], size))
+        else:
+            pieces.append(lax.ppermute(own, "mp", xor_route(size, 2 * k)))
     parts = []
-    for k in range(size // 2):
-        piece = moved(own, "mp", xor_route(size, 2 * k)) if k else own
+    for piece in pieces:
         parts.append(piece)
-        parts.append(moved(piece, "mp", xor_route(size, 1)))
+        parts.append(lax.ppermute(piece, "mp", xor_route(size, 1)))
     return parts
 
 
 def total_mp(part, size):
     k = 1
     while k < size:
-        part = part + moved(part, "mp", xor_route(size, k))
+        part = part + lax.ppermute(part, "mp", xor_route(size, k))
         k *= 2
     return part
 
 
-def before_rows(block, distance):
-    devices = range(lax.axis_size("seq"))
-    return moved(block, "seq", [(i - distance, i) for i in devices if i - distance in devices])
+def swapped(block, offset):
+    n = lax.axis_size("seq")
+    route = []
+    for i in range(offset, n - 1, 2):
+        route += [(i, i + 1), (i + 1, i)]
+    return lax.ppermute(block, "seq", route)
 
 
 def fast_device(
@@ -503,7 +531,7 @@
     backward = tuple(jnp.asarray(t) for t in backward)
 
     def exchange(pieces):
-        return [pieces[0]] + [moved(pieces[k], "seq", xor_route(n, k)) for k in range(1, n)]
+        return [pieces[0]] + [lax.ppermute(pieces[k], "seq", xor_route(n, k)) for k in range(1, n)]
 
     inputs = (queries, key_vecs, value_vecs)
     low = exchange(pack(n, 0, slot_map, ids, inputs))
@@ -511,9 +539,9 @@
     spec = spectrum(filters, filter_len, forward)
 
     att_low = exchange(attend(n, 0, rows, ids, low))
-    parts_low = gather_mp(jnp.concatenate(att_low, axis=0), mp_size)
+    parts_low = gather_mp(jnp.concatenate(att_low, axis=0), mp_size, True)
     att_high = exchange(attend(n, 1, rows, ids, low + high))
-    parts_high = gather_mp(jnp.concatenate(att_high, axis=0), mp_size)
+    parts_high = gather_mp(jnp.concatenate(att_high, axis=0), mp_size, False)
 
     most = mp_size // 2
     first, last = tuple(range(most)), tuple(range(most, mp_size))
@@ -521,15 +549,15 @@
         n, slot_map, ids, incoming, w_out,
         parts_low[:most], parts_high[:most], first, False,
     )
-    res, raw_low, raw_high, squares = project(
+    res, raw_a, raw_b, squares = project(
         n, slot_map, ids, base, w_out,
         parts_low[most:], parts_high[most:], last, True,
     )
-    raw_low = before_rows(raw_low, 1)
-    raw_high = before_rows(raw_high, -1)
+    raw_a = swapped(raw_a, 0)
+    raw_b = swapped(raw_b, 1)
     squares = total_mp(squares, mp_size)
-    sq_low = before_rows(squares[:, :rows], 1)
-    sq_high = before_rows(squares[:, rows:], -1)
+    sq_a = swapped(squares, 0)
+    sq_b = swapped(squares, 1)
     transforms = forward + backward
     part, norm_low = pl.pallas_call(
         functools.partial(conv_own_kernel, model_width),
@@ -546,13 +574,13 @@
     return pl.pallas_call(
         functools.partial(conv_last_kernel, n, model_width),
         out_shape=jax.ShapeDtypeStruct((2 * rows, width), BF),
-        in_specs=[sm(), sm()] + [vm()] * 12,
+        in_specs=[sm(), sm()] + [vm()] * 10,
         out_specs=vm(),
         compiler_params=params(20),
         cost_estimate=cost(20 * rows * rows * width, 24 * rows * width),
         name="conv_last",
     )(
-        slot_map, ids, part, norm_low, raw_low, raw_high, sq_low, sq_high, spec, gain, *transforms
+        slot_map, ids, part, norm_low, raw_a, raw_b, sq_a, sq_b, spec, gain, forward[0], backward[0]
     )
 
 
@@ -570,7 +598,8 @@
         heads % n == 0
         and power_of_two(n)
         and power_of_two(size)
-        and size >= 4
+        and n % 2 == 0
+        and size >= 8
         and rows % 256 == 0
         and filters.shape[1] <= rows
     )

time: 122 us -> 111 us (0.910); the launches traced: 122 us -> 110 us
  waiting for transfers between devices: 48.3 us -> 38.4 us
  starting transfers between devices: 52.5 us -> 50.6 us
    ppermute x33 -> x34, waiting for transfers between devices: 48.3 us -> 38.4 us  [the longest x5 17.5 us: gather_mp(): pieces.append(lax.ppermute(own, 'mp', xor_route(size, 2 * k)))]
    ppermute x33 -> x34, starting transfers between devices: 52.5 us -> 50.6 us  [the longest x12 16.1 us: exchange(): lax.ppermute(pieces[k], 'seq', xor_route(n, k))]
  transfers between devices with their start and end apart: 33 -> 34, of which waited for: 10 -> 11; matrix products, arithmetic and copies ran while one was open for 0% -> 0% of each run, Pallas kernels for 7% -> 8%
where the time goes in v9:
time: 111 us; the launch traced here: 110 us
  starting transfers between devices  50.6 us (46%)
  waiting for transfers between devices  38.4 us (35%)
  Pallas kernels  19.6 us (18%)
    ppermute x5, waiting for transfers between devices, gather_mp(): pieces.append(lax.ppermute(own, 'mp', xor_route(size, 2 * k)))  17.5 us
    ppermute x12, waiting for transfers between devices, exchange(): lax.ppermute(pieces[k], 'seq', xor_route(n, k))  17.1 us
    ppermute x12, starting transfers between devices, exchange(): lax.ppermute(pieces[k], 'seq', xor_route(n, k))  16.1 us
    ppermute x5, starting transfers between devices, gather_mp(): pieces.append(lax.ppermute(own, 'mp', xor_route(size, 2 * k)))  15.8 us
    ppermute x3, starting transfers between devices, total_mp(): part = part + lax.ppermute(part, 'mp', xor_route(size, k))  8.88 us
    ppermute x4, starting transfers between devices, swapped(): return lax.ppermute(block, 'seq', route)  6.56 us
    pallas_call x2, Pallas kernels, attend(): pl.pallas_call(functools.partial(attend_kernel, n, high, rows), out_shape...  5.9 us
    pallas_call x2, Pallas kernels, project(): pl.pallas_call(functools.partial(project_kernel, n, indices), out_shape=s...  4.62 us
  transfers between devices with their start and end apart: 34, of which 11 were waited for; matrix products, arithmetic and copies ran while one was open for 0% of the time, Pallas kernels for 8%

profile of v9, /device:TPU:0, one launch (start us, length us, event | category | flops | bytes accessed | tf_op | source)
XLA Modules:
  0.0 110.0 jit_solution(11055377330122819293)
XLA Ops:
  0.0 0.1 pad_add_fusion.ids_ref
  0.1 0.7 copy-done.7
  0.7 1.8 %shard_map.136 = (bf16[768,128]{1,0:T(8,128)(2,1)S(1)}, bf16[768,128]{1,0:T(8,128)(2,1)S(1)}, bf16[768,128]{1,0:T(8,128)(2,1)S(1)}, bf16[768,128]{1,0:T(8,128)(2,1)S(1)}) custom-call(s32[8]{0:T(128)S(1)} %copy-done.7, s32[2]{0:T(128)S(1)} %pad_add_fusion.ids_ref, bf16[512,512]{1,0:T(8,128)(2,1)} %q_ref.3, bf16[512,512]{1,0:T(8,128)(2,1)} %k_ref.3, ...), custom_call_target="tpu_custom_call" | custom-call | bytes 1572864 | tf_op jit(solution)/shard_map/pallas_call | solution.py:199
  2.6 0.0 copy-start
  2.6 0.0 copy-start.4
  2.6 0.0 copy-start.8
  2.6 3.0 %collective-permute-start = (bf16[768,128]{1,0:T(8,128)(2,1)S(1)}, bf16[768,128]{1,0:T(8,128)(2,1)S(1)}, u32[]{:S(2)}, u32[]{:S(2)}) collective-permute-start(bf16[768,128]{1,0:T(8,128)(2,1)S(1)} %get-tuple-element.28), channel_id=1, source_target_pairs={{0,8},{8,0},{16,24},{24,16},{1,9},{9,1},{17,25},{25,17},{2,10},{10... | collective-permute-start | bytes 589832 | tf_op jit(solution)/shard_map/ppermute | solution.py:534
  5.6 1.5 %collective-permute-start.1 = (bf16[768,128]{1,0:T(8,128)(2,1)S(1)}, bf16[768,128]{1,0:T(8,128)(2,1)S(1)}, u32[]{:S(2)}, u32[]{:S(2)}) collective-permute-start(bf16[768,128]{1,0:T(8,128)(2,1)S(1)} %get-tuple-element.29), channel_id=1, source_target_pairs={{0,16},{8,24},{16,0},{24,8},{1,17},{9,25},{17,1},{25,9},{2,18},{10... | collective-permute-start | bytes 589832 | tf_op jit(solution)/shard_map/ppermute | solution.py:534
  7.2 0.0 collective-permute-start.2
  7.2 1.8 %shard_map.137 = (bf16[768,128]{1,0:T(8,128)(2,1)S(1)}, bf16[768,128]{1,0:T(8,128)(2,1)S(1)}, bf16[768,128]{1,0:T(8,128)(2,1)S(1)}, bf16[768,128]{1,0:T(8,128)(2,1)S(1)}) custom-call(s32[8]{0:T(128)S(1)} %copy-done.7, s32[2]{0:T(128)S(1)} %pad_add_fusion.ids_ref, bf16[512,512]{1,0:T(8,128)(2,1)} %q_ref.3, bf16[512,512]{1,0:T(8,128)(2,1)} %k_ref.3, ...), custom_call_target="tpu_custom_call" | custom-call | bytes 1572864 | tf_op jit(solution)/shard_map/pallas_call | solution.py:199
  9.0 2.0 %collective-permute-start.10 = (bf16[768,128]{1,0:T(8,128)(2,1)S(1)}, bf16[768,128]{1,0:T(8,128)(2,1)S(1)}, u32[]{:S(2)}, u32[]{:S(2)}) collective-permute-start(bf16[768,128]{1,0:T(8,128)(2,1)S(1)} %get-tuple-element.37), channel_id=1, source_target_pairs={{0,16},{8,24},{16,0},{24,8},{1,17},{9,25},{17,1},{25,9},{2,18},{10... | collective-permute-start | bytes 589832 | tf_op jit(solution)/shard_map/ppermute | solution.py:534
  11.1 1.4 %collective-permute-start.11 = (bf16[768,128]{1,0:T(8,128)(2,1)S(1)}, bf16[768,128]{1,0:T(8,128)(2,1)S(1)}, u32[]{:S(2)}, u32[]{:S(2)}) collective-permute-start(bf16[768,128]{1,0:T(8,128)(2,1)S(1)} %get-tuple-element.38), channel_id=1, source_target_pairs={{0,24},{8,16},{16,8},{24,0},{1,25},{9,17},{17,9},{25,1},{2,26},{10... | collective-permute-start | bytes 589832 | tf_op jit(solution)/shard_map/ppermute | solution.py:534
  12.5 0.9 collective-permute-start.9
  13.4 8.2 %collective-permute-done.1.refs_2_ = bf16[768,128]{1,0:T(8,128)(2,1)S(1)} collective-permute-done((bf16[768,128]{1,0:T(8,128)(2,1)S(1)}, bf16[768,128]{1,0:T(8,128)(2,1)S(1)}, u32[]{:S(2)}, u32[]{:S(2)}) %collective-permute-start.1) | collective-permute-done | bytes 196640 | tf_op jit(solution)/shard_map/ppermute | solution.py:534
  21.6 3.0 %collective-permute-done.10.refs_6_ = bf16[768,128]{1,0:T(8,128)(2,1)S(1)} collective-permute-done((bf16[768,128]{1,0:T(8,128)(2,1)S(1)}, bf16[768,128]{1,0:T(8,128)(2,1)S(1)}, u32[]{:S(2)}, u32[]{:S(2)}) %collective-permute-start.10) | collective-permute-done | bytes 196640 | tf_op jit(solution)/shard_map/ppermute | solution.py:534
  24.7 3.6 %attend_high.1 = (bf16[256,128]{1,0:T(8,128)(2,1)S(1)}, bf16[256,128]{1,0:T(8,128)(2,1)S(1)}, bf16[256,128]{1,0:T(8,128)(2,1)S(1)}, bf16[256,128]{1,0:T(8,128)(2,1)S(1)}) custom-call(s32[2]{0:T(128)S(1)} %pad_add_fusion.ids_ref, bf16[768,128]{1,0:T(8,128)(2,1)S(1)} %get-tuple-element.27.refs_0_, bf16[768,128]{1,0:T(8,128)(2,1)S(1)} %collective-permute-done.refs_1_, ...), custom_call_target="tpu_custom_call" | custom-call | flops 872415232 | bytes 2097152 | tf_op jit(solution)/shard_map/attend_high/pallas_call | solution.py:271
  28.3 0.4 collective-permute-start.12
  28.7 1.7 %collective-permute-start.13 = (bf16[256,128]{1,0:T(8,128)(2,1)S(1)}, bf16[256,128]{1,0:T(8,128)(2,1)S(1)}, u32[]{:S(2)}, u32[]{:S(2)}) collective-permute-start(bf16[256,128]{1,0:T(8,128)(2,1)S(1)} %get-tuple-element.41), channel_id=1, source_target_pairs={{0,16},{8,24},{16,0},{24,8},{1,17},{9,25},{17,1},{25,9},{2,18},{10... | collective-permute-start | bytes 196616 | tf_op jit(solution)/shard_map/ppermute | solution.py:534
  30.4 1.4 %collective-permute-start.14 = (bf16[256,128]{1,0:T(8,128)(2,1)S(1)}, bf16[256,128]{1,0:T(8,128)(2,1)S(1)}, u32[]{:S(2)}, u32[]{:S(2)}) collective-permute-start(bf16[256,128]{1,0:T(8,128)(2,1)S(1)} %get-tuple-element.42), channel_id=1, source_target_pairs={{0,24},{8,16},{16,8},{24,0},{1,25},{9,17},{17,9},{25,1},{2,26},{10... | collective-permute-start | bytes 196616 | tf_op jit(solution)/shard_map/ppermute | solution.py:534
  31.8 2.3 %attend_low.1 = (bf16[256,128]{1,0:T(8,128)(2,1)S(1)}, bf16[256,128]{1,0:T(8,128)(2,1)S(1)}, bf16[256,128]{1,0:T(8,128)(2,1)S(1)}, bf16[256,128]{1,0:T(8,128)(2,1)S(1)}) custom-call(s32[2]{0:T(128)S(1)} %pad_add_fusion.ids_ref, bf16[768,128]{1,0:T(8,128)(2,1)S(1)} %get-tuple-element.27.refs_0_, bf16[768,128]{1,0:T(8,128)(2,1)S(1)} %collective-permute-done.refs_1_, ...), custom_call_target="tpu_custom_call" | custom-call | flops 335544320 | bytes 1048576 | tf_op jit(solution)/shard_map/attend_low/pallas_call | solution.py:271
  34.1 0.4 collective-permute-start.3
  34.6 1.7 %collective-permute-start.4 = (bf16[256,128]{1,0:T(8,128)(2,1)S(1)}, bf16[256,128]{1,0:T(8,128)(2,1)S(1)}, u32[]{:S(2)}, u32[]{:S(2)}) collective-permute-start(bf16[256,128]{1,0:T(8,128)(2,1)S(1)} %get-tuple-element.33), channel_id=1, source_target_pairs={{0,16},{8,24},{16,0},{24,8},{1,17},{9,25},{17,1},{25,9},{2,18},{10... | collective-permute-start | bytes 196616 | tf_op jit(solution)/shard_map/ppermute | solution.py:534
  36.3 2.2 %collective-permute-done.3 = bf16[256,128]{1,0:T(8,128)(2,1)S(1)} collective-permute-done((bf16[256,128]{1,0:T(8,128)(2,1)S(1)}, bf16[256,128]{1,0:T(8,128)(2,1)S(1)}, u32[]{:S(2)}, u32[]{:S(2)}) %collective-permute-start.3) | collective-permute-done | bytes 65568 | tf_op jit(solution)/shard_map/ppermute | solution.py:534
  38.5 1.5 %collective-permute-start.5 = (bf16[256,128]{1,0:T(8,128)(2,1)S(1)}, bf16[256,128]{1,0:T(8,128)(2,1)S(1)}, u32[]{:S(2)}, u32[]{:S(2)}) collective-permute-start(bf16[256,128]{1,0:T(8,128)(2,1)S(1)} %get-tuple-element.34), channel_id=1, source_target_pairs={{0,24},{8,16},{16,8},{24,0},{1,25},{9,17},{17,9},{25,1},{2,26},{10... | collective-permute-start | bytes 196616 | tf_op jit(solution)/shard_map/ppermute | solution.py:534
  40.0 3.6 %collective-permute-done.5 = bf16[256,128]{1,0:T(8,128)(2,1)S(1)} collective-permute-done((bf16[256,128]{1,0:T(8,128)(2,1)S(1)}, bf16[256,128]{1,0:T(8,128)(2,1)S(1)}, u32[]{:S(2)}, u32[]{:S(2)}) %collective-permute-start.5) | collective-permute-done | bytes 65568 | tf_op jit(solution)/shard_map/ppermute | solution.py:534
  43.6 2.7 %collective-permute-start.18 = (bf16[1024,128]{1,0:T(8,128)(2,1)S(1)}, bf16[1024,128]{1,0:T(8,128)(2,1)S(1)}, u32[]{:S(2)}, u32[]{:S(2)}) collective-permute-start(bf16[1024,128]{1,0:T(8,128)(2,1)S(1)} %constant_dynamic-update-slice_fusion.refs_0_), channel_id=1, source_target_pairs={{0,4},{1,5},{2,6},{3,7},{4,0},{5,1},{6,2},{7,3},{8,12},{9,13},{10,... | collective-permute-start | bytes 786440 | tf_op jit(solution)/shard_map/ppermute | solution.py:495
  46.4 1.6 %collective-permute-start.16 = (bf16[1024,128]{1,0:T(8,128)(2,1)S(1)}, bf16[1024,128]{1,0:T(8,128)(2,1)S(1)}, u32[]{:S(2)}, u32[]{:S(2)}) collective-permute-start(bf16[1024,128]{1,0:T(8,128)(2,1)S(1)} %constant_dynamic-update-slice_fusion.4.refs_4_), channel_id=1, source_target_pairs={{0,2},{1,3},{2,0},{3,1},{4,6},{5,7},{6,4},{7,5},{8,10},{9,11},{10,... | collective-permute-start | bytes 786440 | tf_op jit(solution)/shard_map/ppermute | solution.py:495
  48.0 0.4 collective-permute-start.7
  48.5 0.7 collective-permute-start.20
  49.2 5.9 %collective-permute-done.18.refs_0_ = bf16[1024,128]{1,0:T(8,128)(2,1)S(1)} collective-permute-done((bf16[1024,128]{1,0:T(8,128)(2,1)S(1)}, bf16[1024,128]{1,0:T(8,128)(2,1)S(1)}, u32[]{:S(2)}, u32[]{:S(2)}) %collective-permute-start.18) | collective-permute-done | bytes 262176 | tf_op jit(solution)/shard_map/ppermute | solution.py:495
  55.1 1.3 %collective-permute-start.21 = (bf16[1024,128]{1,0:T(8,128)(2,1)S(1)}, bf16[1024,128]{1,0:T(8,128)(2,1)S(1)}, u32[]{:S(2)}, u32[]{:S(2)}) collective-permute-start(bf16[1024,128]{1,0:T(8,128)(2,1)S(1)} %collective-permute-done.18.refs_0_), channel_id=1, source_target_pairs={{2,0},{3,1},{4,6},{5,7},{10,8},{11,9},{12,14},{13,15},{18,16},{19,... | collective-permute-start | bytes 786440 | tf_op jit(solution)/shard_map/ppermute | solution.py:485
  56.4 1.1 collective-permute-done.16.refs_6_
  57.5 5.3 %collective-permute-start.23 = (bf16[1024,128]{1,0:T(8,128)(2,1)S(1)}, bf16[1024,128]{1,0:T(8,128)(2,1)S(1)}, u32[]{:S(2)}, u32[]{:S(2)}) collective-permute-start(bf16[1024,128]{1,0:T(8,128)(2,1)S(1)} %constant_dynamic-update-slice_fusion.4.refs_4_), channel_id=1, source_target_pairs={{0,4},{1,5},{2,6},{3,7},{4,0},{5,1},{6,2},{7,3},{8,12},{9,13},{10,... | collective-permute-start | bytes 786440 | tf_op jit(solution)/shard_map/ppermute | solution.py:495
  62.8 0.3 collective-permute-done.7.refs_2_
  63.1 5.7 %collective-permute-start.25 = (bf16[1024,128]{1,0:T(8,128)(2,1)S(1)}, bf16[1024,128]{1,0:T(8,128)(2,1)S(1)}, u32[]{:S(2)}, u32[]{:S(2)}) collective-permute-start(bf16[1024,128]{1,0:T(8,128)(2,1)S(1)} %constant_dynamic-update-slice_fusion.4.refs_4_), channel_id=1, source_target_pairs={{0,6},{1,7},{2,4},{3,5},{4,2},{5,3},{6,0},{7,1},{8,14},{9,15},{10,... | collective-permute-start | bytes 786440 | tf_op jit(solution)/shard_map/ppermute | solution.py:495
  68.8 0.5 collective-permute-start.8
  69.3 0.1 add.12.refs_2_
  69.4 0.1 collective-permute-start.19
  69.6 10.2 %collective-permute-done.23.refs_4_ = bf16[1024,128]{1,0:T(8,128)(2,1)S(1)} collective-permute-done((bf16[1024,128]{1,0:T(8,128)(2,1)S(1)}, bf16[1024,128]{1,0:T(8,128)(2,1)S(1)}, u32[]{:S(2)}, u32[]{:S(2)}) %collective-permute-start.23) | collective-permute-done | bytes 262176 | tf_op jit(solution)/shard_map/ppermute | solution.py:495
  79.7 0.1 collective-permute-start.24
  79.8 0.4 collective-permute-start.26
  80.3 0.1 collective-permute-start.22
  80.4 1.9 %shard_map.138.base_ref = f32[512,512]{1,0:T(8,128)S(1)} custom-call(s32[8]{0:T(128)S(1)} %copy-done.8, s32[2]{0:T(128)S(1)} %pad_add_fusion.ids_ref, bf16[512,512]{1,0:T(8,128)(2,1)S(1)} %copy-done.4, bf16[4096,512]{1,0:T(8,128)(2,1)S(1)} %copy-done, bf16[1024,128]{1,0:T(8,128)(2,1)S(1)} %constant_dynamic-update-slice_fusion.refs_0_, ...), custom_call_target="tpu_custom_call" | custom-call | flops 1073741824 | bytes 6291456 | tf_op jit(solution)/shard_map/pallas_call | solution.py:335
  82.3 0.0 copy-start.11
  82.3 0.0 copy-start.1
  82.3 0.0 copy-start.3
  82.3 0.0 copy-start.5
  82.4 0.0 copy-start.2
  82.4 0.0 copy-start.6
  82.4 2.7 %shard_map.139 = (f32[512,512]{1,0:T(8,128)S(1)}, bf16[256,512]{1,0:T(8,128)(2,1)}, bf16[256,512]{1,0:T(8,128)(2,1)S(1)}, f32[1,512]{1,0:T(1,128)S(1)}) custom-call(s32[8]{0:T(128)S(1)} %copy-done.8, s32[2]{0:T(128)S(1)} %pad_add_fusion.ids_ref, f32[512,512]{1,0:T(8,128)S(1)} %shard_map.138.base_ref, bf16[4096,512]{1,0:T(8,128)(2,1)S(1)} %copy-done, ...), custom_call_target="tpu_custom_call" | custom-call | flops 1073741824 | bytes 6291456 | tf_op jit(solution)/shard_map/pallas_call | solution.py:335
  85.1 1.3 %collective-permute-start.30 = (bf16[256,512]{1,0:T(8,128)(2,1)}, bf16[256,512]{1,0:T(8,128)(2,1)S(1)}, u32[]{:S(2)}, u32[]{:S(2)}) collective-permute-start(bf16[256,512]{1,0:T(8,128)(2,1)} %get-tuple-element.47), channel_id=1, source_target_pairs={{0,8},{8,0},{16,24},{24,16},{1,9},{9,1},{17,25},{25,17},{2,10},{10... | collective-permute-start | bytes 786440 | tf_op jit(solution)/shard_map/ppermute | solution.py:516
  86.4 0.7 collective-permute-start.31
  87.1 0.2 collective-permute-start.27
  87.3 1.0 collective-permute-done.27
  88.3 6.1 %collective-permute-start.28 = (f32[1,512]{1,0:T(1,128)S(1)}, f32[1,512]{1,0:T(1,128)S(1)}, u32[]{:S(2)}, u32[]{:S(2)}) collective-permute-start(f32[1,512]{1,0:T(1,128)S(1)} %add.13), channel_id=1, source_target_pairs={{0,2},{1,3},{2,0},{3,1},{4,6},{5,7},{6,4},{7,5},{8,10},{9,11},{10,... | collective-permute-start | bytes 6152 | tf_op jit(solution)/shard_map/ppermute | solution.py:506
  94.4 0.1 copy.15.len_ref
  94.6 1.4 %collective-permute-done.28 = f32[1,512]{1,0:T(1,128)S(1)} collective-permute-done((f32[1,512]{1,0:T(1,128)S(1)}, f32[1,512]{1,0:T(1,128)S(1)}, u32[]{:S(2)}, u32[]{:S(2)}) %collective-permute-start.28) | collective-permute-done | bytes 2080 | tf_op jit(solution)/shard_map/ppermute | solution.py:506
  96.0 2.6 %collective-permute-start.29 = (f32[1,512]{1,0:T(1,128)S(1)}, f32[1,512]{1,0:T(1,128)S(1)}, u32[]{:S(2)}, u32[]{:S(2)}) collective-permute-start(f32[1,512]{1,0:T(1,128)S(1)} %add.14), channel_id=1, source_target_pairs={{0,4},{1,5},{2,6},{3,7},{4,0},{5,1},{6,2},{7,3},{8,12},{9,13},{10,... | collective-permute-start | bytes 6152 | tf_op jit(solution)/shard_map/ppermute | solution.py:506
  98.6 0.5 spectrum.1.spec_ref
  99.1 1.4 %collective-permute-done.29 = f32[1,512]{1,0:T(1,128)S(1)} collective-permute-done((f32[1,512]{1,0:T(1,128)S(1)}, f32[1,512]{1,0:T(1,128)S(1)}, u32[]{:S(2)}, u32[]{:S(2)}) %collective-permute-start.29) | collective-permute-done | bytes 2080 | tf_op jit(solution)/shard_map/ppermute | solution.py:506
  100.5 3.8 %collective-permute-start.32 = (f32[1,512]{1,0:T(1,128)S(1)}, f32[1,512]{1,0:T(1,128)S(1)}, u32[]{:S(2)}, u32[]{:S(2)}) collective-permute-start(f32[1,512]{1,0:T(1,128)S(1)} %add.15.sq_ref), channel_id=1, source_target_pairs={{0,8},{8,0},{16,24},{24,16},{1,9},{9,1},{17,25},{25,17},{2,10},{10... | collective-permute-start | bytes 6152 | tf_op jit(solution)/shard_map/ppermute | solution.py:516
  104.3 0.8 collective-permute-start.33
  105.1 2.2 %conv_own.1 = (f32[512,512]{1,0:T(8,128)S(1)}, bf16[256,512]{1,0:T(8,128)(2,1)S(1)}) custom-call(f32[512,512]{1,0:T(8,128)S(1)} %get-tuple-element.43.res_ref, f32[1,512]{1,0:T(1,128)S(1)} %add.15.sq_ref, f32[512,512]{1,0:T(8,128)S(1)} %spectrum.1.spec_ref, f32[1,512]{1,0:T(1,128)S(1)} %bitcast.5, f32[1,512]{1,0:T(1,128)S(1)} %bitcast.7, ...), custom_call_target="tpu_custom_call" | custom-call | flops 671088640 | bytes 3145728 | tf_op jit(solution)/shard_map/conv_own/pallas_call | solution.py:562
  107.4 2.7 %conv_last.1 = bf16[512,512]{1,0:T(8,128)(2,1)} custom-call(s32[8]{0:T(128)S(1)} %copy-done.8, s32[2]{0:T(128)S(1)} %pad_add_fusion.ids_ref, f32[512,512]{1,0:T(8,128)S(1)} %get-tuple-element.45.part_ref, bf16[256,512]{1,0:T(8,128)(2,1)S(1)} %get-tuple-element.46.low_ref, bf16[256,512]{1,0:T(8,128)(2,1)S(1)} %collective-permute-done.30.raw_a, ...), custom_call_target="tpu_custom_call" | custom-call | flops 671088640 | bytes 3145728 | tf_op jit(solution)/shard_map/conv_last/pallas_call | solution.py:574
  (51 shorter events, 0.2 us)
Async XLA Ops:
  0.1 0.7 copy-start.7
  2.6 77.8 %copy-start = (bf16[4096,512]{1,0:T(8,128)(2,1)S(1)}, bf16[4096,512]{1,0:T(8,128)(2,1)}, u32[]{:S(2)}) copy-start(bf16[4096,512]{1,0:T(8,128)(2,1)} %w_ref.3) | copy-start | bytes 12582916
  2.6 77.8 %copy-start.4 = (bf16[512,512]{1,0:T(8,128)(2,1)S(1)}, bf16[512,512]{1,0:T(8,128)(2,1)}, u32[]{:S(2)}) copy-start(bf16[512,512]{1,0:T(8,128)(2,1)} %base_ref.1) | copy-start | bytes 1572868
  2.6 77.8 %copy-start.8 = (s32[8]{0:T(128)S(1)}, s32[8]{0:T(128)}, u32[]{:S(2)}) copy-start(s32[8]{0:T(128)} %slots_ref.9) | copy-start | bytes 100
  2.6 9.9 %collective-permute-start = (bf16[768,128]{1,0:T(8,128)(2,1)S(1)}, bf16[768,128]{1,0:T(8,128)(2,1)S(1)}, u32[]{:S(2)}, u32[]{:S(2)}) collective-permute-start(bf16[768,128]{1,0:T(8,128)(2,1)S(1)} %get-tuple-element.28), channel_id=1, source_target_pairs={{0,8},{8,0},{16,24},{24,16},{1,9},{9,1},{17,25},{25,17},{2,10},{10... | collective-permute-start | bytes 589832 | tf_op jit(solution)/shard_map/ppermute | solution.py:534
  5.6 16.0 %collective-permute-start.1 = (bf16[768,128]{1,0:T(8,128)(2,1)S(1)}, bf16[768,128]{1,0:T(8,128)(2,1)S(1)}, u32[]{:S(2)}, u32[]{:S(2)}) collective-permute-start(bf16[768,128]{1,0:T(8,128)(2,1)S(1)} %get-tuple-element.29), channel_id=1, source_target_pairs={{0,16},{8,24},{16,0},{24,8},{1,17},{9,25},{17,1},{25,9},{2,18},{10... | collective-permute-start | bytes 589832 | tf_op jit(solution)/shard_map/ppermute | solution.py:534
  7.2 14.5 %collective-permute-start.2 = (bf16[768,128]{1,0:T(8,128)(2,1)S(1)}, bf16[768,128]{1,0:T(8,128)(2,1)S(1)}, u32[]{:S(2)}, u32[]{:S(2)}) collective-permute-start(bf16[768,128]{1,0:T(8,128)(2,1)S(1)} %get-tuple-element.30), channel_id=1, source_target_pairs={{0,24},{8,16},{16,8},{24,0},{1,25},{9,17},{17,9},{25,1},{2,26},{10... | collective-permute-start | bytes 589832 | tf_op jit(solution)/shard_map/ppermute | solution.py:534
  9.0 15.6 %collective-permute-start.10 = (bf16[768,128]{1,0:T(8,128)(2,1)S(1)}, bf16[768,128]{1,0:T(8,128)(2,1)S(1)}, u32[]{:S(2)}, u32[]{:S(2)}) collective-permute-start(bf16[768,128]{1,0:T(8,128)(2,1)S(1)} %get-tuple-element.37), channel_id=1, source_target_pairs={{0,16},{8,24},{16,0},{24,8},{1,17},{9,25},{17,1},{25,9},{2,18},{10... | collective-permute-start | bytes 589832 | tf_op jit(solution)/shard_map/ppermute | solution.py:534
  11.1 13.6 %collective-permute-start.11 = (bf16[768,128]{1,0:T(8,128)(2,1)S(1)}, bf16[768,128]{1,0:T(8,128)(2,1)S(1)}, u32[]{:S(2)}, u32[]{:S(2)}) collective-permute-start(bf16[768,128]{1,0:T(8,128)(2,1)S(1)} %get-tuple-element.38), channel_id=1, source_target_pairs={{0,24},{8,16},{16,8},{24,0},{1,25},{9,17},{17,9},{25,1},{2,26},{10... | collective-permute-start | bytes 589832 | tf_op jit(solution)/shard_map/ppermute | solution.py:534
  12.5 12.1 %collective-permute-start.9 = (bf16[768,128]{1,0:T(8,128)(2,1)S(1)}, bf16[768,128]{1,0:T(8,128)(2,1)S(1)}, u32[]{:S(2)}, u32[]{:S(2)}) collective-permute-start(bf16[768,128]{1,0:T(8,128)(2,1)S(1)} %get-tuple-element.36), channel_id=1, source_target_pairs={{0,8},{8,0},{16,24},{24,16},{1,9},{9,1},{17,25},{25,17},{2,10},{10... | collective-permute-start | bytes 589832 | tf_op jit(solution)/shard_map/ppermute | solution.py:534
  28.3 18.0 %collective-permute-start.12 = (bf16[256,128]{1,0:T(8,128)(2,1)S(1)}, bf16[256,128]{1,0:T(8,128)(2,1)S(1)}, u32[]{:S(2)}, u32[]{:S(2)}) collective-permute-start(bf16[256,128]{1,0:T(8,128)(2,1)S(1)} %get-tuple-element.40), channel_id=1, source_target_pairs={{0,8},{8,0},{16,24},{24,16},{1,9},{9,1},{17,25},{25,17},{2,10},{10... | collective-permute-start | bytes 196616 | tf_op jit(solution)/shard_map/ppermute | solution.py:534
  28.7 17.6 %collective-permute-start.13 = (bf16[256,128]{1,0:T(8,128)(2,1)S(1)}, bf16[256,128]{1,0:T(8,128)(2,1)S(1)}, u32[]{:S(2)}, u32[]{:S(2)}) collective-permute-start(bf16[256,128]{1,0:T(8,128)(2,1)S(1)} %get-tuple-element.41), channel_id=1, source_target_pairs={{0,16},{8,24},{16,0},{24,8},{1,17},{9,25},{17,1},{25,9},{2,18},{10... | collective-permute-start | bytes 196616 | tf_op jit(solution)/shard_map/ppermute | solution.py:534
  30.4 16.0 %collective-permute-start.14 = (bf16[256,128]{1,0:T(8,128)(2,1)S(1)}, bf16[256,128]{1,0:T(8,128)(2,1)S(1)}, u32[]{:S(2)}, u32[]{:S(2)}) collective-permute-start(bf16[256,128]{1,0:T(8,128)(2,1)S(1)} %get-tuple-element.42), channel_id=1, source_target_pairs={{0,24},{8,16},{16,8},{24,0},{1,25},{9,17},{17,9},{25,1},{2,26},{10... | collective-permute-start | bytes 196616 | tf_op jit(solution)/shard_map/ppermute | solution.py:534
  34.1 4.3 %collective-permute-start.3 = (bf16[256,128]{1,0:T(8,128)(2,1)S(1)}, bf16[256,128]{1,0:T(8,128)(2,1)S(1)}, u32[]{:S(2)}, u32[]{:S(2)}) collective-permute-start(bf16[256,128]{1,0:T(8,128)(2,1)S(1)} %get-tuple-element.32), channel_id=1, source_target_pairs={{0,8},{8,0},{16,24},{24,16},{1,9},{9,1},{17,25},{25,17},{2,10},{10... | collective-permute-start | bytes 196616 | tf_op jit(solution)/shard_map/ppermute | solution.py:534
  34.6 5.4 %collective-permute-start.4 = (bf16[256,128]{1,0:T(8,128)(2,1)S(1)}, bf16[256,128]{1,0:T(8,128)(2,1)S(1)}, u32[]{:S(2)}, u32[]{:S(2)}) collective-permute-start(bf16[256,128]{1,0:T(8,128)(2,1)S(1)} %get-tuple-element.33), channel_id=1, source_target_pairs={{0,16},{8,24},{16,0},{24,8},{1,17},{9,25},{17,1},{25,9},{2,18},{10... | collective-permute-start | bytes 196616 | tf_op jit(solution)/shard_map/ppermute | solution.py:534
  38.5 5.2 %collective-permute-start.5 = (bf16[256,128]{1,0:T(8,128)(2,1)S(1)}, bf16[256,128]{1,0:T(8,128)(2,1)S(1)}, u32[]{:S(2)}, u32[]{:S(2)}) collective-permute-start(bf16[256,128]{1,0:T(8,128)(2,1)S(1)} %get-tuple-element.34), channel_id=1, source_target_pairs={{0,24},{8,16},{16,8},{24,0},{1,25},{9,17},{17,9},{25,1},{2,26},{10... | collective-permute-start | bytes 196616 | tf_op jit(solution)/shard_map/ppermute | solution.py:534
  43.6 11.4 %collective-permute-start.18 = (bf16[1024,128]{1,0:T(8,128)(2,1)S(1)}, bf16[1024,128]{1,0:T(8,128)(2,1)S(1)}, u32[]{:S(2)}, u32[]{:S(2)}) collective-permute-start(bf16[1024,128]{1,0:T(8,128)(2,1)S(1)} %constant_dynamic-update-slice_fusion.refs_0_), channel_id=1, source_target_pairs={{0,4},{1,5},{2,6},{3,7},{4,0},{5,1},{6,2},{7,3},{8,12},{9,13},{10,... | collective-permute-start | bytes 786440 | tf_op jit(solution)/shard_map/ppermute | solution.py:495
  46.4 11.1 %collective-permute-start.16 = (bf16[1024,128]{1,0:T(8,128)(2,1)S(1)}, bf16[1024,128]{1,0:T(8,128)(2,1)S(1)}, u32[]{:S(2)}, u32[]{:S(2)}) collective-permute-start(bf16[1024,128]{1,0:T(8,128)(2,1)S(1)} %constant_dynamic-update-slice_fusion.4.refs_4_), channel_id=1, source_target_pairs={{0,2},{1,3},{2,0},{3,1},{4,6},{5,7},{6,4},{7,5},{8,10},{9,11},{10,... | collective-permute-start | bytes 786440 | tf_op jit(solution)/shard_map/ppermute | solution.py:495
  48.0 9.4 %collective-permute-start.15 = (bf16[1024,128]{1,0:T(8,128)(2,1)S(1)}, bf16[1024,128]{1,0:T(8,128)(2,1)S(1)}, u32[]{:S(2)}, u32[]{:S(2)}) collective-permute-start(bf16[1024,128]{1,0:T(8,128)(2,1)S(1)} %constant_dynamic-update-slice_fusion.4.refs_4_), channel_id=1, source_target_pairs={{0,1},{1,0},{2,3},{3,2},{4,5},{5,4},{6,7},{7,6},{8,9},{9,8},{10,11... | collective-permute-start | bytes 786440 | tf_op jit(solution)/shard_map/ppermute | solution.py:499
  48.0 15.0 %collective-permute-start.7 = (bf16[1024,128]{1,0:T(8,128)(2,1)S(1)}, bf16[1024,128]{1,0:T(8,128)(2,1)S(1)}, u32[]{:S(2)}, u32[]{:S(2)}) collective-permute-start(bf16[1024,128]{1,0:T(8,128)(2,1)S(1)} %constant_dynamic-update-slice_fusion.refs_0_), channel_id=1, source_target_pairs={{0,2},{1,3},{2,0},{3,1},{4,6},{5,7},{6,4},{7,5},{8,10},{9,11},{10,... | collective-permute-start | bytes 786440 | tf_op jit(solution)/shard_map/ppermute | solution.py:495
  48.5 20.3 %collective-permute-start.20 = (bf16[1024,128]{1,0:T(8,128)(2,1)S(1)}, bf16[1024,128]{1,0:T(8,128)(2,1)S(1)}, u32[]{:S(2)}, u32[]{:S(2)}) collective-permute-start(bf16[1024,128]{1,0:T(8,128)(2,1)S(1)} %constant_dynamic-update-slice_fusion.refs_0_), channel_id=1, source_target_pairs={{2,4},{3,5},{4,2},{5,3},{10,12},{11,13},{12,10},{13,11},{18,20},{1... | collective-permute-start | bytes 786440 | tf_op jit(solution)/shard_map/ppermute | solution.py:483
  55.1 13.7 %collective-permute-start.21 = (bf16[1024,128]{1,0:T(8,128)(2,1)S(1)}, bf16[1024,128]{1,0:T(8,128)(2,1)S(1)}, u32[]{:S(2)}, u32[]{:S(2)}) collective-permute-start(bf16[1024,128]{1,0:T(8,128)(2,1)S(1)} %collective-permute-done.18.refs_0_), channel_id=1, source_target_pairs={{2,0},{3,1},{4,6},{5,7},{10,8},{11,9},{12,14},{13,15},{18,16},{19,... | collective-permute-start | bytes 786440 | tf_op jit(solution)/shard_map/ppermute | solution.py:485
  57.5 11.9 %collective-permute-start.6 = (bf16[1024,128]{1,0:T(8,128)(2,1)S(1)}, bf16[1024,128]{1,0:T(8,128)(2,1)S(1)}, u32[]{:S(2)}, u32[]{:S(2)}) collective-permute-start(bf16[1024,128]{1,0:T(8,128)(2,1)S(1)} %constant_dynamic-update-slice_fusion.refs_0_), channel_id=1, source_target_pairs={{0,1},{1,0},{2,3},{3,2},{4,5},{5,4},{6,7},{7,6},{8,9},{9,8},{10,11... | collective-permute-start | bytes 786440 | tf_op jit(solution)/shard_map/ppermute | solution.py:499
  57.5 22.3 %collective-permute-start.23 = (bf16[1024,128]{1,0:T(8,128)(2,1)S(1)}, bf16[1024,128]{1,0:T(8,128)(2,1)S(1)}, u32[]{:S(2)}, u32[]{:S(2)}) collective-permute-start(bf16[1024,128]{1,0:T(8,128)(2,1)S(1)} %constant_dynamic-update-slice_fusion.4.refs_4_), channel_id=1, source_target_pairs={{0,4},{1,5},{2,6},{3,7},{4,0},{5,1},{6,2},{7,3},{8,12},{9,13},{10,... | collective-permute-start | bytes 786440 | tf_op jit(solution)/shard_map/ppermute | solution.py:495
  63.1 16.8 %collective-permute-start.25 = (bf16[1024,128]{1,0:T(8,128)(2,1)S(1)}, bf16[1024,128]{1,0:T(8,128)(2,1)S(1)}, u32[]{:S(2)}, u32[]{:S(2)}) collective-permute-start(bf16[1024,128]{1,0:T(8,128)(2,1)S(1)} %constant_dynamic-update-slice_fusion.4.refs_4_), channel_id=1, source_target_pairs={{0,6},{1,7},{2,4},{3,5},{4,2},{5,3},{6,0},{7,1},{8,14},{9,15},{10,... | collective-permute-start | bytes 786440 | tf_op jit(solution)/shard_map/ppermute | solution.py:495
  68.8 11.5 %collective-permute-start.17 = (bf16[1024,128]{1,0:T(8,128)(2,1)S(1)}, bf16[1024,128]{1,0:T(8,128)(2,1)S(1)}, u32[]{:S(2)}, u32[]{:S(2)}) collective-permute-start(bf16[1024,128]{1,0:T(8,128)(2,1)S(1)} %collective-permute-done.16.refs_6_), channel_id=1, source_target_pairs={{0,1},{1,0},{2,3},{3,2},{4,5},{5,4},{6,7},{7,6},{8,9},{9,8},{10,11... | collective-permute-start | bytes 786440 | tf_op jit(solution)/shard_map/ppermute | solution.py:499
  68.8 11.5 %collective-permute-start.8 = (bf16[1024,128]{1,0:T(8,128)(2,1)S(1)}, bf16[1024,128]{1,0:T(8,128)(2,1)S(1)}, u32[]{:S(2)}, u32[]{:S(2)}) collective-permute-start(bf16[1024,128]{1,0:T(8,128)(2,1)S(1)} %collective-permute-done.7.refs_2_), channel_id=1, source_target_pairs={{0,1},{1,0},{2,3},{3,2},{4,5},{5,4},{6,7},{7,6},{8,9},{9,8},{10,11... | collective-permute-start | bytes 786440 | tf_op jit(solution)/shard_map/ppermute | solution.py:499
  69.4 13.0 %collective-permute-start.19 = (bf16[1024,128]{1,0:T(8,128)(2,1)S(1)}, bf16[1024,128]{1,0:T(8,128)(2,1)S(1)}, u32[]{:S(2)}, u32[]{:S(2)}) collective-permute-start(bf16[1024,128]{1,0:T(8,128)(2,1)S(1)} %collective-permute-done.18.refs_0_), channel_id=1, source_target_pairs={{0,1},{1,0},{2,3},{3,2},{4,5},{5,4},{6,7},{7,6},{8,9},{9,8},{10,11... | collective-permute-start | bytes 786440 | tf_op jit(solution)/shard_map/ppermute | solution.py:499
  79.7 2.7 %collective-permute-start.24 = (bf16[1024,128]{1,0:T(8,128)(2,1)S(1)}, bf16[1024,128]{1,0:T(8,128)(2,1)S(1)}, u32[]{:S(2)}, u32[]{:S(2)}) collective-permute-start(bf16[1024,128]{1,0:T(8,128)(2,1)S(1)} %collective-permute-done.23.refs_4_), channel_id=1, source_target_pairs={{0,1},{1,0},{2,3},{3,2},{4,5},{5,4},{6,7},{7,6},{8,9},{9,8},{10,11... | collective-permute-start | bytes 786440 | tf_op jit(solution)/shard_map/ppermute | solution.py:499
  79.8 2.6 %collective-permute-start.26 = (bf16[1024,128]{1,0:T(8,128)(2,1)S(1)}, bf16[1024,128]{1,0:T(8,128)(2,1)S(1)}, u32[]{:S(2)}, u32[]{:S(2)}) collective-permute-start(bf16[1024,128]{1,0:T(8,128)(2,1)S(1)} %collective-permute-done.25.refs_6_), channel_id=1, source_target_pairs={{0,1},{1,0},{2,3},{3,2},{4,5},{5,4},{6,7},{7,6},{8,9},{9,8},{10,11... | collective-permute-start | bytes 786440 | tf_op jit(solution)/shard_map/ppermute | solution.py:499
  80.3 2.2 %collective-permute-start.22 = (bf16[1024,128]{1,0:T(8,128)(2,1)S(1)}, bf16[1024,128]{1,0:T(8,128)(2,1)S(1)}, u32[]{:S(2)}, u32[]{:S(2)}) collective-permute-start(bf16[1024,128]{1,0:T(8,128)(2,1)S(1)} %add.12.refs_2_), channel_id=1, source_target_pairs={{0,1},{1,0},{2,3},{3,2},{4,5},{5,4},{6,7},{7,6},{8,9},{9,8},{10,11... | collective-permute-start | bytes 786440 | tf_op jit(solution)/shard_map/ppermute | solution.py:499
  82.3 12.1 %copy-start.11 = (s32[512]{0:T(512)S(1)}, s32[512]{0:T(512)}, u32[]{:S(2)}) copy-start(s32[512]{0:T(512)} %param.21) | copy-start | bytes 6148
  82.3 16.3 %copy-start.1 = (bf16[512,256]{1,0:T(8,128)(2,1)S(1)}, bf16[512,256]{1,0:T(8,128)(2,1)}, u32[]{:S(2)}) copy-start(bf16[512,256]{1,0:T(8,128)(2,1)} %constant.16.clone.fh_ref.fh) | copy-start | bytes 786436
  82.3 16.2 %copy-start.3 = (bf16[512,256]{1,0:T(8,128)(2,1)S(1)}, bf16[512,256]{1,0:T(8,128)(2,1)}, u32[]{:S(2)}) copy-start(bf16[512,256]{1,0:T(8,128)(2,1)} %constant.17.clone.fl_ref.fl) | copy-start | bytes 786436
  82.3 16.2 %copy-start.5 = (bf16[512,256]{1,0:T(8,128)(2,1)S(1)}, bf16[512,256]{1,0:T(8,128)(2,1)}, u32[]{:S(2)}) copy-start(bf16[512,256]{1,0:T(8,128)(2,1)} %filters_ref.1) | copy-start | bytes 786436
  82.4 22.8 %copy-start.2 = (bf16[256,512]{1,0:T(8,128)(2,1)S(1)}, bf16[256,512]{1,0:T(8,128)(2,1)}, u32[]{:S(2)}) copy-start(bf16[256,512]{1,0:T(8,128)(2,1)} %constant.18.clone.gh) | copy-start | bytes 786436
  82.4 22.7 %copy-start.6 = (bf16[256,512]{1,0:T(8,128)(2,1)S(1)}, bf16[256,512]{1,0:T(8,128)(2,1)}, u32[]{:S(2)}) copy-start(bf16[256,512]{1,0:T(8,128)(2,1)} %constant.19.clone.gl) | copy-start | bytes 786436
  82.4 22.7 %copy-start.9 = (f32[512]{0:T(512)S(1)}, f32[512]{0:T(512)}, u32[]{:S(2)}) copy-start(f32[512]{0:T(512)} %param.19) | copy-start | bytes 6148
  82.4 22.7 %copy-start.10 = (f32[512]{0:T(512)S(1)}, f32[512]{0:T(512)}, u32[]{:S(2)}) copy-start(f32[512]{0:T(512)} %param.22) | copy-start | bytes 6148
  85.1 22.2 %collective-permute-start.30 = (bf16[256,512]{1,0:T(8,128)(2,1)}, bf16[256,512]{1,0:T(8,128)(2,1)S(1)}, u32[]{:S(2)}, u32[]{:S(2)}) collective-permute-start(bf16[256,512]{1,0:T(8,128)(2,1)} %get-tuple-element.47), channel_id=1, source_target_pairs={{0,8},{8,0},{16,24},{24,16},{1,9},{9,1},{17,25},{25,17},{2,10},{10... | collective-permute-start | bytes 786440 | tf_op jit(solution)/shard_map/ppermute | solution.py:516
  86.4 20.9 %collective-permute-start.31 = (bf16[256,512]{1,0:T(8,128)(2,1)S(1)}, bf16[256,512]{1,0:T(8,128)(2,1)S(1)}, u32[]{:S(2)}, u32[]{:S(2)}) collective-permute-start(bf16[256,512]{1,0:T(8,128)(2,1)S(1)} %get-tuple-element.48), channel_id=1, source_target_pairs={{8,16},{16,8},{9,17},{17,9},{10,18},{18,10},{11,19},{19,11},{12,20... | collective-permute-start | bytes 786440 | tf_op jit(solution)/shard_map/ppermute | solution.py:516
  87.1 1.2 %collective-permute-start.27 = (f32[1,512]{1,0:T(1,128)S(1)}, f32[1,512]{1,0:T(1,128)S(1)}, u32[]{:S(2)}, u32[]{:S(2)}) collective-permute-start(f32[1,512]{1,0:T(1,128)S(1)} %get-tuple-element.44), channel_id=1, source_target_pairs={{0,1},{1,0},{2,3},{3,2},{4,5},{5,4},{6,7},{7,6},{8,9},{9,8},{10,11... | collective-permute-start | bytes 6152 | tf_op jit(solution)/shard_map/ppermute | solution.py:506
  88.3 7.7 %collective-permute-start.28 = (f32[1,512]{1,0:T(1,128)S(1)}, f32[1,512]{1,0:T(1,128)S(1)}, u32[]{:S(2)}, u32[]{:S(2)}) collective-permute-start(f32[1,512]{1,0:T(1,128)S(1)} %add.13), channel_id=1, source_target_pairs={{0,2},{1,3},{2,0},{3,1},{4,6},{5,7},{6,4},{7,5},{8,10},{9,11},{10,... | collective-permute-start | bytes 6152 | tf_op jit(solution)/shard_map/ppermute | solution.py:506
  96.0 4.5 %collective-permute-start.29 = (f32[1,512]{1,0:T(1,128)S(1)}, f32[1,512]{1,0:T(1,128)S(1)}, u32[]{:S(2)}, u32[]{:S(2)}) collective-permute-start(f32[1,512]{1,0:T(1,128)S(1)} %add.14), channel_id=1, source_target_pairs={{0,4},{1,5},{2,6},{3,7},{4,0},{5,1},{6,2},{7,3},{8,12},{9,13},{10,... | collective-permute-start | bytes 6152 | tf_op jit(solution)/shard_map/ppermute | solution.py:506
  100.5 6.8 %collective-permute-start.32 = (f32[1,512]{1,0:T(1,128)S(1)}, f32[1,512]{1,0:T(1,128)S(1)}, u32[]{:S(2)}, u32[]{:S(2)}) collective-permute-start(f32[1,512]{1,0:T(1,128)S(1)} %add.15.sq_ref), channel_id=1, source_target_pairs={{0,8},{8,0},{16,24},{24,16},{1,9},{9,1},{17,25},{25,17},{2,10},{10... | collective-permute-start | bytes 6152 | tf_op jit(solution)/shard_map/ppermute | solution.py:516
  104.3 3.1 %collective-permute-start.33 = (f32[1,512]{1,0:T(1,128)S(1)}, f32[1,512]{1,0:T(1,128)S(1)}, u32[]{:S(2)}, u32[]{:S(2)}) collective-permute-start(f32[1,512]{1,0:T(1,128)S(1)} %add.15.sq_ref), channel_id=1, source_target_pairs={{8,16},{16,8},{9,17},{17,9},{10,18},{18,10},{11,19},{19,11},{12,20... | collective-permute-start | bytes 6152 | tf_op jit(solution)/shard_map/ppermute | solution.py:516
